TPU v7x, 32 devices: a whole 2x2x4 slice. The times are simulated.
32 devices in a mesh: wide: 8 (over z, y), narrow: 4 (over x, core).
Axes of the slice: x: 2, y: 2, z: 4, core: 2. Of those that a mesh axis runs over, the one named last changes fastest.
Arguments:
- codons: int32 [32, 1024], P(('wide', 'narrow')), may hold values from 0 to 69
- offsets: int32 [32], P(('wide', 'narrow')), may hold values from 0 to 112
- positions: int32 [32, 912], P(('wide', 'narrow')), may hold values from 0 to 1023
- targets: int32 [32, 912], P(('wide', 'narrow')), may hold values from 0 to 69
- table_weight: float32 [70, 768], P(None, 'wide'), may hold values from -0.21875 to 0.21875
- attend_weight: float32 [2304, 768], P('wide'), may hold values from -0.21875 to 0.21875
- mixing_weight: float32 [768, 768], P('wide'), may hold values from -1.5 to 1.5
- expand_weight: float32 [3072, 768], P('wide'), may hold values from -0.21875 to 0.21875
- reduce_weight: float32 [3072, 768], P('wide'), may hold values from -0.109375 to 0.109375
- vector_params: float32 [15, 768], P(None, 'wide'), may hold values from -1.5 to 1.5
- attend_moment: float32 [2304, 768], P('wide'), may hold values from -10 to 10
- mixing_moment: float32 [768, 768], P('wide'), may hold values from -10 to 10
- expand_moment: float32 [3072, 768], P('wide'), may hold values from -10 to 10
- reduce_moment: float32 [3072, 768], P('wide'), may hold values from -10 to 10
- table_mean: float32 [70, 768], P(None, 'wide'), may hold values from -6 to 6
- table_square: float32 [70, 768], P(None, 'wide'), may hold values from 2.04288 to 29.184
- vector_mean: float32 [15, 768], P(None, 'wide'), may hold values from -2 to 2
- vector_square: float32 [15, 768], P(None, 'wide'), may hold values from 0.29184 to 4.96128
- step_count: int32 [], replicated, may hold values from 2 to 20
Outputs:
- block_output: bfloat16 [32, 912, 768], P(('wide', 'narrow'))
- entry_gradient: float32 [32, 912, 768], P(('wide', 'narrow'))
- attend_gradient: float32 [2304, 768], P('wide')
- mixing_gradient: float32 [768, 768], P('wide')
- expand_gradient: float32 [3072, 768], P('wide')
- reduce_gradient: float32 [3072, 768], P('wide')
- table_gradient: float32 [70, 768], P(None, 'wide')
- vector_gradient: float32 [15, 768], P(None, 'wide')
- attend_updated: float32 [2304, 768], P('wide')
- mixing_updated: float32 [768, 768], P('wide')
- expand_updated: float32 [3072, 768], P('wide')
- reduce_updated: float32 [3072, 768], P('wide')
- attend_momentum: float32 [2304, 768], P('wide')
- mixing_momentum: float32 [768, 768], P('wide')
- expand_momentum: float32 [3072, 768], P('wide')
- reduce_momentum: float32 [3072, 768], P('wide')
- table_updated: float32 [70, 768], P(None, 'wide')
- table_mean_next: float32 [70, 768], P(None, 'wide')
- table_square_next: float32 [70, 768], P(None, 'wide')
- vector_updated: float32 [15, 768], P(None, 'wide')
- vector_mean_next: float32 [15, 768], P(None, 'wide')
- vector_square_next: float32 [15, 768], P(None, 'wide')
- histogram: float32 [70], replicated
All inputs are finite; a program needn't handle non-finite values.
Results may differ from a plain program's by a relative error of at most 0.012.
The roundings to bfloat16 on the way count: a program that leaves them out, or rounds other values in their place, can miss the bound.
Values may be sent and summed in bfloat16 or wider, within the bound.
No kernel may reach another device: no remote copies, remote signals or barrier semaphores. Data moves between devices by JAX's collectives and lax.ppermute only.
A program may use at most 192 MiB of HBM per device.

v0:
```python
from functools import partial
import math

import jax
import jax.numpy as jnp
from jax import lax
from jax.sharding import PartitionSpec as P

D = 768
HEADS = 12
HEAD_DIM = 64
FF = 3072
VOCAB = 70
SEQ_LEN = 912
NS_ITERS = 5


NORM_EPS = 1e-05
ROPE_BASE = 10000.0
NEWTON_A = 3.4445
NEWTON_B = -4.775
NEWTON_C = 2.0315
MUON_MU = 0.95
MUON_RATE = 0.3
MUON_DECAY = 0.1
SHAPE_FACTOR = 0.2
ADAM_BETA1 = 0.9
ADAM_BETA2 = 0.95
ADAM_EPS = 1e-08
TABLE_RATE = 0.03
TABLE_DECAY = 0.01
VECTOR_RATE = 0.2


def times_plain(left_side, right_side):
    return jnp.dot(left_side, right_side, preferred_element_type=jnp.float32)


def times_trans(left_side, right_side):
    return lax.dot_general(
        left_side, right_side, (((1,), (1,)), ((), ())), preferred_element_type=jnp.float32
    )


def trans_times(left_side, right_side):
    return lax.dot_general(
        left_side, right_side, (((0,), (0,)), ((), ())), preferred_element_type=jnp.float32
    )


def exact_times(left_side, right_side):
    return jnp.dot(
        left_side, right_side, precision=lax.Precision.HIGHEST, preferred_element_type=jnp.float32
    )


def norm_forward(values, gain_row, bias_row):
    center = values - jnp.mean(values, axis=-1, keepdims=True)
    spread = jnp.mean(center * center, axis=-1, keepdims=True)
    inverse = lax.rsqrt(spread + NORM_EPS)
    normal = center * inverse
    return (normal * gain_row + bias_row, normal, inverse)


def norm_backward(upstream, normal, inverse, gain_row):
    scaled = upstream * gain_row
    inner_part = (
        scaled
        - jnp.mean(scaled, axis=-1, keepdims=True)
        - normal * jnp.mean(scaled * normal, axis=-1, keepdims=True)
    )
    return (inverse * inner_part, jnp.sum(upstream * normal, axis=0), jnp.sum(upstream, axis=0))


def rotary_tables(positions):
    half_dim = HEAD_DIM // 2
    frequency = ROPE_BASE ** (-(jnp.arange(half_dim, dtype=jnp.float32) * 2.0 / HEAD_DIM))
    turned = positions.astype(jnp.float32)[..., None] * frequency
    return (jnp.cos(turned)[..., None, :], jnp.sin(turned)[..., None, :])


def rotate(values, cosine, sine_table):
    half_dim = values.shape[-1] // 2
    first_half = values[..., :half_dim]
    second_half = values[..., half_dim:]
    return jnp.concatenate(
        [
            first_half * cosine - second_half * sine_table,
            second_half * cosine + first_half * sine_table,
        ],
        axis=-1,
    )


def unrotate(values, cosine, sine_table):
    half_dim = values.shape[-1] // 2
    first_half = values[..., :half_dim]
    second_half = values[..., half_dim:]
    return jnp.concatenate(
        [
            first_half * cosine + second_half * sine_table,
            second_half * cosine - first_half * sine_table,
        ],
        axis=-1,
    )


def attend_head(operands):
    query_head, key_head, value_head = operands
    scores = jnp.einsum(
        "sqd,skd->sqk", query_head, key_head, preferred_element_type=jnp.float32
    ) * HEAD_DIM ** (-0.5)
    row_peak = jnp.max(scores, axis=-1, keepdims=True)
    exp_scores = jnp.exp(scores - row_peak)
    row_total = jnp.sum(exp_scores, axis=-1, keepdims=True)
    prob_low = (exp_scores / row_total).astype(jnp.bfloat16)
    mixed_head = jnp.einsum(
        "sqk,skd->sqd", prob_low, value_head, preferred_element_type=jnp.float32
    )
    return (mixed_head, (row_peak + jnp.log(row_total))[..., 0])


def attend_back(operands):
    query_head, key_head, value_head, grad_head, log_total = operands
    scores = jnp.einsum(
        "sqd,skd->sqk", query_head, key_head, preferred_element_type=jnp.float32
    ) * HEAD_DIM ** (-0.5)
    prob_rows = jnp.exp(scores - log_total[..., None])
    prob_low = prob_rows.astype(jnp.bfloat16)
    value_grad = jnp.einsum("sqk,sqd->skd", prob_low, grad_head, preferred_element_type=jnp.float32)
    prob_grad = jnp.einsum(
        "sqd,skd->sqk", grad_head, value_head, preferred_element_type=jnp.float32
    )
    row_delta = jnp.sum(prob_grad * prob_rows, axis=-1, keepdims=True)
    score_grad = (prob_rows * (prob_grad - row_delta)).astype(jnp.bfloat16)
    query_grad = jnp.einsum(
        "sqk,skd->sqd", score_grad, key_head, preferred_element_type=jnp.float32
    ) * HEAD_DIM ** (-0.5)
    key_grad = jnp.einsum(
        "sqk,sqd->skd", score_grad, query_head, preferred_element_type=jnp.float32
    ) * HEAD_DIM ** (-0.5)
    return (query_grad, key_grad, value_grad)


def gram_block(matrices, row_span):
    return jnp.concatenate(
        [
            lax.dot_general(
                lax.slice_in_dim(matrix, 0, row_span, axis=1),
                matrix,
                (((0,), (0,)), ((), ())),
                precision=lax.Precision.HIGHEST,
                preferred_element_type=jnp.float32,
            )
            for matrix in matrices
        ],
        axis=1,
    )


def whole_gram(matrices, gram_rows):
    gram_part = lax.psum_scatter(
        gram_block(matrices, gram_rows * lax.axis_size(("wide", "narrow"))),
        ("wide", "narrow"),
        scatter_dimension=0,
        tiled=True,
    )
    return lax.all_gather(gram_part, ("wide", "narrow"), axis=0, tiled=True)


def orthogonal_rows(updates):
    gram_rows = D // lax.axis_size(("wide", "narrow"))
    squares = lax.psum(
        jnp.stack(
            [
                jnp.sum(updates[0] * updates[0]),
                jnp.sum(updates[1] * updates[1]),
                jnp.sum(updates[2] * updates[2]),
                jnp.sum(updates[3] * updates[3]),
            ]
        ),
        ("wide", "narrow"),
    )
    lengths = jnp.sqrt(squares) + 1e-07
    currents = tuple((updates[number] / lengths[number] for number in range(4)))
    gram_now = whole_gram(currents, gram_rows)
    for sweep_step in range(NS_ITERS):
        next_list = []
        for number in range(4):
            gram_piece = gram_now[:, number * D : (number + 1) * D]
            moved_rows = exact_times(currents[number], gram_piece)
            next_list.append(
                NEWTON_A * currents[number]
                + NEWTON_B * moved_rows
                + NEWTON_C * exact_times(moved_rows, gram_piece)
            )
        currents = tuple(next_list)
        if sweep_step + 1 < NS_ITERS:
            gram_now = whole_gram(currents, gram_rows)
    return currents


def muon_rows(weight_parts, moment_parts, grad_parts):
    moment_next = tuple(
        (
            MUON_MU * moment + (1.0 - MUON_MU) * gradient
            for moment, gradient in zip(moment_parts, grad_parts)
        )
    )
    updates = tuple(
        (
            (1.0 - MUON_MU) * gradient + MUON_MU * moment
            for moment, gradient in zip(moment_next, grad_parts)
        )
    )
    currents = orthogonal_rows(updates)
    rows_whole = (3 * D, D, FF, FF)
    updated = tuple(
        (
            weight_parts[number] * (1.0 - MUON_RATE * MUON_DECAY)
            - MUON_RATE * SHAPE_FACTOR * math.sqrt(max(rows_whole[number], D)) * currents[number]
            for number in range(4)
        )
    )
    return (updated, moment_next)


def adam_step(weight, mean_state, square, gradient, step_rate, decay_rate, step_count):
    mean_next = ADAM_BETA1 * mean_state + (1.0 - ADAM_BETA1) * gradient
    square_next = ADAM_BETA2 * square + (1.0 - ADAM_BETA2) * gradient * gradient
    step_float = step_count.astype(jnp.float32)
    mean_hat = mean_next / (1.0 - ADAM_BETA1**step_float)
    square_hat = square_next / (1.0 - ADAM_BETA2**step_float)
    updated = weight - step_rate * (
        mean_hat / (jnp.sqrt(square_hat) + ADAM_EPS) + decay_rate * weight
    )
    return (updated, mean_next, square_next)


def on_device(
    codons,
    offsets,
    positions,
    targets,
    table_weight,
    attend_weight,
    mixing_weight,
    expand_weight,
    reduce_weight,
    vector_params,
    attend_moment,
    mixing_moment,
    expand_moment,
    reduce_moment,
    table_mean,
    table_square,
    vector_mean,
    vector_square,
    step_count,
):
    low_type = jnp.bfloat16
    gathered = (
        lax.all_gather(table_weight.astype(low_type), "wide", axis=1, tiled=True),
        lax.all_gather(attend_weight.astype(low_type), "wide", axis=0, tiled=True),
        lax.all_gather(mixing_weight.astype(low_type), "wide", axis=0, tiled=True),
        lax.all_gather(expand_weight.astype(low_type), "wide", axis=0, tiled=True),
        lax.all_gather(reduce_weight.astype(low_type), "wide", axis=0, tiled=True),
        lax.all_gather(vector_params.astype(low_type), "wide", axis=1, tiled=True),
    )
    table_low, attend_low, mixing_low, expand_low, reduce_low, vector_low = gathered
    vector_full = vector_low.astype(jnp.float32)
    seq_count = codons.shape[0]
    row_count = seq_count * SEQ_LEN
    window = jax.vmap(partial(lax.dynamic_slice_in_dim, slice_size=SEQ_LEN))(codons, offsets)
    vocab_ids = jnp.arange(VOCAB, dtype=jnp.int32)
    token_hot = window.reshape(row_count)[:, None] == vocab_ids[None, :]
    target_hot = (targets.reshape(row_count)[:, None] == vocab_ids[None, :]).astype(jnp.float32)
    embed_scale = math.sqrt(D)
    stream = embed_scale * times_plain(token_hot.astype(low_type), table_low)
    gain_one = vector_full[0]
    bias_one = vector_full[1]
    gain_two = vector_full[2]
    bias_two = vector_full[3]
    gain_last = vector_full[4]
    bias_last = vector_full[5]
    attend_bias = vector_full[6:9].reshape(3 * D)
    mixing_bias = vector_full[9]
    reduce_bias = vector_full[10]
    expand_bias = vector_full[11:15].reshape(FF)
    normed_one, normal_one, inverse_one = norm_forward(stream, gain_one, bias_one)
    normed_one_low = normed_one.astype(low_type)
    projected = times_trans(normed_one_low, attend_low) + attend_bias
    cosine, sine_table = rotary_tables(positions)
    head_shape = (seq_count, SEQ_LEN, HEADS, HEAD_DIM)
    query_rot = rotate(projected[:, :D].reshape(head_shape), cosine, sine_table).astype(low_type)
    key_rot = rotate(projected[:, D : 2 * D].reshape(head_shape), cosine, sine_table).astype(
        low_type
    )
    value_low = projected[:, 2 * D :].reshape(head_shape).astype(low_type)
    query_heads = jnp.transpose(query_rot, (2, 0, 1, 3))
    key_heads = jnp.transpose(key_rot, (2, 0, 1, 3))
    value_heads = jnp.transpose(value_low, (2, 0, 1, 3))
    mixed_heads, log_totals = lax.map(attend_head, (query_heads, key_heads, value_heads))
    mixed_low = jnp.transpose(mixed_heads, (1, 2, 0, 3)).reshape(row_count, D).astype(low_type)
    branch = times_trans(mixed_low, mixing_low) + mixing_bias
    middle = stream + branch
    normed_two, normal_two, inverse_two = norm_forward(middle, gain_two, bias_two)
    normed_two_low = normed_two.astype(low_type)
    hidden_pre = times_trans(normed_two_low, expand_low) + expand_bias
    hidden_act, gelu_back = jax.vjp(partial(jax.nn.gelu, approximate=False), hidden_pre)
    hidden_low = hidden_act.astype(low_type)
    feed_out = times_plain(hidden_low, reduce_low) + reduce_bias
    output = middle + feed_out
    final_norm, normal_last, inverse_last = norm_forward(output, gain_last, bias_last)
    final_low = final_norm.astype(low_type)
    logits = times_trans(final_low, table_low)
    row_peak = jnp.max(logits, axis=-1, keepdims=True)
    shifted = jnp.exp(logits - row_peak)
    prob_rows = shifted / jnp.sum(shifted, axis=-1, keepdims=True)
    prob_total = lax.psum(jnp.sum(prob_rows, axis=0), ("wide", "narrow"))
    histogram = prob_total * (VOCAB / (row_count * lax.axis_size(("wide", "narrow"))))
    table_low, attend_low, mixing_low, expand_low, reduce_low = (
        lax.all_gather(table_weight.astype(low_type), "wide", axis=1, tiled=True),
        lax.all_gather(attend_weight.astype(low_type), "wide", axis=0, tiled=True),
        lax.all_gather(mixing_weight.astype(low_type), "wide", axis=0, tiled=True),
        lax.all_gather(expand_weight.astype(low_type), "wide", axis=0, tiled=True),
        lax.all_gather(reduce_weight.astype(low_type), "wide", axis=0, tiled=True),
    )
    logit_grad = (prob_rows - target_hot).astype(low_type)
    final_grad = times_plain(logit_grad, table_low)
    table_head = trans_times(logit_grad, final_low)
    output_grad, gain_last_grad, bias_last_grad = norm_backward(
        final_grad, normal_last, inverse_last, gain_last
    )
    feed_low = output_grad.astype(low_type)
    reduce_bias_grad = jnp.sum(feed_low, axis=0, dtype=jnp.float32)
    reduce_grad = trans_times(hidden_low, feed_low)
    hidden_grad = times_trans(feed_low, reduce_low)
    pre_grad = gelu_back(hidden_grad)[0].astype(low_type)
    expand_bias_grad = jnp.sum(pre_grad, axis=0, dtype=jnp.float32)
    expand_grad = trans_times(pre_grad, normed_two_low)
    normed_two_grad = times_plain(pre_grad, expand_low)
    middle_part, gain_two_grad, bias_two_grad = norm_backward(
        normed_two_grad, normal_two, inverse_two, gain_two
    )
    middle_grad = output_grad + middle_part
    branch_low = middle_grad.astype(low_type)
    mixing_bias_grad = jnp.sum(branch_low, axis=0, dtype=jnp.float32)
    mixing_grad = trans_times(branch_low, mixed_low)
    mixed_grad = times_plain(branch_low, mixing_low).astype(low_type)
    grad_heads = jnp.transpose(mixed_grad.reshape(head_shape), (2, 0, 1, 3))
    query_back, key_back, value_back = lax.map(
        attend_back, (query_heads, key_heads, value_heads, grad_heads, log_totals)
    )
    query_grad = unrotate(jnp.transpose(query_back, (1, 2, 0, 3)), cosine, sine_table).reshape(
        row_count, D
    )
    key_grad = unrotate(jnp.transpose(key_back, (1, 2, 0, 3)), cosine, sine_table).reshape(
        row_count, D
    )
    value_grad = jnp.transpose(value_back, (1, 2, 0, 3)).reshape(row_count, D)
    projected_low = jnp.concatenate([query_grad, key_grad, value_grad], axis=1).astype(low_type)
    attend_bias_grad = jnp.sum(projected_low, axis=0, dtype=jnp.float32)
    attend_grad = trans_times(projected_low, normed_one_low)
    normed_one_grad = times_plain(projected_low, attend_low)
    stream_part, gain_one_grad, bias_one_grad = norm_backward(
        normed_one_grad, normal_one, inverse_one, gain_one
    )
    entry_gradient = middle_grad + stream_part
    table_grad = (
        embed_scale * exact_times(token_hot.astype(jnp.float32).T, entry_gradient) + table_head
    )
    vector_grad = jnp.concatenate(
        [
            jnp.stack(
                [
                    gain_one_grad,
                    bias_one_grad,
                    gain_two_grad,
                    bias_two_grad,
                    gain_last_grad,
                    bias_last_grad,
                ]
            ),
            attend_bias_grad.reshape(3, D),
            mixing_bias_grad[None, :],
            reduce_bias_grad[None, :],
            expand_bias_grad.reshape(4, D),
        ],
        axis=0,
    )
    narrow_size = lax.axis_size("narrow")
    narrow_at = lax.axis_index("narrow")

    def rows_part(array):
        quarter = array.shape[0] // narrow_size
        return lax.dynamic_slice_in_dim(array, narrow_at * quarter, quarter, 0)

    weight_parts = (
        rows_part(attend_weight),
        rows_part(mixing_weight),
        rows_part(expand_weight),
        rows_part(reduce_weight),
    )
    moment_parts = (
        rows_part(attend_moment),
        rows_part(mixing_moment),
        rows_part(expand_moment),
        rows_part(reduce_moment),
    )
    wide_sums = (
        lax.psum_scatter(table_grad, "wide", scatter_dimension=1, tiled=True),
        lax.psum_scatter(attend_grad, "wide", scatter_dimension=0, tiled=True),
        lax.psum_scatter(mixing_grad, "wide", scatter_dimension=0, tiled=True),
        lax.psum_scatter(expand_grad, "wide", scatter_dimension=0, tiled=True),
        lax.psum_scatter(reduce_grad, "wide", scatter_dimension=0, tiled=True),
        lax.psum_scatter(vector_grad, "wide", scatter_dimension=1, tiled=True),
    )
    totals = lax.psum(
        (wide_sums[0], wide_sums[1], wide_sums[2], wide_sums[3], wide_sums[4], wide_sums[5]),
        "narrow",
    )
    matrix_new, moment_next = muon_rows(
        weight_parts,
        moment_parts,
        (rows_part(totals[1]), rows_part(totals[2]), rows_part(totals[3]), rows_part(totals[4])),
    )
    table_new, table_mean_next, table_square_next = adam_step(
        table_weight, table_mean, table_square, totals[0], TABLE_RATE, TABLE_DECAY, step_count
    )
    vector_new, vector_mean_next, vector_square_next = adam_step(
        vector_params, vector_mean, vector_square, totals[5], VECTOR_RATE, 0.0, step_count
    )
    rows_back = (
        lax.all_gather(matrix_new[0], "narrow", axis=0, tiled=True),
        lax.all_gather(matrix_new[1], "narrow", axis=0, tiled=True),
        lax.all_gather(matrix_new[2], "narrow", axis=0, tiled=True),
        lax.all_gather(matrix_new[3], "narrow", axis=0, tiled=True),
        lax.all_gather(moment_next[0], "narrow", axis=0, tiled=True),
        lax.all_gather(moment_next[1], "narrow", axis=0, tiled=True),
        lax.all_gather(moment_next[2], "narrow", axis=0, tiled=True),
        lax.all_gather(moment_next[3], "narrow", axis=0, tiled=True),
    )
    results = (
        (totals[1], totals[2], totals[3], totals[4], totals[0], totals[5])
        + tuple(rows_back)
        + (
            table_new,
            table_mean_next,
            table_square_next,
            vector_new,
            vector_mean_next,
            vector_square_next,
        )
    )
    block_output = output.astype(low_type).reshape(seq_count, SEQ_LEN, D)
    return (block_output, entry_gradient.reshape(seq_count, SEQ_LEN, D)) + results + (histogram,)


def solution(mesh):
    in_specs = (
        P(("wide", "narrow"), None),
        P(("wide", "narrow")),
        P(("wide", "narrow"), None),
        P(("wide", "narrow"), None),
        P(None, "wide"),
        P("wide", None),
        P("wide", None),
        P("wide", None),
        P("wide", None),
        P(None, "wide"),
        P("wide", None),
        P("wide", None),
        P("wide", None),
        P("wide", None),
        P(None, "wide"),
        P(None, "wide"),
        P(None, "wide"),
        P(None, "wide"),
        P(),
    )
    out_specs = (
        P(("wide", "narrow"), None, None),
        P(("wide", "narrow"), None, None),
        P("wide", None),
        P("wide", None),
        P("wide", None),
        P("wide", None),
        P(None, "wide"),
        P(None, "wide"),
        P("wide", None),
        P("wide", None),
        P("wide", None),
        P("wide", None),
        P("wide", None),
        P("wide", None),
        P("wide", None),
        P("wide", None),
        P(None, "wide"),
        P(None, "wide"),
        P(None, "wide"),
        P(None, "wide"),
        P(None, "wide"),
        P(None, "wide"),
        P(),
    )
    return jax.shard_map(
        on_device, mesh=mesh, in_specs=in_specs, out_specs=out_specs, check_vma=False
    )
```

profile of v0, /device:TPU:0, one launch (start us, length us, event | category | flops | bytes accessed | tf_op | source)
XLA Modules:
  0.0 2590.1 jit_solution(14955150038789130338)
XLA Ops:
  13.4 32.4 %all-gather.1 = bf16[8,96,15]{1,2,0:T(8,128)(2,1)S(1)} all-gather(bf16[1,96,15]{1,2,0:T(8,128)(2,1)S(1)} %convert_bitcast_fusion.2), channel_id=1, replica_groups=mesh['wide'=8,'narrow'=4] {'wide'}, dimensions={0}, use_global_device_ids=true | all-gather | bytes 25920 | tf_op jit(solution)/shard_map/all_gather | solution.py:268
  47.7 31.5 %all-gather = bf16[8,96,70]{1,2,0:T(8,128)(2,1)S(1)} all-gather(bf16[1,96,70]{1,2,0:T(8,128)(2,1)S(1)} %convert_bitcast_fusion.1), channel_id=1, replica_groups=mesh['wide'=8,'narrow'=4] {'wide'}, dimensions={0}, use_global_device_ids=true | all-gather | bytes 120960 | tf_op jit(solution)/shard_map/all_gather | solution.py:263
  82.1 5.8 convolution_add_fusion
  105.1 4.1 copy.92
  109.2 4.1 copy.93
  115.8 4.1 copy.94
  119.9 66.0 %while.29 = (s32[]{:T(128)}, bf16[12,1,912,64]{2,3,1,0:T(8,128)(2,1)}, f32[12,1,912]{2,1,0:T(1,128)}, bf16[12,1,912,64]{3,2,1,0:T(8,128)(2,1)}, bf16[12,1,912,64...) while((s32[]{:T(128)}, bf16[12,1,912,64]{2,3,1,0:T(8,128)(2,1)}, f32[12,1,912]{2,1,0:T(1,128)}, ...), condition=%wide.region_5.6_spmd.clone, body=%wide.region_2.5_spmd.sunk.clone | while | flops 220411248 | bytes 10982545 | solution.py:303
  191.3 13.8 all-gather.20.cloned.1.call-done
  205.1 33.3 %multiply_convert_fusion.1 = (bf16[912,3072]{1,0:T(8,128)(2,1)}, f32[912,3072]{1,0:T(8,128)}, f32[912,3072]{1,0:T(8,128)}) fusion(f32[3072]{0:T(1024)S(1)} %add.396, bf16[3072,768]{1,0:T(8,128)(2,1)} %all-gather.20.cloned.1.call-done, f32[912,768]{1,0:T(8,128)} %copy-done.14, f32[768]{0:T(1024)S(1)} %get-tuple-element.196, f32[768]{0:T(1024)S(1)} %get-tuple-element.197, ...), kind=kOutput, calls=%fused_computation.59 | convolution fusion | flops 4491767808 | bytes 35562624 | tf_op jit(solution)/shard_map/dot_general | solution.py:40
  238.5 47.3 %all-gather.22.cloned.1.call-done = bf16[3072,768]{1,0:T(8,128)(2,1)} async-done(((bf16[384,768]{1,0:T(8,128)(2,1)}), bf16[3072,768]{1,0:T(8,128)(2,1)}) %all-gather.22.cloned.1.call-update) | async-done | bytes 4718608 | tf_op jit(solution)/shard_map/all_gather | solution.py:267
  285.8 8.7 fusion.308
  301.0 17.6 convert_reduce_fusion
  318.6 9.9 multiply_reduce_fusion.3
  338.5 134.1 %while.30 = (s32[]{:T(128)}, f32[12,1,912,64]{2,3,1,0:T(8,128)}, f32[12,1,912,64]{2,3,1,0:T(8,128)}, bf16[12,1,912,64]{2,3,1,0:T(8,128)(2,1)}, bf16[12,1,912,64]...) while((s32[]{:T(128)}, f32[12,1,912,64]{2,3,1,0:T(8,128)}, ...), condition=%wide.region_18.19_spmd.clone, body=%wide.region_16.18_spmd.sunk.clone | while | flops 542412928 | bytes 28017064 | solution.py:352
  479.9 7.2 fusion.280
  487.2 10.8 fusion.299
  498.1 10.2 fusion.291
  508.3 106.1 %reduce-scatter.26.cloned.1.call-done = f32[288,768]{1,0:T(8,128)} async-done(((f32[2304,768]{1,0:T(8,128)}), f32[288,768]{1,0:T(8,128)}) %reduce-scatter.26.cloned.1.call-update) | async-done | bytes 884752 | tf_op jit(solution)/shard_map/reduce_scatter | solution.py:413
  614.4 166.4 %reduce-scatter.30.cloned.1.call-done = f32[384,768]{1,0:T(8,128)} async-done(((f32[3072,768]{1,0:T(8,128)}), f32[384,768]{1,0:T(8,128)}) %reduce-scatter.30.cloned.1.call-update) | async-done | bytes 1179664 | tf_op jit(solution)/shard_map/reduce_scatter | solution.py:415
  780.8 166.4 %reduce-scatter.32.cloned.1.call-done = f32[384,768]{1,0:T(8,128)} async-done(((f32[3072,768]{1,0:T(8,128)}), f32[384,768]{1,0:T(8,128)}) %reduce-scatter.32.cloned.1.call-update) | async-done | bytes 1179664 | tf_op jit(solution)/shard_map/reduce_scatter | solution.py:416
  947.5 77.0 %all-reduce.5.cloned.1.call-done = (f32[288,768]{1,0:T(8,128)}, f32[96,768]{1,0:T(8,128)}, f32[384,768]{1,0:T(8,128)}, f32[384,768]{1,0:T(8,128)}) async-done(((f32[288,768]{1,0:T(8,128)}, f32[96,768]{1,0:T(8,128)}, f32[384,768]{1,0:T(8,128)}, f32[384,768]{1,0:T(8,128)}), (f32[288,768]{1,0:T(8,128)}, f32[96,768]{1,0:T(8,128)}, f32[384,768]{1,0:T(8,128)}, f32[384,768]{1,0:T(8,128)})) %all-reduce.5.cloned.1.call-update) | async-done | bytes 3538960 | tf_op jit(solution)/shard_map/psum | solution.py:419
  1035.5 39.8 %all-reduce = (f32[4]{0:T(128)S(1)}, f32[70]{0:T(128)}) all-reduce(f32[4]{0:T(128)S(1)} %pad_maximum_fusion.8, f32[70]{0:T(128)S(1)} %fusion.285), channel_id=1, replica_groups=mesh['wide'=8,'narrow'=4] {'wide','narrow'}, use_global_device_ids=true, to_apply=%region_47.48 | all-reduce | flops 74 | bytes 592 | tf_op jit(solution)/shard_map/psum | solution.py:173
  1092.2 4.0 pad_maximum_fusion
  1096.2 9.6 copy.111
  1105.9 136.4 %reduce-scatter.38.cloned.1.call-done = f32[24,3072]{1,0:T(8,128)} async-done(((f32[768,3072]{1,0:T(8,128)}), f32[24,3072]{1,0:T(8,128)}) %reduce-scatter.38.cloned.1.call-update) | async-done | bytes 294928 | tf_op jit(solution)/shard_map/reduce_scatter | solution.py:162
  1242.6 83.7 %all-gather.24.cloned.1.call-done = f32[768,3072]{1,0:T(8,128)} async-done(((f32[24,3072]{1,0:T(8,128)}), f32[768,3072]{1,0:T(8,128)}) %all-gather.24.cloned.1.call-update) | async-done | bytes 9437200 | tf_op jit(solution)/shard_map/all_gather | solution.py:168
  1352.7 4.0 pad_maximum_fusion.1
  1356.7 9.6 copy.113
  1366.4 134.1 %reduce-scatter.40.cloned.1.call-done = f32[24,3072]{1,0:T(8,128)} async-done(((f32[768,3072]{1,0:T(8,128)}), f32[24,3072]{1,0:T(8,128)}) %reduce-scatter.40.cloned.1.call-update) | async-done | bytes 294928 | tf_op jit(solution)/shard_map/reduce_scatter | solution.py:162
  1500.6 84.6 %all-gather.26.cloned.1.call-done = f32[768,3072]{1,0:T(8,128)} async-done(((f32[24,3072]{1,0:T(8,128)}), f32[768,3072]{1,0:T(8,128)}) %all-gather.26.cloned.1.call-update) | async-done | bytes 9437200 | tf_op jit(solution)/shard_map/all_gather | solution.py:168
  1615.2 9.6 copy.115
  1624.9 134.2 %reduce-scatter.42.cloned.1.call-done = f32[24,3072]{1,0:T(8,128)} async-done(((f32[768,3072]{1,0:T(8,128)}), f32[24,3072]{1,0:T(8,128)}) %reduce-scatter.42.cloned.1.call-update) | async-done | bytes 294928 | tf_op jit(solution)/shard_map/reduce_scatter | solution.py:162
  1759.6 83.4 %all-gather.28.cloned.1.call-done = f32[768,3072]{1,0:T(8,128)} async-done(((f32[24,3072]{1,0:T(8,128)}), f32[768,3072]{1,0:T(8,128)}) %all-gather.28.cloned.1.call-update) | async-done | bytes 9437200 | tf_op jit(solution)/shard_map/all_gather | solution.py:168
  1873.1 9.6 copy.117
  1882.8 134.1 %reduce-scatter.44.cloned.1.call-done = f32[24,3072]{1,0:T(8,128)} async-done(((f32[768,3072]{1,0:T(8,128)}), f32[24,3072]{1,0:T(8,128)}) %reduce-scatter.44.cloned.1.call-update) | async-done | bytes 294928 | tf_op jit(solution)/shard_map/reduce_scatter | solution.py:162
  2016.9 84.4 %all-gather.30.cloned.1.call-done = f32[768,3072]{1,0:T(8,128)} async-done(((f32[24,3072]{1,0:T(8,128)}), f32[768,3072]{1,0:T(8,128)}) %all-gather.30.cloned.1.call-update) | async-done | bytes 9437200 | tf_op jit(solution)/shard_map/all_gather | solution.py:168
  2130.9 9.6 copy.119
  2140.6 134.2 %reduce-scatter.46.cloned.1.call-done = f32[24,3072]{1,0:T(8,128)} async-done(((f32[768,3072]{1,0:T(8,128)}), f32[24,3072]{1,0:T(8,128)}) %reduce-scatter.46.cloned.1.call-update) | async-done | bytes 294928 | tf_op jit(solution)/shard_map/reduce_scatter | solution.py:162
  2275.0 9.1 multiply_reduce_fusion.4
  2295.9 62.9 %all-gather.32.cloned.1.call-done = f32[768,3072]{1,0:T(8,128)} async-done(((f32[24,3072]{1,0:T(8,128)}), f32[768,3072]{1,0:T(8,128)}) %all-gather.32.cloned.1.call-update) | async-done | bytes 9437200 | tf_op jit(solution)/shard_map/all_gather | solution.py:168
  2366.8 55.8 %reduce-scatter.36.cloned.1.call-done = f32[96,15]{1,0:T(8,128)} async-done(((f32[768,15]{1,0:T(8,128)}), f32[96,15]{1,0:T(8,128)}) %reduce-scatter.36.cloned.1.call-update) | async-done | bytes 5776
  2423.4 63.4 %reduce-scatter.34.cloned.1.call-done = f32[96,70]{1,0:T(8,128)} async-done(((f32[768,70]{1,0:T(8,128)}), f32[96,70]{1,0:T(8,128)}) %reduce-scatter.34.cloned.1.call-update) | async-done | bytes 26896
  2487.7 10.5 all-reduce.1
  2499.6 10.1 all_gather.77
  2509.7 6.5 all_gather.78
  2534.2 13.3 all_gather.73
  2553.3 6.2 all_gather.74
  2559.5 10.6 all-gather.36.cloned.1.call-done
  (575 shorter events, 462.1 us)
Async XLA Ops:
  7.2 72.9 %copy-start = (s32[1,1024]{1,0:T(1,128)S(1)}, s32[1,1024]{1,0:T(1,128)}, u32[]{:S(2)}) copy-start(s32[1,1024]{1,0:T(1,128)} %param.23) | copy-start | bytes 12292
  7.2 74.9 %all-gather.16.cloned.1.call-start = ((), (), s32[]{:S(2)}) async-start(), calls=%async_computation.11 | async-start | bytes 3981312 | tf_op jit(solution)/shard_map/all_gather | solution.py:264
  9.4 176.4 %all-gather.18.cloned.1.call-start = ((), (), s32[]{:S(2)}) async-start(), calls=%async_computation.12 | async-start | bytes 1327104 | tf_op jit(solution)/shard_map/all_gather | solution.py:265
  11.2 194.0 %all-gather.20.cloned.1.call-start = ((), (), s32[]{:S(2)}) async-start(), calls=%async_computation.13 | async-start | bytes 5308416 | tf_op jit(solution)/shard_map/all_gather | solution.py:266
  12.1 273.7 %all-gather.22.cloned.1.call-start = ((), (), s32[]{:S(2)}) async-start(), calls=%async_computation.14 | async-start | bytes 5308416 | tf_op jit(solution)/shard_map/all_gather | solution.py:267
  13.1 495.2 %reduce-scatter.28.cloned.1.call-start = ((), (), s32[]{:S(2)}) async-start(), calls=%async_computation.16 | async-start | bytes 2654208 | tf_op jit(solution)/shard_map/reduce_scatter | solution.py:414
  13.3 66.8 %copy-start.8 = (bf16[12,1,912,64]{2,3,1,0:T(8,128)(2,1)}, bf16[12,1,912,64]{2,3,1,0:T(8,128)(2,1)S(1)}, u32[]{:S(2)}) copy-start(bf16[12,1,912,64]{2,3,1,0:T(8,128)(2,1)S(1)} %fusion.305) | copy-start | bytes 4202500
  80.9 105.0 %copy-start.6 = (f32[912,768]{1,0:T(8,128)}, f32[912,768]{1,0:T(8,128)S(1)}, u32[]{:S(2)}) copy-start(f32[912,768]{1,0:T(8,128)S(1)} %get-tuple-element.287) | copy-start | bytes 8404996
  205.1 80.7 %copy-start.15 = (f32[912,768]{1,0:T(8,128)S(1)}, f32[912,768]{1,0:T(8,128)}, u32[]{:S(2)}) copy-start(f32[912,768]{1,0:T(8,128)} %copy-done.14) | copy-start | bytes 8404996
  205.1 80.7 %copy-start.94 = (f32[768]{0:T(1024)S(1)}, f32[768]{0:T(1024)}, u32[]{:S(2)}) copy-start(f32[768]{0:T(1024)} %get-tuple-element.195) | copy-start | bytes 9220
  296.5 650.9 %copy-start.44 = (f32[912,70]{0,1:T(8,128)}, f32[912,70]{0,1:T(8,128)S(1)}, u32[]{:S(2)}) copy-start(f32[912,70]{0,1:T(8,128)S(1)} %get-tuple-element.294) | copy-start | bytes 766084
  296.6 650.8 %copy-start.83 = (f32[912]{0:T(1024)}, f32[912]{0:T(1024)S(1)}, u32[]{:S(2)}) copy-start(f32[912]{0:T(1024)S(1)} %fusion.282) | copy-start | bytes 10948
  338.5 276.0 %reduce-scatter.26.cloned.1.call-start = ((), (), s32[]{:S(2)}) async-start(), calls=%async_computation.15 | async-start | bytes 7962624 | tf_op jit(solution)/shard_map/reduce_scatter | solution.py:413
  338.5 134.1 %copy-start.55 = (f32[912,32]{0,1:T(8,128)S(1)}, f32[912,32]{0,1:T(8,128)}, u32[]{:S(2)}) copy-start(f32[912,32]{0,1:T(8,128)} %copy-done.54) | copy-start | bytes 350212
  338.5 134.1 %copy-start.57 = (f32[912,32]{0,1:T(8,128)S(1)}, f32[912,32]{0,1:T(8,128)}, u32[]{:S(2)}) copy-start(f32[912,32]{0,1:T(8,128)} %copy-done.56) | copy-start | bytes 350212
  487.1 293.7 %reduce-scatter.30.cloned.1.call-start = ((), (), s32[]{:S(2)}) async-start(), calls=%async_computation.17 | async-start | bytes 10616832 | tf_op jit(solution)/shard_map/reduce_scatter | solution.py:415
  498.0 449.3 %reduce-scatter.32.cloned.1.call-start = ((), (), s32[]{:S(2)}) async-start(), calls=%async_computation.18 | async-start | bytes 10616832 | tf_op jit(solution)/shard_map/reduce_scatter | solution.py:416
  508.3 516.3 %all-reduce.5.cloned.1.call-start = ((), (), s32[]{:S(2)}) async-start(), calls=%async_computation.35 | async-start | bytes 7077888 | tf_op jit(solution)/shard_map/psum | solution.py:419
  947.3 295.1 %reduce-scatter.38.cloned.1.call-start = ((), (), s32[]{:S(2)}) async-start(), calls=%async_computation.30 | async-start | bytes 9732096 | tf_op jit(solution)/shard_map/reduce_scatter | solution.py:162
  1026.3 54.7 %copy-start.48 = (f32[96,768]{1,0:T(8,128)}, f32[96,768]{1,0:T(8,128)S(1)}, u32[]{:S(2)}) copy-start(f32[96,768]{1,0:T(8,128)S(1)} %get-tuple-element.252) | copy-start | bytes 884740
  1105.9 220.5 %all-gather.24.cloned.1.call-start = ((), (), s32[]{:S(2)}) async-start(), calls=%async_computation.19 | async-start | bytes 9732096 | tf_op jit(solution)/shard_map/all_gather | solution.py:168
  1242.4 258.1 %reduce-scatter.40.cloned.1.call-start = ((), (), s32[]{:S(2)}) async-start(), calls=%async_computation.31 | async-start | bytes 9732096 | tf_op jit(solution)/shard_map/reduce_scatter | solution.py:162
  1366.4 218.7 %all-gather.26.cloned.1.call-start = ((), (), s32[]{:S(2)}) async-start(), calls=%async_computation.20 | async-start | bytes 9732096 | tf_op jit(solution)/shard_map/all_gather | solution.py:168
  1500.5 258.6 %reduce-scatter.42.cloned.1.call-start = ((), (), s32[]{:S(2)}) async-start(), calls=%async_computation.32 | async-start | bytes 9732096 | tf_op jit(solution)/shard_map/reduce_scatter | solution.py:162
  1624.8 218.2 %copy-start.19 = (f32[96,768]{1,0:T(8,128)S(1)}, f32[96,768]{1,0:T(8,128)}, u32[]{:S(2)}) copy-start(f32[96,768]{1,0:T(8,128)} %copy-done.18) | copy-start | bytes 884740
  1624.8 226.9 %copy-start.21 = (f32[96,768]{1,0:T(8,128)S(1)}, f32[96,768]{1,0:T(8,128)}, u32[]{:S(2)}) copy-start(f32[96,768]{1,0:T(8,128)} %copy-done.20) | copy-start | bytes 884740
  1624.8 218.2 %all-gather.28.cloned.1.call-start = ((), (), s32[]{:S(2)}) async-start(), calls=%async_computation.21 | async-start | bytes 9732096 | tf_op jit(solution)/shard_map/all_gather | solution.py:168
  1759.1 257.7 %reduce-scatter.44.cloned.1.call-start = ((), (), s32[]{:S(2)}) async-start(), calls=%async_computation.33 | async-start | bytes 9732096 | tf_op jit(solution)/shard_map/reduce_scatter | solution.py:162
  1882.7 218.6 %copy-start.23 = (f32[96,768]{1,0:T(8,128)S(1)}, f32[96,768]{1,0:T(8,128)}, u32[]{:S(2)}) copy-start(f32[96,768]{1,0:T(8,128)} %copy-done.22) | copy-start | bytes 884740
  1882.7 227.3 %copy-start.25 = (f32[96,768]{1,0:T(8,128)S(1)}, f32[96,768]{1,0:T(8,128)}, u32[]{:S(2)}) copy-start(f32[96,768]{1,0:T(8,128)} %copy-done.24) | copy-start | bytes 884740
  1882.7 218.6 %all-gather.30.cloned.1.call-start = ((), (), s32[]{:S(2)}) async-start(), calls=%async_computation.22 | async-start | bytes 9732096 | tf_op jit(solution)/shard_map/all_gather | solution.py:168
  2016.9 257.9 %reduce-scatter.46.cloned.1.call-start = ((), (), s32[]{:S(2)}) async-start(), calls=%async_computation.34 | async-start | bytes 9732096 | tf_op jit(solution)/shard_map/reduce_scatter | solution.py:162
  2140.6 218.2 %all-gather.32.cloned.1.call-start = ((), (), s32[]{:S(2)}) async-start(), calls=%async_computation.23 | async-start | bytes 9732096 | tf_op jit(solution)/shard_map/all_gather | solution.py:168
  2274.9 147.7 %reduce-scatter.36.cloned.1.call-start = ((), (), s32[]{:S(2)}) async-start(), calls=%async_computation.29 | async-start | bytes 442368
  2292.7 194.1 %reduce-scatter.34.cloned.1.call-start = ((), (), s32[]{:S(2)}) async-start(), calls=%async_computation.28 | async-start | bytes 442368
  2294.3 229.7 %all-gather.38.cloned.1.call-start = ((), (), s32[]{:S(2)}) async-start(), calls=%async_computation.26 | async-start | bytes 1474560 | tf_op jit(solution)/shard_map/all_gather | solution.py:441
  2295.1 232.7 %all-gather.40.cloned.1.call-start = ((), (), s32[]{:S(2)}) async-start(), calls=%async_computation.27 | async-start | bytes 1474560 | tf_op jit(solution)/shard_map/all_gather | solution.py:442
  2295.8 202.5 %copy-start.78 = (f32[15,96]{1,0:T(8,128)S(1)}, f32[15,96]{1,0:T(8,128)}, u32[]{:S(2)}) copy-start(f32[15,96]{1,0:T(8,128)} %param.32) | copy-start | bytes 17284
  2295.8 202.5 %copy-start.89 = (f32[15,96]{1,0:T(8,128)S(1)}, f32[15,96]{1,0:T(8,128)}, u32[]{:S(2)}) copy-start(f32[15,96]{1,0:T(8,128)} %param.40) | copy-start | bytes 17284
  2295.8 202.5 %copy-start.90 = (f32[15,96]{1,0:T(8,128)S(1)}, f32[15,96]{1,0:T(8,128)}, u32[]{:S(2)}) copy-start(f32[15,96]{1,0:T(8,128)} %param.39) | copy-start | bytes 17284
  2295.9 203.1 %copy-start.68 = (f32[70,96]{1,0:T(8,128)S(1)}, f32[70,96]{1,0:T(8,128)}, u32[]{:S(2)}) copy-start(f32[70,96]{1,0:T(8,128)} %param.27) | copy-start | bytes 80644
  2295.9 203.1 %copy-start.73 = (f32[70,96]{1,0:T(8,128)S(1)}, f32[70,96]{1,0:T(8,128)}, u32[]{:S(2)}) copy-start(f32[70,96]{1,0:T(8,128)} %param.38) | copy-start | bytes 80644
  2295.9 203.1 %copy-start.74 = (f32[70,96]{1,0:T(8,128)S(1)}, f32[70,96]{1,0:T(8,128)}, u32[]{:S(2)}) copy-start(f32[70,96]{1,0:T(8,128)} %param.37) | copy-start | bytes 80644
  2295.9 263.6 %all-gather.34.cloned.1.call-start = ((), (), s32[]{:S(2)}) async-start(), calls=%async_computation.24 | async-start | bytes 1474560 | tf_op jit(solution)/shard_map/all_gather | solution.py:437
  2362.0 137.7 %copy-start.50 = (f32[72,768]{1,0:T(8,128)S(1)}, f32[72,768]{1,0:T(8,128)}, u32[]{:S(2)}) copy-start(f32[72,768]{1,0:T(8,128)} %get-tuple-element.246) | copy-start | bytes 663556
  2362.0 147.8 %copy-start.66 = (f32[24,768]{1,0:T(8,128)S(1)}, f32[24,768]{1,0:T(8,128)}, u32[]{:S(2)}) copy-start(f32[24,768]{1,0:T(8,128)} %copy-done.65) | copy-start | bytes 221188
  2362.0 154.3 %copy-start.27 = (f32[96,768]{1,0:T(8,128)S(1)}, f32[96,768]{1,0:T(8,128)}, u32[]{:S(2)}) copy-start(f32[96,768]{1,0:T(8,128)} %copy-done.26) | copy-start | bytes 884740
  2366.0 204.1 %all-gather.36.cloned.1.call-start = ((), (), s32[]{:S(2)}) async-start(), calls=%async_computation.25 | async-start | bytes 1474560 | tf_op jit(solution)/shard_map/all_gather | solution.py:438
  (80 other events, 595.2 us)
Sparse Core Ops, SparseCore 0:
  10.8 70.3 all-gather.15
  84.0 39.6 all-gather.17
  126.5 78.6 all-gather.19
  207.8 78.0 all-gather.21
  338.6 67.1 reduce-scatter.27
  487.3 127.1 reduce-scatter.25
  618.5 162.3 reduce-scatter.29
  784.9 162.3 reduce-scatter.31
  950.1 74.4 all-reduce.4
  1106.0 136.3 reduce-scatter.37
  1245.3 81.0 all-gather.23
  1366.5 133.9 reduce-scatter.39
  1503.8 81.2 all-gather.25
  1625.0 134.0 reduce-scatter.41
  1761.8 81.1 all-gather.27
  1882.9 133.9 reduce-scatter.43
  2020.0 81.2 all-gather.29
  2140.7 134.0 reduce-scatter.45
  2277.7 81.0 all-gather.31
  2362.5 60.0 reduce-scatter.35
  2426.4 60.4 reduce-scatter.33
  2489.0 17.2 all-gather.37
  2508.5 19.2 all-gather.39
  2529.8 20.6 all-gather.33
  2552.6 17.4 all-gather.35
where the time goes:
time: 2600 us; the launch traced here: 2590 us
  waiting for transfers between devices  1780 us (68%)
  matrix products  429 us (16%)
  blocking collectives  150 us (6%)
  local copies, waits for them, and re-layouts  120 us (5%)
  other arithmetic  87.1 us (3%)
    reduce_scatter x5, waiting for transfers between devices, whole_gram(): lax.psum_scatter(gram_block(matrices, gram_rows * lax.axis_size(('wide',...  673 us
    all_gather x5, waiting for transfers between devices, whole_gram(): return lax.all_gather(gram_part, ('wide', 'narrow'), axis=0, tiled=True)  399 us
    reduce_scatter x1, waiting for transfers between devices, on_device(): lax.psum_scatter(reduce_grad, 'wide', scatter_dimension=0, tiled=True)  166 us
    reduce_scatter x1, waiting for transfers between devices, on_device(): lax.psum_scatter(expand_grad, 'wide', scatter_dimension=0, tiled=True)  166 us
    unnamed x27, waiting for transfers between devices  121 us
    reduce_scatter x1, waiting for transfers between devices, on_device(): lax.psum_scatter(attend_grad, 'wide', scatter_dimension=0, tiled=True)  106 us
    dot_general x41, matrix products, exact_times(): jnp.dot(left_side, right_side, precision=lax.Precision.HIGHEST, preferred...  95.4 us
    psum x1, waiting for transfers between devices, on_device(): lax.psum((wide_sums[0], wide_sums[1], wide_sums[2], wide_sums[3], wide_su...  77 us
  transfers between devices with their start and end apart: 25, of which 20 were waited for; matrix products, arithmetic and copies ran while one was open for 14% of the time, Pallas kernels for 0%

commit v1 on v0

--- a/solution.py
+++ b/solution.py
@@ -3,7 +3,10 @@
 
 import jax
 import jax.numpy as jnp
+import numpy as np
 from jax import lax
+from jax.experimental import pallas as pl
+from jax.experimental.pallas import tpu as pltpu
 from jax.sharding import PartitionSpec as P
 
 D = 768
@@ -142,87 +145,260 @@
     return (query_grad, key_grad, value_grad)
 
 
-def gram_block(matrices, row_span):
+BOTH = ("wide", "narrow")
+GRAM_TILE = 256
+GRAM_SPOTS = ((0, 0), (0, 1), (0, 2), (1, 1), (1, 2), (2, 2))
+
+
+def swap(value, mask):
+    total = lax.axis_size(BOTH)
+    return lax.ppermute(value, BOTH, [(spot, spot ^ mask) for spot in range(total)])
+
+
+def my_index():
+    return lax.axis_index("wide") * lax.axis_size("narrow") + lax.axis_index("narrow")
+
+
+def wide_masks():
+    narrow_size = lax.axis_size("narrow")
+    count = lax.axis_size("wide").bit_length() - 1
+    return [narrow_size << bit for bit in reversed(range(count))]
+
+
+def offsets_of(masks):
+    table = [0]
+    for mask in masks:
+        table = table + [offset ^ mask for offset in table]
+    return np.array(table)
+
+
+def gather_blocks(piece, masks):
+    for mask in masks:
+        piece = jnp.concatenate([piece, swap(piece, mask)], axis=0)
+    return piece
+
+
+def take_blocks(array, index):
+    return jnp.take(array, index, axis=0, mode="clip")
+
+
+def in_order(blocks, masks, unit, base):
+    offsets = offsets_of(masks) // unit
+    place = np.zeros_like(offsets)
+    place[offsets] = np.arange(offsets.size)
+    return take_blocks(blocks, jnp.asarray(place)[jnp.arange(offsets.size) ^ base])
+
+
+def out_of_order(blocks, masks, unit, base):
+    offsets = offsets_of(masks) // unit
+    return take_blocks(blocks, jnp.asarray(offsets) ^ base)
+
+
+def gather_wide(piece):
+    blocks = gather_blocks(piece[None], wide_masks())
+    return in_order(blocks, wide_masks(), lax.axis_size("narrow"), lax.axis_index("wide"))
+
+
+def quarter_rows(array):
+    count = array.shape[0] // lax.axis_size("narrow")
+    return lax.dynamic_slice_in_dim(array, lax.axis_index("narrow") * count, count, 0)
+
+
+def scatter_blocks(keep, send, masks, wide_type):
+    for step, mask in enumerate(masks):
+        send_type = wide_type if step + 2 >= len(masks) else jnp.bfloat16
+        total = keep + swap(send.astype(send_type), mask).astype(jnp.float32)
+        half = total.shape[0] // 2
+        keep, send = total[:half], total[half:]
+    return total
+
+
+def narrow_rows(piece):
+    spot = lax.axis_index("narrow")
+    other = swap(piece, 2)
+    pair = jnp.where(spot // 2 == 0, jnp.stack([piece, other]), jnp.stack([other, piece]))
+    other = swap(pair, 1)
+    quad = jnp.where(
+        spot % 2 == 0, jnp.stack([pair, other], axis=1), jnp.stack([other, pair], axis=1)
+    )
+    return quad.reshape(4 * piece.shape[0], piece.shape[1])
+
+
+def sum_small(blocks):
+    masks = wide_masks()
+    blocks = blocks + swap(blocks, 1)
+    blocks = out_of_order(blocks, masks, lax.axis_size("narrow"), lax.axis_index("wide"))
+    for mask in reversed(masks):
+        half = blocks.shape[0] // 2
+        blocks = blocks[:half] + swap(blocks[half:], mask)
+    piece = blocks[0]
+    return piece + swap(piece, 2)
+
+
+def sum_gram(blocks):
+    wide_at = lax.axis_index("wide")
+    narrow_size = lax.axis_size("narrow")
+    masks = wide_masks()
+    bits = [(mask // narrow_size).bit_length() - 1 for mask in masks]
+    order = list(zip(masks, bits))
+    order = list(reversed(order))
+    for mask, bit in order:
+        side = (wide_at >> bit) % 2
+        half = blocks.shape[0] // 2
+        keep = lax.dynamic_slice_in_dim(blocks, side * half, half, 0)
+        send = lax.dynamic_slice_in_dim(blocks, (1 - side) * half, half, 0)
+        blocks = keep + swap(send, mask)
+    for mask, bit in reversed(order):
+        side = (wide_at >> bit) % 2
+        other = swap(blocks, mask)
+        blocks = jnp.where(
+            side == 0,
+            jnp.concatenate([blocks, other], axis=0),
+            jnp.concatenate([other, blocks], axis=0),
+        )
+    return blocks
+
+
+def split_two(values):
+    high = values.astype(jnp.bfloat16)
+    return high, (values - high.astype(jnp.float32)).astype(jnp.bfloat16)
+
+
+def newton_kernel(gram_ref, out_ref, gram_now, total, left, right):
+    tile = GRAM_TILE
+    trace = jnp.zeros((1, 1), jnp.float32)
+    spot_mask = lax.broadcasted_iota(jnp.int32, (tile, tile), 0) == lax.broadcasted_iota(
+        jnp.int32, (tile, tile), 1
+    )
+    for number, (row, column) in enumerate(GRAM_SPOTS):
+        block = gram_ref[number * tile : (number + 1) * tile, :]
+        if row == column:
+            picked = jnp.where(spot_mask, block, 0.0)
+            trace = trace + jnp.sum(jnp.sum(picked, axis=0, keepdims=True), axis=1, keepdims=True)
+    length = jnp.sqrt(trace) + 1e-07
+    inverse = 1.0 / length
+    scale = inverse * inverse
+    for number, (row, column) in enumerate(GRAM_SPOTS):
+        block = gram_ref[number * tile : (number + 1) * tile, :] * scale
+        gram_now[row * tile : (row + 1) * tile, column * tile : (column + 1) * tile] = block
+        if row != column:
+            gram_now[column * tile : (column + 1) * tile, row * tile : (row + 1) * tile] = block.T
+
+    def set_left(values):
+        high, low = split_two(values)
+        left[:, 0:D] = high
+        left[:, D : 2 * D] = high
+        left[:, 2 * D : 3 * D] = low
+
+    def set_right(values):
+        high, low = split_two(values)
+        right[0:D, :] = high
+        right[D : 2 * D, :] = low
+        right[2 * D : 3 * D, :] = high
+
+    def product():
+        return jnp.dot(left[...], right[...], preferred_element_type=jnp.float32)
+
+    diagonal = lax.broadcasted_iota(jnp.int32, (D, D), 0) == lax.broadcasted_iota(
+        jnp.int32, (D, D), 1
+    )
+
+    def set_factor():
+        set_left(gram_now[...])
+        set_right(gram_now[...])
+        factor = NEWTON_B * gram_now[...] + NEWTON_C * product()
+        factor = factor + jnp.where(diagonal, NEWTON_A, 0.0)
+        set_right(factor)
+        return factor
+
+    def advance():
+        moved = product()
+        set_left(moved)
+        gram_now[...] = product()
+
+    total[...] = set_factor()
+    advance()
+
+    def body(step, carry):
+        set_factor()
+        advance()
+        set_left(total[...])
+        total[...] = product()
+        return carry
+
+    lax.fori_loop(0, NS_ITERS - 2, body, 0)
+    set_factor()
+    set_left(total[...])
+    out_ref[...] = product() * inverse
+
+
+def newton_product(gram_blocks):
+    return pl.pallas_call(
+        newton_kernel,
+        out_shape=jax.ShapeDtypeStruct((D, D), jnp.float32),
+        in_specs=[pl.BlockSpec(memory_space=pltpu.VMEM)],
+        out_specs=pl.BlockSpec(memory_space=pltpu.VMEM),
+        scratch_shapes=[
+            pltpu.VMEM((D, D), jnp.float32),
+            pltpu.VMEM((D, D), jnp.float32),
+            pltpu.VMEM((D, 3 * D), jnp.bfloat16),
+            pltpu.VMEM((3 * D, D), jnp.bfloat16),
+        ],
+        compiler_params=pltpu.CompilerParams(vmem_limit_bytes=48 << 20),
+        name="newton",
+    )(gram_blocks)
+
+
+def pick_rows(parts, spot):
+    most = max(part.shape[0] for part in parts)
+    padded = [jnp.pad(part, ((0, most - part.shape[0]), (0, 0))) for part in parts]
+    picked = padded[-1]
+    for number in reversed(range(len(parts) - 1)):
+        picked = jnp.where(spot == number, padded[number], picked)
+    return picked
+
+
+def local_gram(rows):
+    tiles = [rows[:, at * GRAM_TILE : (at + 1) * GRAM_TILE] for at in range(D // GRAM_TILE)]
     return jnp.concatenate(
         [
             lax.dot_general(
-                lax.slice_in_dim(matrix, 0, row_span, axis=1),
-                matrix,
+                tiles[row],
+                tiles[column],
                 (((0,), (0,)), ((), ())),
                 precision=lax.Precision.HIGHEST,
                 preferred_element_type=jnp.float32,
             )
-            for matrix in matrices
+            for row, column in GRAM_SPOTS
         ],
-        axis=1,
-    )
-
-
-def whole_gram(matrices, gram_rows):
-    gram_part = lax.psum_scatter(
-        gram_block(matrices, gram_rows * lax.axis_size(("wide", "narrow"))),
-        ("wide", "narrow"),
-        scatter_dimension=0,
-        tiled=True,
-    )
-    return lax.all_gather(gram_part, ("wide", "narrow"), axis=0, tiled=True)
-
-
-def orthogonal_rows(updates):
-    gram_rows = D // lax.axis_size(("wide", "narrow"))
-    squares = lax.psum(
-        jnp.stack(
-            [
-                jnp.sum(updates[0] * updates[0]),
-                jnp.sum(updates[1] * updates[1]),
-                jnp.sum(updates[2] * updates[2]),
-                jnp.sum(updates[3] * updates[3]),
-            ]
-        ),
-        ("wide", "narrow"),
-    )
-    lengths = jnp.sqrt(squares) + 1e-07
-    currents = tuple((updates[number] / lengths[number] for number in range(4)))
-    gram_now = whole_gram(currents, gram_rows)
-    for sweep_step in range(NS_ITERS):
-        next_list = []
-        for number in range(4):
-            gram_piece = gram_now[:, number * D : (number + 1) * D]
-            moved_rows = exact_times(currents[number], gram_piece)
-            next_list.append(
-                NEWTON_A * currents[number]
-                + NEWTON_B * moved_rows
-                + NEWTON_C * exact_times(moved_rows, gram_piece)
-            )
-        currents = tuple(next_list)
-        if sweep_step + 1 < NS_ITERS:
-            gram_now = whole_gram(currents, gram_rows)
-    return currents
-
-
-def muon_rows(weight_parts, moment_parts, grad_parts):
+        axis=0,
+    )
+
+
+def muon_rows(weights, moments, gradients):
+    spot = lax.axis_index("narrow")
     moment_next = tuple(
-        (
-            MUON_MU * moment + (1.0 - MUON_MU) * gradient
-            for moment, gradient in zip(moment_parts, grad_parts)
-        )
+        MUON_MU * moment + (1.0 - MUON_MU) * gradient
+        for moment, gradient in zip(moments, gradients)
     )
     updates = tuple(
-        (
-            (1.0 - MUON_MU) * gradient + MUON_MU * moment
-            for moment, gradient in zip(moment_next, grad_parts)
-        )
-    )
-    currents = orthogonal_rows(updates)
+        (1.0 - MUON_MU) * gradient + MUON_MU * moment
+        for moment, gradient in zip(moment_next, gradients)
+    )
+    rows = pick_rows(updates, spot)
+    factor = newton_product(sum_gram(local_gram(rows)))
+    ortho = exact_times(rows, factor).astype(jnp.bfloat16)
+    pair = jnp.stack([ortho, swap(ortho, 2)])
+    quad = jnp.concatenate([pair, swap(pair, 1)], axis=0)
+    place = np.array([0, 2, 1, 3])
     rows_whole = (3 * D, D, FF, FF)
-    updated = tuple(
-        (
-            weight_parts[number] * (1.0 - MUON_RATE * MUON_DECAY)
-            - MUON_RATE * SHAPE_FACTOR * math.sqrt(max(rows_whole[number], D)) * currents[number]
-            for number in range(4)
-        )
-    )
-    return (updated, moment_next)
+    updated = []
+    for number, weight in enumerate(weights):
+        mine = lax.dynamic_index_in_dim(quad, jnp.asarray(place)[spot ^ number], 0, keepdims=False)
+        mine = mine[: weight.shape[0]].astype(jnp.float32)
+        rate = MUON_RATE * SHAPE_FACTOR * math.sqrt(max(rows_whole[number], D))
+        updated.append(weight * (1.0 - MUON_RATE * MUON_DECAY) - rate * mine)
+    return tuple(updated), moment_next
 
 
 def adam_step(weight, mean_state, square, gradient, step_rate, decay_rate, step_count):
@@ -259,24 +435,14 @@
     step_count,
 ):
     low_type = jnp.bfloat16
-    gathered = (
-        lax.all_gather(table_weight.astype(low_type), "wide", axis=1, tiled=True),
-        lax.all_gather(attend_weight.astype(low_type), "wide", axis=0, tiled=True),
-        lax.all_gather(mixing_weight.astype(low_type), "wide", axis=0, tiled=True),
-        lax.all_gather(expand_weight.astype(low_type), "wide", axis=0, tiled=True),
-        lax.all_gather(reduce_weight.astype(low_type), "wide", axis=0, tiled=True),
-        lax.all_gather(vector_params.astype(low_type), "wide", axis=1, tiled=True),
-    )
-    table_low, attend_low, mixing_low, expand_low, reduce_low, vector_low = gathered
-    vector_full = vector_low.astype(jnp.float32)
-    seq_count = codons.shape[0]
-    row_count = seq_count * SEQ_LEN
-    window = jax.vmap(partial(lax.dynamic_slice_in_dim, slice_size=SEQ_LEN))(codons, offsets)
-    vocab_ids = jnp.arange(VOCAB, dtype=jnp.int32)
-    token_hot = window.reshape(row_count)[:, None] == vocab_ids[None, :]
-    target_hot = (targets.reshape(row_count)[:, None] == vocab_ids[None, :]).astype(jnp.float32)
-    embed_scale = math.sqrt(D)
-    stream = embed_scale * times_plain(token_hot.astype(low_type), table_low)
+    wide_at = lax.axis_index("wide")
+    me = my_index()
+    devices = lax.axis_size(BOTH)
+    all_masks = wide_masks() + [2, 1]
+    small = gather_wide(jnp.concatenate([table_weight, vector_params], axis=0).astype(low_type))
+    small = jnp.transpose(small, (1, 0, 2)).reshape(VOCAB + 15, D)
+    table_low = small[:VOCAB]
+    vector_full = small[VOCAB:].astype(jnp.float32)
     gain_one = vector_full[0]
     bias_one = vector_full[1]
     gain_two = vector_full[2]
@@ -286,10 +452,37 @@
     attend_bias = vector_full[6:9].reshape(3 * D)
     mixing_bias = vector_full[9]
     reduce_bias = vector_full[10]
-    expand_bias = vector_full[11:15].reshape(FF)
-    normed_one, normal_one, inverse_one = norm_forward(stream, gain_one, bias_one)
-    normed_one_low = normed_one.astype(low_type)
-    projected = times_trans(normed_one_low, attend_low) + attend_bias
+    expand_bias = out_of_order(
+        vector_full[11:15].reshape(devices, FF // devices), all_masks, 1, me
+    ).reshape(FF)
+    embed_scale = math.sqrt(D)
+    table_stream = embed_scale * table_low.astype(jnp.float32)
+    table_normed = norm_forward(table_stream, gain_one, bias_one)[0].astype(low_type)
+    attend_own = attend_weight.astype(low_type)
+    table_own = times_trans(table_normed, attend_own)
+    table_heads = jnp.transpose(gather_wide(table_own), (1, 0, 2)).reshape(VOCAB, 3 * D)
+    table_heads = table_heads + attend_bias
+
+    mixing_low = gather_blocks(quarter_rows(mixing_weight).astype(low_type)[None], all_masks)
+    mixing_low = in_order(mixing_low, all_masks, 1, me).reshape(D, D)
+    expand_low = gather_blocks(quarter_rows(expand_weight).astype(low_type), all_masks)
+    reduce_low = gather_blocks(quarter_rows(reduce_weight).astype(low_type), all_masks)
+    attend_low = gather_blocks(quarter_rows(attend_weight).astype(low_type)[None], all_masks)
+    attend_low = in_order(attend_low, all_masks, 1, me).reshape(3 * D, D)
+
+    seq_count = codons.shape[0]
+    row_count = seq_count * SEQ_LEN
+    window = jax.vmap(partial(lax.dynamic_slice_in_dim, slice_size=SEQ_LEN))(codons, offsets)
+    vocab_ids = jnp.arange(VOCAB, dtype=jnp.int32)
+    token_hot = window.reshape(row_count)[:, None] == vocab_ids[None, :]
+    token_low = token_hot.astype(low_type)
+    target_hot = (targets.reshape(row_count)[:, None] == vocab_ids[None, :]).astype(jnp.float32)
+    stream = embed_scale * times_plain(token_low, table_low)
+    heads_high, heads_low = split_two(table_heads)
+    projected = times_plain(
+        jnp.concatenate([token_low, token_low], axis=1),
+        jnp.concatenate([heads_high, heads_low], axis=0),
+    )
     cosine, sine_table = rotary_tables(positions)
     head_shape = (seq_count, SEQ_LEN, HEADS, HEAD_DIM)
     query_rot = rotate(projected[:, :D].reshape(head_shape), cosine, sine_table).astype(low_type)
@@ -317,15 +510,7 @@
     row_peak = jnp.max(logits, axis=-1, keepdims=True)
     shifted = jnp.exp(logits - row_peak)
     prob_rows = shifted / jnp.sum(shifted, axis=-1, keepdims=True)
-    prob_total = lax.psum(jnp.sum(prob_rows, axis=0), ("wide", "narrow"))
-    histogram = prob_total * (VOCAB / (row_count * lax.axis_size(("wide", "narrow"))))
-    table_low, attend_low, mixing_low, expand_low, reduce_low = (
-        lax.all_gather(table_weight.astype(low_type), "wide", axis=1, tiled=True),
-        lax.all_gather(attend_weight.astype(low_type), "wide", axis=0, tiled=True),
-        lax.all_gather(mixing_weight.astype(low_type), "wide", axis=0, tiled=True),
-        lax.all_gather(expand_weight.astype(low_type), "wide", axis=0, tiled=True),
-        lax.all_gather(reduce_weight.astype(low_type), "wide", axis=0, tiled=True),
-    )
+    prob_sum = jnp.sum(prob_rows, axis=0)
     logit_grad = (prob_rows - target_hot).astype(low_type)
     final_grad = times_plain(logit_grad, table_low)
     table_head = trans_times(logit_grad, final_low)
@@ -334,11 +519,28 @@
     )
     feed_low = output_grad.astype(low_type)
     reduce_bias_grad = jnp.sum(feed_low, axis=0, dtype=jnp.float32)
-    reduce_grad = trans_times(hidden_low, feed_low)
+    scatter_masks = list(reversed(all_masks))
+    half_ff = FF // 2
+    reduce_part = scatter_blocks(
+        trans_times(hidden_low[:, :half_ff], feed_low),
+        trans_times(hidden_low[:, half_ff:], feed_low),
+        scatter_masks,
+        jnp.float32,
+    )
+    reduce_total = narrow_rows(reduce_part)
     hidden_grad = times_trans(feed_low, reduce_low)
     pre_grad = gelu_back(hidden_grad)[0].astype(low_type)
     expand_bias_grad = jnp.sum(pre_grad, axis=0, dtype=jnp.float32)
-    expand_grad = trans_times(pre_grad, normed_two_low)
+    expand_bias_grad = in_order(
+        expand_bias_grad.reshape(devices, FF // devices), all_masks, 1, me
+    )
+    expand_part = scatter_blocks(
+        trans_times(pre_grad[:, :half_ff], normed_two_low),
+        trans_times(pre_grad[:, half_ff:], normed_two_low),
+        scatter_masks,
+        jnp.float32,
+    )
+    expand_total = narrow_rows(expand_part)
     normed_two_grad = times_plain(pre_grad, expand_low)
     middle_part, gain_two_grad, bias_two_grad = norm_backward(
         normed_two_grad, normal_two, inverse_two, gain_two
@@ -346,7 +548,12 @@
     middle_grad = output_grad + middle_part
     branch_low = middle_grad.astype(low_type)
     mixing_bias_grad = jnp.sum(branch_low, axis=0, dtype=jnp.float32)
-    mixing_grad = trans_times(branch_low, mixed_low)
+    mixing_grad = trans_times(branch_low, mixed_low).reshape(devices, D // devices, D)
+    mixing_grad = out_of_order(mixing_grad, all_masks, 1, me)
+    mixing_part = scatter_blocks(
+        mixing_grad[: devices // 2], mixing_grad[devices // 2 :], scatter_masks, jnp.float32
+    )
+    mixing_total = narrow_rows(mixing_part[0])
     mixed_grad = times_plain(branch_low, mixing_low).astype(low_type)
     grad_heads = jnp.transpose(mixed_grad.reshape(head_shape), (2, 0, 1, 3))
     query_back, key_back, value_back = lax.map(
@@ -361,8 +568,19 @@
     value_grad = jnp.transpose(value_back, (1, 2, 0, 3)).reshape(row_count, D)
     projected_low = jnp.concatenate([query_grad, key_grad, value_grad], axis=1).astype(low_type)
     attend_bias_grad = jnp.sum(projected_low, axis=0, dtype=jnp.float32)
-    attend_grad = trans_times(projected_low, normed_one_low)
+    wide_size = lax.axis_size("wide")
+    token_sums = trans_times(token_low, projected_low)
+    token_sums = jnp.transpose(token_sums.reshape(VOCAB, wide_size, 3 * D // wide_size), (1, 0, 2))
+    token_sums = sum_small(token_sums)
+    attend_total = lax.dot_general(
+        token_sums,
+        table_normed.astype(jnp.float32),
+        (((0,), (0,)), ((), ())),
+        precision=lax.Precision.HIGHEST,
+        preferred_element_type=jnp.float32,
+    )
     normed_one_grad = times_plain(projected_low, attend_low)
+    normed_one, normal_one, inverse_one = norm_forward(stream, gain_one, bias_one)
     stream_part, gain_one_grad, bias_one_grad = norm_backward(
         normed_one_grad, normal_one, inverse_one, gain_one
     )
@@ -389,61 +607,36 @@
         ],
         axis=0,
     )
-    narrow_size = lax.axis_size("narrow")
-    narrow_at = lax.axis_index("narrow")
-
-    def rows_part(array):
-        quarter = array.shape[0] // narrow_size
-        return lax.dynamic_slice_in_dim(array, narrow_at * quarter, quarter, 0)
-
-    weight_parts = (
-        rows_part(attend_weight),
-        rows_part(mixing_weight),
-        rows_part(expand_weight),
-        rows_part(reduce_weight),
-    )
-    moment_parts = (
-        rows_part(attend_moment),
-        rows_part(mixing_moment),
-        rows_part(expand_moment),
-        rows_part(reduce_moment),
-    )
-    wide_sums = (
-        lax.psum_scatter(table_grad, "wide", scatter_dimension=1, tiled=True),
-        lax.psum_scatter(attend_grad, "wide", scatter_dimension=0, tiled=True),
-        lax.psum_scatter(mixing_grad, "wide", scatter_dimension=0, tiled=True),
-        lax.psum_scatter(expand_grad, "wide", scatter_dimension=0, tiled=True),
-        lax.psum_scatter(reduce_grad, "wide", scatter_dimension=0, tiled=True),
-        lax.psum_scatter(vector_grad, "wide", scatter_dimension=1, tiled=True),
-    )
-    totals = lax.psum(
-        (wide_sums[0], wide_sums[1], wide_sums[2], wide_sums[3], wide_sums[4], wide_sums[5]),
-        "narrow",
-    )
+    columns = D // wide_size
+    rows_hist = -(-VOCAB // columns)
+    hist_part = jnp.pad(prob_sum, (0, rows_hist * columns - VOCAB)).reshape(rows_hist, columns)
+    small_grads = jnp.concatenate([table_grad, vector_grad], axis=0)
+    small_grads = jnp.transpose(small_grads.reshape(VOCAB + 15, wide_size, columns), (1, 0, 2))
+    small_grads = jnp.concatenate(
+        [small_grads, jnp.broadcast_to(hist_part, (wide_size, rows_hist, columns))], axis=1
+    )
+    small_total = sum_small(small_grads)
+    table_total = small_total[:VOCAB]
+    vector_total = small_total[VOCAB : VOCAB + 15]
+    prob_total = small_total[VOCAB + 15 :].reshape(rows_hist * columns)[:VOCAB]
+    histogram = prob_total * (VOCAB / (row_count * devices))
+    totals = (attend_total, mixing_total, expand_total, reduce_total)
     matrix_new, moment_next = muon_rows(
-        weight_parts,
-        moment_parts,
-        (rows_part(totals[1]), rows_part(totals[2]), rows_part(totals[3]), rows_part(totals[4])),
+        (attend_weight, mixing_weight, expand_weight, reduce_weight),
+        (attend_moment, mixing_moment, expand_moment, reduce_moment),
+        totals,
     )
     table_new, table_mean_next, table_square_next = adam_step(
-        table_weight, table_mean, table_square, totals[0], TABLE_RATE, TABLE_DECAY, step_count
+        table_weight, table_mean, table_square, table_total, TABLE_RATE, TABLE_DECAY, step_count
     )
     vector_new, vector_mean_next, vector_square_next = adam_step(
-        vector_params, vector_mean, vector_square, totals[5], VECTOR_RATE, 0.0, step_count
-    )
-    rows_back = (
-        lax.all_gather(matrix_new[0], "narrow", axis=0, tiled=True),
-        lax.all_gather(matrix_new[1], "narrow", axis=0, tiled=True),
-        lax.all_gather(matrix_new[2], "narrow", axis=0, tiled=True),
-        lax.all_gather(matrix_new[3], "narrow", axis=0, tiled=True),
-        lax.all_gather(moment_next[0], "narrow", axis=0, tiled=True),
-        lax.all_gather(moment_next[1], "narrow", axis=0, tiled=True),
-        lax.all_gather(moment_next[2], "narrow", axis=0, tiled=True),
-        lax.all_gather(moment_next[3], "narrow", axis=0, tiled=True),
+        vector_params, vector_mean, vector_square, vector_total, VECTOR_RATE, 0.0, step_count
     )
     results = (
-        (totals[1], totals[2], totals[3], totals[4], totals[0], totals[5])
-        + tuple(rows_back)
+        totals
+        + (table_total, vector_total)
+        + matrix_new
+        + moment_next
         + (
             table_new,
             table_mean_next,

time: 2600 us -> 866 us (0.33)
  waiting for transfers between devices: 1780 us -> 174 us
  blocking collectives: 150 us -> 0 us
  matrix products: 429 us -> 291 us
  starting transfers between devices: 1.77 us -> 72.9 us
  Pallas kernels: 0 us -> 50.6 us
  local copies, waits for them, and re-layouts: 120 us -> 159 us
    reduce_scatter x9 -> x0, waiting for transfers between devices: 1110 us -> none  [the longest x5 673 us: whole_gram(): lax.psum_scatter(gram_block(matrices, gram_rows * lax.axis_size(('wide',...]
    all_gather x13 -> x0, waiting for transfers between devices: 475 us -> none  [the longest x5 399 us: whole_gram(): return lax.all_gather(gram_part, ('wide', 'narrow'), axis=0, tiled=True)]
    ppermute x0 -> x65, waiting for transfers between devices: none -> 174 us  [swap(): lax.ppermute(value, BOTH, [(spot, spot ^ mask) for spot in range(total)])]
    unnamed x27 -> x0, waiting for transfers between devices: 121 us -> none
    all_gather x6 -> x0, blocking collectives: 99.9 us -> none  [the longest x1 32.4 us: on_device(): lax.all_gather(vector_params.astype(low_type), 'wide', axis=1, tiled=True)]
    dot_general x41 -> x2, matrix products: 95.4 us -> 6.29 us  [exact_times(): jnp.dot(left_side, right_side, precision=lax.Precision.HIGHEST, preferred...]
    psum x1 -> x0, waiting for transfers between devices: 77 us -> none  [on_device(): lax.psum((wide_sums[0], wide_sums[1], wide_sums[2], wide_sums[3], wide_su...]
    ppermute x0 -> x65, starting transfers between devices: none -> 72.9 us  [swap(): lax.ppermute(value, BOTH, [(spot, spot ^ mask) for spot in range(total)])]
  transfers between devices with their start and end apart: 25 -> 65, of which waited for: 20 -> 23; matrix products, arithmetic and copies ran while one was open for 14% -> 36% of each run, Pallas kernels for 0% -> 6%
where the time goes in v1:
time: 866 us; the launch traced here: 854 us
  matrix products  291 us (34%)
  waiting for transfers between devices  174 us (20%)
  local copies, waits for them, and re-layouts  159 us (18%)
  other arithmetic  93.6 us (11%)
  starting transfers between devices  72.9 us (8%)
  Pallas kernels  50.6 us (6%)
  between operations  11.8 us (1%)
    ppermute x65, waiting for transfers between devices, swap(): lax.ppermute(value, BOTH, [(spot, spot ^ mask) for spot in range(total)])  174 us
    ppermute x65, starting transfers between devices, swap(): lax.ppermute(value, BOTH, [(spot, spot ^ mask) for spot in range(total)])  72.9 us
    dot_general x5, matrix products, times_trans(): lax.dot_general(left_side, right_side, (((1,), (1,)), ((), ())), preferre...  53.9 us
    pallas_call x1, Pallas kernels, newton_product(): pl.pallas_call(newton_kernel, out_shape=jax.ShapeDtypeStruct((D, D), jnp....  50.6 us
    unnamed x227, local copies, waits for them, and re-layouts  35.7 us
    dot_general x12, matrix products, attend_head(): jnp.einsum('sqk,skd->sqd', prob_low, value_head, preferred_element_type=j...  30.1 us
    dot_general x7, matrix products, trans_times(): lax.dot_general(left_side, right_side, (((0,), (0,)), ((), ())), preferre...  29.7 us
    dot_general x12, matrix products, attend_back(): jnp.einsum('sqk,sqd->skd', score_grad, query_head, preferred_element_type...  27.9 us
  transfers between devices with their start and end apart: 65, of which 23 were waited for; matrix products, arithmetic and copies ran while one was open for 36% of the time, Pallas kernels for 6%

profile of v1, /device:TPU:0, one launch (start us, length us, event | category | flops | bytes accessed | tf_op | source)
XLA Modules:
  0.0 854.5 jit_solution(13268052532663975367)
XLA Ops:
  2.2 4.1 collective-permute-start
  69.9 5.3 collective-permute-done.4
  84.1 5.2 collective-permute-done.5
  106.2 3.7 copy.130
  109.8 3.5 copy.129
  113.3 4.0 subtract_convert_fusion.2
  119.4 4.1 copy.132
  123.5 4.1 copy.133
  130.1 4.1 copy.134
  140.6 65.8 %while.29 = (s32[]{:T(128)}, bf16[12,1,912,64]{2,3,1,0:T(8,128)(2,1)}, f32[12,1,912]{2,1,0:T(1,128)}, bf16[12,1,912,64]{3,2,1,0:T(8,128)(2,1)}, bf16[12,1,912,64...) while((s32[]{:T(128)}, bf16[12,1,912,64]{2,3,1,0:T(8,128)(2,1)}, f32[12,1,912]{2,1,0:T(1,128)}, ...), condition=%wide.region_5.6_spmd.clone, body=%wide.region_2.5_spmd.sunk.clone | while | flops 220411248 | bytes 10982545 | solution.py:496
  227.1 3.4 fusion.119
  232.1 12.4 %collective-permute-done.19 = bf16[768,768]{1,0:T(8,128)(2,1)} collective-permute-done((bf16[768,768]{1,0:T(8,128)(2,1)}, bf16[768,768]{1,0:T(8,128)(2,1)}, u32[]{:S(2)}, u32[]{:S(2)}) %collective-permute-start.19) | collective-permute-done | bytes 1179680 | tf_op jit(solution)/shard_map/ppermute | solution.py:155
  250.1 4.8 gather_fusion.6
  254.9 3.2 constant_dynamic-update-slice_fusion.17
  258.2 32.6 %multiply_convert_fusion.1 = (bf16[912,3072]{1,0:T(8,128)(2,1)S(1)}, f32[912,3072]{1,0:T(8,128)}, f32[912,3072]{1,0:T(8,128)}) fusion(f32[3072]{0:T(1024)S(1)} %copy-done.81, bf16[912,768]{1,0:T(8,128)(2,1)S(1)} %add_convert_fusion.2, bf16[3072,768]{1,0:T(8,128)(2,1)} %constant_dynamic-update-slice_fusion.17), kind=kOutput, calls=%fused_computation.70 | convolution fusion | flops 4488265728 | bytes 34148352 | tf_op jit(solution)/shard_map/dot_general | solution.py:43
  290.8 3.7 constant_dynamic-update-slice_fusion.28
  295.3 4.7 fusion.120
  306.7 16.4 %convert_reduce_fusion = (f32[3072]{0:T(1024)}, bf16[912,3072]{1,0:T(8,128)(2,1)}) fusion(f32[912,3072]{1,0:T(8,128)} %get-tuple-element.258, f32[912,3072]{1,0:T(8,128)} %get-tuple-element.330, f32[3072]{0:T(1024)S(1)} %copy-done.81, bf16[912,768]{1,0:T(8,128)(2,1)S(1)} %get-tuple-element.249, bf16[3072,768]{1,0:T(8,128)(2,1)} %copy-done.90), kind=kOutput, calls=%fused_computation.68 | convolution fusion | flops 4350981120 | bytes 34160640 | tf_op jit(solution)/shard_map/dot_general | solution.py:43
  323.1 9.8 %multiply_reduce_fusion.3 = (f32[768]{0:T(1024)}, f32[912]{0:T(1024)S(1)}, f32[912]{0:T(1024)S(1)}, f32[768]{0:T(1024)}, f32[912,768]{1,0:T(8,128)S(1)}) fusion(f32[912,768]{1,0:T(8,128)S(1)} %copy-done.8, f32[912]{0:T(1024)S(1)} %copy-done.75, f32[912]{0:T(1024)S(1)} %copy-done.62, f32[768]{0:T(1024)S(1)} %copy-done.72, ...), kind=kOutput, calls=%fused_computation.100 | convolution fusion | flops 4309655552 | bytes 15949056 | tf_op jit(solution)/shard_map/dot_general | solution.py:39
  332.9 4.0 convolution_convert_fusion.1
  345.2 138.2 %while.30 = (s32[]{:T(128)}, f32[12,1,912,64]{2,3,1,0:T(8,128)}, f32[12,1,912,64]{2,3,1,0:T(8,128)}, bf16[12,1,912,64]{2,3,1,0:T(8,128)(2,1)S(1)}, bf16[12,1,912...) while((s32[]{:T(128)}, f32[12,1,912,64]{2,3,1,0:T(8,128)}, ...), condition=%wide.region_20.21_spmd.clone, body=%wide.region_18.20_spmd.sunk.clone | while | flops 542412928 | bytes 27608040 | solution.py:559
  483.4 4.0 add_convert_fusion.4
  490.4 5.2 multiply_reduce_fusion.4
  501.3 6.5 convolution_convert_fusion
  510.7 4.0 gather_fusion.8
  516.6 3.8 fusion.88
  533.7 6.0 convert_add_fusion.1
  541.4 4.5 convert_add_fusion
  549.2 5.7 collective-permute-done.28
  560.8 8.0 collective-permute-done.39
  570.9 21.8 %collective-permute-done.46 = bf16[768,768]{1,0:T(8,128)(2,1)S(1)} collective-permute-done((bf16[768,768]{1,0:T(8,128)(2,1)S(1)}, bf16[768,768]{1,0:T(8,128)(2,1)S(1)}, u32[]{:S(2)}, u32[]{:S(2)}) %collective-permute-start.46) | collective-permute-done | bytes 1179680 | tf_op jit(solution)/shard_map/ppermute | solution.py:155
  599.3 7.8 collective-permute-done.47
  611.0 5.3 collective-permute-done.41
  616.8 12.6 %collective-permute-done.48 = f32[192,768]{1,0:T(8,128)S(1)} collective-permute-done((f32[192,768]{1,0:T(8,128)S(1)}, f32[192,768]{1,0:T(8,128)S(1)}, u32[]{:S(2)}, u32[]{:S(2)}) %collective-permute-start.48) | collective-permute-done | bytes 589856 | tf_op jit(solution)/shard_map/ppermute | solution.py:155
  630.5 7.6 collective-permute-start.43
  638.1 5.0 collective-permute-done.49
  644.5 7.0 collective-permute-done.50
  665.1 18.7 %collective-permute-done.57 = f32[768,256]{1,0:T(8,128)} collective-permute-done((f32[768,256]{1,0:T(8,128)S(1)}, f32[768,256]{1,0:T(8,128)}, u32[]{:S(2)}, u32[]{:S(2)}) %collective-permute-start.57) | collective-permute-done | bytes 786464 | tf_op jit(solution)/shard_map/ppermute | solution.py:155
  686.3 11.0 %collective-permute-done.58 = f32[384,256]{1,0:T(8,128)} collective-permute-done((f32[384,256]{1,0:T(8,128)}, f32[384,256]{1,0:T(8,128)}, u32[]{:S(2)}, u32[]{:S(2)}) %collective-permute-start.58) | collective-permute-done | bytes 393248 | tf_op jit(solution)/shard_map/ppermute | solution.py:155
  701.1 9.1 %collective-permute-done.59 = f32[192,256]{1,0:T(8,128)S(1)} collective-permute-done((f32[192,256]{1,0:T(8,128)S(1)}, f32[192,256]{1,0:T(8,128)S(1)}, u32[]{:S(2)}, u32[]{:S(2)}) %collective-permute-start.59) | collective-permute-done | bytes 196640 | tf_op jit(solution)/shard_map/ppermute | solution.py:155
  711.3 11.4 %collective-permute-done.60 = f32[192,256]{1,0:T(8,128)S(1)} collective-permute-done((f32[192,256]{1,0:T(8,128)S(1)}, f32[192,256]{1,0:T(8,128)S(1)}, u32[]{:S(2)}, u32[]{:S(2)}) %collective-permute-start.60) | collective-permute-done | bytes 196640 | tf_op jit(solution)/shard_map/ppermute | solution.py:155
  722.8 3.2 convolution_multiply_fusion.2
  726.1 6.9 collective-permute-done.61
  760.8 50.6 %newton.1 = f32[768,768]{1,0:T(8,128)S(1)} custom-call(f32[1536,256]{1,0:T(8,128)S(1)} %maximum_select_fusion.gram_ref), custom_call_target="tpu_custom_call" | custom-call | tf_op jit(solution)/shard_map/newton/pallas_call | solution.py:336
  811.3 3.1 convolution_convert_fusion.3
  817.3 5.5 collective-permute-done.53
  823.3 7.1 collective-permute-done.63
  832.2 5.0 collective-permute-done.55
  (699 shorter events, 462.7 us)
Async XLA Ops:
  2.2 25.8 %collective-permute-start = (bf16[1,85,96]{2,1,0:T(8,128)(2,1)S(1)}, bf16[1,85,96]{2,1,0:T(8,128)(2,1)S(1)}, u32[]{:S(2)}, u32[]{:S(2)}) collective-permute-start(bf16[1,85,96]{2,1,0:T(8,128)(2,1)S(1)} %pad_maximum_fusion.24), channel_id=1, source_target_pairs={{0,16},{1,17},{2,18},{3,19},{4,20},{5,21},{6,22},{7,23},{8,24},{9,... | collective-permute-start | bytes 48968 | tf_op jit(solution)/shard_map/ppermute | solution.py:155
  7.8 21.9 %collective-permute-start.6 = (bf16[1,24,768]{2,1,0:T(8,128)(2,1)S(1)}, bf16[1,24,768]{2,1,0:T(8,128)(2,1)S(1)}, u32[]{:S(2)}, u32[]{:S(2)}) collective-permute-start(bf16[1,24,768]{2,1,0:T(8,128)(2,1)S(1)} %get-tuple-element.262), channel_id=1, source_target_pairs={{0,16},{1,17},{2,18},{3,19},{4,20},{5,21},{6,22},{7,23},{8,24},{9,... | collective-permute-start | bytes 110600 | tf_op jit(solution)/shard_map/ppermute | solution.py:155
  9.5 45.5 %collective-permute-start.11 = (bf16[96,768]{1,0:T(8,128)(2,1)S(1)}, bf16[96,768]{1,0:T(8,128)(2,1)}, u32[]{:S(2)}, u32[]{:S(2)}) collective-permute-start(bf16[96,768]{1,0:T(8,128)(2,1)S(1)} %get-tuple-element.260), channel_id=1, source_target_pairs={{0,16},{1,17},{2,18},{3,19},{4,20},{5,21},{6,22},{7,23},{8,24},{9,... | collective-permute-start | bytes 442376 | tf_op jit(solution)/shard_map/ppermute | solution.py:155
  14.0 42.0 %collective-permute-start.16 = (bf16[96,768]{1,0:T(8,128)(2,1)S(1)}, bf16[96,768]{1,0:T(8,128)(2,1)S(1)}, u32[]{:S(2)}, u32[]{:S(2)}) collective-permute-start(bf16[96,768]{1,0:T(8,128)(2,1)S(1)} %get-tuple-element.256), channel_id=1, source_target_pairs={{0,16},{1,17},{2,18},{3,19},{4,20},{5,21},{6,22},{7,23},{8,24},{9,... | collective-permute-start | bytes 442376 | tf_op jit(solution)/shard_map/ppermute | solution.py:155
  15.6 20.7 %collective-permute-start.21 = (bf16[1,72,768]{2,1,0:T(8,128)(2,1)S(1)}, bf16[1,72,768]{2,1,0:T(8,128)(2,1)S(1)}, u32[]{:S(2)}, u32[]{:S(2)}) collective-permute-start(bf16[1,72,768]{2,1,0:T(8,128)(2,1)S(1)} %get-tuple-element.254), channel_id=1, source_target_pairs={{0,16},{1,17},{2,18},{3,19},{4,20},{5,21},{6,22},{7,23},{8,24},{9,... | collective-permute-start | bytes 331784 | tf_op jit(solution)/shard_map/ppermute | solution.py:155
  34.9 26.7 %collective-permute-start.8 = (bf16[4,24,768]{2,1,0:T(8,128)(2,1)}, bf16[4,24,768]{2,1,0:T(8,128)(2,1)}, u32[]{:S(2)}, u32[]{:S(2)}) collective-permute-start(bf16[4,24,768]{2,1,0:T(8,128)(2,1)} %pad_maximum_fusion.20), channel_id=1, source_target_pairs={{0,4},{1,5},{2,6},{3,7},{4,0},{5,1},{6,2},{7,3},{8,12},{9,13},{10,... | collective-permute-start | bytes 442376 | tf_op jit(solution)/shard_map/ppermute | solution.py:155
  37.1 28.6 %collective-permute-start.22 = (bf16[2,72,768]{2,1,0:T(8,128)(2,1)}, bf16[2,72,768]{2,1,0:T(8,128)(2,1)}, u32[]{:S(2)}, u32[]{:S(2)}) collective-permute-start(bf16[2,72,768]{2,1,0:T(8,128)(2,1)} %pad_maximum_fusion.18), channel_id=1, source_target_pairs={{0,8},{1,9},{2,10},{3,11},{4,12},{5,13},{6,14},{7,15},{8,0},{9,1},... | collective-permute-start | bytes 663560 | tf_op jit(solution)/shard_map/ppermute | solution.py:155
  45.4 15.1 %collective-permute-start.3 = (f32[1,70,288]{2,1,0:T(8,128)}, f32[1,70,288]{2,1,0:T(8,128)}, u32[]{:S(2)}, u32[]{:S(2)}) collective-permute-start(f32[1,70,288]{2,1,0:T(8,128)} %convolution_bitcast_fusion), channel_id=1, source_target_pairs={{0,16},{1,17},{2,18},{3,19},{4,20},{5,21},{6,22},{7,23},{8,24},{9,... | collective-permute-start | bytes 241928 | tf_op jit(solution)/shard_map/ppermute | solution.py:155
  55.9 20.7 %collective-permute-start.12 = (bf16[192,768]{1,0:T(8,128)(2,1)S(1)}, bf16[192,768]{1,0:T(8,128)(2,1)S(1)}, u32[]{:S(2)}, u32[]{:S(2)}) collective-permute-start(bf16[192,768]{1,0:T(8,128)(2,1)S(1)} %pad_maximum_fusion.15), channel_id=1, source_target_pairs={{0,8},{1,9},{2,10},{3,11},{4,12},{5,13},{6,14},{7,15},{8,0},{9,1},... | collective-permute-start | bytes 884744 | tf_op jit(solution)/shard_map/ppermute | solution.py:155
  56.0 24.0 %collective-permute-start.17 = (bf16[192,768]{1,0:T(8,128)(2,1)S(1)}, bf16[192,768]{1,0:T(8,128)(2,1)S(1)}, u32[]{:S(2)}, u32[]{:S(2)}) collective-permute-start(bf16[192,768]{1,0:T(8,128)(2,1)S(1)} %pad_maximum_fusion.16), channel_id=1, source_target_pairs={{0,8},{1,9},{2,10},{3,11},{4,12},{5,13},{6,14},{7,15},{8,0},{9,1},... | collective-permute-start | bytes 884744 | tf_op jit(solution)/shard_map/ppermute | solution.py:155
  61.4 13.7 %collective-permute-start.4 = (f32[2,70,288]{2,1,0:T(8,128)S(1)}, f32[2,70,288]{2,1,0:T(8,128)S(1)}, u32[]{:S(2)}, u32[]{:S(2)}) collective-permute-start(f32[2,70,288]{2,1,0:T(8,128)S(1)} %pad_maximum_fusion.17), channel_id=1, source_target_pairs={{0,8},{1,9},{2,10},{3,11},{4,12},{5,13},{6,14},{7,15},{8,0},{9,1},... | collective-permute-start | bytes 483848 | tf_op jit(solution)/shard_map/ppermute | solution.py:155
  62.5 20.7 %collective-permute-start.9 = (bf16[8,24,768]{2,1,0:T(8,128)(2,1)S(1)}, bf16[8,24,768]{2,1,0:T(8,128)(2,1)S(1)}, u32[]{:S(2)}, u32[]{:S(2)}) collective-permute-start(bf16[8,24,768]{2,1,0:T(8,128)(2,1)S(1)} %pad_maximum_fusion.14), channel_id=1, source_target_pairs={{0,2},{1,3},{2,0},{3,1},{4,6},{5,7},{6,4},{7,5},{8,10},{9,11},{10,... | collective-permute-start | bytes 884744 | tf_op jit(solution)/shard_map/ppermute | solution.py:155
  67.5 66.8 %collective-permute-start.23 = (bf16[4,72,768]{2,1,0:T(8,128)(2,1)}, bf16[4,72,768]{2,1,0:T(8,128)(2,1)}, u32[]{:S(2)}, u32[]{:S(2)}) collective-permute-start(bf16[4,72,768]{2,1,0:T(8,128)(2,1)} %pad_maximum_fusion.12), channel_id=1, source_target_pairs={{0,4},{1,5},{2,6},{3,7},{4,0},{5,1},{6,2},{7,3},{8,12},{9,13},{10,... | collective-permute-start | bytes 1327112 | tf_op jit(solution)/shard_map/ppermute | solution.py:155
  76.1 13.2 %collective-permute-start.5 = (f32[4,70,288]{2,1,0:T(8,128)S(1)}, f32[4,70,288]{2,1,0:T(8,128)S(1)}, u32[]{:S(2)}, u32[]{:S(2)}) collective-permute-start(f32[4,70,288]{2,1,0:T(8,128)S(1)} %pad_maximum_fusion.11), channel_id=1, source_target_pairs={{0,4},{1,5},{2,6},{3,7},{4,0},{5,1},{6,2},{7,3},{8,12},{9,13},{10,... | collective-permute-start | bytes 967688 | tf_op jit(solution)/shard_map/ppermute | solution.py:155
  78.5 59.3 %collective-permute-start.13 = (bf16[384,768]{1,0:T(8,128)(2,1)}, bf16[384,768]{1,0:T(8,128)(2,1)}, u32[]{:S(2)}, u32[]{:S(2)}) collective-permute-start(bf16[384,768]{1,0:T(8,128)(2,1)} %pad_maximum_fusion.9), channel_id=1, source_target_pairs={{0,4},{1,5},{2,6},{3,7},{4,0},{5,1},{6,2},{7,3},{8,12},{9,13},{10,... | collective-permute-start | bytes 1769480 | tf_op jit(solution)/shard_map/ppermute | solution.py:155
  81.0 132.7 %collective-permute-start.18 = (bf16[384,768]{1,0:T(8,128)(2,1)}, bf16[384,768]{1,0:T(8,128)(2,1)}, u32[]{:S(2)}, u32[]{:S(2)}) collective-permute-start(bf16[384,768]{1,0:T(8,128)(2,1)} %pad_maximum_fusion.10), channel_id=1, source_target_pairs={{0,4},{1,5},{2,6},{3,7},{4,0},{5,1},{6,2},{7,3},{8,12},{9,13},{10,... | collective-permute-start | bytes 1769480 | tf_op jit(solution)/shard_map/ppermute | solution.py:155
  84.1 138.1 %collective-permute-start.10 = (bf16[16,24,768]{2,1,0:T(8,128)(2,1)}, bf16[16,24,768]{2,1,0:T(8,128)(2,1)}, u32[]{:S(2)}, u32[]{:S(2)}) collective-permute-start(bf16[16,24,768]{2,1,0:T(8,128)(2,1)} %get-tuple-element.302), channel_id=1, source_target_pairs={{0,1},{1,0},{2,3},{3,2},{4,5},{5,4},{6,7},{7,6},{8,9},{9,8},{10,11... | collective-permute-start | bytes 1769480 | tf_op jit(solution)/shard_map/ppermute | solution.py:155
  136.3 83.2 %collective-permute-start.24 = (bf16[8,72,768]{2,1,0:T(8,128)(2,1)}, bf16[8,72,768]{2,1,0:T(8,128)(2,1)}, u32[]{:S(2)}, u32[]{:S(2)}) collective-permute-start(bf16[8,72,768]{2,1,0:T(8,128)(2,1)} %pad_maximum_fusion.8), channel_id=1, source_target_pairs={{0,2},{1,3},{2,0},{3,1},{4,6},{5,7},{6,4},{7,5},{8,10},{9,11},{10,... | collective-permute-start | bytes 2654216 | tf_op jit(solution)/shard_map/ppermute | solution.py:155
  140.1 70.6 %collective-permute-start.14 = (bf16[768,768]{1,0:T(8,128)(2,1)}, bf16[768,768]{1,0:T(8,128)(2,1)}, u32[]{:S(2)}, u32[]{:S(2)}) collective-permute-start(bf16[768,768]{1,0:T(8,128)(2,1)} %pad_maximum_fusion.4), channel_id=1, source_target_pairs={{0,2},{1,3},{2,0},{3,1},{4,6},{5,7},{6,4},{7,5},{8,10},{9,11},{10,... | collective-permute-start | bytes 3538952 | tf_op jit(solution)/shard_map/ppermute | solution.py:155
  213.6 41.3 %collective-permute-start.15 = (bf16[1536,768]{1,0:T(8,128)(2,1)}, bf16[1536,768]{1,0:T(8,128)(2,1)}, u32[]{:S(2)}, u32[]{:S(2)}) collective-permute-start(bf16[1536,768]{1,0:T(8,128)(2,1)} %get-tuple-element.286), channel_id=1, source_target_pairs={{0,1},{1,0},{2,3},{3,2},{4,5},{5,4},{6,7},{7,6},{8,9},{9,8},{10,11... | collective-permute-start | bytes 7077896 | tf_op jit(solution)/shard_map/ppermute | solution.py:155
  215.8 28.7 %collective-permute-start.19 = (bf16[768,768]{1,0:T(8,128)(2,1)}, bf16[768,768]{1,0:T(8,128)(2,1)}, u32[]{:S(2)}, u32[]{:S(2)}) collective-permute-start(bf16[768,768]{1,0:T(8,128)(2,1)} %pad_maximum_fusion.5), channel_id=1, source_target_pairs={{0,2},{1,3},{2,0},{3,1},{4,6},{5,7},{6,4},{7,5},{8,10},{9,11},{10,... | collective-permute-start | bytes 3538952 | tf_op jit(solution)/shard_map/ppermute | solution.py:155
  222.0 25.4 %collective-permute-start.25 = (bf16[16,72,768]{2,1,0:T(8,128)(2,1)}, bf16[16,72,768]{2,1,0:T(8,128)(2,1)}, u32[]{:S(2)}, u32[]{:S(2)}) collective-permute-start(bf16[16,72,768]{2,1,0:T(8,128)(2,1)} %get-tuple-element.288), channel_id=1, source_target_pairs={{0,1},{1,0},{2,3},{3,2},{4,5},{5,4},{6,7},{7,6},{8,9},{9,8},{10,11... | collective-permute-start | bytes 5308424 | tf_op jit(solution)/shard_map/ppermute | solution.py:155
  247.3 43.5 %collective-permute-start.20 = (bf16[1536,768]{1,0:T(8,128)(2,1)}, bf16[1536,768]{1,0:T(8,128)(2,1)}, u32[]{:S(2)}, u32[]{:S(2)}) collective-permute-start(bf16[1536,768]{1,0:T(8,128)(2,1)} %get-tuple-element.284), channel_id=1, source_target_pairs={{0,1},{1,0},{2,3},{3,2},{4,5},{5,4},{6,7},{7,6},{8,9},{9,8},{10,11... | collective-permute-start | bytes 7077896 | tf_op jit(solution)/shard_map/ppermute | solution.py:155
  500.7 32.9 %collective-permute-start.38 = (bf16[1536,768]{1,0:T(8,128)(2,1)}, bf16[1536,768]{1,0:T(8,128)(2,1)}, u32[]{:S(2)}, u32[]{:S(2)}) collective-permute-start(bf16[1536,768]{1,0:T(8,128)(2,1)} %convolution_convert_fusion.1), channel_id=1, source_target_pairs={{0,1},{1,0},{2,3},{3,2},{4,5},{5,4},{6,7},{7,6},{8,9},{9,8},{10,11... | collective-permute-start | bytes 7077896 | tf_op jit(solution)/shard_map/ppermute | solution.py:155
  507.8 33.6 %collective-permute-start.45 = (bf16[1536,768]{1,0:T(8,128)(2,1)}, bf16[1536,768]{1,0:T(8,128)(2,1)}, u32[]{:S(2)}, u32[]{:S(2)}) collective-permute-start(bf16[1536,768]{1,0:T(8,128)(2,1)} %convolution_convert_fusion), channel_id=1, source_target_pairs={{0,1},{1,0},{2,3},{3,2},{4,5},{5,4},{6,7},{7,6},{8,9},{9,8},{10,11... | collective-permute-start | bytes 7077896 | tf_op jit(solution)/shard_map/ppermute | solution.py:155
  531.4 15.3 %collective-permute-start.27 = (f32[4,70,288]{2,1,0:T(8,128)S(1)}, f32[4,70,288]{2,1,0:T(8,128)S(1)}, u32[]{:S(2)}, u32[]{:S(2)}) collective-permute-start(f32[4,70,288]{2,1,0:T(8,128)S(1)} %slice.377), channel_id=1, source_target_pairs={{0,4},{1,5},{2,6},{3,7},{4,0},{5,1},{6,2},{7,3},{8,12},{9,13},{10,... | collective-permute-start | bytes 967688 | tf_op jit(solution)/shard_map/ppermute | solution.py:155
  533.0 16.0 %collective-permute-start.33 = (bf16[4,24,768]{2,1,0:T(8,128)(2,1)S(1)}, bf16[4,24,768]{2,1,0:T(8,128)(2,1)S(1)}, u32[]{:S(2)}, u32[]{:S(2)}) collective-permute-start(bf16[4,24,768]{2,1,0:T(8,128)(2,1)S(1)} %slice.522), channel_id=1, source_target_pairs={{0,4},{1,5},{2,6},{3,7},{4,0},{5,1},{6,2},{7,3},{8,12},{9,13},{10,... | collective-permute-start | bytes 442376 | tf_op jit(solution)/shard_map/ppermute | solution.py:155
  539.8 29.0 %collective-permute-start.39 = (bf16[768,768]{1,0:T(8,128)(2,1)S(1)}, bf16[768,768]{1,0:T(8,128)(2,1)S(1)}, u32[]{:S(2)}, u32[]{:S(2)}) collective-permute-start(bf16[768,768]{1,0:T(8,128)(2,1)S(1)} %slice.517), channel_id=1, source_target_pairs={{0,2},{1,3},{2,0},{3,1},{4,6},{5,7},{6,4},{7,5},{8,10},{9,11},{10,... | collective-permute-start | bytes 3538952 | tf_op jit(solution)/shard_map/ppermute | solution.py:155
  546.0 46.7 %collective-permute-start.46 = (bf16[768,768]{1,0:T(8,128)(2,1)S(1)}, bf16[768,768]{1,0:T(8,128)(2,1)S(1)}, u32[]{:S(2)}, u32[]{:S(2)}) collective-permute-start(bf16[768,768]{1,0:T(8,128)(2,1)S(1)} %slice.516), channel_id=1, source_target_pairs={{0,2},{1,3},{2,0},{3,1},{4,6},{5,7},{6,4},{7,5},{8,10},{9,11},{10,... | collective-permute-start | bytes 3538952 | tf_op jit(solution)/shard_map/ppermute | solution.py:155
  555.0 39.6 %collective-permute-start.29 = (f32[1,70,288]{2,1,0:T(8,128)S(1)}, f32[1,70,288]{2,1,0:T(8,128)S(1)}, u32[]{:S(2)}, u32[]{:S(2)}) collective-permute-start(f32[1,70,288]{2,1,0:T(8,128)S(1)} %slice.381), channel_id=1, source_target_pairs={{0,16},{1,17},{2,18},{3,19},{4,20},{5,21},{6,22},{7,23},{8,24},{9,... | collective-permute-start | bytes 241928 | tf_op jit(solution)/shard_map/ppermute | solution.py:155
  558.1 38.2 %collective-permute-start.35 = (f32[1,24,768]{2,1,0:T(8,128)S(1)}, f32[1,24,768]{2,1,0:T(8,128)S(1)}, u32[]{:S(2)}, u32[]{:S(2)}) collective-permute-start(f32[1,24,768]{2,1,0:T(8,128)S(1)} %slice.391), channel_id=1, source_target_pairs={{0,16},{1,17},{2,18},{3,19},{4,20},{5,21},{6,22},{7,23},{8,24},{9,... | collective-permute-start | bytes 221192 | tf_op jit(solution)/shard_map/ppermute | solution.py:155
  569.2 27.6 %collective-permute-start.40 = (bf16[384,768]{1,0:T(8,128)(2,1)S(1)}, bf16[384,768]{1,0:T(8,128)(2,1)S(1)}, u32[]{:S(2)}, u32[]{:S(2)}) collective-permute-start(bf16[384,768]{1,0:T(8,128)(2,1)S(1)} %slice.519), channel_id=1, source_target_pairs={{0,4},{1,5},{2,6},{3,7},{4,0},{5,1},{6,2},{7,3},{8,12},{9,13},{10,... | collective-permute-start | bytes 1769480 | tf_op jit(solution)/shard_map/ppermute | solution.py:155
  593.1 14.0 %collective-permute-start.47 = (bf16[384,768]{1,0:T(8,128)(2,1)S(1)}, bf16[384,768]{1,0:T(8,128)(2,1)S(1)}, u32[]{:S(2)}, u32[]{:S(2)}) collective-permute-start(bf16[384,768]{1,0:T(8,128)(2,1)S(1)} %slice.518), channel_id=1, source_target_pairs={{0,4},{1,5},{2,6},{3,7},{4,0},{5,1},{6,2},{7,3},{8,12},{9,13},{10,... | collective-permute-start | bytes 1769480 | tf_op jit(solution)/shard_map/ppermute | solution.py:155
  594.6 14.4 %collective-permute-start.30 = (f32[70,288]{1,0:T(8,128)S(1)}, f32[70,288]{1,0:T(8,128)S(1)}, u32[]{:S(2)}, u32[]{:S(2)}) collective-permute-start(f32[70,288]{1,0:T(8,128)S(1)} %fusion.94), channel_id=1, source_target_pairs={{0,2},{1,3},{2,0},{3,1},{4,6},{5,7},{6,4},{7,5},{8,10},{9,11},{10,... | collective-permute-start | bytes 241928 | tf_op jit(solution)/shard_map/ppermute | solution.py:155
  596.3 34.1 %collective-permute-start.36 = (f32[24,768]{1,0:T(8,128)S(1)}, f32[24,768]{1,0:T(8,128)S(1)}, u32[]{:S(2)}, u32[]{:S(2)}) collective-permute-start(f32[24,768]{1,0:T(8,128)S(1)} %bitcast.300), channel_id=1, source_target_pairs={{0,2},{1,3},{2,0},{3,1},{4,6},{5,7},{6,4},{7,5},{8,10},{9,11},{10,... | collective-permute-start | bytes 221192 | tf_op jit(solution)/shard_map/ppermute | solution.py:155
  597.0 19.3 %collective-permute-start.41 = (f32[192,768]{1,0:T(8,128)S(1)}, f32[192,768]{1,0:T(8,128)S(1)}, u32[]{:S(2)}, u32[]{:S(2)}) collective-permute-start(f32[192,768]{1,0:T(8,128)S(1)} %slice.399), channel_id=1, source_target_pairs={{0,8},{1,9},{2,10},{3,11},{4,12},{5,13},{6,14},{7,15},{8,0},{9,1},... | collective-permute-start | bytes 1769480 | tf_op jit(solution)/shard_map/ppermute | solution.py:155
  607.2 22.2 %collective-permute-start.48 = (f32[192,768]{1,0:T(8,128)S(1)}, f32[192,768]{1,0:T(8,128)S(1)}, u32[]{:S(2)}, u32[]{:S(2)}) collective-permute-start(f32[192,768]{1,0:T(8,128)S(1)} %slice.409), channel_id=1, source_target_pairs={{0,8},{1,9},{2,10},{3,11},{4,12},{5,13},{6,14},{7,15},{8,0},{9,1},... | collective-permute-start | bytes 1769480 | tf_op jit(solution)/shard_map/ppermute | solution.py:155
  616.4 14.1 %collective-permute-start.42 = (f32[96,768]{1,0:T(8,128)S(1)}, f32[96,768]{1,0:T(8,128)S(1)}, u32[]{:S(2)}, u32[]{:S(2)}) collective-permute-start(f32[96,768]{1,0:T(8,128)S(1)} %slice.401), channel_id=1, source_target_pairs={{0,16},{1,17},{2,18},{3,19},{4,20},{5,21},{6,22},{7,23},{8,24},{9,... | collective-permute-start | bytes 884744 | tf_op jit(solution)/shard_map/ppermute | solution.py:155
  629.5 13.6 %collective-permute-start.49 = (f32[96,768]{1,0:T(8,128)S(1)}, f32[96,768]{1,0:T(8,128)S(1)}, u32[]{:S(2)}, u32[]{:S(2)}) collective-permute-start(f32[96,768]{1,0:T(8,128)S(1)} %slice.411), channel_id=1, source_target_pairs={{0,16},{1,17},{2,18},{3,19},{4,20},{5,21},{6,22},{7,23},{8,24},{9,... | collective-permute-start | bytes 884744 | tf_op jit(solution)/shard_map/ppermute | solution.py:155
  630.4 13.9 %collective-permute-start.37 = (f32[2,24,768]{2,1,0:T(8,128)S(1)}, f32[2,24,768]{2,1,0:T(8,128)S(1)}, u32[]{:S(2)}, u32[]{:S(2)}) collective-permute-start(f32[2,24,768]{2,1,0:T(8,128)S(1)} %maximum_select_fusion.10), channel_id=1, source_target_pairs={{0,1},{1,0},{2,3},{3,2},{4,5},{5,4},{6,7},{7,6},{8,9},{9,8},{10,11... | collective-permute-start | bytes 442376 | tf_op jit(solution)/shard_map/ppermute | solution.py:155
  630.5 13.8 %collective-permute-start.43 = (f32[96,768]{1,0:T(8,128)S(1)}, f32[96,768]{1,0:T(8,128)S(1)}, u32[]{:S(2)}, u32[]{:S(2)}) collective-permute-start(f32[96,768]{1,0:T(8,128)S(1)} %slice_add_fusion.10), channel_id=1, source_target_pairs={{0,2},{1,3},{2,0},{3,1},{4,6},{5,7},{6,4},{7,5},{8,10},{9,11},{10,... | collective-permute-start | bytes 884744 | tf_op jit(solution)/shard_map/ppermute | solution.py:155
  663.4 20.4 %collective-permute-start.57 = (f32[768,256]{1,0:T(8,128)S(1)}, f32[768,256]{1,0:T(8,128)}, u32[]{:S(2)}, u32[]{:S(2)}) collective-permute-start(f32[768,256]{1,0:T(8,128)S(1)} %constant_dynamic-slice_fusion.4), channel_id=1, source_target_pairs={{0,4},{1,5},{2,6},{3,7},{4,0},{5,1},{6,2},{7,3},{8,12},{9,13},{10,... | collective-permute-start | bytes 2359304 | tf_op jit(solution)/shard_map/ppermute | solution.py:155
  686.0 11.3 %collective-permute-start.58 = (f32[384,256]{1,0:T(8,128)}, f32[384,256]{1,0:T(8,128)}, u32[]{:S(2)}, u32[]{:S(2)}) collective-permute-start(f32[384,256]{1,0:T(8,128)} %constant_dynamic-slice_fusion.3), channel_id=1, source_target_pairs={{0,8},{1,9},{2,10},{3,11},{4,12},{5,13},{6,14},{7,15},{8,0},{9,1},... | collective-permute-start | bytes 1179656 | tf_op jit(solution)/shard_map/ppermute | solution.py:155
  711.2 11.5 %collective-permute-start.60 = (f32[192,256]{1,0:T(8,128)S(1)}, f32[192,256]{1,0:T(8,128)S(1)}, u32[]{:S(2)}, u32[]{:S(2)}) collective-permute-start(f32[192,256]{1,0:T(8,128)S(1)} %dynamic-slice_add_fusion.2), channel_id=1, source_target_pairs={{0,16},{1,17},{2,18},{3,19},{4,20},{5,21},{6,22},{7,23},{8,24},{9,... | collective-permute-start | bytes 589832 | tf_op jit(solution)/shard_map/ppermute | solution.py:155
  734.5 24.7 %collective-permute-start.62 = (f32[768,256]{1,0:T(8,128)S(1)}, f32[768,256]{1,0:T(8,128)}, u32[]{:S(2)}, u32[]{:S(2)}) collective-permute-start(f32[768,256]{1,0:T(8,128)S(1)} %maximum_select_fusion.3), channel_id=1, source_target_pairs={{0,4},{1,5},{2,6},{3,7},{4,0},{5,1},{6,2},{7,3},{8,12},{9,13},{10,... | collective-permute-start | bytes 2359304 | tf_op jit(solution)/shard_map/ppermute | solution.py:155
  759.1 56.2 %collective-permute-start.52 = (f32[8,86,96]{2,1,0:T(8,128)S(1)}, f32[8,86,96]{2,1,0:T(8,128)S(1)}, u32[]{:S(2)}, u32[]{:S(2)}) collective-permute-start(f32[8,86,96]{2,1,0:T(8,128)S(1)} %pad_maximum_fusion.13), channel_id=1, source_target_pairs={{0,1},{1,0},{2,3},{3,2},{4,5},{5,4},{6,7},{7,6},{8,9},{9,8},{10,11... | collective-permute-start | bytes 792584 | tf_op jit(solution)/shard_map/ppermute | solution.py:155
  814.5 15.8 %collective-permute-start.63 = (bf16[384,768]{1,0:T(8,128)(2,1)S(1)}, bf16[384,768]{1,0:T(8,128)(2,1)S(1)}, u32[]{:S(2)}, u32[]{:S(2)}) collective-permute-start(bf16[384,768]{1,0:T(8,128)(2,1)S(1)} %convolution_convert_fusion.3), channel_id=1, source_target_pairs={{0,2},{1,3},{2,0},{3,1},{4,6},{5,7},{6,4},{7,5},{8,10},{9,11},{10,... | collective-permute-start | bytes 1769480 | tf_op jit(solution)/shard_map/ppermute | solution.py:155
  831.4 17.6 %collective-permute-start.64 = (bf16[2,384,768]{2,1,0:T(8,128)(2,1)}, bf16[2,384,768]{2,1,0:T(8,128)(2,1)}, u32[]{:S(2)}, u32[]{:S(2)}) collective-permute-start(bf16[2,384,768]{2,1,0:T(8,128)(2,1)} %pad_maximum_fusion.6), channel_id=1, source_target_pairs={{0,1},{1,0},{2,3},{3,2},{4,5},{5,4},{6,7},{7,6},{8,9},{9,8},{10,11... | collective-permute-start | bytes 3538952 | tf_op jit(solution)/shard_map/ppermute | solution.py:155
  (120 other events, 1841.0 us)

commit v2 on v1

--- a/solution.py
+++ b/solution.py
@@ -79,70 +79,15 @@
     half_dim = HEAD_DIM // 2
     frequency = ROPE_BASE ** (-(jnp.arange(half_dim, dtype=jnp.float32) * 2.0 / HEAD_DIM))
     turned = positions.astype(jnp.float32)[..., None] * frequency
-    return (jnp.cos(turned)[..., None, :], jnp.sin(turned)[..., None, :])
-
-
-def rotate(values, cosine, sine_table):
-    half_dim = values.shape[-1] // 2
-    first_half = values[..., :half_dim]
-    second_half = values[..., half_dim:]
-    return jnp.concatenate(
-        [
-            first_half * cosine - second_half * sine_table,
-            second_half * cosine + first_half * sine_table,
-        ],
-        axis=-1,
-    )
-
-
-def unrotate(values, cosine, sine_table):
-    half_dim = values.shape[-1] // 2
-    first_half = values[..., :half_dim]
-    second_half = values[..., half_dim:]
-    return jnp.concatenate(
-        [
-            first_half * cosine + second_half * sine_table,
-            second_half * cosine - first_half * sine_table,
-        ],
-        axis=-1,
-    )
-
-
-def attend_head(operands):
-    query_head, key_head, value_head = operands
-    scores = jnp.einsum(
-        "sqd,skd->sqk", query_head, key_head, preferred_element_type=jnp.float32
-    ) * HEAD_DIM ** (-0.5)
-    row_peak = jnp.max(scores, axis=-1, keepdims=True)
-    exp_scores = jnp.exp(scores - row_peak)
-    row_total = jnp.sum(exp_scores, axis=-1, keepdims=True)
-    prob_low = (exp_scores / row_total).astype(jnp.bfloat16)
-    mixed_head = jnp.einsum(
-        "sqk,skd->sqd", prob_low, value_head, preferred_element_type=jnp.float32
-    )
-    return (mixed_head, (row_peak + jnp.log(row_total))[..., 0])
-
-
-def attend_back(operands):
-    query_head, key_head, value_head, grad_head, log_total = operands
-    scores = jnp.einsum(
-        "sqd,skd->sqk", query_head, key_head, preferred_element_type=jnp.float32
-    ) * HEAD_DIM ** (-0.5)
-    prob_rows = jnp.exp(scores - log_total[..., None])
-    prob_low = prob_rows.astype(jnp.bfloat16)
-    value_grad = jnp.einsum("sqk,sqd->skd", prob_low, grad_head, preferred_element_type=jnp.float32)
-    prob_grad = jnp.einsum(
-        "sqd,skd->sqk", grad_head, value_head, preferred_element_type=jnp.float32
-    )
-    row_delta = jnp.sum(prob_grad * prob_rows, axis=-1, keepdims=True)
-    score_grad = (prob_rows * (prob_grad - row_delta)).astype(jnp.bfloat16)
-    query_grad = jnp.einsum(
-        "sqk,skd->sqd", score_grad, key_head, preferred_element_type=jnp.float32
-    ) * HEAD_DIM ** (-0.5)
-    key_grad = jnp.einsum(
-        "sqk,sqd->skd", score_grad, query_head, preferred_element_type=jnp.float32
-    ) * HEAD_DIM ** (-0.5)
-    return (query_grad, key_grad, value_grad)
+    return (jnp.cos(turned), jnp.sin(turned))
+
+
+PAIR = 2 * HEAD_DIM
+SPAN = 1024
+STRIP = 256
+PARTS = 4
+LANES = 128
+ATTEND_CALLS = 3
 
 
 BOTH = ("wide", "narrow")
@@ -197,6 +142,12 @@
 def gather_wide(piece):
     blocks = gather_blocks(piece[None], wide_masks())
     return in_order(blocks, wide_masks(), lax.axis_size("narrow"), lax.axis_index("wide"))
+
+
+def gather_parts(piece):
+    own = gather_blocks(piece, wide_masks())
+    beside = swap(own, 2)
+    return [own, beside, swap(own, 1), swap(beside, 1)]
 
 
 def quarter_rows(array):
@@ -259,30 +210,39 @@
     return blocks
 
 
+def row_dot(left_side, right_side):
+    return lax.dot_general(
+        left_side, right_side, (((1,), (1,)), ((), ())), preferred_element_type=jnp.float32
+    )
+
+
 def split_two(values):
     high = values.astype(jnp.bfloat16)
     return high, (values - high.astype(jnp.float32)).astype(jnp.bfloat16)
 
 
-def newton_kernel(gram_ref, out_ref, gram_now, total, left, right):
+def newton_kernel(gram_ref, rows_ref, out_ref, gram_now, other, left, right, rows_left):
     tile = GRAM_TILE
+    count = rows_ref.shape[0]
     trace = jnp.zeros((1, 1), jnp.float32)
-    spot_mask = lax.broadcasted_iota(jnp.int32, (tile, tile), 0) == lax.broadcasted_iota(
+    diagonal = lax.broadcasted_iota(jnp.int32, (tile, tile), 0) == lax.broadcasted_iota(
         jnp.int32, (tile, tile), 1
     )
     for number, (row, column) in enumerate(GRAM_SPOTS):
-        block = gram_ref[number * tile : (number + 1) * tile, :]
         if row == column:
-            picked = jnp.where(spot_mask, block, 0.0)
+            picked = jnp.where(diagonal, gram_ref[number * tile : (number + 1) * tile, :], 0.0)
             trace = trace + jnp.sum(jnp.sum(picked, axis=0, keepdims=True), axis=1, keepdims=True)
-    length = jnp.sqrt(trace) + 1e-07
-    inverse = 1.0 / length
+    inverse = 1.0 / (jnp.sqrt(trace) + 1e-07)
     scale = inverse * inverse
+
+    def span(number):
+        return slice(number * tile, (number + 1) * tile)
+
     for number, (row, column) in enumerate(GRAM_SPOTS):
-        block = gram_ref[number * tile : (number + 1) * tile, :] * scale
-        gram_now[row * tile : (row + 1) * tile, column * tile : (column + 1) * tile] = block
+        block = gram_ref[span(number), :] * scale
+        gram_now[span(row), span(column)] = block
         if row != column:
-            gram_now[column * tile : (column + 1) * tile, row * tile : (row + 1) * tile] = block.T
+            gram_now[span(column), span(row)] = block.T
 
     def set_left(values):
         high, low = split_two(values)
@@ -296,57 +256,73 @@
         right[D : 2 * D, :] = low
         right[2 * D : 3 * D, :] = high
 
-    def product():
-        return jnp.dot(left[...], right[...], preferred_element_type=jnp.float32)
-
-    diagonal = lax.broadcasted_iota(jnp.int32, (D, D), 0) == lax.broadcasted_iota(
-        jnp.int32, (D, D), 1
-    )
+    def set_rows(values):
+        high, low = split_two(values)
+        rows_left[:, 0:D] = high
+        rows_left[:, D : 2 * D] = high
+        rows_left[:, 2 * D : 3 * D] = low
+
+    def product(target, finish):
+        for column in range(D // tile):
+            rows = (column + 1) * tile
+            block = jnp.dot(left[0:rows, :], right[:, span(column)], preferred_element_type=jnp.float32)
+            for row in range(column + 1):
+                piece = finish(block[span(row), :], row, column)
+                target[span(row), span(column)] = piece
+                if row != column:
+                    target[span(column), span(row)] = piece.T
+
+    def same(block, row, column):
+        return block
+
+    def factor(block, row, column):
+        block = NEWTON_B * gram_now[span(row), span(column)] + NEWTON_C * block
+        if row == column:
+            block = block + jnp.where(diagonal, NEWTON_A, 0.0)
+        return block
 
     def set_factor():
         set_left(gram_now[...])
         set_right(gram_now[...])
-        factor = NEWTON_B * gram_now[...] + NEWTON_C * product()
-        factor = factor + jnp.where(diagonal, NEWTON_A, 0.0)
-        set_right(factor)
-        return factor
-
-    def advance():
-        moved = product()
-        set_left(moved)
-        gram_now[...] = product()
-
-    total[...] = set_factor()
-    advance()
+        product(other, factor)
+        set_right(other[...])
+
+    def rows_product():
+        return jnp.dot(rows_left[...], right[...], preferred_element_type=jnp.float32)
+
+    set_rows(rows_ref[...] * inverse)
 
     def body(step, carry):
         set_factor()
-        advance()
-        set_left(total[...])
-        total[...] = product()
+        product(other, same)
+        set_left(other[...])
+        product(gram_now, same)
+        set_rows(rows_product())
         return carry
 
-    lax.fori_loop(0, NS_ITERS - 2, body, 0)
+    lax.fori_loop(0, NS_ITERS - 1, body, 0)
     set_factor()
-    set_left(total[...])
-    out_ref[...] = product() * inverse
-
-
-def newton_product(gram_blocks):
+    out_ref[...] = rows_product().astype(out_ref.dtype)
+
+
+def newton_rows(gram_blocks, rows):
+    count = rows.shape[0]
     return pl.pallas_call(
         newton_kernel,
-        out_shape=jax.ShapeDtypeStruct((D, D), jnp.float32),
-        in_specs=[pl.BlockSpec(memory_space=pltpu.VMEM)],
+        out_shape=jax.ShapeDtypeStruct((count, D), jnp.bfloat16),
+        in_specs=[pl.BlockSpec(memory_space=pltpu.VMEM)] * 2,
         out_specs=pl.BlockSpec(memory_space=pltpu.VMEM),
         scratch_shapes=[
             pltpu.VMEM((D, D), jnp.float32),
             pltpu.VMEM((D, D), jnp.float32),
             pltpu.VMEM((D, 3 * D), jnp.bfloat16),
             pltpu.VMEM((3 * D, D), jnp.bfloat16),
+            pltpu.VMEM((count, 3 * D), jnp.bfloat16),
         ],
         compiler_params=pltpu.CompilerParams(vmem_limit_bytes=48 << 20),
+        cost_estimate=pl.CostEstimate(flops=60 * D * D * D, bytes_accessed=4 << 20, transcendentals=0),
         name="newton",
-    )(gram_blocks)
+    )(gram_blocks, rows)
 
 
 def pick_rows(parts, spot):
@@ -386,8 +362,7 @@
         for moment, gradient in zip(moment_next, gradients)
     )
     rows = pick_rows(updates, spot)
-    factor = newton_product(sum_gram(local_gram(rows)))
-    ortho = exact_times(rows, factor).astype(jnp.bfloat16)
+    ortho = newton_rows(sum_gram(local_gram(rows)), rows)
     pair = jnp.stack([ortho, swap(ortho, 2)])
     quad = jnp.concatenate([pair, swap(pair, 1)], axis=0)
     place = np.array([0, 2, 1, 3])
@@ -399,6 +374,291 @@
         rate = MUON_RATE * SHAPE_FACTOR * math.sqrt(max(rows_whole[number], D))
         updated.append(weight * (1.0 - MUON_RATE * MUON_DECAY) - rate * mine)
     return tuple(updated), moment_next
+
+
+def turn(values, cosine, sine_table):
+    lane = lax.broadcasted_iota(jnp.int32, values.shape, 1)
+    half = HEAD_DIM // 2
+    partner = jnp.where(
+        lane % HEAD_DIM < half,
+        pltpu.roll(values, PAIR - half, 1),
+        pltpu.roll(values, half, 1),
+    )
+    return values * cosine + partner * sine_table
+
+
+def attend_kernel(
+    hot_ref, tq_ref, tk_ref, tv_ref, cos_ref, sin_ref,
+    q_ref, k_ref, v_ref, mixed_ref, log_ref,
+    q_all, v_turned, mixed_turned, prob_all,
+):
+    hot = hot_ref[...]
+    cosine = cos_ref[...]
+    sine_table = sin_ref[...]
+    queries = jnp.dot(hot, tq_ref[...], preferred_element_type=jnp.float32)
+    queries = turn(queries, cosine, sine_table).astype(jnp.bfloat16) * HEAD_DIM ** (-0.5)
+    queries = queries.astype(jnp.bfloat16)
+    q_ref[...] = queries
+    q_all[0:SEQ_LEN, :] = queries
+    q_all[SEQ_LEN:SPAN, :] = jnp.zeros((SPAN - SEQ_LEN, PAIR), jnp.bfloat16)
+    keys = jnp.dot(hot, tk_ref[...], preferred_element_type=jnp.float32)
+    keys = turn(keys, cosine, sine_table).astype(jnp.bfloat16)
+    k_ref[...] = keys
+    values = jnp.dot(hot, tv_ref[...], preferred_element_type=jnp.float32)
+    v_ref[...] = values.astype(jnp.bfloat16)
+    v_turned[...] = values.T.astype(jnp.bfloat16)
+
+    for head in range(2):
+        lane = lax.broadcasted_iota(jnp.int32, (SEQ_LEN, PAIR), 1)
+        keys_head = jnp.where(lane // HEAD_DIM == head, k_ref[...], jnp.zeros((), jnp.bfloat16))
+        values_head = v_turned[head * HEAD_DIM : (head + 1) * HEAD_DIM, :]
+
+        def body(step, carry):
+            at = pl.multiple_of(step * STRIP, STRIP)
+            scores = row_dot(keys_head, q_all[pl.ds(at, STRIP), :])
+            peak = jnp.max(scores, axis=0, keepdims=True)
+            powers = jnp.exp(scores - peak)
+            total = jnp.sum(powers, axis=0, keepdims=True)
+            prob_low = (powers * (1.0 / total)).astype(jnp.bfloat16)
+            prob_all[:, pl.ds(at, STRIP)] = prob_low
+            log_ref[0, head : head + 1, pl.ds(at, STRIP)] = peak + jnp.log(total)
+            return carry
+
+        lax.fori_loop(0, SPAN // STRIP, body, 0)
+        mixed_turned[head * HEAD_DIM : (head + 1) * HEAD_DIM, :] = jnp.dot(
+            values_head, prob_all[...], preferred_element_type=jnp.float32)
+    mixed_ref[...] = mixed_turned[...].T[0:SEQ_LEN, :].astype(jnp.bfloat16)
+
+
+def attend_call(hot, tables, cosine, sine_table, first, count):
+    whole = lambda step: (0, 0)
+    source = lambda step: (0, step + first)
+    own = lambda step: (0, step)
+    rows_low = jax.ShapeDtypeStruct((SEQ_LEN, count * PAIR), jnp.bfloat16)
+    return pl.pallas_call(
+        attend_kernel,
+        grid=(count,),
+        in_specs=[
+            pl.BlockSpec(hot.shape, whole),
+            pl.BlockSpec((hot.shape[1], PAIR), source),
+            pl.BlockSpec((hot.shape[1], PAIR), lambda step: (0, step + first + D // PAIR)),
+            pl.BlockSpec((hot.shape[1], PAIR), lambda step: (0, step + first + 2 * D // PAIR)),
+            pl.BlockSpec((SEQ_LEN, PAIR), whole),
+            pl.BlockSpec((SEQ_LEN, PAIR), whole),
+        ],
+        out_specs=[
+            pl.BlockSpec((SEQ_LEN, PAIR), own),
+            pl.BlockSpec((SEQ_LEN, PAIR), own),
+            pl.BlockSpec((SEQ_LEN, PAIR), own),
+            pl.BlockSpec((SEQ_LEN, PAIR), own),
+            pl.BlockSpec((1, 2, SPAN), lambda step: (step, 0, 0)),
+        ],
+        out_shape=[rows_low] * 4 + [jax.ShapeDtypeStruct((count, 2, SPAN), jnp.float32)],
+        scratch_shapes=[
+            pltpu.VMEM((SPAN, PAIR), jnp.bfloat16),
+            pltpu.VMEM((PAIR, SEQ_LEN), jnp.bfloat16),
+            pltpu.VMEM((PAIR, SPAN), jnp.float32),
+            pltpu.VMEM((SEQ_LEN, SPAN), jnp.bfloat16),
+        ],
+        compiler_params=pltpu.CompilerParams(vmem_limit_bytes=40 << 20),
+        cost_estimate=pl.CostEstimate(
+            flops=count * 8 * SPAN * SPAN * 256, bytes_accessed=count * 2 << 20,
+            transcendentals=count * 2 * SPAN * SEQ_LEN,
+        ),
+        name="attend",
+    )(hot, tables, tables, tables, cosine, sine_table)
+
+
+def attend_back_kernel(
+    hot_ref, q_ref, k_ref, v_ref, grad_ref, log_ref, cos_ref, sin_ref,
+    low_ref, sums_ref,
+    q_all, grad_all, k_turned, prob_all, score_all, query_turned, key_sum, value_sum,
+):
+    rest = jnp.zeros((SPAN - SEQ_LEN, PAIR), jnp.bfloat16)
+    q_all[0:SEQ_LEN, :] = q_ref[...]
+    q_all[SEQ_LEN:SPAN, :] = rest
+    grad_all[0:SEQ_LEN, :] = grad_ref[...]
+    grad_all[SEQ_LEN:SPAN, :] = rest
+    k_turned[...] = k_ref[...].astype(jnp.float32).T.astype(jnp.bfloat16)
+    lane = lax.broadcasted_iota(jnp.int32, (SEQ_LEN, PAIR), 1)
+    none = jnp.zeros((), jnp.bfloat16)
+
+    for head in range(2):
+        keys_head = jnp.where(lane // HEAD_DIM == head, k_ref[...], none)
+        values_head = jnp.where(lane // HEAD_DIM == head, v_ref[...], none)
+
+        def body(step, carry):
+            at = pl.multiple_of(step * STRIP, STRIP)
+            scores = row_dot(keys_head, q_all[pl.ds(at, STRIP), :])
+            prob_rows = jnp.exp(scores - log_ref[0, head : head + 1, pl.ds(at, STRIP)])
+            prob_all[:, pl.ds(at, STRIP)] = prob_rows.astype(jnp.bfloat16)
+            prob_grad = row_dot(values_head, grad_all[pl.ds(at, STRIP), :])
+            delta = jnp.sum(prob_grad * prob_rows, axis=0, keepdims=True)
+            score_all[:, pl.ds(at, STRIP)] = (prob_rows * (prob_grad - delta)).astype(jnp.bfloat16)
+            return carry
+
+        lax.fori_loop(0, SPAN // STRIP, body, 0)
+        value_part = jnp.dot(prob_all[...], grad_all[...], preferred_element_type=jnp.float32)
+        key_part = jnp.dot(score_all[...], q_all[...], preferred_element_type=jnp.float32)
+        if head == 0:
+            value_sum[...] = value_part
+            key_sum[...] = key_part
+        else:
+            value_sum[...] = jnp.where(lane < HEAD_DIM, value_sum[...], value_part)
+            key_sum[...] = jnp.where(lane < HEAD_DIM, key_sum[...], key_part)
+        query_turned[head * HEAD_DIM : (head + 1) * HEAD_DIM, :] = jnp.dot(
+            k_turned[head * HEAD_DIM : (head + 1) * HEAD_DIM, :],
+            score_all[...],
+            preferred_element_type=jnp.float32,
+        ) * HEAD_DIM ** (-0.5)
+    cosine = cos_ref[...]
+    sine_table = -sin_ref[...]
+    hot = hot_ref[...]
+    query_low = turn(query_turned[...].T[0:SEQ_LEN, :], cosine, sine_table).astype(jnp.bfloat16)
+    key_low = turn(key_sum[...], cosine, sine_table).astype(jnp.bfloat16)
+    value_low = value_sum[...].astype(jnp.bfloat16)
+    for number, low in enumerate((query_low, key_low, value_low)):
+        low_ref[number] = low
+        sums_ref[number] = jnp.dot(hot, low, preferred_element_type=jnp.float32)
+
+
+def attend_back_call(hot_turned, queries, keys, values, gradients, logs, cosine, sine_table, first):
+    count = logs.shape[0]
+    whole = lambda step: (0, 0)
+    own = lambda step: (0, step)
+    rows = pl.BlockSpec((SEQ_LEN, PAIR), own)
+    whole_rows = pl.BlockSpec((SEQ_LEN, PAIR), whole)
+    return pl.pallas_call(
+        attend_back_kernel,
+        grid=(count,),
+        in_specs=[
+            pl.BlockSpec(hot_turned.shape, whole),
+            rows,
+            rows,
+            rows,
+            pl.BlockSpec((SEQ_LEN, PAIR), lambda step: (0, step + first)),
+            pl.BlockSpec((1, 2, SPAN), lambda step: (step, 0, 0)),
+            whole_rows,
+            whole_rows,
+        ],
+        out_specs=[
+            pl.BlockSpec((3, SEQ_LEN, PAIR), lambda step: (0, 0, step)),
+            pl.BlockSpec((3, hot_turned.shape[0], PAIR), lambda step: (0, 0, step)),
+        ],
+        out_shape=[
+            jax.ShapeDtypeStruct((3, SEQ_LEN, count * PAIR), jnp.bfloat16),
+            jax.ShapeDtypeStruct((3, hot_turned.shape[0], count * PAIR), jnp.float32),
+        ],
+        scratch_shapes=[
+            pltpu.VMEM((SPAN, PAIR), jnp.bfloat16),
+            pltpu.VMEM((SPAN, PAIR), jnp.bfloat16),
+            pltpu.VMEM((PAIR, SEQ_LEN), jnp.bfloat16),
+            pltpu.VMEM((SEQ_LEN, SPAN), jnp.bfloat16),
+            pltpu.VMEM((SEQ_LEN, SPAN), jnp.bfloat16),
+            pltpu.VMEM((PAIR, SPAN), jnp.float32),
+            pltpu.VMEM((SEQ_LEN, PAIR), jnp.float32),
+            pltpu.VMEM((SEQ_LEN, PAIR), jnp.float32),
+        ],
+        compiler_params=pltpu.CompilerParams(vmem_limit_bytes=48 << 20),
+        cost_estimate=pl.CostEstimate(
+            flops=count * 20 * SPAN * SPAN * 256, bytes_accessed=count * 3 << 20,
+            transcendentals=count * 2 * SPAN * SEQ_LEN,
+        ),
+        name="attend_back",
+    )(hot_turned, queries, keys, values, gradients, logs, cosine, sine_table)
+
+
+ERF_P = 0.3275911
+ERF_A = (0.254829592, -0.284496736, 1.421413741, -1.453152027, 1.061405429)
+
+def normal_parts(values):
+    size = jnp.abs(values)
+    bell = jnp.exp(values * values * -0.5)
+    step = 1.0 / (1.0 + (ERF_P * 0.5**0.5) * size)
+    series = ERF_A[4]
+    for factor in (ERF_A[3], ERF_A[2], ERF_A[1], ERF_A[0]):
+        series = series * step + factor
+    tail = (0.5 * series) * step * bell
+    return jnp.where(values < 0.0, tail, 1.0 - tail), bell * (1.0 / math.sqrt(2.0 * math.pi))
+
+def feed_kernel(rows_ref, bias_ref, e0, e1, e2, e3, r0, r1, r2, r3, hidden_ref, slope_ref, out_ref, expand_held, reduce_held, pre, sems):
+    step = pl.program_id(0)
+    @pl.when(step == 0)
+    def _():
+        for number in range(PARTS):
+            pltpu.make_async_copy((e0,e1,e2,e3)[number], expand_held.at[number], sems.at[number]).start()
+            pltpu.make_async_copy((r0,r1,r2,r3)[number], reduce_held.at[number], sems.at[PARTS + number]).start()
+    pltpu.make_async_copy(e0, expand_held.at[step], sems.at[step]).wait()
+    for at in range(0, SEQ_LEN, 304):
+        spot = slice(at, at + 304)
+        values = row_dot(rows_ref[spot, :], expand_held[step]) + bias_ref[...]
+        below, bell = normal_parts(values)
+        hidden_ref[spot, :] = (values * below).astype(jnp.bfloat16)
+        slope_ref[spot, :] = (below + values * bell).astype(jnp.bfloat16)
+    pltpu.make_async_copy(r0, reduce_held.at[step], sems.at[PARTS + step]).wait()
+    part = jnp.dot(hidden_ref[...], reduce_held[step], preferred_element_type=jnp.float32)
+    @pl.when(step == 0)
+    def _():
+        out_ref[...] = part
+    @pl.when(step > 0)
+    def _():
+        out_ref[...] += part
+
+def feed_call(rows, bias, expands, reduces):
+    whole = lambda step: (0, 0)
+    chunk = pl.BlockSpec((SEQ_LEN, D), lambda step: (0, step))
+    anywhere = pl.BlockSpec(memory_space=pl.ANY)
+    return pl.pallas_call(
+        feed_kernel, grid=(PARTS,),
+        in_specs=[pl.BlockSpec((SEQ_LEN, D), whole), pl.BlockSpec((1, D), lambda step: (0, step))] + [anywhere] * 8,
+        out_specs=[chunk, chunk, pl.BlockSpec((SEQ_LEN, D), whole)],
+        out_shape=[jax.ShapeDtypeStruct((SEQ_LEN, FF), jnp.bfloat16)] * 2 + [jax.ShapeDtypeStruct((SEQ_LEN, D), jnp.float32)],
+        scratch_shapes=[pltpu.VMEM((PARTS, D, D), jnp.bfloat16), pltpu.VMEM((PARTS, D, D), jnp.bfloat16), pltpu.VMEM((SEQ_LEN, D), jnp.float32), pltpu.SemaphoreType.DMA((2 * PARTS,))],
+        compiler_params=pltpu.CompilerParams(vmem_limit_bytes=48 << 20),
+        cost_estimate=pl.CostEstimate(flops=4 * SEQ_LEN * D * FF, bytes_accessed=24 << 20, transcendentals=SEQ_LEN * FF),
+        name="feed",
+    )(rows, bias, *expands, *reduces)
+
+def feed_back_kernel(grad_ref, slope_ref, e0, e1, e2, e3, r0, r1, r2, r3, pre_ref, out_ref, bias_ref, expand_held, reduce_held, sems):
+    step = pl.program_id(0)
+    @pl.when(step == 0)
+    def _():
+        for number in range(PARTS):
+            pltpu.make_async_copy((r0,r1,r2,r3)[number], reduce_held.at[number], sems.at[PARTS + number]).start()
+            pltpu.make_async_copy((e0,e1,e2,e3)[number], expand_held.at[number], sems.at[number]).start()
+    pltpu.make_async_copy(r0, reduce_held.at[step], sems.at[PARTS + step]).wait()
+    total = jnp.zeros((1, D), jnp.float32)
+    for at in range(0, SEQ_LEN, 304):
+        spot = slice(at, at + 304)
+        grad = row_dot(grad_ref[spot, :], reduce_held[step]) * slope_ref[spot, :].astype(jnp.float32)
+        low = grad.astype(jnp.bfloat16)
+        pre_ref[spot, :] = low
+        total = total + jnp.sum(low.astype(jnp.float32), axis=0, keepdims=True)
+    bias_ref[...] = total
+    low = pre_ref[...]
+    pltpu.make_async_copy(e0, expand_held.at[step], sems.at[step]).wait()
+    part = jnp.dot(low, expand_held[step], preferred_element_type=jnp.float32)
+    @pl.when(step == 0)
+    def _():
+        out_ref[...] = part
+    @pl.when(step > 0)
+    def _():
+        out_ref[...] += part
+
+def feed_back_call(grad, slope, expands, reduces):
+    whole = lambda step: (0, 0)
+    chunk = pl.BlockSpec((SEQ_LEN, D), lambda step: (0, step))
+    anywhere = pl.BlockSpec(memory_space=pl.ANY)
+    return pl.pallas_call(
+        feed_back_kernel, grid=(PARTS,),
+        in_specs=[pl.BlockSpec((SEQ_LEN, D), whole), chunk] + [anywhere] * 8,
+        out_specs=[chunk, pl.BlockSpec((SEQ_LEN, D), whole), pl.BlockSpec((1, D), lambda step: (0, step))],
+        out_shape=[jax.ShapeDtypeStruct((SEQ_LEN, FF), jnp.bfloat16), jax.ShapeDtypeStruct((SEQ_LEN, D), jnp.float32), jax.ShapeDtypeStruct((1, FF), jnp.float32)],
+        scratch_shapes=[pltpu.VMEM((PARTS, D, D), jnp.bfloat16), pltpu.VMEM((PARTS, D, D), jnp.bfloat16), pltpu.SemaphoreType.DMA((2 * PARTS,))],
+        compiler_params=pltpu.CompilerParams(vmem_limit_bytes=48 << 20),
+        cost_estimate=pl.CostEstimate(flops=4 * SEQ_LEN * D * FF, bytes_accessed=24 << 20, transcendentals=0),
+        name="feed_back",
+    )(grad, slope, *expands, *reduces)
 
 
 def adam_step(weight, mean_state, square, gradient, step_rate, decay_rate, step_count):
@@ -465,8 +725,8 @@
 
     mixing_low = gather_blocks(quarter_rows(mixing_weight).astype(low_type)[None], all_masks)
     mixing_low = in_order(mixing_low, all_masks, 1, me).reshape(D, D)
-    expand_low = gather_blocks(quarter_rows(expand_weight).astype(low_type), all_masks)
-    reduce_low = gather_blocks(quarter_rows(reduce_weight).astype(low_type), all_masks)
+    expand_parts = gather_parts(quarter_rows(expand_weight).astype(low_type))
+    reduce_parts = gather_parts(quarter_rows(reduce_weight).astype(low_type))
     attend_low = gather_blocks(quarter_rows(attend_weight).astype(low_type)[None], all_masks)
     attend_low = in_order(attend_low, all_masks, 1, me).reshape(3 * D, D)
 
@@ -478,31 +738,30 @@
     token_low = token_hot.astype(low_type)
     target_hot = (targets.reshape(row_count)[:, None] == vocab_ids[None, :]).astype(jnp.float32)
     stream = embed_scale * times_plain(token_low, table_low)
+    token_ids = window.reshape(row_count)
+    lane_ids = jnp.arange(2 * LANES, dtype=jnp.int32) % LANES
+    hot = (token_ids[:, None] == lane_ids[None, :]).astype(low_type)
+    hot_turned = (token_ids[None, :] == lane_ids[:LANES, None]).astype(low_type)
     heads_high, heads_low = split_two(table_heads)
-    projected = times_plain(
-        jnp.concatenate([token_low, token_low], axis=1),
-        jnp.concatenate([heads_high, heads_low], axis=0),
-    )
-    cosine, sine_table = rotary_tables(positions)
-    head_shape = (seq_count, SEQ_LEN, HEADS, HEAD_DIM)
-    query_rot = rotate(projected[:, :D].reshape(head_shape), cosine, sine_table).astype(low_type)
-    key_rot = rotate(projected[:, D : 2 * D].reshape(head_shape), cosine, sine_table).astype(
-        low_type
-    )
-    value_low = projected[:, 2 * D :].reshape(head_shape).astype(low_type)
-    query_heads = jnp.transpose(query_rot, (2, 0, 1, 3))
-    key_heads = jnp.transpose(key_rot, (2, 0, 1, 3))
-    value_heads = jnp.transpose(value_low, (2, 0, 1, 3))
-    mixed_heads, log_totals = lax.map(attend_head, (query_heads, key_heads, value_heads))
-    mixed_low = jnp.transpose(mixed_heads, (1, 2, 0, 3)).reshape(row_count, D).astype(low_type)
+    spare = ((0, LANES - VOCAB), (0, 0))
+    tables = jnp.concatenate([jnp.pad(heads_high, spare), jnp.pad(heads_low, spare)], axis=0)
+    cosine, sine_table = rotary_tables(positions.reshape(row_count))
+    cosine = jnp.concatenate([cosine] * 4, axis=1)
+    sine_table = jnp.concatenate([-sine_table, sine_table] * 2, axis=1)
+    pairs = D // PAIR // ATTEND_CALLS
+    attended = [
+        attend_call(hot, tables, cosine, sine_table, number * pairs, pairs)
+        for number in range(ATTEND_CALLS)
+    ]
+    mixed_low = jnp.concatenate([parts[3] for parts in attended], axis=1)
     branch = times_trans(mixed_low, mixing_low) + mixing_bias
     middle = stream + branch
     normed_two, normal_two, inverse_two = norm_forward(middle, gain_two, bias_two)
     normed_two_low = normed_two.astype(low_type)
-    hidden_pre = times_trans(normed_two_low, expand_low) + expand_bias
-    hidden_act, gelu_back = jax.vjp(partial(jax.nn.gelu, approximate=False), hidden_pre)
-    hidden_low = hidden_act.astype(low_type)
-    feed_out = times_plain(hidden_low, reduce_low) + reduce_bias
+    hidden_low, slope_low, feed_out = feed_call(
+        normed_two_low, expand_bias[None, :], expand_parts, reduce_parts
+    )
+    feed_out = feed_out + reduce_bias
     output = middle + feed_out
     final_norm, normal_last, inverse_last = norm_forward(output, gain_last, bias_last)
     final_low = final_norm.astype(low_type)
@@ -528,9 +787,9 @@
         jnp.float32,
     )
     reduce_total = narrow_rows(reduce_part)
-    hidden_grad = times_trans(feed_low, reduce_low)
-    pre_grad = gelu_back(hidden_grad)[0].astype(low_type)
-    expand_bias_grad = jnp.sum(pre_grad, axis=0, dtype=jnp.float32)
+    pre_grad, normed_two_grad, expand_bias_grad = feed_back_call(
+        feed_low, slope_low, expand_parts, reduce_parts
+    )
     expand_bias_grad = in_order(
         expand_bias_grad.reshape(devices, FF // devices), all_masks, 1, me
     )
@@ -541,7 +800,6 @@
         jnp.float32,
     )
     expand_total = narrow_rows(expand_part)
-    normed_two_grad = times_plain(pre_grad, expand_low)
     middle_part, gain_two_grad, bias_two_grad = norm_backward(
         normed_two_grad, normal_two, inverse_two, gain_two
     )
@@ -555,21 +813,25 @@
     )
     mixing_total = narrow_rows(mixing_part[0])
     mixed_grad = times_plain(branch_low, mixing_low).astype(low_type)
-    grad_heads = jnp.transpose(mixed_grad.reshape(head_shape), (2, 0, 1, 3))
-    query_back, key_back, value_back = lax.map(
-        attend_back, (query_heads, key_heads, value_heads, grad_heads, log_totals)
-    )
-    query_grad = unrotate(jnp.transpose(query_back, (1, 2, 0, 3)), cosine, sine_table).reshape(
-        row_count, D
-    )
-    key_grad = unrotate(jnp.transpose(key_back, (1, 2, 0, 3)), cosine, sine_table).reshape(
-        row_count, D
-    )
-    value_grad = jnp.transpose(value_back, (1, 2, 0, 3)).reshape(row_count, D)
-    projected_low = jnp.concatenate([query_grad, key_grad, value_grad], axis=1).astype(low_type)
-    attend_bias_grad = jnp.sum(projected_low, axis=0, dtype=jnp.float32)
+    backs = [
+        attend_back_call(
+            hot_turned,
+            *attended[number][:3],
+            mixed_grad,
+            attended[number][4],
+            cosine,
+            sine_table,
+            number * pairs,
+        )
+        for number in range(ATTEND_CALLS)
+    ]
+    token_sums = jnp.concatenate([back[1][:, :VOCAB] for back in backs], axis=2)
+    token_sums = jnp.transpose(token_sums, (1, 0, 2)).reshape(VOCAB, 3 * D)
+    attend_bias_grad = jnp.sum(token_sums, axis=0)
+    projected_low = jnp.concatenate(
+        [back[0][number] for number in range(3) for back in backs], axis=1
+    )
     wide_size = lax.axis_size("wide")
-    token_sums = trans_times(token_low, projected_low)
     token_sums = jnp.transpose(token_sums.reshape(VOCAB, wide_size, 3 * D // wide_size), (1, 0, 2))
     token_sums = sum_small(token_sums)
     attend_total = lax.dot_general(

time: 866 us -> 621 us (0.72)
  matrix products: 291 us -> 49.2 us
  Pallas kernels: 50.6 us -> 176 us
  local copies, waits for them, and re-layouts: 159 us -> 77.1 us
  other arithmetic: 93.6 us -> 57.3 us
  starting transfers between devices: 72.9 us -> 61.7 us
    dot_general x84 -> x0, matrix products: 167 us -> none  [the longest x12 30.1 us: attend_head(): jnp.einsum('sqk,skd->sqd', prob_low, value_head, preferred_element_type=j...]
    pallas_call x1 -> x9, Pallas kernels: 50.6 us -> 176 us  [the longest x3 53.9 us: attend_back_call(): pl.pallas_call(attend_back_kernel, grid=(count,), in_specs=[pl.BlockSpec(...]
    dot_general x5 -> x3, matrix products: 53.9 us -> 4.92 us  [times_trans(): lax.dot_general(left_side, right_side, (((1,), (1,)), ((), ())), preferre...]
    convert_element_type x13 -> x2, other arithmetic: 15.1 us -> 1 us  [the longest x1 0.82 us: on_device(): hot_turned = (token_ids[None, :] == lane_ids[:LANES, None]).astype(low_type)]
    slice x5 -> x4, local copies, waits for them, and re-layouts: 13.8 us -> 0.05 us  [the longest x3 0.05 us: on_device(): token_sums = jnp.concatenate([back[1][:, :VOCAB] for back in backs], axis=2)]
    concatenate x14, local copies, waits for them, and re-layouts: 14.8 us -> 1.53 us  [on_device(): small_grads = jnp.concatenate([table_grad, vector_grad], axis=0)]
    dot_general x7 -> x4, matrix products: 26.9 us -> 14.2 us  [times_plain(): return jnp.dot(left_side, right_side, preferred_element_type=jnp.float32)]
    concatenate x8 -> x4, local copies, waits for them, and re-layouts: 20.8 us -> 8.13 us  [gather_blocks(): piece = jnp.concatenate([piece, swap(piece, mask)], axis=0)]
  transfers between devices with their start and end apart: 65 -> 67, of which waited for: 23 -> 25; matrix products, arithmetic and copies ran while one was open for 36% -> 26% of each run, Pallas kernels for 6% -> 29%
where the time goes in v2:
time: 621 us; the launch traced here: 613 us
  waiting for transfers between devices  180 us (29%)
  Pallas kernels  176 us (28%)
  local copies, waits for them, and re-layouts  77.1 us (12%)
  starting transfers between devices  61.7 us (10%)
  other arithmetic  57.3 us (9%)
  matrix products  49.2 us (8%)
  between operations  12.2 us (2%)
    ppermute x67, waiting for transfers between devices, swap(): lax.ppermute(value, BOTH, [(spot, spot ^ mask) for spot in range(total)])  180 us
    ppermute x67, starting transfers between devices, swap(): lax.ppermute(value, BOTH, [(spot, spot ^ mask) for spot in range(total)])  61.7 us
    pallas_call x3, Pallas kernels, attend_back_call(): pl.pallas_call(attend_back_kernel, grid=(count,), in_specs=[pl.BlockSpec(...  53.9 us
    pallas_call x3, Pallas kernels, attend_call(): pl.pallas_call(attend_kernel, grid=(count,), in_specs=[pl.BlockSpec(hot.s...  43.4 us
    pallas_call x1, Pallas kernels, newton_rows(): pl.pallas_call(newton_kernel, out_shape=jax.ShapeDtypeStruct((count, D),...  37.7 us
    unnamed x234, local copies, waits for them, and re-layouts  34.6 us
    pallas_call x1, Pallas kernels, feed_call(): pl.pallas_call(feed_kernel, grid=(PARTS,), in_specs=[pl.BlockSpec((SEQ_LE...  23.3 us
    dot_general x6, matrix products, trans_times(): lax.dot_general(left_side, right_side, (((0,), (0,)), ((), ())), preferre...  21.6 us
  transfers between devices with their start and end apart: 67, of which 25 were waited for; matrix products, arithmetic and copies ran while one was open for 26% of the time, Pallas kernels for 29%

profile of v2, /device:TPU:0, one launch (start us, length us, event | category | flops | bytes accessed | tf_op | source)
XLA Modules:
  0.0 612.8 jit_solution(17461524149564547596)
XLA Ops:
  2.2 4.0 collective-permute-start.6
  8.8 3.0 collective-permute-start.11
  14.5 2.9 collective-permute-start.23
  41.7 3.0 collective-permute-start.3
  59.5 9.5 %collective-permute-done.4 = f32[2,70,288]{2,1,0:T(8,128)S(1)} collective-permute-done((f32[2,70,288]{2,1,0:T(8,128)S(1)}, f32[2,70,288]{2,1,0:T(8,128)S(1)}, u32[]{:S(2)}, u32[]{:S(2)}) %collective-permute-start.4) | collective-permute-done | bytes 161312 | tf_op jit(solution)/shard_map/ppermute | solution.py:100
  76.2 5.9 collective-permute-done.5
  84.5 14.8 %attend.5 = (bf16[912,256]{1,0:T(8,128)(2,1)S(1)}, bf16[912,256]{1,0:T(8,128)(2,1)S(1)}, bf16[912,256]{1,0:T(8,128)(2,1)S(1)}, bf16[912,256]{1,0:T(8,128)(2,1)S(1)}, f32[2,2,1024]{2,1,0:T(2,128)S(1)}) custom-call(bf16[912,256]{1,0:T(8,128)(2,1)S(1)} %compare_convert_fusion.hot_ref, bf16[256,2304]{1,0:T(8,128)(2,1)S(1)} %fusion.6.tq_ref.tk_ref.tv_ref, ...), custom_call_target="tpu_custom_call" | custom-call | flops 4294967296 | bytes 4194304 | tf_op jit(solution)/shard_map/attend/pallas_call | solution.py:438
  107.6 14.3 %attend.4 = (bf16[912,256]{1,0:T(8,128)(2,1)S(1)}, bf16[912,256]{1,0:T(8,128)(2,1)S(1)}, bf16[912,256]{1,0:T(8,128)(2,1)S(1)}, bf16[912,256]{1,0:T(8,128)(2,1)S(1)}, f32[2,2,1024]{2,1,0:T(2,128)S(1)}) custom-call(bf16[912,256]{1,0:T(8,128)(2,1)S(1)} %compare_convert_fusion.hot_ref, bf16[256,2304]{1,0:T(8,128)(2,1)S(1)} %fusion.6.tq_ref.tk_ref.tv_ref, ...), custom_call_target="tpu_custom_call" | custom-call | flops 4294967296 | bytes 4194304 | tf_op jit(solution)/shard_map/attend/pallas_call | solution.py:438
  124.3 14.3 %attend.3 = (bf16[912,256]{1,0:T(8,128)(2,1)S(1)}, bf16[912,256]{1,0:T(8,128)(2,1)S(1)}, bf16[912,256]{1,0:T(8,128)(2,1)S(1)}, bf16[912,256]{1,0:T(8,128)(2,1)S(1)}, f32[2,2,1024]{2,1,0:T(2,128)S(1)}) custom-call(bf16[912,256]{1,0:T(8,128)(2,1)S(1)} %compare_convert_fusion.hot_ref, bf16[256,2304]{1,0:T(8,128)(2,1)S(1)} %fusion.6.tq_ref.tk_ref.tv_ref, ...), custom_call_target="tpu_custom_call" | custom-call | flops 4294967296 | bytes 4194304 | tf_op jit(solution)/shard_map/attend/pallas_call | solution.py:438
  147.3 2.9 gather_fusion.4
  150.3 6.4 %collective-permute-done.20.r1 = bf16[768,768]{1,0:T(8,128)(2,1)} collective-permute-done((bf16[768,768]{1,0:T(8,128)(2,1)S(1)}, bf16[768,768]{1,0:T(8,128)(2,1)}, u32[]{:S(2)}, u32[]{:S(2)}) %collective-permute-start.20) | collective-permute-done | bytes 1179680 | tf_op jit(solution)/shard_map/ppermute | solution.py:100
  156.7 4.1 fusion.49
  162.9 6.5 %collective-permute-done.26 = bf16[8,72,768]{2,1,0:T(8,128)(2,1)} collective-permute-done((bf16[8,72,768]{2,1,0:T(8,128)(2,1)}, bf16[8,72,768]{2,1,0:T(8,128)(2,1)}, u32[]{:S(2)}, u32[]{:S(2)}) %collective-permute-start.26) | collective-permute-done | bytes 884768 | tf_op jit(solution)/shard_map/ppermute | solution.py:100
  169.4 2.5 constant_dynamic-update-slice_fusion.14
  173.0 23.3 %feed.1 = (bf16[912,3072]{1,0:T(8,128)(2,1)}, bf16[912,3072]{1,0:T(8,128)(2,1)}, f32[912,768]{1,0:T(8,128)}) custom-call(bf16[912,768]{1,0:T(8,128)(2,1)} %add_convert_fusion.1.rows_ref, f32[1,3072]{1,0:T(1,128)S(1)} %broadcast_in_dim_reshape.2.bias_ref, bf16[768,768]{1,0:T(8,128)(2,1)S(1)} %pad_maximum_fusion.1.e0, ...), custom_call_target="tpu_custom_call" | custom-call | flops 8606711808 | bytes 25165824 | tf_op jit(solution)/shard_map/feed/pallas_call | solution.py:611
  203.9 17.3 %feed_back.1 = (bf16[912,3072]{1,0:T(8,128)(2,1)}, f32[912,768]{1,0:T(8,128)}, f32[1,3072]{1,0:T(1,128)S(1)}) custom-call(bf16[912,768]{1,0:T(8,128)(2,1)} %get-tuple-element.124.grad_ref, bf16[912,3072]{1,0:T(8,128)(2,1)} %get-tuple-element.54.slope_ref, bf16[768,768]{1,0:T(8,128)(2,1)S(1)} %pad_maximum_fusion.1.e0, ...), custom_call_target="tpu_custom_call" | custom-call | flops 8606711808 | bytes 25165824 | tf_op jit(solution)/shard_map/feed_back/pallas_call | solution.py:652
  221.2 3.2 multiply_reduce_fusion.1
  225.8 2.9 fusion.37
  231.4 4.0 convolution_convert_fusion
  235.8 4.0 convolution_convert_fusion.1
  239.9 3.8 gather_fusion.8
  249.8 17.8 %attend_back.5 = (bf16[3,912,256]{2,1,0:T(8,128)(2,1)S(1)}, f32[3,128,256]{2,1,0:T(8,128)S(1)}) custom-call(bf16[128,912]{1,0:T(8,128)(2,1)S(1)} %copy-done.10, bf16[912,256]{1,0:T(8,128)(2,1)S(1)} %copy-done.15, bf16[912,256]{1,0:T(8,128)(2,1)S(1)} %copy-done.17, bf16[912,256]{1,0:T(8,128)(2,1)S(1)} %copy-done.19, bf16[912,768]{1,0:T(8,128)(2,1)S(1)} %copy-done.12, ...), custom_call_target="tpu_custom_call" | custom-call | flops 10737418240 | bytes 6291456 | tf_op jit(solution)/shard_map/attend_back/pallas_call | solution.py:531
  267.8 18.2 %attend_back.4 = (bf16[3,912,256]{2,1,0:T(8,128)(2,1)S(1)}, f32[3,128,256]{2,1,0:T(8,128)S(1)}) custom-call(bf16[128,912]{1,0:T(8,128)(2,1)S(1)} %copy-done.11, bf16[912,256]{1,0:T(8,128)(2,1)S(1)} %copy-done.27, bf16[912,256]{1,0:T(8,128)(2,1)S(1)} %copy-done.29, bf16[912,256]{1,0:T(8,128)(2,1)S(1)} %copy-done.31, bf16[912,768]{1,0:T(8,128)(2,1)S(1)} %copy-done.12, ...), custom_call_target="tpu_custom_call" | custom-call | flops 10737418240 | bytes 6291456 | tf_op jit(solution)/shard_map/attend_back/pallas_call | solution.py:531
  286.1 17.9 %attend_back.3 = (bf16[3,912,256]{2,1,0:T(8,128)(2,1)S(1)}, f32[3,128,256]{2,1,0:T(8,128)S(1)}) custom-call(bf16[128,912]{1,0:T(8,128)(2,1)S(1)} %copy-done.11, bf16[912,256]{1,0:T(8,128)(2,1)S(1)} %copy-done.21, bf16[912,256]{1,0:T(8,128)(2,1)S(1)} %copy-done.23, bf16[912,256]{1,0:T(8,128)(2,1)S(1)} %copy-done.25, bf16[912,768]{1,0:T(8,128)(2,1)S(1)} %copy-done.13, ...), custom_call_target="tpu_custom_call" | custom-call | flops 10737418240 | bytes 6291456 | tf_op jit(solution)/shard_map/attend_back/pallas_call | solution.py:531
  306.4 2.8 reshape_reshape.3
  317.2 2.7 gather_fusion.7
  325.7 5.9 convert_add_fusion
  333.3 4.5 convert_add_fusion.1
  341.2 5.9 collective-permute-done.30
  347.3 2.6 collective-permute-done.36
  350.3 10.4 %collective-permute-done.48 = bf16[768,768]{1,0:T(8,128)(2,1)S(1)} collective-permute-done((bf16[768,768]{1,0:T(8,128)(2,1)S(1)}, bf16[768,768]{1,0:T(8,128)(2,1)S(1)}, u32[]{:S(2)}, u32[]{:S(2)}) %collective-permute-start.48) | collective-permute-done | bytes 1179680 | tf_op jit(solution)/shard_map/ppermute | solution.py:100
  361.5 22.8 %collective-permute-done.41 = bf16[768,768]{1,0:T(8,128)(2,1)S(1)} collective-permute-done((bf16[768,768]{1,0:T(8,128)(2,1)S(1)}, bf16[768,768]{1,0:T(8,128)(2,1)S(1)}, u32[]{:S(2)}, u32[]{:S(2)}) %collective-permute-start.41) | collective-permute-done | bytes 1179680 | tf_op jit(solution)/shard_map/ppermute | solution.py:100
  388.6 9.7 %collective-permute-done.42 = bf16[384,768]{1,0:T(8,128)(2,1)S(1)} collective-permute-done((bf16[384,768]{1,0:T(8,128)(2,1)S(1)}, bf16[384,768]{1,0:T(8,128)(2,1)S(1)}, u32[]{:S(2)}, u32[]{:S(2)}) %collective-permute-start.42) | collective-permute-done | bytes 589856 | tf_op jit(solution)/shard_map/ppermute | solution.py:100
  404.3 14.9 %collective-permute-done.43 = f32[192,768]{1,0:T(8,128)S(1)} collective-permute-done((f32[192,768]{1,0:T(8,128)S(1)}, f32[192,768]{1,0:T(8,128)S(1)}, u32[]{:S(2)}, u32[]{:S(2)}) %collective-permute-start.43) | collective-permute-done | bytes 589856 | tf_op jit(solution)/shard_map/ppermute | solution.py:100
  421.1 11.9 %collective-permute-done.44 = f32[96,768]{1,0:T(8,128)S(1)} collective-permute-done((f32[96,768]{1,0:T(8,128)S(1)}, f32[96,768]{1,0:T(8,128)S(1)}, u32[]{:S(2)}, u32[]{:S(2)}) %collective-permute-start.44) | collective-permute-done | bytes 294944 | tf_op jit(solution)/shard_map/ppermute | solution.py:100
  434.8 7.3 %collective-permute-done.45 = f32[96,768]{1,0:T(8,128)S(1)} collective-permute-done((f32[96,768]{1,0:T(8,128)S(1)}, f32[96,768]{1,0:T(8,128)S(1)}, u32[]{:S(2)}, u32[]{:S(2)}) %collective-permute-start.45) | collective-permute-done | bytes 294944 | tf_op jit(solution)/shard_map/ppermute | solution.py:100
  457.9 15.3 %collective-permute-done.59 = f32[768,256]{1,0:T(8,128)S(1)} collective-permute-done((f32[768,256]{1,0:T(8,128)S(1)}, f32[768,256]{1,0:T(8,128)S(1)}, u32[]{:S(2)}, u32[]{:S(2)}) %collective-permute-start.59) | collective-permute-done | bytes 786464 | tf_op jit(solution)/shard_map/ppermute | solution.py:100
  475.2 8.6 %collective-permute-done.60 = f32[384,256]{1,0:T(8,128)S(1)} collective-permute-done((f32[384,256]{1,0:T(8,128)S(1)}, f32[384,256]{1,0:T(8,128)S(1)}, u32[]{:S(2)}, u32[]{:S(2)}) %collective-permute-start.60) | collective-permute-done | bytes 393248 | tf_op jit(solution)/shard_map/ppermute | solution.py:100
  486.8 2.8 constant_dynamic-update-slice_fusion.19
  489.7 4.6 gather_fusion.6
  494.3 2.8 collective-permute-start.62
  497.0 8.2 %multiply_reduce_fusion.2 = (f32[768]{0:T(1024)S(1)}, f32[912]{0:T(1024)S(1)}, f32[912]{0:T(1024)S(1)}, f32[768]{0:T(1024)S(1)}, f32[912,768]{1,0:T(8,128)S(1)}) fusion(f32[912,768]{1,0:T(8,128)} %get-tuple-element.168, f32[912]{0:T(1024)S(1)} %copy-done.94, f32[912]{0:T(1024)S(1)} %copy-done.90, f32[768]{0:T(1024)S(1)} %mul.400, ...), kind=kOutput, calls=%fused_computation.19 | convolution fusion | flops 3234517504 | bytes 13368576 | tf_op jit(solution)/shard_map/dot_general | solution.py:39
  505.7 11.0 %collective-permute-done.63 = f32[384,256]{1,0:T(8,128)S(1)} collective-permute-done((f32[384,256]{1,0:T(8,128)S(1)}, f32[384,256]{1,0:T(8,128)S(1)}, u32[]{:S(2)}, u32[]{:S(2)}) %collective-permute-start.63) | collective-permute-done | bytes 393248 | tf_op jit(solution)/shard_map/ppermute | solution.py:100
  525.0 10.6 %collective-permute-done.64 = f32[768,256]{1,0:T(8,128)} collective-permute-done((f32[768,256]{1,0:T(8,128)S(1)}, f32[768,256]{1,0:T(8,128)}, u32[]{:S(2)}, u32[]{:S(2)}) %collective-permute-start.64) | collective-permute-done | bytes 786464 | tf_op jit(solution)/shard_map/ppermute | solution.py:100
  537.2 37.7 %newton.1 = bf16[384,768]{1,0:T(8,128)(2,1)S(1)} custom-call(f32[1536,256]{1,0:T(8,128)S(1)} %maximum_select_fusion.gram_ref, f32[384,768]{1,0:T(8,128)S(1)} %get-tuple-element.116.rows_ref), custom_call_target="tpu_custom_call" | custom-call | flops 27179089920 | bytes 4194304 | tf_op jit(solution)/shard_map/newton/pallas_call | solution.py:310
  578.5 4.3 collective-permute-done.55
  583.5 4.9 collective-permute-done.65
  589.5 5.1 collective-permute-done.57
  (561 shorter events, 176.8 us)
Async XLA Ops:
  2.2 26.0 %collective-permute-start.6 = (bf16[1,24,768]{2,1,0:T(8,128)(2,1)S(1)}, bf16[1,24,768]{2,1,0:T(8,128)(2,1)S(1)}, u32[]{:S(2)}, u32[]{:S(2)}) collective-permute-start(bf16[1,24,768]{2,1,0:T(8,128)(2,1)S(1)} %get-tuple-element.133), channel_id=1, source_target_pairs={{0,16},{1,17},{2,18},{3,19},{4,20},{5,21},{6,22},{7,23},{8,24},{9,... | collective-permute-start | bytes 110600 | tf_op jit(solution)/shard_map/ppermute | solution.py:100
  7.7 18.7 %collective-permute-start = (bf16[1,85,96]{2,1,0:T(8,128)(2,1)S(1)}, bf16[1,85,96]{2,1,0:T(8,128)(2,1)S(1)}, u32[]{:S(2)}, u32[]{:S(2)}) collective-permute-start(bf16[1,85,96]{2,1,0:T(8,128)(2,1)S(1)} %pad_maximum_fusion.23), channel_id=1, source_target_pairs={{0,16},{1,17},{2,18},{3,19},{4,20},{5,21},{6,22},{7,23},{8,24},{9,... | collective-permute-start | bytes 48968 | tf_op jit(solution)/shard_map/ppermute | solution.py:100
  8.8 40.0 %collective-permute-start.11 = (bf16[96,768]{1,0:T(8,128)(2,1)S(1)}, bf16[96,768]{1,0:T(8,128)(2,1)}, u32[]{:S(2)}, u32[]{:S(2)}) collective-permute-start(bf16[96,768]{1,0:T(8,128)(2,1)S(1)} %dynamic-slice_convert_fusion.1), channel_id=1, source_target_pairs={{0,16},{1,17},{2,18},{3,19},{4,20},{5,21},{6,22},{7,23},{8,24},{9,... | collective-permute-start | bytes 442376 | tf_op jit(solution)/shard_map/ppermute | solution.py:100
  12.8 37.0 %collective-permute-start.17 = (bf16[96,768]{1,0:T(8,128)(2,1)S(1)}, bf16[96,768]{1,0:T(8,128)(2,1)}, u32[]{:S(2)}, u32[]{:S(2)}) collective-permute-start(bf16[96,768]{1,0:T(8,128)(2,1)S(1)} %dynamic-slice_convert_fusion), channel_id=1, source_target_pairs={{0,16},{1,17},{2,18},{3,19},{4,20},{5,21},{6,22},{7,23},{8,24},{9,... | collective-permute-start | bytes 442376 | tf_op jit(solution)/shard_map/ppermute | solution.py:100
  14.5 20.3 %collective-permute-start.23 = (bf16[1,72,768]{2,1,0:T(8,128)(2,1)S(1)}, bf16[1,72,768]{2,1,0:T(8,128)(2,1)S(1)}, u32[]{:S(2)}, u32[]{:S(2)}) collective-permute-start(bf16[1,72,768]{2,1,0:T(8,128)(2,1)S(1)} %get-tuple-element.129), channel_id=1, source_target_pairs={{0,16},{1,17},{2,18},{3,19},{4,20},{5,21},{6,22},{7,23},{8,24},{9,... | collective-permute-start | bytes 331784 | tf_op jit(solution)/shard_map/ppermute | solution.py:100
  33.4 19.6 %collective-permute-start.8 = (bf16[4,24,768]{2,1,0:T(8,128)(2,1)}, bf16[4,24,768]{2,1,0:T(8,128)(2,1)}, u32[]{:S(2)}, u32[]{:S(2)}) collective-permute-start(bf16[4,24,768]{2,1,0:T(8,128)(2,1)} %pad_maximum_fusion.19), channel_id=1, source_target_pairs={{0,4},{1,5},{2,6},{3,7},{4,0},{5,1},{6,2},{7,3},{8,12},{9,13},{10,... | collective-permute-start | bytes 442376 | tf_op jit(solution)/shard_map/ppermute | solution.py:100
  35.5 21.6 %collective-permute-start.24 = (bf16[2,72,768]{2,1,0:T(8,128)(2,1)}, bf16[2,72,768]{2,1,0:T(8,128)(2,1)S(1)}, u32[]{:S(2)}, u32[]{:S(2)}) collective-permute-start(bf16[2,72,768]{2,1,0:T(8,128)(2,1)} %pad_maximum_fusion.17), channel_id=1, source_target_pairs={{0,8},{1,9},{2,10},{3,11},{4,12},{5,13},{6,14},{7,15},{8,0},{9,1},... | collective-permute-start | bytes 663560 | tf_op jit(solution)/shard_map/ppermute | solution.py:100
  49.7 19.8 %collective-permute-start.12 = (bf16[192,768]{1,0:T(8,128)(2,1)S(1)}, bf16[192,768]{1,0:T(8,128)(2,1)S(1)}, u32[]{:S(2)}, u32[]{:S(2)}) collective-permute-start(bf16[192,768]{1,0:T(8,128)(2,1)S(1)} %pad_maximum_fusion.14), channel_id=1, source_target_pairs={{0,8},{1,9},{2,10},{3,11},{4,12},{5,13},{6,14},{7,15},{8,0},{9,1},... | collective-permute-start | bytes 884744 | tf_op jit(solution)/shard_map/ppermute | solution.py:100
  50.8 22.2 %collective-permute-start.18 = (bf16[192,768]{1,0:T(8,128)(2,1)S(1)}, bf16[192,768]{1,0:T(8,128)(2,1)S(1)}, u32[]{:S(2)}, u32[]{:S(2)}) collective-permute-start(bf16[192,768]{1,0:T(8,128)(2,1)S(1)} %pad_maximum_fusion.15), channel_id=1, source_target_pairs={{0,8},{1,9},{2,10},{3,11},{4,12},{5,13},{6,14},{7,15},{8,0},{9,1},... | collective-permute-start | bytes 884744 | tf_op jit(solution)/shard_map/ppermute | solution.py:100
  52.9 16.1 %collective-permute-start.4 = (f32[2,70,288]{2,1,0:T(8,128)S(1)}, f32[2,70,288]{2,1,0:T(8,128)S(1)}, u32[]{:S(2)}, u32[]{:S(2)}) collective-permute-start(f32[2,70,288]{2,1,0:T(8,128)S(1)} %pad_maximum_fusion.16), channel_id=1, source_target_pairs={{0,8},{1,9},{2,10},{3,11},{4,12},{5,13},{6,14},{7,15},{8,0},{9,1},... | collective-permute-start | bytes 483848 | tf_op jit(solution)/shard_map/ppermute | solution.py:100
  53.9 21.4 %collective-permute-start.9 = (bf16[8,24,768]{2,1,0:T(8,128)(2,1)S(1)}, bf16[8,24,768]{2,1,0:T(8,128)(2,1)S(1)}, u32[]{:S(2)}, u32[]{:S(2)}) collective-permute-start(bf16[8,24,768]{2,1,0:T(8,128)(2,1)S(1)} %pad_maximum_fusion.13), channel_id=1, source_target_pairs={{0,2},{1,3},{2,0},{3,1},{4,6},{5,7},{6,4},{7,5},{8,10},{9,11},{10,... | collective-permute-start | bytes 884744 | tf_op jit(solution)/shard_map/ppermute | solution.py:100
  58.0 80.8 %collective-permute-start.25 = (bf16[4,72,768]{2,1,0:T(8,128)(2,1)}, bf16[4,72,768]{2,1,0:T(8,128)(2,1)}, u32[]{:S(2)}, u32[]{:S(2)}) collective-permute-start(bf16[4,72,768]{2,1,0:T(8,128)(2,1)} %pad_maximum_fusion.11), channel_id=1, source_target_pairs={{0,4},{1,5},{2,6},{3,7},{4,0},{5,1},{6,2},{7,3},{8,12},{9,13},{10,... | collective-permute-start | bytes 1327112 | tf_op jit(solution)/shard_map/ppermute | solution.py:100
  69.0 13.2 %collective-permute-start.5 = (f32[4,70,288]{2,1,0:T(8,128)S(1)}, f32[4,70,288]{2,1,0:T(8,128)S(1)}, u32[]{:S(2)}, u32[]{:S(2)}) collective-permute-start(f32[4,70,288]{2,1,0:T(8,128)S(1)} %pad_maximum_fusion.10), channel_id=1, source_target_pairs={{0,4},{1,5},{2,6},{3,7},{4,0},{5,1},{6,2},{7,3},{8,12},{9,13},{10,... | collective-permute-start | bytes 967688 | tf_op jit(solution)/shard_map/ppermute | solution.py:100
  71.5 29.5 %collective-permute-start.13 = (bf16[384,768]{1,0:T(8,128)(2,1)}, bf16[384,768]{1,0:T(8,128)(2,1)}, u32[]{:S(2)}, u32[]{:S(2)}) collective-permute-start(bf16[384,768]{1,0:T(8,128)(2,1)} %pad_maximum_fusion.6), channel_id=1, source_target_pairs={{0,4},{1,5},{2,6},{3,7},{4,0},{5,1},{6,2},{7,3},{8,12},{9,13},{10,... | collective-permute-start | bytes 1769480 | tf_op jit(solution)/shard_map/ppermute | solution.py:100
  74.9 30.0 %collective-permute-start.19 = (bf16[384,768]{1,0:T(8,128)(2,1)}, bf16[384,768]{1,0:T(8,128)(2,1)}, u32[]{:S(2)}, u32[]{:S(2)}) collective-permute-start(bf16[384,768]{1,0:T(8,128)(2,1)} %pad_maximum_fusion.7), channel_id=1, source_target_pairs={{0,4},{1,5},{2,6},{3,7},{4,0},{5,1},{6,2},{7,3},{8,12},{9,13},{10,... | collective-permute-start | bytes 1769480 | tf_op jit(solution)/shard_map/ppermute | solution.py:100
  76.2 68.6 %collective-permute-start.10 = (bf16[16,24,768]{2,1,0:T(8,128)(2,1)}, bf16[16,24,768]{2,1,0:T(8,128)(2,1)}, u32[]{:S(2)}, u32[]{:S(2)}) collective-permute-start(bf16[16,24,768]{2,1,0:T(8,128)(2,1)} %get-tuple-element.143), channel_id=1, source_target_pairs={{0,1},{1,0},{2,3},{3,2},{4,5},{5,4},{6,7},{7,6},{8,9},{9,8},{10,11... | collective-permute-start | bytes 1769480 | tf_op jit(solution)/shard_map/ppermute | solution.py:100
  102.3 47.8 %collective-permute-start.14 = (bf16[768,768]{1,0:T(8,128)(2,1)S(1)}, bf16[768,768]{1,0:T(8,128)(2,1)}, u32[]{:S(2)}, u32[]{:S(2)}) collective-permute-start(bf16[768,768]{1,0:T(8,128)(2,1)S(1)} %pad_maximum_fusion.1.e0), channel_id=1, source_target_pairs={{0,2},{1,3},{2,0},{3,1},{4,6},{5,7},{6,4},{7,5},{8,10},{9,11},{10,... | collective-permute-start | bytes 3538952 | tf_op jit(solution)/shard_map/ppermute | solution.py:100
  106.1 50.6 %collective-permute-start.20 = (bf16[768,768]{1,0:T(8,128)(2,1)S(1)}, bf16[768,768]{1,0:T(8,128)(2,1)}, u32[]{:S(2)}, u32[]{:S(2)}) collective-permute-start(bf16[768,768]{1,0:T(8,128)(2,1)S(1)} %pad_maximum_fusion.2.r0), channel_id=1, source_target_pairs={{0,2},{1,3},{2,0},{3,1},{4,6},{5,7},{6,4},{7,5},{8,10},{9,11},{10,... | collective-permute-start | bytes 3538952 | tf_op jit(solution)/shard_map/ppermute | solution.py:100
  142.2 27.2 %collective-permute-start.26 = (bf16[8,72,768]{2,1,0:T(8,128)(2,1)}, bf16[8,72,768]{2,1,0:T(8,128)(2,1)}, u32[]{:S(2)}, u32[]{:S(2)}) collective-permute-start(bf16[8,72,768]{2,1,0:T(8,128)(2,1)} %pad_maximum_fusion.5), channel_id=1, source_target_pairs={{0,2},{1,3},{2,0},{3,1},{4,6},{5,7},{6,4},{7,5},{8,10},{9,11},{10,... | collective-permute-start | bytes 2654216 | tf_op jit(solution)/shard_map/ppermute | solution.py:100
  144.8 27.2 %collective-permute-start.15 = (bf16[768,768]{1,0:T(8,128)(2,1)S(1)}, bf16[768,768]{1,0:T(8,128)(2,1)}, u32[]{:S(2)}, u32[]{:S(2)}) collective-permute-start(bf16[768,768]{1,0:T(8,128)(2,1)S(1)} %pad_maximum_fusion.1.e0), channel_id=1, source_target_pairs={{0,1},{1,0},{2,3},{3,2},{4,5},{5,4},{6,7},{7,6},{8,9},{9,8},{10,11... | collective-permute-start | bytes 3538952 | tf_op jit(solution)/shard_map/ppermute | solution.py:100
  144.9 27.1 %collective-permute-start.21 = (bf16[768,768]{1,0:T(8,128)(2,1)S(1)}, bf16[768,768]{1,0:T(8,128)(2,1)}, u32[]{:S(2)}, u32[]{:S(2)}) collective-permute-start(bf16[768,768]{1,0:T(8,128)(2,1)S(1)} %pad_maximum_fusion.2.r0), channel_id=1, source_target_pairs={{0,1},{1,0},{2,3},{3,2},{4,5},{5,4},{6,7},{7,6},{8,9},{9,8},{10,11... | collective-permute-start | bytes 3538952 | tf_op jit(solution)/shard_map/ppermute | solution.py:100
  150.2 21.8 %collective-permute-start.16 = (bf16[768,768]{1,0:T(8,128)(2,1)}, bf16[768,768]{1,0:T(8,128)(2,1)S(1)}, u32[]{:S(2)}, u32[]{:S(2)}) collective-permute-start(bf16[768,768]{1,0:T(8,128)(2,1)} %collective-permute-done.14.e1), channel_id=1, source_target_pairs={{0,1},{1,0},{2,3},{3,2},{4,5},{5,4},{6,7},{7,6},{8,9},{9,8},{10,11... | collective-permute-start | bytes 3538952 | tf_op jit(solution)/shard_map/ppermute | solution.py:100
  156.7 15.3 %collective-permute-start.22 = (bf16[768,768]{1,0:T(8,128)(2,1)}, bf16[768,768]{1,0:T(8,128)(2,1)S(1)}, u32[]{:S(2)}, u32[]{:S(2)}) collective-permute-start(bf16[768,768]{1,0:T(8,128)(2,1)} %collective-permute-done.20.r1), channel_id=1, source_target_pairs={{0,1},{1,0},{2,3},{3,2},{4,5},{5,4},{6,7},{7,6},{8,9},{9,8},{10,11... | collective-permute-start | bytes 3538952 | tf_op jit(solution)/shard_map/ppermute | solution.py:100
  171.9 314.9 %collective-permute-start.27 = (bf16[16,72,768]{2,1,0:T(8,128)(2,1)}, bf16[16,72,768]{2,1,0:T(8,128)(2,1)}, u32[]{:S(2)}, u32[]{:S(2)}) collective-permute-start(bf16[16,72,768]{2,1,0:T(8,128)(2,1)} %get-tuple-element.137), channel_id=1, source_target_pairs={{0,1},{1,0},{2,3},{3,2},{4,5},{5,4},{6,7},{7,6},{8,9},{9,8},{10,11... | collective-permute-start | bytes 5308424 | tf_op jit(solution)/shard_map/ppermute | solution.py:100
  235.3 90.3 %collective-permute-start.47 = (bf16[1536,768]{1,0:T(8,128)(2,1)}, bf16[1536,768]{1,0:T(8,128)(2,1)}, u32[]{:S(2)}, u32[]{:S(2)}) collective-permute-start(bf16[1536,768]{1,0:T(8,128)(2,1)} %convolution_convert_fusion), channel_id=1, source_target_pairs={{0,1},{1,0},{2,3},{3,2},{4,5},{5,4},{6,7},{7,6},{8,9},{9,8},{10,11... | collective-permute-start | bytes 7077896 | tf_op jit(solution)/shard_map/ppermute | solution.py:100
  239.9 93.4 %collective-permute-start.40 = (bf16[1536,768]{1,0:T(8,128)(2,1)}, bf16[1536,768]{1,0:T(8,128)(2,1)}, u32[]{:S(2)}, u32[]{:S(2)}) collective-permute-start(bf16[1536,768]{1,0:T(8,128)(2,1)} %convolution_convert_fusion.1), channel_id=1, source_target_pairs={{0,1},{1,0},{2,3},{3,2},{4,5},{5,4},{6,7},{7,6},{8,9},{9,8},{10,11... | collective-permute-start | bytes 7077896 | tf_op jit(solution)/shard_map/ppermute | solution.py:100
  245.9 66.1 %collective-permute-start.33 = (bf16[16,24,768]{2,1,0:T(8,128)(2,1)}, bf16[16,24,768]{2,1,0:T(8,128)(2,1)}, u32[]{:S(2)}, u32[]{:S(2)}) collective-permute-start(bf16[16,24,768]{2,1,0:T(8,128)(2,1)} %slice.499), channel_id=1, source_target_pairs={{0,1},{1,0},{2,3},{3,2},{4,5},{5,4},{6,7},{7,6},{8,9},{9,8},{10,11... | collective-permute-start | bytes 1769480 | tf_op jit(solution)/shard_map/ppermute | solution.py:100
  321.1 17.5 %collective-permute-start.29 = (f32[4,70,288]{2,1,0:T(8,128)S(1)}, f32[4,70,288]{2,1,0:T(8,128)S(1)}, u32[]{:S(2)}, u32[]{:S(2)}) collective-permute-start(f32[4,70,288]{2,1,0:T(8,128)S(1)} %slice.373), channel_id=1, source_target_pairs={{0,4},{1,5},{2,6},{3,7},{4,0},{5,1},{6,2},{7,3},{8,12},{9,13},{10,... | collective-permute-start | bytes 967688 | tf_op jit(solution)/shard_map/ppermute | solution.py:100
  324.3 14.9 %collective-permute-start.35 = (bf16[4,24,768]{2,1,0:T(8,128)(2,1)S(1)}, bf16[4,24,768]{2,1,0:T(8,128)(2,1)S(1)}, u32[]{:S(2)}, u32[]{:S(2)}) collective-permute-start(bf16[4,24,768]{2,1,0:T(8,128)(2,1)S(1)} %slice.501), channel_id=1, source_target_pairs={{0,4},{1,5},{2,6},{3,7},{4,0},{5,1},{6,2},{7,3},{8,12},{9,13},{10,... | collective-permute-start | bytes 442376 | tf_op jit(solution)/shard_map/ppermute | solution.py:100
  331.7 29.0 %collective-permute-start.48 = (bf16[768,768]{1,0:T(8,128)(2,1)S(1)}, bf16[768,768]{1,0:T(8,128)(2,1)S(1)}, u32[]{:S(2)}, u32[]{:S(2)}) collective-permute-start(bf16[768,768]{1,0:T(8,128)(2,1)S(1)} %slice.495), channel_id=1, source_target_pairs={{0,2},{1,3},{2,0},{3,1},{4,6},{5,7},{6,4},{7,5},{8,10},{9,11},{10,... | collective-permute-start | bytes 3538952 | tf_op jit(solution)/shard_map/ppermute | solution.py:100
  337.9 46.4 %collective-permute-start.41 = (bf16[768,768]{1,0:T(8,128)(2,1)S(1)}, bf16[768,768]{1,0:T(8,128)(2,1)S(1)}, u32[]{:S(2)}, u32[]{:S(2)}) collective-permute-start(bf16[768,768]{1,0:T(8,128)(2,1)S(1)} %slice.496), channel_id=1, source_target_pairs={{0,2},{1,3},{2,0},{3,1},{4,6},{5,7},{6,4},{7,5},{8,10},{9,11},{10,... | collective-permute-start | bytes 3538952 | tf_op jit(solution)/shard_map/ppermute | solution.py:100
  347.2 37.9 %collective-permute-start.31 = (f32[1,70,288]{2,1,0:T(8,128)S(1)}, f32[1,70,288]{2,1,0:T(8,128)S(1)}, u32[]{:S(2)}, u32[]{:S(2)}) collective-permute-start(f32[1,70,288]{2,1,0:T(8,128)S(1)} %slice.377), channel_id=1, source_target_pairs={{0,16},{1,17},{2,18},{3,19},{4,20},{5,21},{6,22},{7,23},{8,24},{9,... | collective-permute-start | bytes 241928 | tf_op jit(solution)/shard_map/ppermute | solution.py:100
  349.9 36.7 %collective-permute-start.37 = (f32[1,24,768]{2,1,0:T(8,128)S(1)}, f32[1,24,768]{2,1,0:T(8,128)S(1)}, u32[]{:S(2)}, u32[]{:S(2)}) collective-permute-start(f32[1,24,768]{2,1,0:T(8,128)S(1)} %slice.387), channel_id=1, source_target_pairs={{0,16},{1,17},{2,18},{3,19},{4,20},{5,21},{6,22},{7,23},{8,24},{9,... | collective-permute-start | bytes 221192 | tf_op jit(solution)/shard_map/ppermute | solution.py:100
  361.0 26.3 %collective-permute-start.49 = (bf16[384,768]{1,0:T(8,128)(2,1)S(1)}, bf16[384,768]{1,0:T(8,128)(2,1)S(1)}, u32[]{:S(2)}, u32[]{:S(2)}) collective-permute-start(bf16[384,768]{1,0:T(8,128)(2,1)S(1)} %slice.497), channel_id=1, source_target_pairs={{0,4},{1,5},{2,6},{3,7},{4,0},{5,1},{6,2},{7,3},{8,12},{9,13},{10,... | collective-permute-start | bytes 1769480 | tf_op jit(solution)/shard_map/ppermute | solution.py:100
  384.6 13.7 %collective-permute-start.42 = (bf16[384,768]{1,0:T(8,128)(2,1)S(1)}, bf16[384,768]{1,0:T(8,128)(2,1)S(1)}, u32[]{:S(2)}, u32[]{:S(2)}) collective-permute-start(bf16[384,768]{1,0:T(8,128)(2,1)S(1)} %slice.498), channel_id=1, source_target_pairs={{0,4},{1,5},{2,6},{3,7},{4,0},{5,1},{6,2},{7,3},{8,12},{9,13},{10,... | collective-permute-start | bytes 1769480 | tf_op jit(solution)/shard_map/ppermute | solution.py:100
  385.1 13.5 %collective-permute-start.32 = (f32[70,288]{1,0:T(8,128)S(1)}, f32[70,288]{1,0:T(8,128)S(1)}, u32[]{:S(2)}, u32[]{:S(2)}) collective-permute-start(f32[70,288]{1,0:T(8,128)S(1)} %fusion.26), channel_id=1, source_target_pairs={{0,2},{1,3},{2,0},{3,1},{4,6},{5,7},{6,4},{7,5},{8,10},{9,11},{10,... | collective-permute-start | bytes 241928 | tf_op jit(solution)/shard_map/ppermute | solution.py:100
  386.6 32.8 %collective-permute-start.38 = (f32[24,768]{1,0:T(8,128)S(1)}, f32[24,768]{1,0:T(8,128)S(1)}, u32[]{:S(2)}, u32[]{:S(2)}) collective-permute-start(f32[24,768]{1,0:T(8,128)S(1)} %bitcast.152), channel_id=1, source_target_pairs={{0,2},{1,3},{2,0},{3,1},{4,6},{5,7},{6,4},{7,5},{8,10},{9,11},{10,... | collective-permute-start | bytes 221192 | tf_op jit(solution)/shard_map/ppermute | solution.py:100
  387.5 14.4 %collective-permute-start.50 = (f32[192,768]{1,0:T(8,128)S(1)}, f32[192,768]{1,0:T(8,128)S(1)}, u32[]{:S(2)}, u32[]{:S(2)}) collective-permute-start(f32[192,768]{1,0:T(8,128)S(1)} %slice.401), channel_id=1, source_target_pairs={{0,8},{1,9},{2,10},{3,11},{4,12},{5,13},{6,14},{7,15},{8,0},{9,1},... | collective-permute-start | bytes 1769480 | tf_op jit(solution)/shard_map/ppermute | solution.py:100
  398.5 20.7 %collective-permute-start.43 = (f32[192,768]{1,0:T(8,128)S(1)}, f32[192,768]{1,0:T(8,128)S(1)}, u32[]{:S(2)}, u32[]{:S(2)}) collective-permute-start(f32[192,768]{1,0:T(8,128)S(1)} %slice.393), channel_id=1, source_target_pairs={{0,8},{1,9},{2,10},{3,11},{4,12},{5,13},{6,14},{7,15},{8,0},{9,1},... | collective-permute-start | bytes 1769480 | tf_op jit(solution)/shard_map/ppermute | solution.py:100
  401.9 17.6 %collective-permute-start.51 = (f32[96,768]{1,0:T(8,128)S(1)}, f32[96,768]{1,0:T(8,128)S(1)}, u32[]{:S(2)}, u32[]{:S(2)}) collective-permute-start(f32[96,768]{1,0:T(8,128)S(1)} %slice.403), channel_id=1, source_target_pairs={{0,16},{1,17},{2,18},{3,19},{4,20},{5,21},{6,22},{7,23},{8,24},{9,... | collective-permute-start | bytes 884744 | tf_op jit(solution)/shard_map/ppermute | solution.py:100
  419.4 13.7 %collective-permute-start.44 = (f32[96,768]{1,0:T(8,128)S(1)}, f32[96,768]{1,0:T(8,128)S(1)}, u32[]{:S(2)}, u32[]{:S(2)}) collective-permute-start(f32[96,768]{1,0:T(8,128)S(1)} %slice.395), channel_id=1, source_target_pairs={{0,16},{1,17},{2,18},{3,19},{4,20},{5,21},{6,22},{7,23},{8,24},{9,... | collective-permute-start | bytes 884744 | tf_op jit(solution)/shard_map/ppermute | solution.py:100
  419.5 15.1 %collective-permute-start.39 = (f32[2,24,768]{2,1,0:T(8,128)S(1)}, f32[2,24,768]{2,1,0:T(8,128)S(1)}, u32[]{:S(2)}, u32[]{:S(2)}) collective-permute-start(f32[2,24,768]{2,1,0:T(8,128)S(1)} %maximum_select_fusion.10), channel_id=1, source_target_pairs={{0,1},{1,0},{2,3},{3,2},{4,5},{5,4},{6,7},{7,6},{8,9},{9,8},{10,11... | collective-permute-start | bytes 442376 | tf_op jit(solution)/shard_map/ppermute | solution.py:100
  419.6 15.0 %collective-permute-start.52 = (f32[96,768]{1,0:T(8,128)S(1)}, f32[96,768]{1,0:T(8,128)S(1)}, u32[]{:S(2)}, u32[]{:S(2)}) collective-permute-start(f32[96,768]{1,0:T(8,128)S(1)} %slice_add_fusion.9), channel_id=1, source_target_pairs={{0,2},{1,3},{2,0},{3,1},{4,6},{5,7},{6,4},{7,5},{8,10},{9,11},{10,... | collective-permute-start | bytes 884744 | tf_op jit(solution)/shard_map/ppermute | solution.py:100
  453.6 19.6 %collective-permute-start.59 = (f32[768,256]{1,0:T(8,128)S(1)}, f32[768,256]{1,0:T(8,128)S(1)}, u32[]{:S(2)}, u32[]{:S(2)}) collective-permute-start(f32[768,256]{1,0:T(8,128)S(1)} %constant_dynamic-slice_fusion.3), channel_id=1, source_target_pairs={{0,4},{1,5},{2,6},{3,7},{4,0},{5,1},{6,2},{7,3},{8,12},{9,13},{10,... | collective-permute-start | bytes 2359304 | tf_op jit(solution)/shard_map/ppermute | solution.py:100
  516.8 18.8 %collective-permute-start.64 = (f32[768,256]{1,0:T(8,128)S(1)}, f32[768,256]{1,0:T(8,128)}, u32[]{:S(2)}, u32[]{:S(2)}) collective-permute-start(f32[768,256]{1,0:T(8,128)S(1)} %maximum_select_fusion.3), channel_id=1, source_target_pairs={{0,4},{1,5},{2,6},{3,7},{4,0},{5,1},{6,2},{7,3},{8,12},{9,13},{10,... | collective-permute-start | bytes 2359304 | tf_op jit(solution)/shard_map/ppermute | solution.py:100
  524.9 51.6 %collective-permute-start.54 = (f32[8,86,96]{2,1,0:T(8,128)S(1)}, f32[8,86,96]{2,1,0:T(8,128)S(1)}, u32[]{:S(2)}, u32[]{:S(2)}) collective-permute-start(f32[8,86,96]{2,1,0:T(8,128)S(1)} %pad_maximum_fusion.12), channel_id=1, source_target_pairs={{0,1},{1,0},{2,3},{3,2},{4,5},{5,4},{6,7},{7,6},{8,9},{9,8},{10,11... | collective-permute-start | bytes 792584 | tf_op jit(solution)/shard_map/ppermute | solution.py:100
  574.9 13.5 %collective-permute-start.65 = (bf16[384,768]{1,0:T(8,128)(2,1)S(1)}, bf16[384,768]{1,0:T(8,128)(2,1)S(1)}, u32[]{:S(2)}, u32[]{:S(2)}) collective-permute-start(bf16[384,768]{1,0:T(8,128)(2,1)S(1)} %newton.1), channel_id=1, source_target_pairs={{0,2},{1,3},{2,0},{3,1},{4,6},{5,7},{6,4},{7,5},{8,10},{9,11},{10,... | collective-permute-start | bytes 1769480 | tf_op jit(solution)/shard_map/ppermute | solution.py:100
  588.6 18.7 %collective-permute-start.66 = (bf16[2,384,768]{2,1,0:T(8,128)(2,1)S(1)}, bf16[2,384,768]{2,1,0:T(8,128)(2,1)}, u32[]{:S(2)}, u32[]{:S(2)}) collective-permute-start(bf16[2,384,768]{2,1,0:T(8,128)(2,1)S(1)} %pad_maximum_fusion.3), channel_id=1, source_target_pairs={{0,1},{1,0},{2,3},{3,2},{4,5},{5,4},{6,7},{7,6},{8,9},{9,8},{10,11... | collective-permute-start | bytes 3538952 | tf_op jit(solution)/shard_map/ppermute | solution.py:100
  (126 other events, 1338.9 us)

commit v3 on v2

--- a/solution.py
+++ b/solution.py
@@ -86,8 +86,11 @@
 SPAN = 1024
 STRIP = 256
 PARTS = 4
+BLOCK = 96
+PART_BLOCKS = D // BLOCK
 LANES = 128
 ATTEND_CALLS = 3
+BACK_CALLS = 6
 
 
 BOTH = ("wide", "narrow")
@@ -117,6 +120,16 @@
     return np.array(table)
 
 
+def gate(value, others):
+    leaves, form = jax.tree.flatten(value)
+    held = lax.optimization_barrier(tuple(leaves) + tuple(jax.tree.leaves(others)))
+    return jax.tree.unflatten(form, held[: len(leaves)])
+
+
+def padded_rows(array):
+    return jnp.pad(array, ((0, -array.shape[0] % 16), (0, 0)))
+
+
 def gather_blocks(piece, masks):
     for mask in masks:
         piece = jnp.concatenate([piece, swap(piece, mask)], axis=0)
@@ -127,11 +140,16 @@
     return jnp.take(array, index, axis=0, mode="clip")
 
 
-def in_order(blocks, masks, unit, base):
+def places_of(masks, unit):
     offsets = offsets_of(masks) // unit
     place = np.zeros_like(offsets)
     place[offsets] = np.arange(offsets.size)
-    return take_blocks(blocks, jnp.asarray(place)[jnp.arange(offsets.size) ^ base])
+    return place
+
+
+def in_order(blocks, masks, unit, base):
+    place = places_of(masks, unit)
+    return take_blocks(blocks, jnp.asarray(place)[jnp.arange(place.size) ^ base])
 
 
 def out_of_order(blocks, masks, unit, base):
@@ -139,32 +157,94 @@
     return take_blocks(blocks, jnp.asarray(offsets) ^ base)
 
 
-def gather_wide(piece):
-    blocks = gather_blocks(piece[None], wide_masks())
-    return in_order(blocks, wide_masks(), lax.axis_size("narrow"), lax.axis_index("wide"))
-
-
-def gather_parts(piece):
-    own = gather_blocks(piece, wide_masks())
-    beside = swap(own, 2)
-    return [own, beside, swap(own, 1), swap(beside, 1)]
-
-
 def quarter_rows(array):
     count = array.shape[0] // lax.axis_size("narrow")
     return lax.dynamic_slice_in_dim(array, lax.axis_index("narrow") * count, count, 0)
 
 
-def scatter_blocks(keep, send, masks, wide_type):
-    for step, mask in enumerate(masks):
-        send_type = wide_type if step + 2 >= len(masks) else jnp.bfloat16
-        total = keep + swap(send.astype(send_type), mask).astype(jnp.float32)
-        half = total.shape[0] // 2
-        keep, send = total[:half], total[half:]
-    return total
-
-
-def narrow_rows(piece):
+def side_of(mask):
+    return (my_index() // mask) % 2
+
+
+def split_static(array, axis):
+    return lax.index_in_dim(array, 0, axis, False), lax.index_in_dim(array, 1, axis, False)
+
+
+def split_sided(array, axis, mask):
+    side = side_of(mask)
+    return (
+        lax.dynamic_index_in_dim(array, side, axis, False),
+        lax.dynamic_index_in_dim(array, 1 - side, axis, False),
+    )
+
+
+def halves(item, mask):
+    array, marks, sided = item
+    axis = marks.index(mask)
+    keep, send = split_sided(array, axis, mask) if sided else split_static(array, axis)
+    return (keep, marks[:axis] + marks[axis + 1 :], sided), send
+
+
+def hop(items, mask, kind):
+    pairs = [halves(item, mask) for item in items]
+    rows = [send.astype(kind).reshape(-1, send.shape[-1]) for _, send in pairs]
+    flat = jnp.concatenate(rows, axis=0) if len(rows) > 1 else rows[0]
+    token = yield flat
+    got = gate(swap(flat, mask), token)
+    results, at = [], 0
+    for ((keep, marks, sided), send), row in zip(pairs, rows):
+        part = got[at : at + row.shape[0]].reshape(send.shape).astype(jnp.float32)
+        results.append((keep + part, marks, sided))
+        at += row.shape[0]
+    return results
+
+
+def finish(steps, token):
+    try:
+        steps.send(token)
+    except StopIteration as stop:
+        return stop.value
+
+
+def finish_hop(steps):
+    next(steps)
+    return finish(steps, ())
+
+
+def columns_of(items, start, stop):
+    return [(array[..., start:stop], marks, sided) for array, marks, sided in items]
+
+
+def sum_chain(items, kind):
+    masks = wide_masks()
+    width = items[0][0].shape[-1]
+    ways = [columns_of(items, 0, width // 2), columns_of(items, width // 2, width)]
+    for pair in ((masks[-1], 2), (2, masks[-1])):
+        steps = [hop(way, mask, jnp.bfloat16) for way, mask in zip(ways, pair)]
+        token = yield tuple(next(step) for step in steps)
+        ways = [finish(step, token) for step in steps]
+    items = [
+        (jnp.concatenate([left[0], right[0]], axis=-1), left[1], left[2])
+        for left, right in zip(*ways)
+    ]
+    for mask in reversed(masks[:-1]):
+        items = yield from hop(items, mask, kind)
+    return [item[0] for item in items]
+
+
+def drain(chain, token):
+    while True:
+        try:
+            chain.send(token)
+        except StopIteration as stop:
+            return stop.value
+
+
+def bits_shape(count, tail):
+    return (2,) * (count.bit_length() - 1) + tuple(tail)
+
+
+def join_narrow(piece):
     spot = lax.axis_index("narrow")
     other = swap(piece, 2)
     pair = jnp.where(spot // 2 == 0, jnp.stack([piece, other]), jnp.stack([other, piece]))
@@ -172,42 +252,49 @@
     quad = jnp.where(
         spot % 2 == 0, jnp.stack([pair, other], axis=1), jnp.stack([other, pair], axis=1)
     )
-    return quad.reshape(4 * piece.shape[0], piece.shape[1])
+    return quad.reshape((4,) + piece.shape)
 
 
 def sum_small(blocks):
+    total = blocks + swap(blocks, 1)
+    first = total
+    total = total.reshape(bits_shape(blocks.shape[0], blocks.shape[1:]))
     masks = wide_masks()
-    blocks = blocks + swap(blocks, 1)
-    blocks = out_of_order(blocks, masks, lax.axis_size("narrow"), lax.axis_index("wide"))
-    for mask in reversed(masks):
-        half = blocks.shape[0] // 2
-        blocks = blocks[:half] + swap(blocks[half:], mask)
-    piece = blocks[0]
-    return piece + swap(piece, 2)
+    while masks:
+        mask = masks[-1]
+        keep, send = split_sided(total, len(masks) - 1, mask)
+        total = keep + swap(send, mask)
+        masks = masks[:-1]
+    return total + swap(total, 2), first
+
+
+def sum_wide(value):
+    for mask in reversed(wide_masks()):
+        value = value + swap(value, mask)
+    return value
 
 
 def sum_gram(blocks):
-    wide_at = lax.axis_index("wide")
-    narrow_size = lax.axis_size("narrow")
-    masks = wide_masks()
-    bits = [(mask // narrow_size).bit_length() - 1 for mask in masks]
-    order = list(zip(masks, bits))
-    order = list(reversed(order))
-    for mask, bit in order:
-        side = (wide_at >> bit) % 2
-        half = blocks.shape[0] // 2
-        keep = lax.dynamic_slice_in_dim(blocks, side * half, half, 0)
-        send = lax.dynamic_slice_in_dim(blocks, (1 - side) * half, half, 0)
-        blocks = keep + swap(send, mask)
-    for mask, bit in reversed(order):
-        side = (wide_at >> bit) % 2
-        other = swap(blocks, mask)
-        blocks = jnp.where(
-            side == 0,
-            jnp.concatenate([blocks, other], axis=0),
-            jnp.concatenate([other, blocks], axis=0),
-        )
-    return blocks
+    masks = list(reversed(wide_masks()))
+    ways = [masks, [masks[1], masks[0]] + masks[2:]]
+    half = blocks.shape[0] // 2
+    parts = [blocks[:half], blocks[half:]]
+    for step in range(len(masks)):
+        for number, way in enumerate(ways):
+            part = parts[number]
+            split = part.reshape((2, part.shape[0] // 2) + part.shape[1:])
+            keep, send = split_sided(split, 0, way[step])
+            parts[number] = keep + swap(send, way[step])
+    for step in reversed(range(len(masks))):
+        for number, way in enumerate(ways):
+            part = parts[number]
+            other = swap(part, way[step])
+            parts[number] = jnp.where(
+                side_of(way[step]) == 0,
+                jnp.concatenate([part, other], axis=0),
+                jnp.concatenate([other, part], axis=0),
+            )
+    return parts
 
 
 def row_dot(left_side, right_side):
@@ -221,25 +308,40 @@
     return high, (values - high.astype(jnp.float32)).astype(jnp.bfloat16)
 
 
-def newton_kernel(gram_ref, rows_ref, out_ref, gram_now, other, left, right, rows_left):
+def rounded(values):
+    return lax.reduce_precision(values, 8, 7)
+
+
+def newton_kernel(
+    low_ref, high_ref, rows_ref, add_left_ref, add_right_ref, out_ref,
+    gram_now, other, left, right, rows_left,
+):
     tile = GRAM_TILE
-    count = rows_ref.shape[0]
     trace = jnp.zeros((1, 1), jnp.float32)
     diagonal = lax.broadcasted_iota(jnp.int32, (tile, tile), 0) == lax.broadcasted_iota(
         jnp.int32, (tile, tile), 1
     )
+
+    def span(number):
+        return slice(number * tile, (number + 1) * tile)
+
+    half = len(GRAM_SPOTS) // 2
     for number, (row, column) in enumerate(GRAM_SPOTS):
+        source = low_ref if number < half else high_ref
+        block = source[span(number % half), :] + lax.dot_general(
+            add_left_ref[:, span(row)],
+            add_right_ref[:, span(column)],
+            (((0,), (0,)), ((), ())),
+            preferred_element_type=jnp.float32,
+        )
+        gram_now[span(row), span(column)] = block
         if row == column:
-            picked = jnp.where(diagonal, gram_ref[number * tile : (number + 1) * tile, :], 0.0)
+            picked = jnp.where(diagonal, block, 0.0)
             trace = trace + jnp.sum(jnp.sum(picked, axis=0, keepdims=True), axis=1, keepdims=True)
     inverse = 1.0 / (jnp.sqrt(trace) + 1e-07)
     scale = inverse * inverse
-
-    def span(number):
-        return slice(number * tile, (number + 1) * tile)
-
-    for number, (row, column) in enumerate(GRAM_SPOTS):
-        block = gram_ref[span(number), :] * scale
+    for row, column in GRAM_SPOTS:
+        block = gram_now[span(row), span(column)] * scale
         gram_now[span(row), span(column)] = block
         if row != column:
             gram_now[span(column), span(row)] = block.T
@@ -305,12 +407,12 @@
     out_ref[...] = rows_product().astype(out_ref.dtype)
 
 
-def newton_rows(gram_blocks, rows):
+def newton_rows(gram_parts, rows, add_left, add_right):
     count = rows.shape[0]
     return pl.pallas_call(
         newton_kernel,
         out_shape=jax.ShapeDtypeStruct((count, D), jnp.bfloat16),
-        in_specs=[pl.BlockSpec(memory_space=pltpu.VMEM)] * 2,
+        in_specs=[pl.BlockSpec(memory_space=pltpu.VMEM)] * 5,
         out_specs=pl.BlockSpec(memory_space=pltpu.VMEM),
         scratch_shapes=[
             pltpu.VMEM((D, D), jnp.float32),
@@ -322,7 +424,7 @@
         compiler_params=pltpu.CompilerParams(vmem_limit_bytes=48 << 20),
         cost_estimate=pl.CostEstimate(flops=60 * D * D * D, bytes_accessed=4 << 20, transcendentals=0),
         name="newton",
-    )(gram_blocks, rows)
+    )(*gram_parts, rows, add_left, add_right)
 
 
 def pick_rows(parts, spot):
@@ -351,29 +453,121 @@
     )
 
 
-def muon_rows(weights, moments, gradients):
-    spot = lax.axis_index("narrow")
-    moment_next = tuple(
-        MUON_MU * moment + (1.0 - MUON_MU) * gradient
-        for moment, gradient in zip(moments, gradients)
-    )
-    updates = tuple(
-        (1.0 - MUON_MU) * gradient + MUON_MU * moment
-        for moment, gradient in zip(moment_next, gradients)
-    )
-    rows = pick_rows(updates, spot)
-    ortho = newton_rows(sum_gram(local_gram(rows)), rows)
-    pair = jnp.stack([ortho, swap(ortho, 2)])
-    quad = jnp.concatenate([pair, swap(pair, 1)], axis=0)
-    place = np.array([0, 2, 1, 3])
-    rows_whole = (3 * D, D, FF, FF)
-    updated = []
-    for number, weight in enumerate(weights):
-        mine = lax.dynamic_index_in_dim(quad, jnp.asarray(place)[spot ^ number], 0, keepdims=False)
-        mine = mine[: weight.shape[0]].astype(jnp.float32)
-        rate = MUON_RATE * SHAPE_FACTOR * math.sqrt(max(rows_whole[number], D))
-        updated.append(weight * (1.0 - MUON_RATE * MUON_DECAY) - rate * mine)
-    return tuple(updated), moment_next
+def pack_kernel(spot_ref, *refs):
+    out_ref = refs[-1]
+    at = 0
+    for ref in refs[:-1]:
+        count = ref.shape[0]
+        out_ref[at : at + count, :] = ref[...].astype(jnp.bfloat16)
+        at += count
+        room = -count % 16
+        if room:
+            out_ref[at : at + room, :] = jnp.zeros((room, D), jnp.bfloat16)
+            at += room
+
+
+def pack_rows(weights, spot):
+    units = [weight.shape[0] // lax.axis_size("narrow") for weight in weights]
+    total = sum(unit + -unit % 16 for unit in units)
+    if any(unit % 8 for unit in units):
+        return jnp.concatenate(
+            [padded_rows(quarter_rows(weight).astype(jnp.bfloat16)) for weight in weights], axis=0
+        )
+    return pl.pallas_call(
+        pack_kernel,
+        grid_spec=pltpu.PrefetchScalarGridSpec(
+            num_scalar_prefetch=1,
+            grid=(1,),
+            in_specs=[pl.BlockSpec((unit, D), lambda step, spot: (spot[0], 0)) for unit in units],
+            out_specs=pl.BlockSpec((total, D), lambda step, spot: (0, 0)),
+        ),
+        out_shape=jax.ShapeDtypeStruct((total, D), jnp.bfloat16),
+        name="pack",
+    )(spot[None].astype(jnp.int32), *weights)
+
+
+def sums_kernel(*refs):
+    *parts, out_ref, bias_ref, held = refs
+    for number, part in enumerate(parts):
+        width = part.shape[2]
+        for kind in range(3):
+            start = kind * D + number * width
+            held[:, start : start + width] = part[kind]
+    bias_ref[...] = jnp.sum(held[...], axis=0, keepdims=True)
+    count, rows, columns = out_ref.shape
+    for number in range(count):
+        out_ref[number] = held[0:rows, number * columns : (number + 1) * columns]
+
+
+def sums_blocks(parts, wide_size):
+    whole = pl.BlockSpec(memory_space=pltpu.VMEM)
+    return pl.pallas_call(
+        sums_kernel,
+        in_specs=[whole] * len(parts),
+        out_specs=[whole, whole],
+        out_shape=[
+            jax.ShapeDtypeStruct((wide_size, VOCAB, 3 * D // wide_size), jnp.float32),
+            jax.ShapeDtypeStruct((1, 3 * D), jnp.float32),
+        ],
+        scratch_shapes=[pltpu.VMEM((LANES, 3 * D), jnp.float32)],
+        name="token_sums",
+    )(*parts)
+
+
+def update_kernel(rates, spot_ref, pair_ref, other_ref, *refs):
+    count = len(rates)
+    for number in range(count):
+        weight_ref, out_ref = refs[number], refs[count + number]
+        rows = weight_ref.shape[0]
+        way = spot_ref[0] ^ number
+        mine = jnp.where(
+            way % 2 == 0, pair_ref[way // 2, 0:rows, :], other_ref[way // 2, 0:rows, :]
+        )
+        out_ref[...] = (
+            weight_ref[...] * (1.0 - MUON_RATE * MUON_DECAY)
+            - rates[number] * mine.astype(jnp.float32)
+        )
+
+
+def update_rows(spot, pair, other, weights, rates):
+    whole = pl.BlockSpec(memory_space=pltpu.VMEM)
+    return pl.pallas_call(
+        partial(update_kernel, rates),
+        in_specs=[pl.BlockSpec(memory_space=pltpu.SMEM)] + [whole] * (2 + len(weights)),
+        out_specs=[whole] * len(weights),
+        out_shape=[jax.ShapeDtypeStruct(weight.shape, jnp.float32) for weight in weights],
+        compiler_params=pltpu.CompilerParams(vmem_limit_bytes=40 << 20),
+        name="update",
+    )(spot[None].astype(jnp.int32), pair, other, *weights)
+
+
+def heads_kernel(place_ref, blocks_ref, bias_ref, out_ref, held):
+    count, rows, columns = blocks_ref.shape
+    held[...] = jnp.zeros_like(held)
+    for number in range(count):
+        spot = slice(number * columns, (number + 1) * columns)
+        held[0:rows, spot] = blocks_ref[place_ref[number]] + bias_ref[:, spot]
+    high, low = split_two(held[...])
+    out_ref[0:LANES, :] = high
+    out_ref[LANES : 2 * LANES, :] = low
+
+
+def heads_table(blocks, place, bias):
+    return pl.pallas_call(
+        heads_kernel,
+        grid_spec=pltpu.PrefetchScalarGridSpec(
+            num_scalar_prefetch=1,
+            grid=(1,),
+            in_specs=[
+                pl.BlockSpec(blocks.shape, lambda step, place: (0, 0, 0)),
+                pl.BlockSpec(bias.shape, lambda step, place: (0, 0)),
+            ],
+            out_specs=pl.BlockSpec((2 * LANES, 3 * D), lambda step, place: (0, 0)),
+            scratch_shapes=[pltpu.VMEM((LANES, 3 * D), jnp.float32)],
+        ),
+        out_shape=jax.ShapeDtypeStruct((2 * LANES, 3 * D), jnp.bfloat16),
+        name="heads_table",
+    )(place, blocks, bias)
 
 
 def turn(values, cosine, sine_table):
@@ -408,10 +602,11 @@
     v_ref[...] = values.astype(jnp.bfloat16)
     v_turned[...] = values.T.astype(jnp.bfloat16)
 
-    for head in range(2):
+    def one_head(head, carry):
         lane = lax.broadcasted_iota(jnp.int32, (SEQ_LEN, PAIR), 1)
         keys_head = jnp.where(lane // HEAD_DIM == head, k_ref[...], jnp.zeros((), jnp.bfloat16))
-        values_head = v_turned[head * HEAD_DIM : (head + 1) * HEAD_DIM, :]
+        head_rows = pl.ds(pl.multiple_of(head * HEAD_DIM, HEAD_DIM), HEAD_DIM)
+        values_head = v_turned[head_rows, :]
 
         def body(step, carry):
             at = pl.multiple_of(step * STRIP, STRIP)
@@ -421,12 +616,16 @@
             total = jnp.sum(powers, axis=0, keepdims=True)
             prob_low = (powers * (1.0 / total)).astype(jnp.bfloat16)
             prob_all[:, pl.ds(at, STRIP)] = prob_low
-            log_ref[0, head : head + 1, pl.ds(at, STRIP)] = peak + jnp.log(total)
+            log_ref[0, pl.ds(head, 1), pl.ds(at, STRIP)] = peak + jnp.log(total)
             return carry
 
         lax.fori_loop(0, SPAN // STRIP, body, 0)
-        mixed_turned[head * HEAD_DIM : (head + 1) * HEAD_DIM, :] = jnp.dot(
-            values_head, prob_all[...], preferred_element_type=jnp.float32)
+        mixed_turned[head_rows, :] = jnp.dot(
+            values_head, prob_all[...], preferred_element_type=jnp.float32
+        )
+        return carry
+
+    lax.fori_loop(0, 2, one_head, 0)
     mixed_ref[...] = mixed_turned[...].T[0:SEQ_LEN, :].astype(jnp.bfloat16)
 
 
@@ -462,8 +661,8 @@
         ],
         compiler_params=pltpu.CompilerParams(vmem_limit_bytes=40 << 20),
         cost_estimate=pl.CostEstimate(
-            flops=count * 8 * SPAN * SPAN * 256, bytes_accessed=count * 2 << 20,
-            transcendentals=count * 2 * SPAN * SEQ_LEN,
+            flops=count * SPAN * SPAN, bytes_accessed=1 << 16,
+            transcendentals=0,
         ),
         name="attend",
     )(hot, tables, tables, tables, cosine, sine_table)
@@ -483,14 +682,15 @@
     lane = lax.broadcasted_iota(jnp.int32, (SEQ_LEN, PAIR), 1)
     none = jnp.zeros((), jnp.bfloat16)
 
-    for head in range(2):
+    def one_head(head, carry):
+        head_rows = pl.ds(pl.multiple_of(head * HEAD_DIM, HEAD_DIM), HEAD_DIM)
         keys_head = jnp.where(lane // HEAD_DIM == head, k_ref[...], none)
         values_head = jnp.where(lane // HEAD_DIM == head, v_ref[...], none)
 
         def body(step, carry):
             at = pl.multiple_of(step * STRIP, STRIP)
             scores = row_dot(keys_head, q_all[pl.ds(at, STRIP), :])
-            prob_rows = jnp.exp(scores - log_ref[0, head : head + 1, pl.ds(at, STRIP)])
+            prob_rows = jnp.exp(scores - log_ref[0, pl.ds(head, 1), pl.ds(at, STRIP)])
             prob_all[:, pl.ds(at, STRIP)] = prob_rows.astype(jnp.bfloat16)
             prob_grad = row_dot(values_head, grad_all[pl.ds(at, STRIP), :])
             delta = jnp.sum(prob_grad * prob_rows, axis=0, keepdims=True)
@@ -500,17 +700,15 @@
         lax.fori_loop(0, SPAN // STRIP, body, 0)
         value_part = jnp.dot(prob_all[...], grad_all[...], preferred_element_type=jnp.float32)
         key_part = jnp.dot(score_all[...], q_all[...], preferred_element_type=jnp.float32)
-        if head == 0:
-            value_sum[...] = value_part
-            key_sum[...] = key_part
-        else:
-            value_sum[...] = jnp.where(lane < HEAD_DIM, value_sum[...], value_part)
-            key_sum[...] = jnp.where(lane < HEAD_DIM, key_sum[...], key_part)
-        query_turned[head * HEAD_DIM : (head + 1) * HEAD_DIM, :] = jnp.dot(
-            k_turned[head * HEAD_DIM : (head + 1) * HEAD_DIM, :],
-            score_all[...],
-            preferred_element_type=jnp.float32,
-        ) * HEAD_DIM ** (-0.5)
+        value_sum[...] = jnp.where(lane // HEAD_DIM == head, value_part, value_sum[...])
+        key_sum[...] = jnp.where(lane // HEAD_DIM == head, key_part, key_sum[...])
+        query_turned[head_rows, :] = (
+            jnp.dot(k_turned[head_rows, :], score_all[...], preferred_element_type=jnp.float32)
+            * HEAD_DIM ** (-0.5)
+        )
+        return carry
+
+    lax.fori_loop(0, 2, one_head, 0)
     cosine = cos_ref[...]
     sine_table = -sin_ref[...]
     hot = hot_ref[...]
@@ -522,11 +720,11 @@
         sums_ref[number] = jnp.dot(hot, low, preferred_element_type=jnp.float32)
 
 
-def attend_back_call(hot_turned, queries, keys, values, gradients, logs, cosine, sine_table, first):
-    count = logs.shape[0]
+def attend_back_call(
+    hot_turned, queries, keys, values, gradients, logs, cosine, sine_table, first, inside, count
+):
     whole = lambda step: (0, 0)
-    own = lambda step: (0, step)
-    rows = pl.BlockSpec((SEQ_LEN, PAIR), own)
+    rows = pl.BlockSpec((SEQ_LEN, PAIR), lambda step: (0, step + inside))
     whole_rows = pl.BlockSpec((SEQ_LEN, PAIR), whole)
     return pl.pallas_call(
         attend_back_kernel,
@@ -537,7 +735,7 @@
             rows,
             rows,
             pl.BlockSpec((SEQ_LEN, PAIR), lambda step: (0, step + first)),
-            pl.BlockSpec((1, 2, SPAN), lambda step: (step, 0, 0)),
+            pl.BlockSpec((1, 2, SPAN), lambda step: (step + inside, 0, 0)),
             whole_rows,
             whole_rows,
         ],
@@ -561,8 +759,8 @@
         ],
         compiler_params=pltpu.CompilerParams(vmem_limit_bytes=48 << 20),
         cost_estimate=pl.CostEstimate(
-            flops=count * 20 * SPAN * SPAN * 256, bytes_accessed=count * 3 << 20,
-            transcendentals=count * 2 * SPAN * SEQ_LEN,
+            flops=count * SPAN * SPAN, bytes_accessed=1 << 16,
+            transcendentals=0,
         ),
         name="attend_back",
     )(hot_turned, queries, keys, values, gradients, logs, cosine, sine_table)
@@ -581,22 +779,46 @@
     tail = (0.5 * series) * step * bell
     return jnp.where(values < 0.0, tail, 1.0 - tail), bell * (1.0 / math.sqrt(2.0 * math.pi))
 
-def feed_kernel(rows_ref, bias_ref, e0, e1, e2, e3, r0, r1, r2, r3, hidden_ref, slope_ref, out_ref, expand_held, reduce_held, pre, sems):
+def start_parts(place_ref, source_ref, starts, held, sems):
+    for part in range(PARTS):
+        for number, start in enumerate(starts):
+
+            def body(spot, carry):
+                pltpu.make_async_copy(
+                    source_ref.at[place_ref[part * PART_BLOCKS + spot], pl.ds(start, BLOCK), :],
+                    held[number].at[part, spot],
+                    sems.at[number, part],
+                ).start()
+                return carry
+
+            lax.fori_loop(0, PART_BLOCKS, body, 0)
+
+
+def wait_part(source_ref, number, held, sems, step):
+    pltpu.make_async_copy(
+        source_ref.at[pl.ds(0, PART_BLOCKS), pl.ds(0, BLOCK), :],
+        held[number].at[step],
+        sems.at[number, step],
+    ).wait()
+    return held[number][step].reshape(D, D)
+
+
+def feed_kernel(starts, place_ref, rows_ref, bias_ref, source_ref, hidden_ref, slope_ref, out_ref, expand_held, reduce_held, sems):
+    held = (expand_held, reduce_held)
     step = pl.program_id(0)
     @pl.when(step == 0)
     def _():
-        for number in range(PARTS):
-            pltpu.make_async_copy((e0,e1,e2,e3)[number], expand_held.at[number], sems.at[number]).start()
-            pltpu.make_async_copy((r0,r1,r2,r3)[number], reduce_held.at[number], sems.at[PARTS + number]).start()
-    pltpu.make_async_copy(e0, expand_held.at[step], sems.at[step]).wait()
+        start_parts(place_ref, source_ref, starts, held, sems)
+
+    expand = wait_part(source_ref, 0, held, sems, step)
     for at in range(0, SEQ_LEN, 304):
         spot = slice(at, at + 304)
-        values = row_dot(rows_ref[spot, :], expand_held[step]) + bias_ref[...]
+        values = row_dot(rows_ref[spot, :], expand) + bias_ref[...]
         below, bell = normal_parts(values)
         hidden_ref[spot, :] = (values * below).astype(jnp.bfloat16)
         slope_ref[spot, :] = (below + values * bell).astype(jnp.bfloat16)
-    pltpu.make_async_copy(r0, reduce_held.at[step], sems.at[PARTS + step]).wait()
-    part = jnp.dot(hidden_ref[...], reduce_held[step], preferred_element_type=jnp.float32)
+    reduce = wait_part(source_ref, 1, held, sems, step)
+    part = jnp.dot(hidden_ref[...], reduce, preferred_element_type=jnp.float32)
     @pl.when(step == 0)
     def _():
         out_ref[...] = part
@@ -604,40 +826,55 @@
     def _():
         out_ref[...] += part
 
-def feed_call(rows, bias, expands, reduces):
-    whole = lambda step: (0, 0)
-    chunk = pl.BlockSpec((SEQ_LEN, D), lambda step: (0, step))
-    anywhere = pl.BlockSpec(memory_space=pl.ANY)
+def feed_call(place, rows, bias, source, starts):
+    whole = lambda step, place: (0, 0)
+    chunk = pl.BlockSpec((SEQ_LEN, D), lambda step, place: (0, step))
     return pl.pallas_call(
-        feed_kernel, grid=(PARTS,),
-        in_specs=[pl.BlockSpec((SEQ_LEN, D), whole), pl.BlockSpec((1, D), lambda step: (0, step))] + [anywhere] * 8,
-        out_specs=[chunk, chunk, pl.BlockSpec((SEQ_LEN, D), whole)],
-        out_shape=[jax.ShapeDtypeStruct((SEQ_LEN, FF), jnp.bfloat16)] * 2 + [jax.ShapeDtypeStruct((SEQ_LEN, D), jnp.float32)],
-        scratch_shapes=[pltpu.VMEM((PARTS, D, D), jnp.bfloat16), pltpu.VMEM((PARTS, D, D), jnp.bfloat16), pltpu.VMEM((SEQ_LEN, D), jnp.float32), pltpu.SemaphoreType.DMA((2 * PARTS,))],
+        partial(feed_kernel, starts),
+        grid_spec=pltpu.PrefetchScalarGridSpec(
+            num_scalar_prefetch=1,
+            grid=(PARTS,),
+            in_specs=[
+                pl.BlockSpec((SEQ_LEN, D), whole),
+                pl.BlockSpec((1, D), lambda step, place: (0, step)),
+                pl.BlockSpec(memory_space=pl.ANY),
+            ],
+            out_specs=[chunk, chunk, pl.BlockSpec((SEQ_LEN, D), whole)],
+            scratch_shapes=[
+                pltpu.VMEM((PARTS, PART_BLOCKS, BLOCK, D), jnp.bfloat16),
+                pltpu.VMEM((PARTS, PART_BLOCKS, BLOCK, D), jnp.bfloat16),
+                pltpu.SemaphoreType.DMA((2, PARTS)),
+            ],
+        ),
+        out_shape=[jax.ShapeDtypeStruct((SEQ_LEN, FF), jnp.bfloat16)] * 2
+        + [jax.ShapeDtypeStruct((SEQ_LEN, D), jnp.float32)],
         compiler_params=pltpu.CompilerParams(vmem_limit_bytes=48 << 20),
-        cost_estimate=pl.CostEstimate(flops=4 * SEQ_LEN * D * FF, bytes_accessed=24 << 20, transcendentals=SEQ_LEN * FF),
+        cost_estimate=pl.CostEstimate(
+            flops=SEQ_LEN * D * FF, bytes_accessed=1 << 16, transcendentals=0
+        ),
         name="feed",
-    )(rows, bias, *expands, *reduces)
-
-def feed_back_kernel(grad_ref, slope_ref, e0, e1, e2, e3, r0, r1, r2, r3, pre_ref, out_ref, bias_ref, expand_held, reduce_held, sems):
+    )(place, rows, bias, source)
+
+
+def feed_back_kernel(starts, place_ref, grad_ref, slope_ref, source_ref, pre_ref, out_ref, bias_ref, expand_held, reduce_held, sems):
+    held = (expand_held, reduce_held)
     step = pl.program_id(0)
     @pl.when(step == 0)
     def _():
-        for number in range(PARTS):
-            pltpu.make_async_copy((r0,r1,r2,r3)[number], reduce_held.at[number], sems.at[PARTS + number]).start()
-            pltpu.make_async_copy((e0,e1,e2,e3)[number], expand_held.at[number], sems.at[number]).start()
-    pltpu.make_async_copy(r0, reduce_held.at[step], sems.at[PARTS + step]).wait()
+        start_parts(place_ref, source_ref, starts, held, sems)
+
+    reduce = wait_part(source_ref, 1, held, sems, step)
     total = jnp.zeros((1, D), jnp.float32)
     for at in range(0, SEQ_LEN, 304):
         spot = slice(at, at + 304)
-        grad = row_dot(grad_ref[spot, :], reduce_held[step]) * slope_ref[spot, :].astype(jnp.float32)
+        grad = row_dot(grad_ref[spot, :], reduce) * slope_ref[spot, :].astype(jnp.float32)
         low = grad.astype(jnp.bfloat16)
         pre_ref[spot, :] = low
         total = total + jnp.sum(low.astype(jnp.float32), axis=0, keepdims=True)
     bias_ref[...] = total
     low = pre_ref[...]
-    pltpu.make_async_copy(e0, expand_held.at[step], sems.at[step]).wait()
-    part = jnp.dot(low, expand_held[step], preferred_element_type=jnp.float32)
+    expand = wait_part(source_ref, 0, held, sems, step)
+    part = jnp.dot(low, expand, preferred_element_type=jnp.float32)
     @pl.when(step == 0)
     def _():
         out_ref[...] = part
@@ -645,20 +882,41 @@
     def _():
         out_ref[...] += part
 
-def feed_back_call(grad, slope, expands, reduces):
-    whole = lambda step: (0, 0)
-    chunk = pl.BlockSpec((SEQ_LEN, D), lambda step: (0, step))
-    anywhere = pl.BlockSpec(memory_space=pl.ANY)
+def feed_back_call(place, grad, slope, source, starts):
+    whole = lambda step, place: (0, 0)
+    chunk = pl.BlockSpec((SEQ_LEN, D), lambda step, place: (0, step))
     return pl.pallas_call(
-        feed_back_kernel, grid=(PARTS,),
-        in_specs=[pl.BlockSpec((SEQ_LEN, D), whole), chunk] + [anywhere] * 8,
-        out_specs=[chunk, pl.BlockSpec((SEQ_LEN, D), whole), pl.BlockSpec((1, D), lambda step: (0, step))],
-        out_shape=[jax.ShapeDtypeStruct((SEQ_LEN, FF), jnp.bfloat16), jax.ShapeDtypeStruct((SEQ_LEN, D), jnp.float32), jax.ShapeDtypeStruct((1, FF), jnp.float32)],
-        scratch_shapes=[pltpu.VMEM((PARTS, D, D), jnp.bfloat16), pltpu.VMEM((PARTS, D, D), jnp.bfloat16), pltpu.SemaphoreType.DMA((2 * PARTS,))],
+        partial(feed_back_kernel, starts),
+        grid_spec=pltpu.PrefetchScalarGridSpec(
+            num_scalar_prefetch=1,
+            grid=(PARTS,),
+            in_specs=[
+                pl.BlockSpec((SEQ_LEN, D), whole),
+                chunk,
+                pl.BlockSpec(memory_space=pl.ANY),
+            ],
+            out_specs=[
+                chunk,
+                pl.BlockSpec((SEQ_LEN, D), whole),
+                pl.BlockSpec((1, D), lambda step, place: (0, step)),
+            ],
+            scratch_shapes=[
+                pltpu.VMEM((PARTS, PART_BLOCKS, BLOCK, D), jnp.bfloat16),
+                pltpu.VMEM((PARTS, PART_BLOCKS, BLOCK, D), jnp.bfloat16),
+                pltpu.SemaphoreType.DMA((2, PARTS)),
+            ],
+        ),
+        out_shape=[
+            jax.ShapeDtypeStruct((SEQ_LEN, FF), jnp.bfloat16),
+            jax.ShapeDtypeStruct((SEQ_LEN, D), jnp.float32),
+            jax.ShapeDtypeStruct((1, FF), jnp.float32),
+        ],
         compiler_params=pltpu.CompilerParams(vmem_limit_bytes=48 << 20),
-        cost_estimate=pl.CostEstimate(flops=4 * SEQ_LEN * D * FF, bytes_accessed=24 << 20, transcendentals=0),
+        cost_estimate=pl.CostEstimate(
+            flops=SEQ_LEN * D * FF, bytes_accessed=1 << 16, transcendentals=0
+        ),
         name="feed_back",
-    )(grad, slope, *expands, *reduces)
+    )(place, grad, slope, source)
 
 
 def adam_step(weight, mean_state, square, gradient, step_rate, decay_rate, step_count):
@@ -698,8 +956,24 @@
     wide_at = lax.axis_index("wide")
     me = my_index()
     devices = lax.axis_size(BOTH)
-    all_masks = wide_masks() + [2, 1]
-    small = gather_wide(jnp.concatenate([table_weight, vector_params], axis=0).astype(low_type))
+    masks = wide_masks()
+    narrow_size = lax.axis_size("narrow")
+    wide_size = lax.axis_size("wide")
+    hidden_masks = masks[:-1] + [2, masks[-1], 1]
+    all_masks = masks + [2, 1]
+    small = jnp.concatenate([table_weight, vector_params], axis=0).astype(low_type)
+    small = gather_blocks(small[None], masks)
+    packed = (expand_weight, reduce_weight, attend_weight, mixing_weight)
+    units = [weight.shape[0] // narrow_size for weight in packed]
+    starts = np.cumsum([0] + [unit + -unit % 16 for unit in units])
+    weights_low = lax.all_gather(pack_rows(packed, lax.axis_index("narrow")), BOTH, axis=0)
+
+    def weight_rows(number, unit):
+        start = int(starts[number])
+        return weights_low[:, start : start + unit].reshape(-1, D)
+
+    codons, positions, targets = gate((codons, positions, targets), small)
+    small = in_order(small, masks, narrow_size, wide_at)
     small = jnp.transpose(small, (1, 0, 2)).reshape(VOCAB + 15, D)
     table_low = small[:VOCAB]
     vector_full = small[VOCAB:].astype(jnp.float32)
@@ -709,26 +983,34 @@
     bias_two = vector_full[3]
     gain_last = vector_full[4]
     bias_last = vector_full[5]
-    attend_bias = vector_full[6:9].reshape(3 * D)
+    attend_bias = vector_full[6:9].reshape(1, 3 * D)
     mixing_bias = vector_full[9]
     reduce_bias = vector_full[10]
     expand_bias = out_of_order(
-        vector_full[11:15].reshape(devices, FF // devices), all_masks, 1, me
+        vector_full[11:15].reshape(devices, FF // devices), hidden_masks, 1, me
     ).reshape(FF)
     embed_scale = math.sqrt(D)
     table_stream = embed_scale * table_low.astype(jnp.float32)
     table_normed = norm_forward(table_stream, gain_one, bias_one)[0].astype(low_type)
-    attend_own = attend_weight.astype(low_type)
-    table_own = times_trans(table_normed, attend_own)
-    table_heads = jnp.transpose(gather_wide(table_own), (1, 0, 2)).reshape(VOCAB, 3 * D)
-    table_heads = table_heads + attend_bias
-
-    mixing_low = gather_blocks(quarter_rows(mixing_weight).astype(low_type)[None], all_masks)
-    mixing_low = in_order(mixing_low, all_masks, 1, me).reshape(D, D)
-    expand_parts = gather_parts(quarter_rows(expand_weight).astype(low_type))
-    reduce_parts = gather_parts(quarter_rows(reduce_weight).astype(low_type))
-    attend_low = gather_blocks(quarter_rows(attend_weight).astype(low_type)[None], all_masks)
-    attend_low = in_order(attend_low, all_masks, 1, me).reshape(3 * D, D)
+    table_own = times_trans(table_normed, attend_weight.astype(low_type))
+    place = jnp.asarray(places_of(masks, narrow_size), jnp.int32)[jnp.arange(wide_size) ^ wide_at]
+    tables = heads_table(gather_blocks(table_own[None], masks), place, attend_bias)
+
+    unit = FF // devices
+    hidden_place = jnp.asarray(offsets_of(hidden_masks)) ^ me
+    if unit == BLOCK:
+        feed_place, feed_source, feed_starts = hidden_place, weights_low, tuple(starts[:2])
+    else:
+        feed_source = jnp.concatenate(
+            [
+                take_blocks(weights_low[:, start : start + unit], hidden_place).reshape(-1, BLOCK, D)
+                for start in (int(starts[0]), int(starts[1]))
+            ],
+            axis=1,
+        )
+        feed_place, feed_starts = jnp.arange(FF // BLOCK), (0, BLOCK)
+    feed_place = feed_place.astype(jnp.int32)
+    feed_starts = tuple(int(start) for start in feed_starts)
 
     seq_count = codons.shape[0]
     row_count = seq_count * SEQ_LEN
@@ -742,24 +1024,25 @@
     lane_ids = jnp.arange(2 * LANES, dtype=jnp.int32) % LANES
     hot = (token_ids[:, None] == lane_ids[None, :]).astype(low_type)
     hot_turned = (token_ids[None, :] == lane_ids[:LANES, None]).astype(low_type)
-    heads_high, heads_low = split_two(table_heads)
-    spare = ((0, LANES - VOCAB), (0, 0))
-    tables = jnp.concatenate([jnp.pad(heads_high, spare), jnp.pad(heads_low, spare)], axis=0)
     cosine, sine_table = rotary_tables(positions.reshape(row_count))
     cosine = jnp.concatenate([cosine] * 4, axis=1)
     sine_table = jnp.concatenate([-sine_table, sine_table] * 2, axis=1)
     pairs = D // PAIR // ATTEND_CALLS
-    attended = [
-        attend_call(hot, tables, cosine, sine_table, number * pairs, pairs)
-        for number in range(ATTEND_CALLS)
-    ]
+    attended = []
+
+    for number in range(ATTEND_CALLS):
+        attended.append(
+            attend_call(hot, tables, cosine, sine_table, number * pairs, pairs)
+        )
+    last_mask = masks[-1]
     mixed_low = jnp.concatenate([parts[3] for parts in attended], axis=1)
+    mixing_low = weight_rows(3, D // devices)
     branch = times_trans(mixed_low, mixing_low) + mixing_bias
     middle = stream + branch
     normed_two, normal_two, inverse_two = norm_forward(middle, gain_two, bias_two)
     normed_two_low = normed_two.astype(low_type)
     hidden_low, slope_low, feed_out = feed_call(
-        normed_two_low, expand_bias[None, :], expand_parts, reduce_parts
+        feed_place, normed_two_low, expand_bias[None, :], feed_source, feed_starts
     )
     feed_out = feed_out + reduce_bias
     output = middle + feed_out
@@ -778,62 +1061,94 @@
     )
     feed_low = output_grad.astype(low_type)
     reduce_bias_grad = jnp.sum(feed_low, axis=0, dtype=jnp.float32)
-    scatter_masks = list(reversed(all_masks))
     half_ff = FF // 2
-    reduce_part = scatter_blocks(
-        trans_times(hidden_low[:, :half_ff], feed_low),
-        trans_times(hidden_low[:, half_ff:], feed_low),
-        scatter_masks,
-        jnp.float32,
-    )
-    reduce_total = narrow_rows(reduce_part)
+    static_marks = [masks[-1], 2] + list(reversed(masks[:-1]))
+    static_shape = (2,) * len(static_marks) + (unit, D)
+
+    reduce_send = trans_times(hidden_low[:, half_ff:], feed_low).astype(low_type)
+    reduce_sum = trans_times(hidden_low[:, :half_ff], feed_low) + swap(reduce_send, 1)
+    reduce_chain = sum_chain([(reduce_sum.reshape(static_shape), static_marks, False)], jnp.float32)
+    sent = next(reduce_chain)
     pre_grad, normed_two_grad, expand_bias_grad = feed_back_call(
-        feed_low, slope_low, expand_parts, reduce_parts
-    )
-    expand_bias_grad = in_order(
-        expand_bias_grad.reshape(devices, FF // devices), all_masks, 1, me
-    )
-    expand_part = scatter_blocks(
-        trans_times(pre_grad[:, :half_ff], normed_two_low),
-        trans_times(pre_grad[:, half_ff:], normed_two_low),
-        scatter_masks,
-        jnp.float32,
-    )
-    expand_total = narrow_rows(expand_part)
+        feed_place, gate(feed_low, sent), slope_low, feed_source, feed_starts
+    )
+    sent = reduce_chain.send(pre_grad)
+    expand_send = trans_times(
+        gate(pre_grad, sent)[:, half_ff:], normed_two_low
+    ).astype(low_type)
+    expand_sum = trans_times(pre_grad[:, :half_ff], normed_two_low) + swap(expand_send, 1)
     middle_part, gain_two_grad, bias_two_grad = norm_backward(
         normed_two_grad, normal_two, inverse_two, gain_two
     )
     middle_grad = output_grad + middle_part
     branch_low = middle_grad.astype(low_type)
     mixing_bias_grad = jnp.sum(branch_low, axis=0, dtype=jnp.float32)
-    mixing_grad = trans_times(branch_low, mixed_low).reshape(devices, D // devices, D)
-    mixing_grad = out_of_order(mixing_grad, all_masks, 1, me)
-    mixing_part = scatter_blocks(
-        mixing_grad[: devices // 2], mixing_grad[devices // 2 :], scatter_masks, jnp.float32
-    )
-    mixing_total = narrow_rows(mixing_part[0])
+    mixing_sum = trans_times(branch_low, mixed_low).reshape(
+        bits_shape(devices, (D // devices, D))
+    )
+    (mixing_item,) = finish_hop(hop([(mixing_sum, all_masks, True)], 1, low_type))
     mixed_grad = times_plain(branch_low, mixing_low).astype(low_type)
-    backs = [
-        attend_back_call(
-            hot_turned,
-            *attended[number][:3],
-            mixed_grad,
-            attended[number][4],
-            cosine,
-            sine_table,
-            number * pairs,
+    expand_chain = sum_chain(
+        [(expand_sum.reshape(static_shape), static_marks, False), mixing_item], low_type
+    )
+    expand_sent = next(expand_chain)
+    reduce_sent = reduce_chain.send(expand_sum)
+
+    backs = []
+    back_pairs = D // PAIR // BACK_CALLS
+
+    def back_step(waits):
+        number = len(backs)
+        first = number * back_pairs
+        source = attended[first // pairs]
+        order = (backs[-1][1],) if backs else ()
+        backs.append(
+            attend_back_call(
+                hot_turned,
+                *source[:3],
+                gate(mixed_grad, (waits, order)),
+                source[4],
+                cosine,
+                sine_table,
+                first,
+                first % pairs,
+                back_pairs,
+            )
         )
-        for number in range(ATTEND_CALLS)
-    ]
-    token_sums = jnp.concatenate([back[1][:, :VOCAB] for back in backs], axis=2)
-    token_sums = jnp.transpose(token_sums, (1, 0, 2)).reshape(VOCAB, 3 * D)
-    attend_bias_grad = jnp.sum(token_sums, axis=0)
-    projected_low = jnp.concatenate(
-        [back[0][number] for number in range(3) for back in backs], axis=1
-    )
-    wide_size = lax.axis_size("wide")
-    token_sums = jnp.transpose(token_sums.reshape(VOCAB, wide_size, 3 * D // wide_size), (1, 0, 2))
-    token_sums = sum_small(token_sums)
+        return backs[-1][1]
+
+    back_step((expand_sent, reduce_sent))
+    token = back_step(())
+    expand_sent = expand_chain.send(token)
+    reduce_sent = reduce_chain.send(token)
+    token = back_step((expand_sent, reduce_sent))
+    expand_sent = expand_chain.send(token)
+    token = back_step(expand_sent)
+    (reduce_sum,) = drain(reduce_chain, token)
+    token = back_step(())
+    expand_sent = expand_chain.send(token)
+    token = back_step(expand_sent)
+    expand_sum, mixing_sum = drain(expand_chain, token)
+    token_sums, attend_bias_grad = sums_blocks([back[1] for back in backs], wide_size)
+    dense = join_narrow(jnp.concatenate([reduce_sum, expand_sum, mixing_sum], axis=0))
+    reduce_total = dense[:, :unit].reshape(-1, D)
+    expand_total = dense[:, unit : 2 * unit].reshape(-1, D)
+    mixing_total = dense[:, 2 * unit :].reshape(-1, D)
+    spot = lax.axis_index("narrow")
+
+    def step_of(moment, gradient):
+        moment_next = MUON_MU * moment + (1.0 - MUON_MU) * gradient
+        return moment_next, (1.0 - MUON_MU) * gradient + MUON_MU * moment_next
+
+    mixing_next, mixing_step = step_of(mixing_moment, mixing_total)
+    expand_next, expand_step = step_of(expand_moment, expand_total)
+    reduce_next, reduce_step = step_of(reduce_moment, reduce_total)
+    attend_base = (MUON_MU * MUON_MU) * attend_moment
+    gram_parts = sum_gram(
+        local_gram(pick_rows((attend_base, mixing_step, expand_step, reduce_step), spot))
+    )
+
+    token_sums, token_first = sum_small(token_sums)
     attend_total = lax.dot_general(
         token_sums,
         table_normed.astype(jnp.float32),
@@ -841,7 +1156,31 @@
         precision=lax.Precision.HIGHEST,
         preferred_element_type=jnp.float32,
     )
-    normed_one_grad = times_plain(projected_low, attend_low)
+    attend_next, attend_step = step_of(attend_moment, attend_total)
+    gradient_rate = (1.0 - MUON_MU) * (1.0 + MUON_MU)
+    crossed = exact_times(
+        token_sums, jnp.concatenate([attend_moment, token_sums.T], axis=1)
+    )
+    crossed = sum_wide(crossed)
+    table_wide = table_normed.astype(jnp.float32)
+    added = gradient_rate * (
+        (MUON_MU * MUON_MU) * crossed[:, :D]
+        + (0.5 * gradient_rate) * exact_times(crossed[:, D:], table_wide)
+    )
+    added = jnp.where(spot == 0, added, 0.0)
+    added_high = rounded(added)
+    added_low = rounded(added - added_high)
+    added_least = added - added_high - added_low
+    table_three = [table_normed] * 3
+    added_three = [part.astype(low_type) for part in (added_high, added_low, added_least)]
+    room = ((0, -(-6 * VOCAB // 16) * 16 - 6 * VOCAB), (0, 0))
+    add_left = jnp.pad(jnp.concatenate(added_three + table_three, axis=0), room)
+    add_right = jnp.pad(jnp.concatenate(table_three + added_three, axis=0), room)
+
+    lows = gate([back[0] for back in backs], token_first)
+    projected_low = jnp.concatenate([low[kind] for kind in range(3) for low in lows], axis=1)
+    attend_low = gate(weights_low, token_first)[:, int(starts[2]) : int(starts[2]) + units[2]]
+    normed_one_grad = times_plain(projected_low, attend_low.reshape(3 * D, D))
     normed_one, normal_one, inverse_one = norm_forward(stream, gain_one, bias_one)
     stream_part, gain_one_grad, bias_one_grad = norm_backward(
         normed_one_grad, normal_one, inverse_one, gain_one
@@ -849,6 +1188,31 @@
     entry_gradient = middle_grad + stream_part
     table_grad = (
         embed_scale * exact_times(token_hot.astype(jnp.float32).T, entry_gradient) + table_head
+    )
+    (
+        gain_two_grad,
+        bias_two_grad,
+        gain_last_grad,
+        bias_last_grad,
+        mixing_bias_grad,
+        reduce_bias_grad,
+        expand_bias_grad,
+        prob_sum,
+    ) = gate(
+        (
+            gain_two_grad,
+            bias_two_grad,
+            gain_last_grad,
+            bias_last_grad,
+            mixing_bias_grad,
+            reduce_bias_grad,
+            expand_bias_grad,
+            prob_sum,
+        ),
+        token_first,
+    )
+    expand_bias_grad = in_order(
+        expand_bias_grad.reshape(devices, FF // devices), hidden_masks, 1, me
     )
     vector_grad = jnp.concatenate(
         [
@@ -877,17 +1241,22 @@
     small_grads = jnp.concatenate(
         [small_grads, jnp.broadcast_to(hist_part, (wide_size, rows_hist, columns))], axis=1
     )
-    small_total = sum_small(small_grads)
+    small_total, _ = sum_small(small_grads)
     table_total = small_total[:VOCAB]
     vector_total = small_total[VOCAB : VOCAB + 15]
     prob_total = small_total[VOCAB + 15 :].reshape(rows_hist * columns)[:VOCAB]
     histogram = prob_total * (VOCAB / (row_count * devices))
     totals = (attend_total, mixing_total, expand_total, reduce_total)
-    matrix_new, moment_next = muon_rows(
-        (attend_weight, mixing_weight, expand_weight, reduce_weight),
-        (attend_moment, mixing_moment, expand_moment, reduce_moment),
-        totals,
-    )
+    moment_next = (attend_next, mixing_next, expand_next, reduce_next)
+    rows = pick_rows((attend_step, mixing_step, expand_step, reduce_step), spot)
+    rows = gate(rows, small_total)
+    ortho = newton_rows(gram_parts, rows, add_left, add_right)
+    pair = jnp.stack([ortho, swap(ortho, 2)])
+    matrices = (attend_weight, mixing_weight, expand_weight, reduce_weight)
+    rates = tuple(
+        MUON_RATE * SHAPE_FACTOR * math.sqrt(max(rows, D)) for rows in (3 * D, D, FF, FF)
+    )
+    matrix_new = tuple(update_rows(spot, pair, swap(pair, 1), matrices, rates))
     table_new, table_mean_next, table_square_next = adam_step(
         table_weight, table_mean, table_square, table_total, TABLE_RATE, TABLE_DECAY, step_count
     )

time: 621 us -> 525 us (0.85)
  waiting for transfers between devices: 180 us -> 113 us
  local copies, waits for them, and re-layouts: 77.1 us -> 50.2 us
  starting transfers between devices: 61.7 us -> 49.6 us
  Pallas kernels: 176 us -> 188 us
    ppermute x67 -> x50, waiting for transfers between devices: 180 us -> 101 us  [swap(): lax.ppermute(value, BOTH, [(spot, spot ^ mask) for spot in range(total)])]
    unnamed x234 -> x241, local copies, waits for them, and re-layouts: 34.6 us -> 19 us
    gather x9 -> x3, local copies, waits for them, and re-layouts: 16.9 us -> 1.73 us  [take_blocks(): return jnp.take(array, index, axis=0, mode='clip')]
    ppermute x67 -> x50, starting transfers between devices: 61.7 us -> 49.6 us  [swap(): lax.ppermute(value, BOTH, [(spot, spot ^ mask) for spot in range(total)])]
    all_gather x0 -> x1, waiting for transfers between devices: none -> 11.9 us  [on_device(): lax.all_gather(pack_rows(packed, lax.axis_index('narrow')), BOTH, axis=0)]
    concatenate x18 -> x6, other arithmetic: 14.4 us -> 2.94 us  [gather_blocks(): piece = jnp.concatenate([piece, swap(piece, mask)], axis=0)]
    pallas_call x2 -> x6, Pallas kernels: 40.6 us -> 52 us  [the longest x1 22.7 us: feed_call(): pl.pallas_call(partial(feed_kernel, starts), grid_spec=pltpu.PrefetchScal...]
    add x24 -> x37, other arithmetic: 5.94 us -> 14.8 us  [the longest x17 7.63 us: hop(): results.append((keep + part, marks, sided))]
  transfers between devices with their start and end apart: 67 -> 51, of which waited for: 25 -> 21; matrix products, arithmetic and copies ran while one was open for 26% -> 18% of each run, Pallas kernels for 29% -> 24%
where the time goes in v3:
time: 525 us; the launch traced here: 518 us
  Pallas kernels  188 us (36%)
  waiting for transfers between devices  113 us (22%)
  other arithmetic  55 us (10%)
  local copies, waits for them, and re-layouts  50.2 us (10%)
  starting transfers between devices  49.6 us (9%)
  matrix products  43.8 us (8%)
  between operations  18.3 us (3%)
    ppermute x50, waiting for transfers between devices, swap(): lax.ppermute(value, BOTH, [(spot, spot ^ mask) for spot in range(total)])  101 us
    pallas_call x6, Pallas kernels, attend_back_call(): pl.pallas_call(attend_back_kernel, grid=(count,), in_specs=[pl.BlockSpec(...  54.6 us
    ppermute x50, starting transfers between devices, swap(): lax.ppermute(value, BOTH, [(spot, spot ^ mask) for spot in range(total)])  49.6 us
    pallas_call x3, Pallas kernels, attend_call(): pl.pallas_call(attend_kernel, grid=(count,), in_specs=[pl.BlockSpec(hot.s...  43.4 us
    pallas_call x1, Pallas kernels, newton_rows(): pl.pallas_call(newton_kernel, out_shape=jax.ShapeDtypeStruct((count, D),...  38.4 us
    pallas_call x1, Pallas kernels, feed_call(): pl.pallas_call(partial(feed_kernel, starts), grid_spec=pltpu.PrefetchScal...  22.7 us
    dot_general x6, matrix products, trans_times(): lax.dot_general(left_side, right_side, (((0,), (0,)), ((), ())), preferre...  20.7 us
    unnamed x241, local copies, waits for them, and re-layouts  19 us
  transfers between devices with their start and end apart: 51, of which 21 were waited for; matrix products, arithmetic and copies ran while one was open for 18% of the time, Pallas kernels for 24%

profile of v3, /device:TPU:0, one launch (start us, length us, event | category | flops | bytes accessed | tf_op | source)
XLA Modules:
  0.0 518.4 jit_solution(18423335780710423535)
XLA Ops:
  9.4 4.1 collective-permute-start
  21.5 2.6 collective-permute-done.2
  25.9 3.0 collective-permute-start.3
  30.7 8.1 %collective-permute-done.3 = f32[1,70,288]{2,1,0:T(8,128)S(1)} collective-permute-done((f32[1,70,288]{2,1,0:T(8,128)S(1)}, f32[1,70,288]{2,1,0:T(8,128)S(1)}, u32[]{:S(2)}, u32[]{:S(2)}) %collective-permute-start.3) | collective-permute-done | bytes 80672 | tf_op jit(solution)/shard_map/ppermute | solution.py:103
  39.1 6.1 %collective-permute-done.4 = f32[2,70,288]{2,1,0:T(8,128)S(1)} collective-permute-done((f32[2,70,288]{2,1,0:T(8,128)S(1)}, f32[2,70,288]{2,1,0:T(8,128)S(1)}, u32[]{:S(2)}, u32[]{:S(2)}) %collective-permute-start.4) | collective-permute-done | bytes 161312 | tf_op jit(solution)/shard_map/ppermute | solution.py:103
  50.3 2.1 multiply_reduce_fusion.12
  52.4 10.8 %collective-permute-done.5 = f32[4,70,288]{2,1,0:T(8,128)} collective-permute-done((f32[4,70,288]{2,1,0:T(8,128)}, f32[4,70,288]{2,1,0:T(8,128)}, u32[]{:S(2)}, u32[]{:S(2)}) %collective-permute-start.5) | collective-permute-done | bytes 322592 | tf_op jit(solution)/shard_map/ppermute | solution.py:103
  65.2 3.3 heads_table.1.tq_ref.tk_ref.tv_ref
  69.8 14.6 %attend.5 = (bf16[912,256]{1,0:T(8,128)(2,1)S(1)}, bf16[912,256]{1,0:T(8,128)(2,1)S(1)}, bf16[912,256]{1,0:T(8,128)(2,1)S(1)}, bf16[912,256]{1,0:T(8,128)(2,1)S(1)}, f32[2,2,1024]{2,1,0:T(2,128)S(1)}) custom-call(bf16[912,256]{1,0:T(8,128)(2,1)S(1)} %compare_convert_fusion.hot_ref, bf16[256,2304]{1,0:T(8,128)(2,1)S(1)} %copy-done.2, ...), custom_call_target="tpu_custom_call" | custom-call | flops 2097152 | bytes 65536 | tf_op jit(solution)/shard_map/attend/pallas_call | solution.py:637
  84.4 14.4 %attend.4 = (bf16[912,256]{1,0:T(8,128)(2,1)S(1)}, bf16[912,256]{1,0:T(8,128)(2,1)S(1)}, bf16[912,256]{1,0:T(8,128)(2,1)S(1)}, bf16[912,256]{1,0:T(8,128)(2,1)S(1)}, f32[2,2,1024]{2,1,0:T(2,128)S(1)}) custom-call(bf16[912,256]{1,0:T(8,128)(2,1)S(1)} %compare_convert_fusion.hot_ref, bf16[256,2304]{1,0:T(8,128)(2,1)S(1)} %copy-done.2, ...), custom_call_target="tpu_custom_call" | custom-call | flops 2097152 | bytes 65536 | tf_op jit(solution)/shard_map/attend/pallas_call | solution.py:637
  98.9 14.4 %attend.3 = (bf16[912,256]{1,0:T(8,128)(2,1)S(1)}, bf16[912,256]{1,0:T(8,128)(2,1)S(1)}, bf16[912,256]{1,0:T(8,128)(2,1)S(1)}, bf16[912,256]{1,0:T(8,128)(2,1)S(1)}, f32[2,2,1024]{2,1,0:T(2,128)S(1)}) custom-call(bf16[912,256]{1,0:T(8,128)(2,1)S(1)} %compare_convert_fusion.hot_ref, bf16[256,2304]{1,0:T(8,128)(2,1)S(1)} %copy-done.2, ...), custom_call_target="tpu_custom_call" | custom-call | flops 2097152 | bytes 65536 | tf_op jit(solution)/shard_map/attend/pallas_call | solution.py:637
  114.5 11.9 %all-gather.3.cloned.1.call-done = bf16[9728,768]{1,0:T(8,128)(2,1)} async-done(((bf16[304,768]{1,0:T(8,128)(2,1)}), bf16[9728,768]{1,0:T(8,128)(2,1)}) %all-gather.3.cloned.1.call-update) | async-done | bytes 14942224 | tf_op jit(solution)/shard_map/all_gather | solution.py:969
  127.7 4.1 fusion.85
  132.9 22.7 %feed.1 = (bf16[912,3072]{1,0:T(8,128)(2,1)}, bf16[912,3072]{1,0:T(8,128)(2,1)}, f32[912,768]{1,0:T(8,128)S(1)}) custom-call(s32[32]{0:T(128)S(1)} %broadcast_xor_fusion.place_ref, bf16[912,768]{1,0:T(8,128)(2,1)S(1)} %add_convert_fusion.1.rows_ref, f32[1,3072]{1,0:T(1,128)S(1)} %broadcast_in_dim_reshape.2.bias_ref, bf16[32,304,768]{2,1,0:T(8,128)(2,1)} %bitcast.284), custom_call_target="tpu_custom_call" | custom-call | flops 2151677952 | bytes 65536 | tf_op jit(solution)/shard_map/feed/pallas_call | solution.py:832
  159.6 2.6 convert_reduce_fusion
  162.1 4.5 convolution_convert_fusion.1
  166.9 4.6 collective-permute-done.6
  171.5 5.3 %convert_add_fusion.1 = f32[1536,768]{1,0:T(8,128)S(1)} fusion(bf16[1536,768]{1,0:T(8,128)(2,1)} %collective-permute-done.6, bf16[912,768]{1,0:T(8,128)(2,1)S(1)} %get-tuple-element.109.grad_ref, bf16[912,3072]{1,0:T(8,128)(2,1)} %get-tuple-element.108), kind=kOutput, calls=%fused_computation.6 | convolution fusion | flops 2154037248 | bytes 11280384 | tf_op jit(solution)/shard_map/dot_general | solution.py:49
  181.0 17.9 %feed_back.1 = (bf16[912,3072]{1,0:T(8,128)(2,1)}, f32[912,768]{1,0:T(8,128)S(1)}, f32[1,3072]{1,0:T(1,128)S(1)}) custom-call(s32[32]{0:T(128)S(1)} %broadcast_xor_fusion.place_ref, bf16[912,768]{1,0:T(8,128)(2,1)S(1)} %get-tuple-element.109.grad_ref, bf16[912,3072]{1,0:T(8,128)(2,1)} %get-tuple-element.110.slope_ref, bf16[32,304,768]{2,1,0:T(8,128)(2,1)} %bitcast.285), custom_call_target="tpu_custom_call" | custom-call | flops 2151677952 | bytes 65536 | tf_op jit(solution)/shard_map/feed_back/pallas_call | solution.py:888
  205.5 4.0 convolution_convert_fusion
  215.1 2.5 multiply_reduce_fusion.4
  222.0 5.2 convert_add_fusion
  235.0 9.0 %attend_back.6 = (bf16[3,912,128]{2,1,0:T(8,128)(2,1)S(1)}, f32[3,128,128]{2,1,0:T(8,128)S(1)}) custom-call(bf16[128,912]{1,0:T(8,128)(2,1)S(1)} %compare_convert_fusion.1.hot_ref, bf16[912,256]{1,0:T(8,128)(2,1)S(1)} %copy-done.18, bf16[912,256]{1,0:T(8,128)(2,1)S(1)} %copy-done.20, bf16[912,256]{1,0:T(8,128)(2,1)S(1)} %copy-done.22, ...), custom_call_target="tpu_custom_call" | custom-call | flops 1048576 | bytes 65536 | tf_op jit(solution)/shard_map/attend_back/pallas_call | solution.py:729
  244.0 9.2 %attend_back.7 = (bf16[3,912,128]{2,1,0:T(8,128)(2,1)S(1)}, f32[3,128,128]{2,1,0:T(8,128)S(1)}) custom-call(bf16[128,912]{1,0:T(8,128)(2,1)S(1)} %compare_convert_fusion.1.hot_ref, bf16[912,256]{1,0:T(8,128)(2,1)S(1)} %copy-done.18, bf16[912,256]{1,0:T(8,128)(2,1)S(1)} %copy-done.20, bf16[912,256]{1,0:T(8,128)(2,1)S(1)} %copy-done.22, ...), custom_call_target="tpu_custom_call" | custom-call | flops 1048576 | bytes 65536 | tf_op jit(solution)/shard_map/attend_back/pallas_call | solution.py:729
  264.5 9.0 %attend_back.8 = (bf16[3,912,128]{2,1,0:T(8,128)(2,1)S(1)}, f32[3,128,128]{2,1,0:T(8,128)S(1)}) custom-call(bf16[128,912]{1,0:T(8,128)(2,1)S(1)} %compare_convert_fusion.1.hot_ref, bf16[912,256]{1,0:T(8,128)(2,1)S(1)} %copy-done.12, bf16[912,256]{1,0:T(8,128)(2,1)S(1)} %copy-done.14, bf16[912,256]{1,0:T(8,128)(2,1)S(1)} %copy-done.16, ...), custom_call_target="tpu_custom_call" | custom-call | flops 1048576 | bytes 65536 | tf_op jit(solution)/shard_map/attend_back/pallas_call | solution.py:729
  276.6 9.0 %attend_back.9 = (bf16[3,912,128]{2,1,0:T(8,128)(2,1)S(1)}, f32[3,128,128]{2,1,0:T(8,128)S(1)}) custom-call(bf16[128,912]{1,0:T(8,128)(2,1)S(1)} %compare_convert_fusion.1.hot_ref, bf16[912,256]{1,0:T(8,128)(2,1)S(1)} %copy-done.12, bf16[912,256]{1,0:T(8,128)(2,1)S(1)} %copy-done.14, bf16[912,256]{1,0:T(8,128)(2,1)S(1)} %copy-done.16, ...), custom_call_target="tpu_custom_call" | custom-call | flops 1048576 | bytes 65536 | tf_op jit(solution)/shard_map/attend_back/pallas_call | solution.py:729
  285.7 9.0 %attend_back.10 = (bf16[3,912,128]{2,1,0:T(8,128)(2,1)S(1)}, f32[3,128,128]{2,1,0:T(8,128)S(1)}) custom-call(bf16[128,912]{1,0:T(8,128)(2,1)S(1)} %compare_convert_fusion.1.hot_ref, bf16[912,256]{1,0:T(8,128)(2,1)S(1)} %get-tuple-element.142.q_ref, bf16[912,256]{1,0:T(8,128)(2,1)S(1)} %get-tuple-element.143.k_ref, bf16[912,256]{1,0:T(8,128)(2,1)S(1)} %copy-done.10, ...), custom_call_target="tpu_custom_call" | custom-call | flops 1048576 | bytes 65536 | tf_op jit(solution)/shard_map/attend_back/pallas_call | solution.py:729
  297.3 9.4 %attend_back.11 = (bf16[3,912,128]{2,1,0:T(8,128)(2,1)S(1)}, f32[3,128,128]{2,1,0:T(8,128)S(1)}) custom-call(bf16[128,912]{1,0:T(8,128)(2,1)S(1)} %compare_convert_fusion.1.hot_ref, bf16[912,256]{1,0:T(8,128)(2,1)S(1)} %get-tuple-element.142.q_ref, bf16[912,256]{1,0:T(8,128)(2,1)S(1)} %get-tuple-element.143.k_ref, bf16[912,256]{1,0:T(8,128)(2,1)S(1)} %copy-done.10, ...), custom_call_target="tpu_custom_call" | custom-call | flops 1048576 | bytes 65536 | tf_op jit(solution)/shard_map/attend_back/pallas_call | solution.py:729
  308.3 2.5 token_sums.1
  310.8 2.3 copy.100
  324.1 2.4 slice.372
  326.9 4.0 multiply_reduce_fusion.2
  339.3 2.7 maximum_select_fusion.2
  351.4 4.7 collective-permute-done.21
  359.5 6.6 %collective-permute-done.22 = f32[70,288]{0,1:T(8,128)S(1)} collective-permute-done((f32[70,288]{0,1:T(8,128)S(1)}, f32[70,288]{0,1:T(8,128)S(1)}, u32[]{:S(2)}, u32[]{:S(2)}) %collective-permute-start.22) | collective-permute-done | bytes 80672 | tf_op jit(solution)/shard_map/ppermute | solution.py:103
  367.4 4.4 collective-permute-done.23
  375.9 2.1 maximum_select_fusion
  391.4 8.9 %collective-permute-done.39 = f32[384,256]{1,0:T(8,128)S(1)} collective-permute-done((f32[384,256]{1,0:T(8,128)S(1)}, f32[384,256]{1,0:T(8,128)S(1)}, u32[]{:S(2)}, u32[]{:S(2)}) %collective-permute-start.39) | collective-permute-done | bytes 393248 | tf_op jit(solution)/shard_map/ppermute | solution.py:103
  401.5 4.7 collective-permute-done.40
  406.2 2.5 collective-permute-done.34
  409.3 7.3 %collective-permute-done.41 = f32[96,256]{1,0:T(8,128)S(1)} collective-permute-done((f32[96,256]{1,0:T(8,128)S(1)}, f32[96,256]{1,0:T(8,128)S(1)}, u32[]{:S(2)}, u32[]{:S(2)}) %collective-permute-start.41) | collective-permute-done | bytes 98336 | tf_op jit(solution)/shard_map/ppermute | solution.py:103
  419.7 7.4 %collective-permute-done.42 = f32[96,256]{1,0:T(8,128)S(1)} collective-permute-done((f32[96,256]{1,0:T(8,128)S(1)}, f32[96,256]{1,0:T(8,128)S(1)}, u32[]{:S(2)}, u32[]{:S(2)}) %collective-permute-start.42) | collective-permute-done | bytes 98336 | tf_op jit(solution)/shard_map/ppermute | solution.py:103
  428.1 3.0 collective-permute-start.47
  434.8 5.7 %collective-permute-done.37 = f32[192,256]{1,0:T(8,128)S(1)} collective-permute-done((f32[192,256]{1,0:T(8,128)S(1)}, f32[192,256]{1,0:T(8,128)S(1)}, u32[]{:S(2)}, u32[]{:S(2)}) %collective-permute-start.37) | collective-permute-done | bytes 196640 | tf_op jit(solution)/shard_map/ppermute | solution.py:103
  444.4 3.5 concatenate.225
  450.5 38.4 %newton.1 = bf16[384,768]{1,0:T(8,128)(2,1)S(1)} custom-call(f32[768,256]{1,0:T(8,128)S(1)} %maximum_select_fusion.3.low_ref, f32[768,256]{1,0:T(8,128)S(1)} %maximum_select_fusion.4.high_ref, f32[384,768]{1,0:T(8,128)S(1)} %get-tuple-element.174.rows_ref, bf16[432,768]{1,0:T(8,128)(2,1)S(1)} %pad.27.add_left_ref, bf16[432,768]{1,0:T(8,128)(2,1)S(1)} %pad.28.add_right_ref), custom_call_target="tpu_custom_call" | custom-call | flops 27179089920 | bytes 4194304 | tf_op jit(solution)/shard_map/newton/pallas_call | solution.py:412
  489.6 11.8 %collective-permute-done.48 = bf16[384,768]{1,0:T(8,128)(2,1)S(1)} collective-permute-done((bf16[384,768]{1,0:T(8,128)(2,1)S(1)}, bf16[384,768]{1,0:T(8,128)(2,1)S(1)}, u32[]{:S(2)}, u32[]{:S(2)}) %collective-permute-start.48) | collective-permute-done | bytes 589856 | tf_op jit(solution)/shard_map/ppermute | solution.py:103
  507.7 3.5 update.1
  (555 shorter events, 148.4 us)
Async XLA Ops:
  7.3 119.1 %all-gather.3.cloned.1.call-start = ((), (), s32[]{:S(2)}) async-start(), calls=%async_computation | async-start | bytes 15409152 | tf_op jit(solution)/shard_map/all_gather | solution.py:969
  9.4 5.9 %collective-permute-start = (bf16[1,85,96]{2,1,0:T(8,128)(2,1)S(1)}, bf16[1,85,96]{2,1,0:T(8,128)(2,1)S(1)}, u32[]{:S(2)}, u32[]{:S(2)}) collective-permute-start(bf16[1,85,96]{2,1,0:T(8,128)(2,1)S(1)} %pad_maximum_fusion.21), channel_id=1, source_target_pairs={{0,16},{1,17},{2,18},{3,19},{4,20},{5,21},{6,22},{7,23},{8,24},{9,... | collective-permute-start | bytes 48968 | tf_op jit(solution)/shard_map/ppermute | solution.py:103
  25.9 12.9 %collective-permute-start.3 = (f32[1,70,288]{2,1,0:T(8,128)S(1)}, f32[1,70,288]{2,1,0:T(8,128)S(1)}, u32[]{:S(2)}, u32[]{:S(2)}) collective-permute-start(f32[1,70,288]{2,1,0:T(8,128)S(1)} %convolution_bitcast_fusion), channel_id=1, source_target_pairs={{0,16},{1,17},{2,18},{3,19},{4,20},{5,21},{6,22},{7,23},{8,24},{9,... | collective-permute-start | bytes 241928 | tf_op jit(solution)/shard_map/ppermute | solution.py:103
  38.8 6.4 %collective-permute-start.4 = (f32[2,70,288]{2,1,0:T(8,128)S(1)}, f32[2,70,288]{2,1,0:T(8,128)S(1)}, u32[]{:S(2)}, u32[]{:S(2)}) collective-permute-start(f32[2,70,288]{2,1,0:T(8,128)S(1)} %pad_maximum_fusion.16), channel_id=1, source_target_pairs={{0,8},{1,9},{2,10},{3,11},{4,12},{5,13},{6,14},{7,15},{8,0},{9,1},... | collective-permute-start | bytes 483848 | tf_op jit(solution)/shard_map/ppermute | solution.py:103
  46.1 17.1 %collective-permute-start.5 = (f32[4,70,288]{2,1,0:T(8,128)}, f32[4,70,288]{2,1,0:T(8,128)}, u32[]{:S(2)}, u32[]{:S(2)}) collective-permute-start(f32[4,70,288]{2,1,0:T(8,128)} %pad_maximum_fusion.11), channel_id=1, source_target_pairs={{0,4},{1,5},{2,6},{3,7},{4,0},{5,1},{6,2},{7,3},{8,12},{9,13},{10,... | collective-permute-start | bytes 967688 | tf_op jit(solution)/shard_map/ppermute | solution.py:103
  166.6 4.9 collective-permute-start.6
  178.9 21.3 %collective-permute-start.7 = (bf16[768,384]{1,0:T(8,128)(2,1)}, bf16[768,384]{1,0:T(8,128)(2,1)}, u32[]{:S(2)}, u32[]{:S(2)}) collective-permute-start(bf16[768,384]{1,0:T(8,128)(2,1)} %bitcast.15), channel_id=1, source_target_pairs={{0,4},{1,5},{2,6},{3,7},{4,0},{5,1},{6,2},{7,3},{8,12},{9,13},{10,... | collective-permute-start | bytes 1769480 | tf_op jit(solution)/shard_map/ppermute | solution.py:103
  180.4 19.8 %collective-permute-start.8 = (bf16[768,384]{1,0:T(8,128)(2,1)}, bf16[768,384]{1,0:T(8,128)(2,1)S(1)}, u32[]{:S(2)}, u32[]{:S(2)}) collective-permute-start(bf16[768,384]{1,0:T(8,128)(2,1)} %bitcast.16), channel_id=1, source_target_pairs={{0,2},{1,3},{2,0},{3,1},{4,6},{5,7},{6,4},{7,5},{8,10},{9,11},{10,... | collective-permute-start | bytes 1769480 | tf_op jit(solution)/shard_map/ppermute | solution.py:103
  209.5 12.5 %collective-permute-start.9 = (bf16[1536,768]{1,0:T(8,128)(2,1)}, bf16[1536,768]{1,0:T(8,128)(2,1)}, u32[]{:S(2)}, u32[]{:S(2)}) collective-permute-start(bf16[1536,768]{1,0:T(8,128)(2,1)} %convolution_convert_fusion), channel_id=1, source_target_pairs={{0,1},{1,0},{2,3},{3,2},{4,5},{5,4},{6,7},{7,6},{8,9},{9,8},{10,11... | collective-permute-start | bytes 7077896 | tf_op jit(solution)/shard_map/ppermute | solution.py:103
  214.7 5.1 collective-permute-start.10
  217.6 10.1 %collective-permute-start.12 = (bf16[384,384]{1,0:T(8,128)(2,1)}, bf16[384,384]{1,0:T(8,128)(2,1)S(1)}, u32[]{:S(2)}, u32[]{:S(2)}) collective-permute-start(bf16[384,384]{1,0:T(8,128)(2,1)} %bitcast.347), channel_id=1, source_target_pairs={{0,4},{1,5},{2,6},{3,7},{4,0},{5,1},{6,2},{7,3},{8,12},{9,13},{10,... | collective-permute-start | bytes 884744 | tf_op jit(solution)/shard_map/ppermute | solution.py:103
  219.1 9.5 %collective-permute-start.11 = (bf16[384,384]{1,0:T(8,128)(2,1)S(1)}, bf16[384,384]{1,0:T(8,128)(2,1)S(1)}, u32[]{:S(2)}, u32[]{:S(2)}) collective-permute-start(bf16[384,384]{1,0:T(8,128)(2,1)S(1)} %bitcast.346), channel_id=1, source_target_pairs={{0,2},{1,3},{2,0},{3,1},{4,6},{5,7},{6,4},{7,5},{8,10},{9,11},{10,... | collective-permute-start | bytes 884744 | tf_op jit(solution)/shard_map/ppermute | solution.py:103
  229.1 24.2 %collective-permute-start.14 = (bf16[960,384]{1,0:T(8,128)(2,1)S(1)}, bf16[960,384]{1,0:T(8,128)(2,1)}, u32[]{:S(2)}, u32[]{:S(2)}) collective-permute-start(bf16[960,384]{1,0:T(8,128)(2,1)S(1)} %pad_maximum_fusion.5), channel_id=1, source_target_pairs={{0,2},{1,3},{2,0},{3,1},{4,6},{5,7},{6,4},{7,5},{8,10},{9,11},{10,... | collective-permute-start | bytes 2211848 | tf_op jit(solution)/shard_map/ppermute | solution.py:103
  231.5 24.0 %collective-permute-start.13 = (bf16[960,384]{1,0:T(8,128)(2,1)}, bf16[960,384]{1,0:T(8,128)(2,1)}, u32[]{:S(2)}, u32[]{:S(2)}) collective-permute-start(bf16[960,384]{1,0:T(8,128)(2,1)} %pad_maximum_fusion.4), channel_id=1, source_target_pairs={{0,4},{1,5},{2,6},{3,7},{4,0},{5,1},{6,2},{7,3},{8,12},{9,13},{10,... | collective-permute-start | bytes 2211848 | tf_op jit(solution)/shard_map/ppermute | solution.py:103
  233.0 20.3 %collective-permute-start.15 = (f32[192,768]{1,0:T(8,128)}, f32[192,768]{1,0:T(8,128)}, u32[]{:S(2)}, u32[]{:S(2)}) collective-permute-start(f32[192,768]{1,0:T(8,128)} %bitcast.36), channel_id=1, source_target_pairs={{0,8},{1,9},{2,10},{3,11},{4,12},{5,13},{6,14},{7,15},{8,0},{9,1},... | collective-permute-start | bytes 1769480 | tf_op jit(solution)/shard_map/ppermute | solution.py:103
  259.6 13.9 %collective-permute-start.17 = (bf16[480,384]{1,0:T(8,128)(2,1)S(1)}, bf16[480,384]{1,0:T(8,128)(2,1)S(1)}, u32[]{:S(2)}, u32[]{:S(2)}) collective-permute-start(bf16[480,384]{1,0:T(8,128)(2,1)S(1)} %pad_maximum_fusion.13), channel_id=1, source_target_pairs={{0,4},{1,5},{2,6},{3,7},{4,0},{5,1},{6,2},{7,3},{8,12},{9,13},{10,... | collective-permute-start | bytes 1105928 | tf_op jit(solution)/shard_map/ppermute | solution.py:103
  261.1 12.5 %collective-permute-start.16 = (bf16[480,384]{1,0:T(8,128)(2,1)S(1)}, bf16[480,384]{1,0:T(8,128)(2,1)S(1)}, u32[]{:S(2)}, u32[]{:S(2)}) collective-permute-start(bf16[480,384]{1,0:T(8,128)(2,1)S(1)} %pad_maximum_fusion.12), channel_id=1, source_target_pairs={{0,2},{1,3},{2,0},{3,1},{4,6},{5,7},{6,4},{7,5},{8,10},{9,11},{10,... | collective-permute-start | bytes 1105928 | tf_op jit(solution)/shard_map/ppermute | solution.py:103
  263.0 22.7 %collective-permute-start.24 = (f32[96,768]{1,0:T(8,128)S(1)}, f32[96,768]{1,0:T(8,128)S(1)}, u32[]{:S(2)}, u32[]{:S(2)}) collective-permute-start(f32[96,768]{1,0:T(8,128)S(1)} %slice_bitcast_fusion.10), channel_id=1, source_target_pairs={{0,16},{1,17},{2,18},{3,19},{4,20},{5,21},{6,22},{7,23},{8,24},{9,... | collective-permute-start | bytes 884744 | tf_op jit(solution)/shard_map/ppermute | solution.py:103
  274.9 19.9 %collective-permute-start.18 = (bf16[240,768]{1,0:T(8,128)(2,1)S(1)}, bf16[240,768]{1,0:T(8,128)(2,1)S(1)}, u32[]{:S(2)}, u32[]{:S(2)}) collective-permute-start(bf16[240,768]{1,0:T(8,128)(2,1)S(1)} %pad_maximum_fusion.14), channel_id=1, source_target_pairs={{0,8},{1,9},{2,10},{3,11},{4,12},{5,13},{6,14},{7,15},{8,0},{9,1},... | collective-permute-start | bytes 1105928 | tf_op jit(solution)/shard_map/ppermute | solution.py:103
  295.9 19.1 %collective-permute-start.25 = (bf16[120,768]{1,0:T(8,128)(2,1)}, bf16[120,768]{1,0:T(8,128)(2,1)}, u32[]{:S(2)}, u32[]{:S(2)}) collective-permute-start(bf16[120,768]{1,0:T(8,128)(2,1)} %pad_maximum_fusion.17), channel_id=1, source_target_pairs={{0,16},{1,17},{2,18},{3,19},{4,20},{5,21},{6,22},{7,23},{8,24},{9,... | collective-permute-start | bytes 552968 | tf_op jit(solution)/shard_map/ppermute | solution.py:103
  313.1 6.6 %collective-permute-start.19 = (f32[8,70,288]{2,0,1:T(8,128)}, f32[8,70,288]{2,0,1:T(8,128)}, u32[]{:S(2)}, u32[]{:S(2)}) collective-permute-start(f32[8,70,288]{2,0,1:T(8,128)} %copy.100), channel_id=1, source_target_pairs={{0,1},{1,0},{2,3},{3,2},{4,5},{5,4},{6,7},{7,6},{8,9},{9,8},{10,11... | collective-permute-start | bytes 1935368 | tf_op jit(solution)/shard_map/ppermute | solution.py:103
  318.3 21.1 %collective-permute-start.26 = (f32[216,768]{1,0:T(8,128)}, f32[216,768]{1,0:T(8,128)}, u32[]{:S(2)}, u32[]{:S(2)}) collective-permute-start(f32[216,768]{1,0:T(8,128)} %get-tuple-element.245), channel_id=1, source_target_pairs={{0,2},{1,3},{2,0},{3,1},{4,6},{5,7},{6,4},{7,5},{8,10},{9,11},{10,... | collective-permute-start | bytes 1990664 | tf_op jit(solution)/shard_map/ppermute | solution.py:103
  322.0 22.1 %collective-permute-start.20 = (f32[2,2,70,288]{3,2,1,0:T(8,128)}, f32[2,2,70,288]{3,2,1,0:T(8,128)}, u32[]{:S(2)}, u32[]{:S(2)}) collective-permute-start(f32[2,2,70,288]{3,2,1,0:T(8,128)} %dynamic-slice_bitcast_fusion), channel_id=1, source_target_pairs={{0,4},{1,5},{2,6},{3,7},{4,0},{5,1},{6,2},{7,3},{8,12},{9,13},{10,... | collective-permute-start | bytes 967688 | tf_op jit(solution)/shard_map/ppermute | solution.py:103
  339.3 8.0 %collective-permute-start.28 = (f32[8,86,96]{2,1,0:T(8,128)}, f32[8,86,96]{2,1,0:T(8,128)}, u32[]{:S(2)}, u32[]{:S(2)}) collective-permute-start(f32[8,86,96]{2,1,0:T(8,128)} %pad_maximum_fusion.15), channel_id=1, source_target_pairs={{0,1},{1,0},{2,3},{3,2},{4,5},{5,4},{6,7},{7,6},{8,9},{9,8},{10,11... | collective-permute-start | bytes 792584 | tf_op jit(solution)/shard_map/ppermute | solution.py:103
  342.0 33.9 %collective-permute-start.27 = (f32[2,216,768]{2,1,0:T(8,128)}, f32[2,216,768]{2,1,0:T(8,128)}, u32[]{:S(2)}, u32[]{:S(2)}) collective-permute-start(f32[2,216,768]{2,1,0:T(8,128)} %maximum_select_fusion.2), channel_id=1, source_target_pairs={{0,1},{1,0},{2,3},{3,2},{4,5},{5,4},{6,7},{7,6},{8,9},{9,8},{10,11... | collective-permute-start | bytes 3981320 | tf_op jit(solution)/shard_map/ppermute | solution.py:103
  346.8 9.2 %collective-permute-start.21 = (f32[2,70,288]{1,2,0:T(8,128)}, f32[2,70,288]{1,2,0:T(8,128)}, u32[]{:S(2)}, u32[]{:S(2)}) collective-permute-start(f32[2,70,288]{1,2,0:T(8,128)} %bitcast.92), channel_id=1, source_target_pairs={{0,8},{1,9},{2,10},{3,11},{4,12},{5,13},{6,14},{7,15},{8,0},{9,1},... | collective-permute-start | bytes 483848 | tf_op jit(solution)/shard_map/ppermute | solution.py:103
  349.1 9.5 %collective-permute-start.29 = (f32[2,2,86,96]{3,2,1,0:T(8,128)}, f32[2,2,86,96]{3,2,1,0:T(8,128)}, u32[]{:S(2)}, u32[]{:S(2)}) collective-permute-start(f32[2,2,86,96]{3,2,1,0:T(8,128)} %dynamic-slice_bitcast_fusion.5), channel_id=1, source_target_pairs={{0,4},{1,5},{2,6},{3,7},{4,0},{5,1},{6,2},{7,3},{8,12},{9,13},{10,... | collective-permute-start | bytes 396296 | tf_op jit(solution)/shard_map/ppermute | solution.py:103
  357.1 9.0 %collective-permute-start.22 = (f32[70,288]{0,1:T(8,128)S(1)}, f32[70,288]{0,1:T(8,128)S(1)}, u32[]{:S(2)}, u32[]{:S(2)}) collective-permute-start(f32[70,288]{0,1:T(8,128)S(1)} %dynamic-slice_bitcast_fusion.6), channel_id=1, source_target_pairs={{0,16},{1,17},{2,18},{3,19},{4,20},{5,21},{6,22},{7,23},{8,24},{9,... | collective-permute-start | bytes 241928 | tf_op jit(solution)/shard_map/ppermute | solution.py:103
  366.1 5.7 %collective-permute-start.23 = (f32[70,288]{0,1:T(8,128)S(1)}, f32[70,288]{0,1:T(8,128)S(1)}, u32[]{:S(2)}, u32[]{:S(2)}) collective-permute-start(f32[70,288]{0,1:T(8,128)S(1)} %bitcast_add_fusion.8), channel_id=1, source_target_pairs={{0,2},{1,3},{2,0},{3,1},{4,6},{5,7},{6,4},{7,5},{8,10},{9,11},{10,... | collective-permute-start | bytes 241928 | tf_op jit(solution)/shard_map/ppermute | solution.py:103
  367.4 21.8 %collective-permute-start.30 = (f32[2,86,96]{2,1,0:T(8,128)S(1)}, f32[2,86,96]{2,1,0:T(8,128)S(1)}, u32[]{:S(2)}, u32[]{:S(2)}) collective-permute-start(f32[2,86,96]{2,1,0:T(8,128)S(1)} %dynamic-slice_bitcast_fusion.9), channel_id=1, source_target_pairs={{0,8},{1,9},{2,10},{3,11},{4,12},{5,13},{6,14},{7,15},{8,0},{9,1},... | collective-permute-start | bytes 198152 | tf_op jit(solution)/shard_map/ppermute | solution.py:103
  372.7 16.6 %collective-permute-start.45 = (f32[70,838]{1,0:T(8,128)S(1)}, f32[70,838]{1,0:T(8,128)S(1)}, u32[]{:S(2)}, u32[]{:S(2)}) collective-permute-start(f32[70,838]{1,0:T(8,128)S(1)} %fusion.14), channel_id=1, source_target_pairs={{0,4},{1,5},{2,6},{3,7},{4,0},{5,1},{6,2},{7,3},{8,12},{9,13},{10,... | collective-permute-start | bytes 703928 | tf_op jit(solution)/shard_map/ppermute | solution.py:103
  388.2 12.1 %collective-permute-start.39 = (f32[384,256]{1,0:T(8,128)S(1)}, f32[384,256]{1,0:T(8,128)S(1)}, u32[]{:S(2)}, u32[]{:S(2)}) collective-permute-start(f32[384,256]{1,0:T(8,128)S(1)} %dynamic-slice_bitcast_fusion.1), channel_id=1, source_target_pairs={{0,8},{1,9},{2,10},{3,11},{4,12},{5,13},{6,14},{7,15},{8,0},{9,1},... | collective-permute-start | bytes 1179656 | tf_op jit(solution)/shard_map/ppermute | solution.py:103
  388.4 12.9 %collective-permute-start.33 = (f32[384,256]{1,0:T(8,128)S(1)}, f32[384,256]{1,0:T(8,128)S(1)}, u32[]{:S(2)}, u32[]{:S(2)}) collective-permute-start(f32[384,256]{1,0:T(8,128)S(1)} %dynamic-slice_bitcast_fusion.2), channel_id=1, source_target_pairs={{0,4},{1,5},{2,6},{3,7},{4,0},{5,1},{6,2},{7,3},{8,12},{9,13},{10,... | collective-permute-start | bytes 1179656 | tf_op jit(solution)/shard_map/ppermute | solution.py:103
  389.3 38.7 %collective-permute-start.46 = (f32[70,838]{1,0:T(8,128)S(1)}, f32[70,838]{1,0:T(8,128)S(1)}, u32[]{:S(2)}, u32[]{:S(2)}) collective-permute-start(f32[70,838]{1,0:T(8,128)S(1)} %add.571), channel_id=1, source_target_pairs={{0,8},{1,9},{2,10},{3,11},{4,12},{5,13},{6,14},{7,15},{8,0},{9,1},... | collective-permute-start | bytes 703928 | tf_op jit(solution)/shard_map/ppermute | solution.py:103
  400.4 5.7 %collective-permute-start.40 = (f32[192,256]{1,0:T(8,128)S(1)}, f32[192,256]{1,0:T(8,128)S(1)}, u32[]{:S(2)}, u32[]{:S(2)}) collective-permute-start(f32[192,256]{1,0:T(8,128)S(1)} %dynamic-slice_bitcast_fusion.3), channel_id=1, source_target_pairs={{0,4},{1,5},{2,6},{3,7},{4,0},{5,1},{6,2},{7,3},{8,12},{9,13},{10,... | collective-permute-start | bytes 589832 | tf_op jit(solution)/shard_map/ppermute | solution.py:103
  401.4 7.4 %collective-permute-start.34 = (f32[192,256]{1,0:T(8,128)S(1)}, f32[192,256]{1,0:T(8,128)S(1)}, u32[]{:S(2)}, u32[]{:S(2)}) collective-permute-start(f32[192,256]{1,0:T(8,128)S(1)} %dynamic-slice_bitcast_fusion.4), channel_id=1, source_target_pairs={{0,8},{1,9},{2,10},{3,11},{4,12},{5,13},{6,14},{7,15},{8,0},{9,1},... | collective-permute-start | bytes 589832 | tf_op jit(solution)/shard_map/ppermute | solution.py:103
  406.2 10.4 %collective-permute-start.41 = (f32[96,256]{1,0:T(8,128)S(1)}, f32[96,256]{1,0:T(8,128)S(1)}, u32[]{:S(2)}, u32[]{:S(2)}) collective-permute-start(f32[96,256]{1,0:T(8,128)S(1)} %dynamic-slice_bitcast_fusion.7), channel_id=1, source_target_pairs={{0,16},{1,17},{2,18},{3,19},{4,20},{5,21},{6,22},{7,23},{8,24},{9,... | collective-permute-start | bytes 294920 | tf_op jit(solution)/shard_map/ppermute | solution.py:103
  408.8 9.8 %collective-permute-start.35 = (f32[96,256]{1,0:T(8,128)S(1)}, f32[96,256]{1,0:T(8,128)S(1)}, u32[]{:S(2)}, u32[]{:S(2)}) collective-permute-start(f32[96,256]{1,0:T(8,128)S(1)} %dynamic-slice_bitcast_fusion.8), channel_id=1, source_target_pairs={{0,16},{1,17},{2,18},{3,19},{4,20},{5,21},{6,22},{7,23},{8,24},{9,... | collective-permute-start | bytes 294920 | tf_op jit(solution)/shard_map/ppermute | solution.py:103
  416.6 10.4 %collective-permute-start.42 = (f32[96,256]{1,0:T(8,128)S(1)}, f32[96,256]{1,0:T(8,128)S(1)}, u32[]{:S(2)}, u32[]{:S(2)}) collective-permute-start(f32[96,256]{1,0:T(8,128)S(1)} %bitcast_add_fusion.9), channel_id=1, source_target_pairs={{0,16},{1,17},{2,18},{3,19},{4,20},{5,21},{6,22},{7,23},{8,24},{9,... | collective-permute-start | bytes 294920 | tf_op jit(solution)/shard_map/ppermute | solution.py:103
  418.7 12.4 %collective-permute-start.36 = (f32[96,256]{1,0:T(8,128)S(1)}, f32[96,256]{1,0:T(8,128)S(1)}, u32[]{:S(2)}, u32[]{:S(2)}) collective-permute-start(f32[96,256]{1,0:T(8,128)S(1)} %bitcast_add_fusion.10), channel_id=1, source_target_pairs={{0,16},{1,17},{2,18},{3,19},{4,20},{5,21},{6,22},{7,23},{8,24},{9,... | collective-permute-start | bytes 294920 | tf_op jit(solution)/shard_map/ppermute | solution.py:103
  427.1 5.7 %collective-permute-start.43 = (f32[192,256]{1,0:T(8,128)S(1)}, f32[192,256]{1,0:T(8,128)S(1)}, u32[]{:S(2)}, u32[]{:S(2)}) collective-permute-start(f32[192,256]{1,0:T(8,128)S(1)} %maximum_select_fusion.8), channel_id=1, source_target_pairs={{0,4},{1,5},{2,6},{3,7},{4,0},{5,1},{6,2},{7,3},{8,12},{9,13},{10,... | collective-permute-start | bytes 589832 | tf_op jit(solution)/shard_map/ppermute | solution.py:103
  428.0 5.4 %collective-permute-start.31 = (f32[86,96]{1,0:T(8,128)S(1)}, f32[86,96]{1,0:T(8,128)S(1)}, u32[]{:S(2)}, u32[]{:S(2)}) collective-permute-start(f32[86,96]{1,0:T(8,128)S(1)} %dynamic-slice_bitcast_fusion.10), channel_id=1, source_target_pairs={{0,16},{1,17},{2,18},{3,19},{4,20},{5,21},{6,22},{7,23},{8,24},{9,... | collective-permute-start | bytes 99080 | tf_op jit(solution)/shard_map/ppermute | solution.py:103
  428.1 14.4 %collective-permute-start.47 = (f32[70,838]{1,0:T(8,128)S(1)}, f32[70,838]{1,0:T(8,128)S(1)}, u32[]{:S(2)}, u32[]{:S(2)}) collective-permute-start(f32[70,838]{1,0:T(8,128)S(1)} %add.572), channel_id=1, source_target_pairs={{0,16},{1,17},{2,18},{3,19},{4,20},{5,21},{6,22},{7,23},{8,24},{9,... | collective-permute-start | bytes 703928 | tf_op jit(solution)/shard_map/ppermute | solution.py:103
  431.1 9.5 %collective-permute-start.37 = (f32[192,256]{1,0:T(8,128)S(1)}, f32[192,256]{1,0:T(8,128)S(1)}, u32[]{:S(2)}, u32[]{:S(2)}) collective-permute-start(f32[192,256]{1,0:T(8,128)S(1)} %maximum_select_fusion.7), channel_id=1, source_target_pairs={{0,8},{1,9},{2,10},{3,11},{4,12},{5,13},{6,14},{7,15},{8,0},{9,1},... | collective-permute-start | bytes 589832 | tf_op jit(solution)/shard_map/ppermute | solution.py:103
  432.9 15.1 %collective-permute-start.44 = (f32[384,256]{1,0:T(8,128)S(1)}, f32[384,256]{1,0:T(8,128)}, u32[]{:S(2)}, u32[]{:S(2)}) collective-permute-start(f32[384,256]{1,0:T(8,128)S(1)} %maximum_select_fusion.6), channel_id=1, source_target_pairs={{0,8},{1,9},{2,10},{3,11},{4,12},{5,13},{6,14},{7,15},{8,0},{9,1},... | collective-permute-start | bytes 1179656 | tf_op jit(solution)/shard_map/ppermute | solution.py:103
  433.4 8.4 %collective-permute-start.32 = (f32[86,96]{1,0:T(8,128)S(1)}, f32[86,96]{1,0:T(8,128)S(1)}, u32[]{:S(2)}, u32[]{:S(2)}) collective-permute-start(f32[86,96]{1,0:T(8,128)S(1)} %bitcast_add_fusion.13), channel_id=1, source_target_pairs={{0,2},{1,3},{2,0},{3,1},{4,6},{5,7},{6,4},{7,5},{8,10},{9,11},{10,... | collective-permute-start | bytes 99080 | tf_op jit(solution)/shard_map/ppermute | solution.py:103
  440.6 8.7 %collective-permute-start.38 = (f32[384,256]{1,0:T(8,128)S(1)}, f32[384,256]{1,0:T(8,128)}, u32[]{:S(2)}, u32[]{:S(2)}) collective-permute-start(f32[384,256]{1,0:T(8,128)S(1)} %maximum_select_fusion.5), channel_id=1, source_target_pairs={{0,4},{1,5},{2,6},{3,7},{4,0},{5,1},{6,2},{7,3},{8,12},{9,13},{10,... | collective-permute-start | bytes 1179656 | tf_op jit(solution)/shard_map/ppermute | solution.py:103
  489.0 12.5 %collective-permute-start.48 = (bf16[384,768]{1,0:T(8,128)(2,1)S(1)}, bf16[384,768]{1,0:T(8,128)(2,1)S(1)}, u32[]{:S(2)}, u32[]{:S(2)}) collective-permute-start(bf16[384,768]{1,0:T(8,128)(2,1)S(1)} %newton.1), channel_id=1, source_target_pairs={{0,2},{1,3},{2,0},{3,1},{4,6},{5,7},{6,4},{7,5},{8,10},{9,11},{10,... | collective-permute-start | bytes 1769480 | tf_op jit(solution)/shard_map/ppermute | solution.py:103
  (115 other events, 985.0 us)
Sparse Core Ops, SparseCore 0:
  11.6 114.7 all-gather.2

commit v4 on v3

--- a/solution.py
+++ b/solution.py
@@ -130,6 +130,11 @@
     return jnp.pad(array, ((0, -array.shape[0] % 16), (0, 0)))
 
 
+def together(values):
+    leaves, form = jax.tree.flatten(values)
+    return jax.tree.unflatten(form, lax.optimization_barrier(tuple(leaves)))
+
+
 def gather_blocks(piece, masks):
     for mask in masks:
         piece = jnp.concatenate([piece, swap(piece, mask)], axis=0)
@@ -244,56 +249,73 @@
     return (2,) * (count.bit_length() - 1) + tuple(tail)
 
 
-def join_narrow(piece):
-    spot = lax.axis_index("narrow")
-    other = swap(piece, 2)
-    pair = jnp.where(spot // 2 == 0, jnp.stack([piece, other]), jnp.stack([other, piece]))
-    other = swap(pair, 1)
-    quad = jnp.where(
-        spot % 2 == 0, jnp.stack([pair, other], axis=1), jnp.stack([other, pair], axis=1)
-    )
-    return quad.reshape((4,) + piece.shape)
+class Chain:
+    def __init__(self, steps):
+        self.steps, self.result = steps, None
+        self.request = next(steps)
+
+    def give(self, got):
+        try:
+            self.request = self.steps.send(got)
+        except StopIteration as stop:
+            self.request, self.result = [], stop.value
+
+
+def advance(chains, meanwhile=None, needs=()):
+    sends, needs = together(([[array for array, _ in chain.request] for chain in chains], needs))
+    gots = [
+        [swap(array, mask) for array, (_, mask) in zip(send, chain.request)]
+        for send, chain in zip(sends, chains)
+    ]
+    made = meanwhile(needs) if meanwhile else ()
+    gots, made = together((gots, made))
+    for chain, got in zip(chains, gots):
+        chain.give(got)
+    return made
 
 
 def sum_small(blocks):
-    total = blocks + swap(blocks, 1)
-    first = total
-    total = total.reshape(bits_shape(blocks.shape[0], blocks.shape[1:]))
+    (got,) = yield [(blocks, 1)]
+    total = (blocks + got).reshape(bits_shape(blocks.shape[0], blocks.shape[1:]))
     masks = wide_masks()
     while masks:
         mask = masks[-1]
         keep, send = split_sided(total, len(masks) - 1, mask)
-        total = keep + swap(send, mask)
+        (got,) = yield [(send, mask)]
+        total = keep + got
         masks = masks[:-1]
-    return total + swap(total, 2), first
+    (got,) = yield [(total, 2)]
+    return total + got
 
 
 def sum_wide(value):
     for mask in reversed(wide_masks()):
-        value = value + swap(value, mask)
+        (got,) = yield [(value, mask)]
+        value = value + got
     return value
 
 
-def sum_gram(blocks):
+def sum_gram(parts):
     masks = list(reversed(wide_masks()))
     ways = [masks, [masks[1], masks[0]] + masks[2:]]
-    half = blocks.shape[0] // 2
-    parts = [blocks[:half], blocks[half:]]
+    parts = list(parts)
     for step in range(len(masks)):
-        for number, way in enumerate(ways):
-            part = parts[number]
-            split = part.reshape((2, part.shape[0] // 2) + part.shape[1:])
-            keep, send = split_sided(split, 0, way[step])
-            parts[number] = keep + swap(send, way[step])
+        pairs = [
+            split_sided(part.reshape((2, part.shape[0] // 2) + part.shape[1:]), 0, way[step])
+            for part, way in zip(parts, ways)
+        ]
+        gots = yield [(send, way[step]) for (_, send), way in zip(pairs, ways)]
+        parts = [keep + got for (keep, _), got in zip(pairs, gots)]
     for step in reversed(range(len(masks))):
-        for number, way in enumerate(ways):
-            part = parts[number]
-            other = swap(part, way[step])
-            parts[number] = jnp.where(
+        gots = yield [(part, way[step]) for part, way in zip(parts, ways)]
+        parts = [
+            jnp.where(
                 side_of(way[step]) == 0,
-                jnp.concatenate([part, other], axis=0),
-                jnp.concatenate([other, part], axis=0),
+                jnp.concatenate([part, got], axis=0),
+                jnp.concatenate([got, part], axis=0),
             )
+            for part, got, way in zip(parts, gots, ways)
+        ]
     return parts
 
 
@@ -308,12 +330,8 @@
     return high, (values - high.astype(jnp.float32)).astype(jnp.bfloat16)
 
 
-def rounded(values):
-    return lax.reduce_precision(values, 8, 7)
-
-
 def newton_kernel(
-    low_ref, high_ref, rows_ref, add_left_ref, add_right_ref, out_ref,
+    low_ref, high_ref, rows_ref, added_ref, table_ref, out_ref,
     gram_now, other, left, right, rows_left,
 ):
     tile = GRAM_TILE
@@ -325,15 +343,24 @@
     def span(number):
         return slice(number * tile, (number + 1) * tile)
 
+    def turned_dot(left_side, right_side):
+        return lax.dot_general(
+            left_side,
+            right_side,
+            (((0,), (0,)), ((), ())),
+            preferred_element_type=jnp.float32,
+        )
+
+    added_high, added_low = split_two(added_ref[...])
+    added_rest = added_ref[...] - added_high.astype(jnp.float32) - added_low.astype(jnp.float32)
+    added_parts = (added_high, added_low, added_rest.astype(jnp.bfloat16))
     half = len(GRAM_SPOTS) // 2
     for number, (row, column) in enumerate(GRAM_SPOTS):
         source = low_ref if number < half else high_ref
-        block = source[span(number % half), :] + lax.dot_general(
-            add_left_ref[:, span(row)],
-            add_right_ref[:, span(column)],
-            (((0,), (0,)), ((), ())),
-            preferred_element_type=jnp.float32,
-        )
+        block = source[span(number % half), :]
+        for part in added_parts:
+            block = block + turned_dot(part[:, span(row)], table_ref[:, span(column)])
+            block = block + turned_dot(table_ref[:, span(row)], part[:, span(column)])
         gram_now[span(row), span(column)] = block
         if row == column:
             picked = jnp.where(diagonal, block, 0.0)
@@ -407,7 +434,7 @@
     out_ref[...] = rows_product().astype(out_ref.dtype)
 
 
-def newton_rows(gram_parts, rows, add_left, add_right):
+def newton_rows(gram_parts, rows, added, table):
     count = rows.shape[0]
     return pl.pallas_call(
         newton_kernel,
@@ -424,33 +451,7 @@
         compiler_params=pltpu.CompilerParams(vmem_limit_bytes=48 << 20),
         cost_estimate=pl.CostEstimate(flops=60 * D * D * D, bytes_accessed=4 << 20, transcendentals=0),
         name="newton",
-    )(*gram_parts, rows, add_left, add_right)
-
-
-def pick_rows(parts, spot):
-    most = max(part.shape[0] for part in parts)
-    padded = [jnp.pad(part, ((0, most - part.shape[0]), (0, 0))) for part in parts]
-    picked = padded[-1]
-    for number in reversed(range(len(parts) - 1)):
-        picked = jnp.where(spot == number, padded[number], picked)
-    return picked
-
-
-def local_gram(rows):
-    tiles = [rows[:, at * GRAM_TILE : (at + 1) * GRAM_TILE] for at in range(D // GRAM_TILE)]
-    return jnp.concatenate(
-        [
-            lax.dot_general(
-                tiles[row],
-                tiles[column],
-                (((0,), (0,)), ((), ())),
-                precision=lax.Precision.HIGHEST,
-                preferred_element_type=jnp.float32,
-            )
-            for row, column in GRAM_SPOTS
-        ],
-        axis=0,
-    )
+    )(*gram_parts, rows, added, table)
 
 
 def pack_kernel(spot_ref, *refs):
@@ -486,70 +487,256 @@
     )(spot[None].astype(jnp.int32), *weights)
 
 
-def sums_kernel(*refs):
-    *parts, out_ref, bias_ref, held = refs
-    for number, part in enumerate(parts):
+def entry_kernel(scale, *refs):
+    (hot_ref, table_ref, gain_ref, middle_ref, weight_ref), refs = refs[:5], refs[5:]
+    *low_refs, entry_ref, sums_ref, table_sum_ref = refs
+    step = pl.program_id(0)
+    hot = hot_ref[:, 0:LANES]
+    stream = scale * jnp.dot(hot, table_ref[...], preferred_element_type=jnp.float32)
+    grads = None
+    for kind in range(3):
+        low = jnp.concatenate([ref[kind] for ref in low_refs], axis=1)
+        part = jnp.dot(
+            low, weight_ref[kind * D : (kind + 1) * D, :], preferred_element_type=jnp.float32
+        )
+        grads = part if grads is None else grads + part
+    center = stream - jnp.mean(stream, axis=-1, keepdims=True)
+    inverse = lax.rsqrt(jnp.mean(center * center, axis=-1, keepdims=True) + NORM_EPS)
+    normal = center * inverse
+    scaled = grads * gain_ref[...]
+    inner = (
+        scaled
+        - jnp.mean(scaled, axis=-1, keepdims=True)
+        - normal * jnp.mean(scaled * normal, axis=-1, keepdims=True)
+    )
+    entry = middle_ref[...] + inverse * inner
+    entry_ref[...] = entry
+    sums = jnp.concatenate(
+        [
+            jnp.sum(grads * normal, axis=0, keepdims=True),
+            jnp.sum(grads, axis=0, keepdims=True),
+        ],
+        axis=0,
+    )
+    high = entry.astype(jnp.bfloat16)
+    rest = entry - high.astype(jnp.float32)
+    middle = rest.astype(jnp.bfloat16)
+    low = (rest - middle.astype(jnp.float32)).astype(jnp.bfloat16)
+    table_sum = None
+    for part in (high, middle, low):
+        part = lax.dot_general(
+            hot, part, (((0,), (0,)), ((), ())), preferred_element_type=jnp.float32
+        )
+        table_sum = part if table_sum is None else table_sum + part
+
+    @pl.when(step == 0)
+    def _():
+        sums_ref[...] = sums
+        table_sum_ref[...] = scale * table_sum
+
+    @pl.when(step > 0)
+    def _():
+        sums_ref[...] += sums
+        table_sum_ref[...] += scale * table_sum
+
+
+def entry_call(scale, hot, table, gain, middle_grad, weight, lows):
+    rows = SEQ_LEN // 3
+    whole = lambda step: (0, 0)
+    own = lambda step: (step, 0)
+    return pl.pallas_call(
+        partial(entry_kernel, scale),
+        grid=(3,),
+        in_specs=[
+            pl.BlockSpec((rows, hot.shape[1]), own),
+            pl.BlockSpec(table.shape, whole),
+            pl.BlockSpec(gain.shape, whole),
+            pl.BlockSpec((rows, D), own),
+            pl.BlockSpec(weight.shape, whole),
+        ]
+        + [pl.BlockSpec((3, rows, low.shape[2]), lambda step: (0, step, 0)) for low in lows],
+        out_specs=[
+            pl.BlockSpec((rows, D), own),
+            pl.BlockSpec((2, D), whole),
+            pl.BlockSpec((LANES, D), whole),
+        ],
+        out_shape=[
+            jax.ShapeDtypeStruct((SEQ_LEN, D), jnp.float32),
+            jax.ShapeDtypeStruct((2, D), jnp.float32),
+            jax.ShapeDtypeStruct((LANES, D), jnp.float32),
+        ],
+        compiler_params=pltpu.CompilerParams(vmem_limit_bytes=48 << 20),
+        cost_estimate=pl.CostEstimate(flops=1 << 20, bytes_accessed=1 << 16, transcendentals=0),
+        name="entry",
+    )(hot, table, gain, middle_grad, weight, *lows)
+
+
+def small_kernel(parts, spot_rows, table_sum_ref, head_ref, hist_ref, *refs):
+    part_refs, refs = refs[:parts], refs[parts:]
+    *row_refs, out_ref, sums, held = refs
+    for number, part in enumerate(part_refs):
         width = part.shape[2]
         for kind in range(3):
             start = kind * D + number * width
-            held[:, start : start + width] = part[kind]
-    bias_ref[...] = jnp.sum(held[...], axis=0, keepdims=True)
+            sums[:, start : start + width] = part[kind]
+    held[0:VOCAB, :] = table_sum_ref[0:VOCAB, :] + head_ref[...]
+    bias = jnp.sum(sums[...], axis=0, keepdims=True)
+    for kind in range(3):
+        held[VOCAB + 6 + kind : VOCAB + 7 + kind, :] = bias[:, kind * D : (kind + 1) * D]
+    for ref, at in zip(row_refs, spot_rows):
+        for row in range(ref.shape[0]):
+            for part in range(ref.shape[1] // D):
+                held[at : at + 1, :] = ref[row : row + 1, part * D : (part + 1) * D]
+                at += 1
     count, rows, columns = out_ref.shape
+    narrow = D // count
+    wide = columns - narrow
+    base = held.shape[0]
     for number in range(count):
-        out_ref[number] = held[0:rows, number * columns : (number + 1) * columns]
-
-
-def sums_blocks(parts, wide_size):
+        out_ref[number, 0:VOCAB, 0:wide] = sums[0:VOCAB, number * wide : (number + 1) * wide]
+        out_ref[number, VOCAB:rows, 0:wide] = jnp.zeros((rows - VOCAB, wide), jnp.float32)
+        out_ref[number, 0:base, wide:columns] = held[:, number * narrow : (number + 1) * narrow]
+        out_ref[number, base:rows, wide:columns] = hist_ref[...]
+
+
+def small_blocks(parts, table_sum, head, hist, rows, wide_size):
     whole = pl.BlockSpec(memory_space=pltpu.VMEM)
+    total = VOCAB + 15 + hist.shape[0]
+    arrays = [array for array, _ in rows]
     return pl.pallas_call(
-        sums_kernel,
-        in_specs=[whole] * len(parts),
-        out_specs=[whole, whole],
-        out_shape=[
-            jax.ShapeDtypeStruct((wide_size, VOCAB, 3 * D // wide_size), jnp.float32),
-            jax.ShapeDtypeStruct((1, 3 * D), jnp.float32),
+        partial(small_kernel, len(parts), tuple(VOCAB + place for _, place in rows)),
+        in_specs=[whole] * (3 + len(parts) + len(rows)),
+        out_specs=whole,
+        out_shape=jax.ShapeDtypeStruct((wide_size, total, 4 * D // wide_size), jnp.float32),
+        scratch_shapes=[
+            pltpu.VMEM((LANES, 3 * D), jnp.float32),
+            pltpu.VMEM((VOCAB + 15, D), jnp.float32),
         ],
-        scratch_shapes=[pltpu.VMEM((LANES, 3 * D), jnp.float32)],
-        name="token_sums",
-    )(*parts)
-
-
-def update_kernel(rates, spot_ref, pair_ref, other_ref, *refs):
+        cost_estimate=pl.CostEstimate(flops=1 << 20, bytes_accessed=1 << 16, transcendentals=0),
+        name="small_grads",
+    )(table_sum, head, hist, *parts, *arrays)
+
+
+def dense_kernel(units, spot_ref, own_ref, beside_ref, core_ref, cross_ref, *refs):
+    base_ref, *refs = refs
+    count = len(units)
+    moment_refs, refs = refs[:count], refs[count:]
+    total_refs, next_refs, refs = refs[:count], refs[count : 2 * count], refs[2 * count :]
+    rows_ref, low_ref, high_ref, left, right = refs
+    spot = spot_ref[0]
+    for device in range(4):
+        way = spot ^ device
+        for kind, source in enumerate((own_ref, core_ref, beside_ref, cross_ref)):
+
+            @pl.when(way == kind)
+            def _():
+                at = 0
+                for total_ref, unit in zip(total_refs, units):
+                    total_ref[device * unit : (device + 1) * unit, :] = source[at : at + unit, :]
+                    at += unit
+
+    rows_ref[...] = jnp.zeros_like(rows_ref)
+
+    @pl.when(spot == 0)
+    def _():
+        rows_ref[0 : base_ref.shape[0], :] = (MUON_MU * MUON_MU) * base_ref[...]
+
+    for number in range(count):
+        gradient = total_refs[number][...]
+        moment_next = MUON_MU * moment_refs[number][...] + (1.0 - MUON_MU) * gradient
+        next_refs[number][...] = moment_next
+        place = count - number
+
+        @pl.when(spot == place)
+        def _():
+            rows_ref[0 : gradient.shape[0], :] = (
+                1.0 - MUON_MU
+            ) * gradient + MUON_MU * moment_next
+
+    high, low = split_two(rows_ref[...])
+    depth = rows_ref.shape[0]
+    right[0:depth, :] = high
+    right[depth : 2 * depth, :] = low
+    right[2 * depth : 3 * depth, :] = high
+    turned_high, turned_low = split_two(rows_ref[...].T)
+    left[:, 0:depth] = turned_high
+    left[:, depth : 2 * depth] = turned_high
+    left[:, 2 * depth : 3 * depth] = turned_low
+    half = len(GRAM_SPOTS) // 2
+    for number, (row, column) in enumerate(GRAM_SPOTS):
+        target = low_ref if number < half else high_ref
+        at = (number % half) * GRAM_TILE
+        target[at : at + GRAM_TILE, :] = jnp.dot(
+            left[row * GRAM_TILE : (row + 1) * GRAM_TILE, :],
+            right[:, column * GRAM_TILE : (column + 1) * GRAM_TILE],
+            preferred_element_type=jnp.float32,
+        )
+
+
+def dense_step(spot, units, pieces, base, moments):
+    whole = pl.BlockSpec(memory_space=pltpu.VMEM)
+    most = max(moment.shape[0] for moment in moments)
+    shapes = [jax.ShapeDtypeStruct(moment.shape, jnp.float32) for moment in moments]
+    half = jax.ShapeDtypeStruct((len(GRAM_SPOTS) // 2 * GRAM_TILE, GRAM_TILE), jnp.float32)
+    results = pl.pallas_call(
+        partial(dense_kernel, units),
+        in_specs=[pl.BlockSpec(memory_space=pltpu.SMEM)] + [whole] * (5 + len(moments)),
+        out_specs=[whole] * (2 * len(moments) + 3),
+        out_shape=shapes + shapes + [jax.ShapeDtypeStruct((most, D), jnp.float32), half, half],
+        scratch_shapes=[
+            pltpu.VMEM((D, 3 * most), jnp.bfloat16),
+            pltpu.VMEM((3 * most, D), jnp.bfloat16),
+        ],
+        compiler_params=pltpu.CompilerParams(vmem_limit_bytes=48 << 20),
+        cost_estimate=pl.CostEstimate(flops=1 << 20, bytes_accessed=1 << 16, transcendentals=0),
+        name="dense_step",
+    )(spot[None].astype(jnp.int32), *pieces, base, *moments)
+    count = len(moments)
+    return results[:count], results[count : 2 * count], results[2 * count], results[2 * count + 1 :]
+
+
+def update_kernel(rates, spot_ref, *refs):
     count = len(rates)
+    sources, refs = refs[:4], refs[4:]
     for number in range(count):
         weight_ref, out_ref = refs[number], refs[count + number]
         rows = weight_ref.shape[0]
         way = spot_ref[0] ^ number
-        mine = jnp.where(
-            way % 2 == 0, pair_ref[way // 2, 0:rows, :], other_ref[way // 2, 0:rows, :]
-        )
-        out_ref[...] = (
-            weight_ref[...] * (1.0 - MUON_RATE * MUON_DECAY)
-            - rates[number] * mine.astype(jnp.float32)
-        )
-
-
-def update_rows(spot, pair, other, weights, rates):
+        for kind, source in enumerate(sources):
+
+            @pl.when(way == kind)
+            def _():
+                out_ref[...] = weight_ref[...] * (1.0 - MUON_RATE * MUON_DECAY) - rates[
+                    number
+                ] * source[0:rows, :].astype(jnp.float32)
+
+
+def update_rows(spot, orthos, weights, rates):
     whole = pl.BlockSpec(memory_space=pltpu.VMEM)
     return pl.pallas_call(
         partial(update_kernel, rates),
-        in_specs=[pl.BlockSpec(memory_space=pltpu.SMEM)] + [whole] * (2 + len(weights)),
+        in_specs=[pl.BlockSpec(memory_space=pltpu.SMEM)] + [whole] * (4 + len(weights)),
         out_specs=[whole] * len(weights),
         out_shape=[jax.ShapeDtypeStruct(weight.shape, jnp.float32) for weight in weights],
         compiler_params=pltpu.CompilerParams(vmem_limit_bytes=40 << 20),
+        cost_estimate=pl.CostEstimate(flops=1 << 20, bytes_accessed=1 << 16, transcendentals=0),
         name="update",
-    )(spot[None].astype(jnp.int32), pair, other, *weights)
+    )(spot[None].astype(jnp.int32), *orthos, *weights)
 
 
 def heads_kernel(place_ref, blocks_ref, bias_ref, out_ref, held):
     count, rows, columns = blocks_ref.shape
-    held[...] = jnp.zeros_like(held)
+    held[rows : held.shape[0], :] = jnp.zeros((held.shape[0] - rows, 3 * D), jnp.float32)
     for number in range(count):
         spot = slice(number * columns, (number + 1) * columns)
         held[0:rows, spot] = blocks_ref[place_ref[number]] + bias_ref[:, spot]
     high, low = split_two(held[...])
-    out_ref[0:LANES, :] = high
-    out_ref[LANES : 2 * LANES, :] = low
+    some = held.shape[0]
+    none = jnp.zeros((LANES - some, 3 * D), jnp.bfloat16)
+    out_ref[0:some, :] = high
+    out_ref[some:LANES, :] = none
+    out_ref[LANES : LANES + some, :] = low
+    out_ref[LANES + some : 2 * LANES, :] = none
 
 
 def heads_table(blocks, place, bias):
@@ -563,7 +750,7 @@
                 pl.BlockSpec(bias.shape, lambda step, place: (0, 0)),
             ],
             out_specs=pl.BlockSpec((2 * LANES, 3 * D), lambda step, place: (0, 0)),
-            scratch_shapes=[pltpu.VMEM((LANES, 3 * D), jnp.float32)],
+            scratch_shapes=[pltpu.VMEM((VOCAB + -VOCAB % 16, 3 * D), jnp.float32)],
         ),
         out_shape=jax.ShapeDtypeStruct((2 * LANES, 3 * D), jnp.bfloat16),
         name="heads_table",
@@ -963,10 +1150,12 @@
     all_masks = masks + [2, 1]
     small = jnp.concatenate([table_weight, vector_params], axis=0).astype(low_type)
     small = gather_blocks(small[None], masks)
-    packed = (expand_weight, reduce_weight, attend_weight, mixing_weight)
+    packed = (expand_weight, reduce_weight, mixing_weight, attend_weight)
     units = [weight.shape[0] // narrow_size for weight in packed]
     starts = np.cumsum([0] + [unit + -unit % 16 for unit in units])
-    weights_low = lax.all_gather(pack_rows(packed, lax.axis_index("narrow")), BOTH, axis=0)
+    packed_low = pack_rows(packed, lax.axis_index("narrow"))
+    weights_low = lax.all_gather(packed_low[: int(starts[3])], BOTH, axis=0)
+    attend_own = packed_low[int(starts[3]) : int(starts[3]) + units[3]]
 
     def weight_rows(number, unit):
         start = int(starts[number])
@@ -992,9 +1181,9 @@
     embed_scale = math.sqrt(D)
     table_stream = embed_scale * table_low.astype(jnp.float32)
     table_normed = norm_forward(table_stream, gain_one, bias_one)[0].astype(low_type)
-    table_own = times_trans(table_normed, attend_weight.astype(low_type))
-    place = jnp.asarray(places_of(masks, narrow_size), jnp.int32)[jnp.arange(wide_size) ^ wide_at]
-    tables = heads_table(gather_blocks(table_own[None], masks), place, attend_bias)
+    table_own = times_trans(table_normed, attend_own)
+    place = jnp.asarray(places_of(all_masks, 1), jnp.int32)[jnp.arange(devices) ^ me]
+    tables = heads_table(gather_blocks(table_own[None], all_masks), place, attend_bias)
 
     unit = FF // devices
     hidden_place = jnp.asarray(offsets_of(hidden_masks)) ^ me
@@ -1036,7 +1225,8 @@
         )
     last_mask = masks[-1]
     mixed_low = jnp.concatenate([parts[3] for parts in attended], axis=1)
-    mixing_low = weight_rows(3, D // devices)
+    mixing_low = weight_rows(2, D // devices)
+    attend_low = lax.all_gather(gate(attend_own, mixed_low), BOTH, axis=0)
     branch = times_trans(mixed_low, mixing_low) + mixing_bias
     middle = stream + branch
     normed_two, normal_two, inverse_two = norm_forward(middle, gain_two, bias_two)
@@ -1066,15 +1256,15 @@
     static_shape = (2,) * len(static_marks) + (unit, D)
 
     reduce_send = trans_times(hidden_low[:, half_ff:], feed_low).astype(low_type)
-    reduce_sum = trans_times(hidden_low[:, :half_ff], feed_low) + swap(reduce_send, 1)
-    reduce_chain = sum_chain([(reduce_sum.reshape(static_shape), static_marks, False)], jnp.float32)
-    sent = next(reduce_chain)
     pre_grad, normed_two_grad, expand_bias_grad = feed_back_call(
-        feed_place, gate(feed_low, sent), slope_low, feed_source, feed_starts
-    )
-    sent = reduce_chain.send(pre_grad)
+        feed_place, gate(feed_low, reduce_send), slope_low, feed_source, feed_starts
+    )
+    reduce_got = gate(swap(reduce_send, 1), pre_grad)
+    reduce_sum = trans_times(hidden_low[:, :half_ff], feed_low) + reduce_got
+    reduce_chain = sum_chain([(reduce_sum.reshape(static_shape), static_marks, False)], low_type)
+    reduce_sent = next(reduce_chain)
     expand_send = trans_times(
-        gate(pre_grad, sent)[:, half_ff:], normed_two_low
+        gate(pre_grad, reduce_sent)[:, half_ff:], normed_two_low
     ).astype(low_type)
     expand_sum = trans_times(pre_grad[:, :half_ff], normed_two_low) + swap(expand_send, 1)
     middle_part, gain_two_grad, bias_two_grad = norm_backward(
@@ -1092,7 +1282,6 @@
         [(expand_sum.reshape(static_shape), static_marks, False), mixing_item], low_type
     )
     expand_sent = next(expand_chain)
-    reduce_sent = reduce_chain.send(expand_sum)
 
     backs = []
     back_pairs = D // PAIR // BACK_CALLS
@@ -1117,38 +1306,96 @@
         )
         return backs[-1][1]
 
-    back_step((expand_sent, reduce_sent))
+    mixed_grad, attend_low = lax.optimization_barrier((mixed_grad, attend_low))
+    back_step(expand_sent)
     token = back_step(())
     expand_sent = expand_chain.send(token)
     reduce_sent = reduce_chain.send(token)
     token = back_step((expand_sent, reduce_sent))
     expand_sent = expand_chain.send(token)
+    reduce_sent = reduce_chain.send(token)
+    token = back_step((expand_sent, reduce_sent))
+    reduce_sent = reduce_chain.send(token)
+    token = back_step(reduce_sent)
+    expand_sent = expand_chain.send(token)
     token = back_step(expand_sent)
     (reduce_sum,) = drain(reduce_chain, token)
-    token = back_step(())
-    expand_sent = expand_chain.send(token)
-    token = back_step(expand_sent)
     expand_sum, mixing_sum = drain(expand_chain, token)
-    token_sums, attend_bias_grad = sums_blocks([back[1] for back in backs], wide_size)
-    dense = join_narrow(jnp.concatenate([reduce_sum, expand_sum, mixing_sum], axis=0))
-    reduce_total = dense[:, :unit].reshape(-1, D)
-    expand_total = dense[:, unit : 2 * unit].reshape(-1, D)
-    mixing_total = dense[:, 2 * unit :].reshape(-1, D)
+    dense = jnp.concatenate([reduce_sum, expand_sum, mixing_sum], axis=0)
     spot = lax.axis_index("narrow")
+    dense, backs = together((dense, backs))
+
+    def one_chain(value, mask):
+        (got,) = yield [(value, mask)]
+        return got
+
+    columns = D // wide_size
+    rows_hist = -(-VOCAB // columns)
+
+    def make_small(backs):
+        entry_gradient, one_sums, table_sum = entry_call(
+            embed_scale,
+            hot,
+            jnp.pad(table_low, ((0, LANES - VOCAB), (0, 0))),
+            gain_one[None, :],
+            middle_grad,
+            attend_low.reshape(3 * D, D),
+            [back[0] for back in backs],
+        )
+        hist_part = jnp.pad(prob_sum, (0, rows_hist * columns - VOCAB)).reshape(rows_hist, columns)
+        expand_ordered = in_order(
+            expand_bias_grad.reshape(devices, FF // devices), hidden_masks, 1, me
+        )
+        small_grads = small_blocks(
+            [back[1] for back in backs],
+            table_sum,
+            table_head,
+            hist_part,
+            (
+                (one_sums, 0),
+                (gain_two_grad[None, :], 2),
+                (bias_two_grad[None, :], 3),
+                (gain_last_grad[None, :], 4),
+                (bias_last_grad[None, :], 5),
+                (mixing_bias_grad[None, :], 9),
+                (reduce_bias_grad[None, :], 10),
+                (expand_ordered.reshape(1, FF), 11),
+            ),
+            wide_size,
+        )
+        return entry_gradient, small_grads
+
+    beside_chain = Chain(one_chain(dense, 2))
+    entry_gradient, small_grads = advance([beside_chain], make_small, backs)
+    beside = beside_chain.result
+    cores = [Chain(one_chain(dense, 1)), Chain(one_chain(beside, 1))]
+    small_chain = Chain(sum_small(small_grads))
+    advance(cores + [small_chain])
+    pieces = (dense, beside, cores[0].result, cores[1].result)
+
+    def make_dense(pieces):
+        return dense_step(
+            spot,
+            (unit, unit, D // devices),
+            pieces,
+            attend_moment,
+            (reduce_moment, expand_moment, mixing_moment),
+        )
+
+    dense_totals, dense_next, dense_rows, gram_own = advance([small_chain], make_dense, pieces)
+    reduce_total, expand_total, mixing_total = dense_totals
+    reduce_next, expand_next, mixing_next = dense_next
 
     def step_of(moment, gradient):
         moment_next = MUON_MU * moment + (1.0 - MUON_MU) * gradient
         return moment_next, (1.0 - MUON_MU) * gradient + MUON_MU * moment_next
 
-    mixing_next, mixing_step = step_of(mixing_moment, mixing_total)
-    expand_next, expand_step = step_of(expand_moment, expand_total)
-    reduce_next, reduce_step = step_of(reduce_moment, reduce_total)
-    attend_base = (MUON_MU * MUON_MU) * attend_moment
-    gram_parts = sum_gram(
-        local_gram(pick_rows((attend_base, mixing_step, expand_step, reduce_step), spot))
-    )
-
-    token_sums, token_first = sum_small(token_sums)
+    gram_chain = Chain(sum_gram(gram_own))
+    while small_chain.request:
+        advance([chain for chain in (gram_chain, small_chain) if chain.request])
+    small_total = small_chain.result
+    token_sums = small_total[:VOCAB, : 3 * D // wide_size]
+    small_total = small_total[:, 3 * D // wide_size :]
     attend_total = lax.dot_general(
         token_sums,
         table_normed.astype(jnp.float32),
@@ -1161,120 +1408,63 @@
     crossed = exact_times(
         token_sums, jnp.concatenate([attend_moment, token_sums.T], axis=1)
     )
-    crossed = sum_wide(crossed)
+    crossed_chain = Chain(sum_wide(crossed))
+    while crossed_chain.request:
+        advance([chain for chain in (gram_chain, crossed_chain) if chain.request])
+    while gram_chain.request:
+        advance([gram_chain])
+    crossed = crossed_chain.result
+    gram_parts = gram_chain.result
     table_wide = table_normed.astype(jnp.float32)
     added = gradient_rate * (
         (MUON_MU * MUON_MU) * crossed[:, :D]
         + (0.5 * gradient_rate) * exact_times(crossed[:, D:], table_wide)
     )
     added = jnp.where(spot == 0, added, 0.0)
-    added_high = rounded(added)
-    added_low = rounded(added - added_high)
-    added_least = added - added_high - added_low
-    table_three = [table_normed] * 3
-    added_three = [part.astype(low_type) for part in (added_high, added_low, added_least)]
-    room = ((0, -(-6 * VOCAB // 16) * 16 - 6 * VOCAB), (0, 0))
-    add_left = jnp.pad(jnp.concatenate(added_three + table_three, axis=0), room)
-    add_right = jnp.pad(jnp.concatenate(table_three + added_three, axis=0), room)
-
-    lows = gate([back[0] for back in backs], token_first)
-    projected_low = jnp.concatenate([low[kind] for kind in range(3) for low in lows], axis=1)
-    attend_low = gate(weights_low, token_first)[:, int(starts[2]) : int(starts[2]) + units[2]]
-    normed_one_grad = times_plain(projected_low, attend_low.reshape(3 * D, D))
-    normed_one, normal_one, inverse_one = norm_forward(stream, gain_one, bias_one)
-    stream_part, gain_one_grad, bias_one_grad = norm_backward(
-        normed_one_grad, normal_one, inverse_one, gain_one
-    )
-    entry_gradient = middle_grad + stream_part
-    table_grad = (
-        embed_scale * exact_times(token_hot.astype(jnp.float32).T, entry_gradient) + table_head
-    )
-    (
-        gain_two_grad,
-        bias_two_grad,
-        gain_last_grad,
-        bias_last_grad,
-        mixing_bias_grad,
-        reduce_bias_grad,
-        expand_bias_grad,
-        prob_sum,
-    ) = gate(
-        (
-            gain_two_grad,
-            bias_two_grad,
-            gain_last_grad,
-            bias_last_grad,
-            mixing_bias_grad,
-            reduce_bias_grad,
-            expand_bias_grad,
-            prob_sum,
-        ),
-        token_first,
-    )
-    expand_bias_grad = in_order(
-        expand_bias_grad.reshape(devices, FF // devices), hidden_masks, 1, me
-    )
-    vector_grad = jnp.concatenate(
-        [
-            jnp.stack(
-                [
-                    gain_one_grad,
-                    bias_one_grad,
-                    gain_two_grad,
-                    bias_two_grad,
-                    gain_last_grad,
-                    bias_last_grad,
-                ]
-            ),
-            attend_bias_grad.reshape(3, D),
-            mixing_bias_grad[None, :],
-            reduce_bias_grad[None, :],
-            expand_bias_grad.reshape(4, D),
-        ],
-        axis=0,
-    )
-    columns = D // wide_size
-    rows_hist = -(-VOCAB // columns)
-    hist_part = jnp.pad(prob_sum, (0, rows_hist * columns - VOCAB)).reshape(rows_hist, columns)
-    small_grads = jnp.concatenate([table_grad, vector_grad], axis=0)
-    small_grads = jnp.transpose(small_grads.reshape(VOCAB + 15, wide_size, columns), (1, 0, 2))
-    small_grads = jnp.concatenate(
-        [small_grads, jnp.broadcast_to(hist_part, (wide_size, rows_hist, columns))], axis=1
-    )
-    small_total, _ = sum_small(small_grads)
     table_total = small_total[:VOCAB]
     vector_total = small_total[VOCAB : VOCAB + 15]
     prob_total = small_total[VOCAB + 15 :].reshape(rows_hist * columns)[:VOCAB]
     histogram = prob_total * (VOCAB / (row_count * devices))
     totals = (attend_total, mixing_total, expand_total, reduce_total)
     moment_next = (attend_next, mixing_next, expand_next, reduce_next)
-    rows = pick_rows((attend_step, mixing_step, expand_step, reduce_step), spot)
-    rows = gate(rows, small_total)
-    ortho = newton_rows(gram_parts, rows, add_left, add_right)
-    pair = jnp.stack([ortho, swap(ortho, 2)])
+    most = dense_rows.shape[0]
+    attend_rows = jnp.pad(attend_step, ((0, most - attend_step.shape[0]), (0, 0)))
+    rows = jnp.where(spot == 0, attend_rows, dense_rows)
+    ortho = newton_rows(gram_parts, rows, added, table_normed)
+    ortho, table_total, vector_total = together((ortho, table_total, vector_total))
+    across = swap(ortho, 2)
+    table_new, table_mean_next, table_square_next = adam_step(
+        table_weight, table_mean, table_square, table_total, TABLE_RATE, TABLE_DECAY, step_count
+    )
+    vector_new, vector_mean_next, vector_square_next = adam_step(
+        vector_params, vector_mean, vector_square, vector_total, VECTOR_RATE, 0.0, step_count
+    )
+    across, adam_results = together(
+        (
+            across,
+            (
+                table_new,
+                table_mean_next,
+                table_square_next,
+                vector_new,
+                vector_mean_next,
+                vector_square_next,
+            ),
+        )
+    )
+    orthos = (ortho, swap(ortho, 1), across, swap(across, 1))
     matrices = (attend_weight, mixing_weight, expand_weight, reduce_weight)
     rates = tuple(
         MUON_RATE * SHAPE_FACTOR * math.sqrt(max(rows, D)) for rows in (3 * D, D, FF, FF)
     )
-    matrix_new = tuple(update_rows(spot, pair, swap(pair, 1), matrices, rates))
-    table_new, table_mean_next, table_square_next = adam_step(
-        table_weight, table_mean, table_square, table_total, TABLE_RATE, TABLE_DECAY, step_count
-    )
-    vector_new, vector_mean_next, vector_square_next = adam_step(
-        vector_params, vector_mean, vector_square, vector_total, VECTOR_RATE, 0.0, step_count
-    )
+    matrix_new = tuple(update_rows(spot, orthos, matrices, rates))
     results = (
         totals
         + (table_total, vector_total)
         + matrix_new
         + moment_next
         + (
-            table_new,
-            table_mean_next,
-            table_square_next,
-            vector_new,
-            vector_mean_next,
-            vector_square_next,
+            *adam_results,
         )
     )
     block_output = output.astype(low_type).reshape(seq_count, SEQ_LEN, D)

time: 525 us -> 505 us (0.962)
  waiting for transfers between devices: 113 us -> 88.1 us
  other arithmetic: 55 us -> 31.6 us
  Pallas kernels: 188 us -> 208 us
  matrix products: 43.8 us -> 32.2 us
  starting transfers between devices: 49.6 us -> 60.5 us
  local copies, waits for them, and re-layouts: 50.2 us -> 60.4 us
    pallas_call x1 -> x3, Pallas kernels: 2.55 us -> 19.9 us  [the longest x1 11.6 us: entry_call(): pl.pallas_call(partial(entry_kernel, scale), grid=(3,), in_specs=[pl.Bloc...]
    ppermute x50 -> x49, waiting for transfers between devices: 101 us -> 85.9 us  [swap(): lax.ppermute(value, BOTH, [(spot, spot ^ mask) for spot in range(total)])]
    ppermute x50 -> x49, starting transfers between devices: 49.6 us -> 60.4 us  [swap(): lax.ppermute(value, BOTH, [(spot, spot ^ mask) for spot in range(total)])]
    select_n x11 -> x8, other arithmetic: 11 us -> 0.35 us  [the longest x6 0.22 us: sum_gram(): jnp.where(side_of(way[step]) == 0, jnp.concatenate([part, got], axis=0),...]
    all_gather x1 -> x2, waiting for transfers between devices: 11.9 us -> 2.24 us  [the longest x1 2.22 us: on_device(): attend_low = lax.all_gather(gate(attend_own, mixed_low), BOTH, axis=0)]
    unnamed x241 -> x239, local copies, waits for them, and re-layouts: 19 us -> 25.4 us
  transfers between devices with their start and end apart: 51 -> 51, of which waited for: 21 -> 21; matrix products, arithmetic and copies ran while one was open for 18% -> 16% of each run, Pallas kernels for 24% -> 28%
where the time goes in v4:
time: 505 us; the launch traced here: 499 us
  Pallas kernels  208 us (41%)
  waiting for transfers between devices  88.1 us (17%)
  starting transfers between devices  60.5 us (12%)
  local copies, waits for them, and re-layouts  60.4 us (12%)
  matrix products  32.2 us (6%)
  other arithmetic  31.6 us (6%)
  between operations  17.8 us (4%)
    ppermute x49, waiting for transfers between devices, swap(): lax.ppermute(value, BOTH, [(spot, spot ^ mask) for spot in range(total)])  85.9 us
    ppermute x49, starting transfers between devices, swap(): lax.ppermute(value, BOTH, [(spot, spot ^ mask) for spot in range(total)])  60.4 us
    pallas_call x6, Pallas kernels, attend_back_call(): pl.pallas_call(attend_back_kernel, grid=(count,), in_specs=[pl.BlockSpec(...  54.2 us
    pallas_call x3, Pallas kernels, attend_call(): pl.pallas_call(attend_kernel, grid=(count,), in_specs=[pl.BlockSpec(hot.s...  43.4 us
    pallas_call x1, Pallas kernels, newton_rows(): pl.pallas_call(newton_kernel, out_shape=jax.ShapeDtypeStruct((count, D),...  40 us
    unnamed x239, local copies, waits for them, and re-layouts  25.4 us
    pallas_call x1, Pallas kernels, feed_call(): pl.pallas_call(partial(feed_kernel, starts), grid_spec=pltpu.PrefetchScal...  22.6 us
    dot_general x6, matrix products, trans_times(): lax.dot_general(left_side, right_side, (((0,), (0,)), ((), ())), preferre...  21.7 us
  transfers between devices with their start and end apart: 51, of which 21 were waited for; matrix products, arithmetic and copies ran while one was open for 16% of the time, Pallas kernels for 28%

profile of v4, /device:TPU:0, one launch (start us, length us, event | category | flops | bytes accessed | tf_op | source)
XLA Modules:
  0.0 499.0 jit_solution(18059953140910332345)
XLA Ops:
  11.2 4.1 collective-permute-start
  23.3 3.8 collective-permute-done.2
  31.0 3.1 collective-permute-start.3
  37.0 2.0 collective-permute-start.4
  46.4 4.9 collective-permute-done.5
  54.3 6.8 %collective-permute-done.6 = f32[8,70,72]{2,1,0:T(8,128)S(1)} collective-permute-done((f32[8,70,72]{2,1,0:T(8,128)S(1)}, f32[8,70,72]{2,1,0:T(8,128)S(1)}, u32[]{:S(2)}, u32[]{:S(2)}) %collective-permute-start.6) | collective-permute-done | bytes 161312 | tf_op jit(solution)/shard_map/ppermute | solution.py:103
  65.0 4.6 heads_table.1.tq_ref.tk_ref.tv_ref
  70.9 14.6 %attend.5 = (bf16[912,256]{1,0:T(8,128)(2,1)S(1)}, bf16[912,256]{1,0:T(8,128)(2,1)S(1)}, bf16[912,256]{1,0:T(8,128)(2,1)S(1)}, bf16[912,256]{1,0:T(8,128)(2,1)S(1)}, f32[2,2,1024]{2,1,0:T(2,128)S(1)}) custom-call(bf16[912,256]{1,0:T(8,128)(2,1)S(1)} %compare_convert_fusion.hot_ref.refs_0_, bf16[256,2304]{1,0:T(8,128)(2,1)S(1)} %copy-done.2, ...), custom_call_target="tpu_custom_call" | custom-call | flops 2097152 | bytes 65536 | tf_op jit(solution)/shard_map/attend/pallas_call | solution.py:824
  85.5 14.4 %attend.4 = (bf16[912,256]{1,0:T(8,128)(2,1)S(1)}, bf16[912,256]{1,0:T(8,128)(2,1)S(1)}, bf16[912,256]{1,0:T(8,128)(2,1)S(1)}, bf16[912,256]{1,0:T(8,128)(2,1)S(1)}, f32[2,2,1024]{2,1,0:T(2,128)S(1)}) custom-call(bf16[912,256]{1,0:T(8,128)(2,1)S(1)} %compare_convert_fusion.hot_ref.refs_0_, bf16[256,2304]{1,0:T(8,128)(2,1)S(1)} %copy-done.2, ...), custom_call_target="tpu_custom_call" | custom-call | flops 2097152 | bytes 65536 | tf_op jit(solution)/shard_map/attend/pallas_call | solution.py:824
  101.5 14.4 %attend.3 = (bf16[912,256]{1,0:T(8,128)(2,1)S(1)}, bf16[912,256]{1,0:T(8,128)(2,1)S(1)}, bf16[912,256]{1,0:T(8,128)(2,1)S(1)}, bf16[912,256]{1,0:T(8,128)(2,1)S(1)}, f32[2,2,1024]{2,1,0:T(2,128)S(1)}) custom-call(bf16[912,256]{1,0:T(8,128)(2,1)S(1)} %compare_convert_fusion.hot_ref.refs_0_, bf16[256,2304]{1,0:T(8,128)(2,1)S(1)} %copy-done.2, ...), custom_call_target="tpu_custom_call" | custom-call | flops 2097152 | bytes 65536 | tf_op jit(solution)/shard_map/attend/pallas_call | solution.py:824
  124.2 22.6 %feed.1 = (bf16[912,3072]{1,0:T(8,128)(2,1)}, bf16[912,3072]{1,0:T(8,128)(2,1)}, f32[912,768]{1,0:T(8,128)S(1)}) custom-call(s32[32]{0:T(128)S(1)} %broadcast_xor_fusion.place_ref, bf16[912,768]{1,0:T(8,128)(2,1)S(1)} %add_convert_fusion.1.rows_ref, f32[1,3072]{1,0:T(1,128)S(1)} %broadcast_in_dim_reshape.2.bias_ref, bf16[32,224,768]{2,1,0:T(8,128)(2,1)} %bitcast.225), custom_call_target="tpu_custom_call" | custom-call | flops 2151677952 | bytes 65536 | tf_op jit(solution)/shard_map/feed/pallas_call | solution.py:1019
  150.9 3.1 convert_reduce_fusion
  154.1 4.0 convolution_convert_fusion.1
  161.1 18.0 %feed_back.1 = (bf16[912,3072]{1,0:T(8,128)(2,1)}, f32[912,768]{1,0:T(8,128)S(1)}, f32[1,3072]{1,0:T(1,128)S(1)}) custom-call(s32[32]{0:T(128)S(1)} %broadcast_xor_fusion.place_ref, bf16[912,768]{1,0:T(8,128)(2,1)S(1)} %copy-done.5, bf16[912,3072]{1,0:T(8,128)(2,1)} %get-tuple-element.192.slope_ref, bf16[32,224,768]{2,1,0:T(8,128)(2,1)} %bitcast.226), custom_call_target="tpu_custom_call" | custom-call | flops 2151677952 | bytes 65536 | tf_op jit(solution)/shard_map/feed_back/pallas_call | solution.py:1075
  181.0 4.7 fusion.6
  185.7 2.5 convert_add_fusion.1
  190.8 4.0 convolution_convert_fusion
  200.8 2.2 collective-permute-done.11
  207.4 5.2 %convert_add_fusion = f32[1536,768]{1,0:T(8,128)S(1)} fusion(bf16[1536,768]{1,0:T(8,128)(2,1)} %collective-permute-done.10, bf16[912,768]{1,0:T(8,128)(2,1)S(1)} %add_convert_fusion.1.rows_ref, bf16[912,3072]{1,0:T(8,128)(2,1)} %get-tuple-element.201), kind=kOutput, calls=%fused_computation.6 | convolution fusion | flops 2154037248 | bytes 11280384 | tf_op jit(solution)/shard_map/dot_general | solution.py:49
  219.9 2.2 all-gather.7.cloned.1.call-done
  225.9 8.9 %attend_back.6 = (bf16[3,912,128]{2,1,0:T(8,128)(2,1)S(1)}, f32[3,128,128]{2,1,0:T(8,128)S(1)}) custom-call(bf16[128,912]{1,0:T(8,128)(2,1)S(1)} %compare_convert_fusion.1.hot_ref, bf16[912,256]{1,0:T(8,128)(2,1)S(1)} %copy-done.20, bf16[912,256]{1,0:T(8,128)(2,1)S(1)} %copy-done.22, bf16[912,256]{1,0:T(8,128)(2,1)S(1)} %copy-done.24, ...), custom_call_target="tpu_custom_call" | custom-call | flops 1048576 | bytes 65536 | tf_op jit(solution)/shard_map/attend_back/pallas_call | solution.py:916
  234.9 9.3 %attend_back.7 = (bf16[3,912,128]{2,1,0:T(8,128)(2,1)S(1)}, f32[3,128,128]{2,1,0:T(8,128)S(1)}) custom-call(bf16[128,912]{1,0:T(8,128)(2,1)S(1)} %compare_convert_fusion.1.hot_ref, bf16[912,256]{1,0:T(8,128)(2,1)S(1)} %copy-done.20, bf16[912,256]{1,0:T(8,128)(2,1)S(1)} %copy-done.22, bf16[912,256]{1,0:T(8,128)(2,1)S(1)} %copy-done.24, ...), custom_call_target="tpu_custom_call" | custom-call | flops 1048576 | bytes 65536 | tf_op jit(solution)/shard_map/attend_back/pallas_call | solution.py:916
  244.3 2.5 fusion.8
  255.7 2.1 collective-permute-start.19
  258.1 8.9 %attend_back.8 = (bf16[3,912,128]{2,1,0:T(8,128)(2,1)S(1)}, f32[3,128,128]{2,1,0:T(8,128)S(1)}) custom-call(bf16[128,912]{1,0:T(8,128)(2,1)S(1)} %compare_convert_fusion.1.hot_ref, bf16[912,256]{1,0:T(8,128)(2,1)S(1)} %copy-done.14, bf16[912,256]{1,0:T(8,128)(2,1)S(1)} %copy-done.16, bf16[912,256]{1,0:T(8,128)(2,1)S(1)} %copy-done.18, ...), custom_call_target="tpu_custom_call" | custom-call | flops 1048576 | bytes 65536 | tf_op jit(solution)/shard_map/attend_back/pallas_call | solution.py:916
  272.2 8.9 %attend_back.9 = (bf16[3,912,128]{2,1,0:T(8,128)(2,1)S(1)}, f32[3,128,128]{2,1,0:T(8,128)S(1)}) custom-call(bf16[128,912]{1,0:T(8,128)(2,1)S(1)} %compare_convert_fusion.1.hot_ref, bf16[912,256]{1,0:T(8,128)(2,1)S(1)} %copy-done.14, bf16[912,256]{1,0:T(8,128)(2,1)S(1)} %copy-done.16, bf16[912,256]{1,0:T(8,128)(2,1)S(1)} %copy-done.18, ...), custom_call_target="tpu_custom_call" | custom-call | flops 1048576 | bytes 65536 | tf_op jit(solution)/shard_map/attend_back/pallas_call | solution.py:916
  283.0 8.9 %attend_back.10 = (bf16[3,912,128]{2,1,0:T(8,128)(2,1)S(1)}, f32[3,128,128]{2,1,0:T(8,128)S(1)}) custom-call(bf16[128,912]{1,0:T(8,128)(2,1)S(1)} %compare_convert_fusion.1.hot_ref, bf16[912,256]{1,0:T(8,128)(2,1)S(1)} %get-tuple-element.224.q_ref, bf16[912,256]{1,0:T(8,128)(2,1)S(1)} %copy-done.10, bf16[912,256]{1,0:T(8,128)(2,1)S(1)} %copy-done.12, ...), custom_call_target="tpu_custom_call" | custom-call | flops 1048576 | bytes 65536 | tf_op jit(solution)/shard_map/attend_back/pallas_call | solution.py:916
  294.4 9.1 %attend_back.11 = (bf16[3,912,128]{2,1,0:T(8,128)(2,1)S(1)}, f32[3,128,128]{2,1,0:T(8,128)S(1)}) custom-call(bf16[128,912]{1,0:T(8,128)(2,1)S(1)} %compare_convert_fusion.1.hot_ref, bf16[912,256]{1,0:T(8,128)(2,1)S(1)} %get-tuple-element.224.q_ref, bf16[912,256]{1,0:T(8,128)(2,1)S(1)} %copy-done.10, bf16[912,256]{1,0:T(8,128)(2,1)S(1)} %copy-done.12, ...), custom_call_target="tpu_custom_call" | custom-call | flops 1048576 | bytes 65536 | tf_op jit(solution)/shard_map/attend_back/pallas_call | solution.py:916
  313.3 2.4 fusion.61.head_ref
  320.1 11.6 %entry.1 = (f32[912,768]{1,0:T(8,128)}, f32[2,768]{1,0:T(2,128)S(1)}, f32[128,768]{1,0:T(8,128)S(1)}) custom-call(bf16[912,256]{1,0:T(8,128)(2,1)S(1)} %compare_convert_fusion.hot_ref.refs_0_, bf16[128,768]{1,0:T(8,128)(2,1)S(1)} %pad.12.refs_1_, f32[1,768]{1,0:T(1,128)S(1)} %slice.298.refs_2_, f32[912,768]{1,0:T(8,128)} %copy-done.64, ...), custom_call_target="tpu_custom_call" | custom-call | flops 1048576 | bytes 65536 | tf_op jit(solution)/shard_map/entry/pallas_call | solution.py:547
  333.0 3.0 small_grads.1
  338.5 3.0 collective-permute-done.24.core_ref
  344.1 5.3 %dense_step.1 = (f32[384,768]{1,0:T(8,128)}, f32[384,768]{1,0:T(8,128)}, f32[96,768]{1,0:T(8,128)}, f32[384,768]{1,0:T(8,128)}, f32[384,768]{1,0:T(8,128)}, /*in...) custom-call(s32[1]{0:T(128)} %bitcast.7.spot_ref, ...), custom_call_target="tpu_custom_call" | custom-call | flops 1048576 | bytes 65536 | tf_op jit(solution)/shard_map/dense_step/pallas_call | solution.py:681
  349.5 7.8 %collective-permute-done.27 = f32[2,2,86,384]{3,1,2,0:T(2,128)S(1)} collective-permute-done((f32[2,2,86,384]{3,1,2,0:T(2,128)S(1)}, f32[2,2,86,384]{3,1,2,0:T(2,128)S(1)}, u32[]{:S(2)}, u32[]{:S(2)}) %collective-permute-start.27) | collective-permute-done | bytes 528416 | tf_op jit(solution)/shard_map/ppermute | solution.py:103
  360.0 13.8 %collective-permute-done.30 = f32[2,86,384]{2,1,0:T(8,128)S(1)} collective-permute-done((f32[2,86,384]{2,1,0:T(8,128)S(1)}, f32[2,86,384]{2,1,0:T(8,128)S(1)}, u32[]{:S(2)}, u32[]{:S(2)}) %collective-permute-start.30) | collective-permute-done | bytes 264224 | tf_op jit(solution)/shard_map/ppermute | solution.py:103
  377.9 7.8 %collective-permute-done.33 = f32[86,384]{1,0:T(8,128)S(1)} collective-permute-done((f32[86,384]{1,0:T(8,128)S(1)}, f32[86,384]{1,0:T(8,128)S(1)}, u32[]{:S(2)}, u32[]{:S(2)}) %collective-permute-start.33) | collective-permute-done | bytes 132128 | tf_op jit(solution)/shard_map/ppermute | solution.py:103
  386.0 2.9 collective-permute-start.35
  388.9 3.6 collective-permute-done.34
  392.5 2.4 collective-permute-done.35
  396.1 2.9 collective-permute-start.38
  399.0 2.8 collective-permute-done.37
  407.6 6.0 %collective-permute-done.40 = f32[192,256]{1,0:T(8,128)S(1)} collective-permute-done((f32[192,256]{1,0:T(8,128)S(1)}, f32[192,256]{1,0:T(8,128)S(1)}, u32[]{:S(2)}, u32[]{:S(2)}) %collective-permute-start.40) | collective-permute-done | bytes 196640 | tf_op jit(solution)/shard_map/ppermute | solution.py:103
  413.7 5.4 %collective-permute-start.43 = (f32[384,256]{1,0:T(8,128)S(1)}, f32[384,256]{1,0:T(8,128)S(1)}, u32[]{:S(2)}, u32[]{:S(2)}) collective-permute-start(f32[384,256]{1,0:T(8,128)S(1)} %maximum_select_fusion.2), channel_id=1, source_target_pairs={{0,4},{1,5},{2,6},{3,7},{4,0},{5,1},{6,2},{7,3},{8,12},{9,13},{10,... | collective-permute-start | bytes 1179656 | tf_op jit(solution)/shard_map/ppermute | solution.py:103
  423.2 9.2 %collective-permute-done.45 = f32[70,838]{1,0:T(8,128)S(1)} collective-permute-done((f32[70,838]{1,0:T(8,128)S(1)}, f32[70,838]{1,0:T(8,128)S(1)}, u32[]{:S(2)}, u32[]{:S(2)}) %collective-permute-start.45) | collective-permute-done | bytes 234672 | tf_op jit(solution)/shard_map/ppermute | solution.py:103
  433.0 40.0 %newton.1.refs_0_ = bf16[384,768]{1,0:T(8,128)(2,1)} custom-call(f32[768,256]{1,0:T(8,128)S(1)} %maximum_select_fusion.low_ref, f32[768,256]{1,0:T(8,128)S(1)} %maximum_select_fusion.1.high_ref, f32[384,768]{1,0:T(8,128)S(1)} %pad_select_fusion.rows_ref, f32[70,768]{1,0:T(8,128)S(1)} %fusion.14.added_ref, bf16[70,768]{1,0:T(8,128)(2,1)S(1)} %copy-done.28), custom_call_target="tpu_custom_call" | custom-call | flops 27179089920 | bytes 4194304 | tf_op jit(solution)/shard_map/newton/pallas_call | solution.py:439
  473.0 4.9 collective-permute-start.47
  481.6 4.5 collective-permute-done.47.refs_2_
  488.3 3.6 update.1
  (521 shorter events, 138.0 us)
Async XLA Ops:
  7.2 111.7 %all-gather.5.cloned.1.call-start = ((), (), s32[]{:S(2)}) async-start(), calls=%async_computation | async-start | bytes 11354112 | tf_op jit(solution)/shard_map/all_gather | solution.py:1157
  11.1 211.0 %all-gather.7.cloned.1.call-start = ((), (), s32[]{:S(2)}) async-start(), calls=%async_computation.1 | async-start | bytes 3649536 | tf_op jit(solution)/shard_map/all_gather | solution.py:1229
  11.2 6.1 %collective-permute-start = (bf16[1,85,96]{2,1,0:T(8,128)(2,1)S(1)}, bf16[1,85,96]{2,1,0:T(8,128)(2,1)S(1)}, u32[]{:S(2)}, u32[]{:S(2)}) collective-permute-start(bf16[1,85,96]{2,1,0:T(8,128)(2,1)S(1)} %pad_maximum_fusion.17), channel_id=1, source_target_pairs={{0,16},{1,17},{2,18},{3,19},{4,20},{5,21},{6,22},{7,23},{8,24},{9,... | collective-permute-start | bytes 48968 | tf_op jit(solution)/shard_map/ppermute | solution.py:103
  17.3 4.1 collective-permute-start.1
  21.5 5.6 %collective-permute-start.2 = (bf16[4,85,96]{2,1,0:T(8,128)(2,1)S(1)}, bf16[4,85,96]{2,1,0:T(8,128)(2,1)S(1)}, u32[]{:S(2)}, u32[]{:S(2)}) collective-permute-start(bf16[4,85,96]{2,1,0:T(8,128)(2,1)S(1)} %pad_maximum_fusion.14), channel_id=1, source_target_pairs={{0,4},{1,5},{2,6},{3,7},{4,0},{5,1},{6,2},{7,3},{8,12},{9,13},{10,... | collective-permute-start | bytes 195848 | tf_op jit(solution)/shard_map/ppermute | solution.py:103
  31.0 6.0 %collective-permute-start.3 = (f32[1,70,72]{2,1,0:T(8,128)S(1)}, f32[1,70,72]{2,1,0:T(8,128)S(1)}, u32[]{:S(2)}, u32[]{:S(2)}) collective-permute-start(f32[1,70,72]{2,1,0:T(8,128)S(1)} %get-tuple-element.408), channel_id=1, source_target_pairs={{0,16},{1,17},{2,18},{3,19},{4,20},{5,21},{6,22},{7,23},{8,24},{9,... | collective-permute-start | bytes 60488 | tf_op jit(solution)/shard_map/ppermute | solution.py:103
  37.0 7.6 %collective-permute-start.4 = (f32[2,70,72]{2,1,0:T(8,128)S(1)}, f32[2,70,72]{2,1,0:T(8,128)S(1)}, u32[]{:S(2)}, u32[]{:S(2)}) collective-permute-start(f32[2,70,72]{2,1,0:T(8,128)S(1)} %pad_maximum_fusion.15), channel_id=1, source_target_pairs={{0,8},{1,9},{2,10},{3,11},{4,12},{5,13},{6,14},{7,15},{8,0},{9,1},... | collective-permute-start | bytes 120968 | tf_op jit(solution)/shard_map/ppermute | solution.py:103
  44.6 6.8 %collective-permute-start.5 = (f32[4,70,72]{2,1,0:T(8,128)S(1)}, f32[4,70,72]{2,1,0:T(8,128)S(1)}, u32[]{:S(2)}, u32[]{:S(2)}) collective-permute-start(f32[4,70,72]{2,1,0:T(8,128)S(1)} %pad_maximum_fusion.13), channel_id=1, source_target_pairs={{0,4},{1,5},{2,6},{3,7},{4,0},{5,1},{6,2},{7,3},{8,12},{9,13},{10,... | collective-permute-start | bytes 241928 | tf_op jit(solution)/shard_map/ppermute | solution.py:103
  51.4 9.7 %collective-permute-start.6 = (f32[8,70,72]{2,1,0:T(8,128)S(1)}, f32[8,70,72]{2,1,0:T(8,128)S(1)}, u32[]{:S(2)}, u32[]{:S(2)}) collective-permute-start(f32[8,70,72]{2,1,0:T(8,128)S(1)} %pad_maximum_fusion.10), channel_id=1, source_target_pairs={{0,2},{1,3},{2,0},{3,1},{4,6},{5,7},{6,4},{7,5},{8,10},{9,11},{10,... | collective-permute-start | bytes 483848 | tf_op jit(solution)/shard_map/ppermute | solution.py:103
  158.1 27.6 %collective-permute-start.8 = (bf16[1536,768]{1,0:T(8,128)(2,1)}, bf16[1536,768]{1,0:T(8,128)(2,1)}, u32[]{:S(2)}, u32[]{:S(2)}) collective-permute-start(bf16[1536,768]{1,0:T(8,128)(2,1)} %convolution_convert_fusion.1), channel_id=1, source_target_pairs={{0,1},{1,0},{2,3},{3,2},{4,5},{5,4},{6,7},{7,6},{8,9},{9,8},{10,11... | collective-permute-start | bytes 7077896 | tf_op jit(solution)/shard_map/ppermute | solution.py:103
  194.8 12.6 %collective-permute-start.10 = (bf16[1536,768]{1,0:T(8,128)(2,1)}, bf16[1536,768]{1,0:T(8,128)(2,1)}, u32[]{:S(2)}, u32[]{:S(2)}) collective-permute-start(bf16[1536,768]{1,0:T(8,128)(2,1)} %convolution_convert_fusion), channel_id=1, source_target_pairs={{0,1},{1,0},{2,3},{3,2},{4,5},{5,4},{6,7},{7,6},{8,9},{9,8},{10,11... | collective-permute-start | bytes 7077896 | tf_op jit(solution)/shard_map/ppermute | solution.py:103
  204.8 39.4 %collective-permute-start.9 = (bf16[768,384]{1,0:T(8,128)(2,1)}, bf16[768,384]{1,0:T(8,128)(2,1)}, u32[]{:S(2)}, u32[]{:S(2)}) collective-permute-start(bf16[768,384]{1,0:T(8,128)(2,1)} %bitcast.17), channel_id=1, source_target_pairs={{0,4},{1,5},{2,6},{3,7},{4,0},{5,1},{6,2},{7,3},{8,12},{9,13},{10,... | collective-permute-start | bytes 1769480 | tf_op jit(solution)/shard_map/ppermute | solution.py:103
  206.4 37.9 %collective-permute-start.15 = (bf16[768,384]{1,0:T(8,128)(2,1)}, bf16[768,384]{1,0:T(8,128)(2,1)}, u32[]{:S(2)}, u32[]{:S(2)}) collective-permute-start(bf16[768,384]{1,0:T(8,128)(2,1)} %bitcast.19), channel_id=1, source_target_pairs={{0,2},{1,3},{2,0},{3,1},{4,6},{5,7},{6,4},{7,5},{8,10},{9,11},{10,... | collective-permute-start | bytes 1769480 | tf_op jit(solution)/shard_map/ppermute | solution.py:103
  215.9 34.4 %collective-permute-start.14 = (bf16[960,384]{1,0:T(8,128)(2,1)}, bf16[960,384]{1,0:T(8,128)(2,1)}, u32[]{:S(2)}, u32[]{:S(2)}) collective-permute-start(bf16[960,384]{1,0:T(8,128)(2,1)} %pad_maximum_fusion.1), channel_id=1, source_target_pairs={{0,2},{1,3},{2,0},{3,1},{4,6},{5,7},{6,4},{7,5},{8,10},{9,11},{10,... | collective-permute-start | bytes 2211848 | tf_op jit(solution)/shard_map/ppermute | solution.py:103
  217.9 34.5 %collective-permute-start.13 = (bf16[960,384]{1,0:T(8,128)(2,1)}, bf16[960,384]{1,0:T(8,128)(2,1)}, u32[]{:S(2)}, u32[]{:S(2)}) collective-permute-start(bf16[960,384]{1,0:T(8,128)(2,1)} %pad_maximum_fusion), channel_id=1, source_target_pairs={{0,4},{1,5},{2,6},{3,7},{4,0},{5,1},{6,2},{7,3},{8,12},{9,13},{10,... | collective-permute-start | bytes 2211848 | tf_op jit(solution)/shard_map/ppermute | solution.py:103
  248.4 18.7 %collective-permute-start.16 = (bf16[384,384]{1,0:T(8,128)(2,1)}, bf16[384,384]{1,0:T(8,128)(2,1)}, u32[]{:S(2)}, u32[]{:S(2)}) collective-permute-start(bf16[384,384]{1,0:T(8,128)(2,1)} %bitcast.46), channel_id=1, source_target_pairs={{0,4},{1,5},{2,6},{3,7},{4,0},{5,1},{6,2},{7,3},{8,12},{9,13},{10,... | collective-permute-start | bytes 884744 | tf_op jit(solution)/shard_map/ppermute | solution.py:103
  249.5 18.9 %collective-permute-start.12 = (bf16[384,384]{1,0:T(8,128)(2,1)}, bf16[384,384]{1,0:T(8,128)(2,1)}, u32[]{:S(2)}, u32[]{:S(2)}) collective-permute-start(bf16[384,384]{1,0:T(8,128)(2,1)} %bitcast.31), channel_id=1, source_target_pairs={{0,2},{1,3},{2,0},{3,1},{4,6},{5,7},{6,4},{7,5},{8,10},{9,11},{10,... | collective-permute-start | bytes 884744 | tf_op jit(solution)/shard_map/ppermute | solution.py:103
  255.7 15.4 %collective-permute-start.19 = (bf16[480,384]{1,0:T(8,128)(2,1)S(1)}, bf16[480,384]{1,0:T(8,128)(2,1)S(1)}, u32[]{:S(2)}, u32[]{:S(2)}) collective-permute-start(bf16[480,384]{1,0:T(8,128)(2,1)S(1)} %pad_maximum_fusion.8), channel_id=1, source_target_pairs={{0,4},{1,5},{2,6},{3,7},{4,0},{5,1},{6,2},{7,3},{8,12},{9,13},{10,... | collective-permute-start | bytes 1105928 | tf_op jit(solution)/shard_map/ppermute | solution.py:103
  257.9 13.2 %collective-permute-start.18 = (bf16[480,384]{1,0:T(8,128)(2,1)S(1)}, bf16[480,384]{1,0:T(8,128)(2,1)S(1)}, u32[]{:S(2)}, u32[]{:S(2)}) collective-permute-start(bf16[480,384]{1,0:T(8,128)(2,1)S(1)} %pad_maximum_fusion.7), channel_id=1, source_target_pairs={{0,2},{1,3},{2,0},{3,1},{4,6},{5,7},{6,4},{7,5},{8,10},{9,11},{10,... | collective-permute-start | bytes 1105928 | tf_op jit(solution)/shard_map/ppermute | solution.py:103
  269.4 11.8 %collective-permute-start.17 = (bf16[192,768]{1,0:T(8,128)(2,1)S(1)}, bf16[192,768]{1,0:T(8,128)(2,1)S(1)}, u32[]{:S(2)}, u32[]{:S(2)}) collective-permute-start(bf16[192,768]{1,0:T(8,128)(2,1)S(1)} %bitcast.273), channel_id=1, source_target_pairs={{0,8},{1,9},{2,10},{3,11},{4,12},{5,13},{6,14},{7,15},{8,0},{9,1},... | collective-permute-start | bytes 884744 | tf_op jit(solution)/shard_map/ppermute | solution.py:103
  271.6 21.2 %collective-permute-start.21 = (bf16[240,768]{1,0:T(8,128)(2,1)S(1)}, bf16[240,768]{1,0:T(8,128)(2,1)S(1)}, u32[]{:S(2)}, u32[]{:S(2)}) collective-permute-start(bf16[240,768]{1,0:T(8,128)(2,1)S(1)} %pad_maximum_fusion.9), channel_id=1, source_target_pairs={{0,8},{1,9},{2,10},{3,11},{4,12},{5,13},{6,14},{7,15},{8,0},{9,1},... | collective-permute-start | bytes 1105928 | tf_op jit(solution)/shard_map/ppermute | solution.py:103
  281.3 22.4 %collective-permute-start.20 = (bf16[96,768]{1,0:T(8,128)(2,1)S(1)}, bf16[96,768]{1,0:T(8,128)(2,1)S(1)}, u32[]{:S(2)}, u32[]{:S(2)}) collective-permute-start(bf16[96,768]{1,0:T(8,128)(2,1)S(1)} %fusion.38), channel_id=1, source_target_pairs={{0,16},{1,17},{2,18},{3,19},{4,20},{5,21},{6,22},{7,23},{8,24},{9,... | collective-permute-start | bytes 442376 | tf_op jit(solution)/shard_map/ppermute | solution.py:103
  293.0 10.7 %collective-permute-start.22 = (bf16[120,768]{1,0:T(8,128)(2,1)S(1)}, bf16[120,768]{1,0:T(8,128)(2,1)S(1)}, u32[]{:S(2)}, u32[]{:S(2)}) collective-permute-start(bf16[120,768]{1,0:T(8,128)(2,1)S(1)} %pad_maximum_fusion.11), channel_id=1, source_target_pairs={{0,16},{1,17},{2,18},{3,19},{4,20},{5,21},{6,22},{7,23},{8,24},{9,... | collective-permute-start | bytes 552968 | tf_op jit(solution)/shard_map/ppermute | solution.py:103
  304.4 31.7 %collective-permute-start.23 = (f32[216,768]{1,0:T(8,128)S(1)}, f32[216,768]{1,0:T(8,128)S(1)}, u32[]{:S(2)}, u32[]{:S(2)}) collective-permute-start(f32[216,768]{1,0:T(8,128)S(1)} %pad_maximum_fusion.2.own_ref), channel_id=1, source_target_pairs={{0,2},{1,3},{2,0},{3,1},{4,6},{5,7},{6,4},{7,5},{8,10},{9,11},{10,... | collective-permute-start | bytes 1990664 | tf_op jit(solution)/shard_map/ppermute | solution.py:103
  337.8 4.6 collective-permute-start.26
  337.9 3.6 collective-permute-start.24
  338.4 4.1 collective-permute-start.25
  343.1 14.1 %collective-permute-start.27 = (f32[2,2,86,384]{3,1,2,0:T(2,128)S(1)}, f32[2,2,86,384]{3,1,2,0:T(2,128)S(1)}, u32[]{:S(2)}, u32[]{:S(2)}) collective-permute-start(f32[2,2,86,384]{3,1,2,0:T(2,128)S(1)} %bitcast.265), channel_id=1, source_target_pairs={{0,4},{1,5},{2,6},{3,7},{4,0},{5,1},{6,2},{7,3},{8,12},{9,13},{10,... | collective-permute-start | bytes 1585160 | tf_op jit(solution)/shard_map/ppermute | solution.py:103
  357.4 16.4 %collective-permute-start.28 = (f32[384,256]{1,0:T(8,128)S(1)}, f32[384,256]{1,0:T(8,128)S(1)}, u32[]{:S(2)}, u32[]{:S(2)}) collective-permute-start(f32[384,256]{1,0:T(8,128)S(1)} %dynamic-slice_bitcast_fusion.1), channel_id=1, source_target_pairs={{0,4},{1,5},{2,6},{3,7},{4,0},{5,1},{6,2},{7,3},{8,12},{9,13},{10,... | collective-permute-start | bytes 1179656 | tf_op jit(solution)/shard_map/ppermute | solution.py:103
  357.9 15.8 %collective-permute-start.29 = (f32[384,256]{1,0:T(8,128)S(1)}, f32[384,256]{1,0:T(8,128)S(1)}, u32[]{:S(2)}, u32[]{:S(2)}) collective-permute-start(f32[384,256]{1,0:T(8,128)S(1)} %dynamic-slice_bitcast_fusion), channel_id=1, source_target_pairs={{0,8},{1,9},{2,10},{3,11},{4,12},{5,13},{6,14},{7,15},{8,0},{9,1},... | collective-permute-start | bytes 1179656 | tf_op jit(solution)/shard_map/ppermute | solution.py:103
  359.4 14.4 %collective-permute-start.30 = (f32[2,86,384]{2,1,0:T(8,128)S(1)}, f32[2,86,384]{2,1,0:T(8,128)S(1)}, u32[]{:S(2)}, u32[]{:S(2)}) collective-permute-start(f32[2,86,384]{2,1,0:T(8,128)S(1)} %dynamic-slice_bitcast_fusion.2), channel_id=1, source_target_pairs={{0,8},{1,9},{2,10},{3,11},{4,12},{5,13},{6,14},{7,15},{8,0},{9,1},... | collective-permute-start | bytes 792584 | tf_op jit(solution)/shard_map/ppermute | solution.py:103
  374.0 11.6 %collective-permute-start.31 = (f32[192,256]{1,0:T(8,128)S(1)}, f32[192,256]{1,0:T(8,128)S(1)}, u32[]{:S(2)}, u32[]{:S(2)}) collective-permute-start(f32[192,256]{1,0:T(8,128)S(1)} %dynamic-slice_bitcast_fusion.4), channel_id=1, source_target_pairs={{0,8},{1,9},{2,10},{3,11},{4,12},{5,13},{6,14},{7,15},{8,0},{9,1},... | collective-permute-start | bytes 589832 | tf_op jit(solution)/shard_map/ppermute | solution.py:103
  375.6 10.1 %collective-permute-start.32 = (f32[192,256]{1,0:T(8,128)S(1)}, f32[192,256]{1,0:T(8,128)S(1)}, u32[]{:S(2)}, u32[]{:S(2)}) collective-permute-start(f32[192,256]{1,0:T(8,128)S(1)} %dynamic-slice_bitcast_fusion.3), channel_id=1, source_target_pairs={{0,4},{1,5},{2,6},{3,7},{4,0},{5,1},{6,2},{7,3},{8,12},{9,13},{10,... | collective-permute-start | bytes 589832 | tf_op jit(solution)/shard_map/ppermute | solution.py:103
  377.1 8.5 %collective-permute-start.33 = (f32[86,384]{1,0:T(8,128)S(1)}, f32[86,384]{1,0:T(8,128)S(1)}, u32[]{:S(2)}, u32[]{:S(2)}) collective-permute-start(f32[86,384]{1,0:T(8,128)S(1)} %dynamic-slice_bitcast_fusion.5), channel_id=1, source_target_pairs={{0,16},{1,17},{2,18},{3,19},{4,20},{5,21},{6,22},{7,23},{8,24},{9,... | collective-permute-start | bytes 396296 | tf_op jit(solution)/shard_map/ppermute | solution.py:103
  385.8 9.1 %collective-permute-start.36 = (f32[86,384]{1,0:T(8,128)S(1)}, f32[86,384]{1,0:T(8,128)S(1)}, u32[]{:S(2)}, u32[]{:S(2)}) collective-permute-start(f32[86,384]{1,0:T(8,128)S(1)} %bitcast_add_fusion.7), channel_id=1, source_target_pairs={{0,2},{1,3},{2,0},{3,1},{4,6},{5,7},{6,4},{7,5},{8,10},{9,11},{10,... | collective-permute-start | bytes 396296 | tf_op jit(solution)/shard_map/ppermute | solution.py:103
  385.9 6.6 %collective-permute-start.34 = (f32[96,256]{1,0:T(8,128)S(1)}, f32[96,256]{1,0:T(8,128)S(1)}, u32[]{:S(2)}, u32[]{:S(2)}) collective-permute-start(f32[96,256]{1,0:T(8,128)S(1)} %dynamic-slice_bitcast_fusion.7), channel_id=1, source_target_pairs={{0,16},{1,17},{2,18},{3,19},{4,20},{5,21},{6,22},{7,23},{8,24},{9,... | collective-permute-start | bytes 294920 | tf_op jit(solution)/shard_map/ppermute | solution.py:103
  386.0 8.9 %collective-permute-start.35 = (f32[96,256]{1,0:T(8,128)S(1)}, f32[96,256]{1,0:T(8,128)S(1)}, u32[]{:S(2)}, u32[]{:S(2)}) collective-permute-start(f32[96,256]{1,0:T(8,128)S(1)} %dynamic-slice_bitcast_fusion.6), channel_id=1, source_target_pairs={{0,16},{1,17},{2,18},{3,19},{4,20},{5,21},{6,22},{7,23},{8,24},{9,... | collective-permute-start | bytes 294920 | tf_op jit(solution)/shard_map/ppermute | solution.py:103
  396.0 7.8 %collective-permute-start.39 = (f32[70,838]{1,0:T(8,128)S(1)}, f32[70,838]{1,0:T(8,128)S(1)}, u32[]{:S(2)}, u32[]{:S(2)}) collective-permute-start(f32[70,838]{1,0:T(8,128)S(1)} %fusion.15), channel_id=1, source_target_pairs={{0,4},{1,5},{2,6},{3,7},{4,0},{5,1},{6,2},{7,3},{8,12},{9,13},{10,... | collective-permute-start | bytes 703928 | tf_op jit(solution)/shard_map/ppermute | solution.py:103
  396.0 5.8 %collective-permute-start.37 = (f32[96,256]{1,0:T(8,128)S(1)}, f32[96,256]{1,0:T(8,128)S(1)}, u32[]{:S(2)}, u32[]{:S(2)}) collective-permute-start(f32[96,256]{1,0:T(8,128)S(1)} %bitcast_add_fusion.9), channel_id=1, source_target_pairs={{0,16},{1,17},{2,18},{3,19},{4,20},{5,21},{6,22},{7,23},{8,24},{9,... | collective-permute-start | bytes 294920 | tf_op jit(solution)/shard_map/ppermute | solution.py:103
  396.1 7.6 %collective-permute-start.38 = (f32[96,256]{1,0:T(8,128)S(1)}, f32[96,256]{1,0:T(8,128)S(1)}, u32[]{:S(2)}, u32[]{:S(2)}) collective-permute-start(f32[96,256]{1,0:T(8,128)S(1)} %bitcast_add_fusion.8), channel_id=1, source_target_pairs={{0,16},{1,17},{2,18},{3,19},{4,20},{5,21},{6,22},{7,23},{8,24},{9,... | collective-permute-start | bytes 294920 | tf_op jit(solution)/shard_map/ppermute | solution.py:103
  403.8 9.8 %collective-permute-start.42 = (f32[70,838]{1,0:T(8,128)S(1)}, f32[70,838]{1,0:T(8,128)S(1)}, u32[]{:S(2)}, u32[]{:S(2)}) collective-permute-start(f32[70,838]{1,0:T(8,128)S(1)} %add.478), channel_id=1, source_target_pairs={{0,8},{1,9},{2,10},{3,11},{4,12},{5,13},{6,14},{7,15},{8,0},{9,1},... | collective-permute-start | bytes 703928 | tf_op jit(solution)/shard_map/ppermute | solution.py:103
  404.3 9.3 %collective-permute-start.40 = (f32[192,256]{1,0:T(8,128)S(1)}, f32[192,256]{1,0:T(8,128)S(1)}, u32[]{:S(2)}, u32[]{:S(2)}) collective-permute-start(f32[192,256]{1,0:T(8,128)S(1)} %maximum_select_fusion.4), channel_id=1, source_target_pairs={{0,8},{1,9},{2,10},{3,11},{4,12},{5,13},{6,14},{7,15},{8,0},{9,1},... | collective-permute-start | bytes 589832 | tf_op jit(solution)/shard_map/ppermute | solution.py:103
  405.9 7.7 %collective-permute-start.41 = (f32[192,256]{1,0:T(8,128)S(1)}, f32[192,256]{1,0:T(8,128)S(1)}, u32[]{:S(2)}, u32[]{:S(2)}) collective-permute-start(f32[192,256]{1,0:T(8,128)S(1)} %maximum_select_fusion.5), channel_id=1, source_target_pairs={{0,4},{1,5},{2,6},{3,7},{4,0},{5,1},{6,2},{7,3},{8,12},{9,13},{10,... | collective-permute-start | bytes 589832 | tf_op jit(solution)/shard_map/ppermute | solution.py:103
  413.7 18.7 %collective-permute-start.43 = (f32[384,256]{1,0:T(8,128)S(1)}, f32[384,256]{1,0:T(8,128)S(1)}, u32[]{:S(2)}, u32[]{:S(2)}) collective-permute-start(f32[384,256]{1,0:T(8,128)S(1)} %maximum_select_fusion.2), channel_id=1, source_target_pairs={{0,4},{1,5},{2,6},{3,7},{4,0},{5,1},{6,2},{7,3},{8,12},{9,13},{10,... | collective-permute-start | bytes 1179656 | tf_op jit(solution)/shard_map/ppermute | solution.py:103
  419.2 13.3 %collective-permute-start.44 = (f32[384,256]{1,0:T(8,128)S(1)}, f32[384,256]{1,0:T(8,128)S(1)}, u32[]{:S(2)}, u32[]{:S(2)}) collective-permute-start(f32[384,256]{1,0:T(8,128)S(1)} %maximum_select_fusion.3), channel_id=1, source_target_pairs={{0,8},{1,9},{2,10},{3,11},{4,12},{5,13},{6,14},{7,15},{8,0},{9,1},... | collective-permute-start | bytes 1179656 | tf_op jit(solution)/shard_map/ppermute | solution.py:103
  422.5 10.0 %collective-permute-start.45 = (f32[70,838]{1,0:T(8,128)S(1)}, f32[70,838]{1,0:T(8,128)S(1)}, u32[]{:S(2)}, u32[]{:S(2)}) collective-permute-start(f32[70,838]{1,0:T(8,128)S(1)} %add.479), channel_id=1, source_target_pairs={{0,16},{1,17},{2,18},{3,19},{4,20},{5,21},{6,22},{7,23},{8,24},{9,... | collective-permute-start | bytes 703928 | tf_op jit(solution)/shard_map/ppermute | solution.py:103
  473.0 13.1 %collective-permute-start.47 = (bf16[384,768]{1,0:T(8,128)(2,1)}, bf16[384,768]{1,0:T(8,128)(2,1)}, u32[]{:S(2)}, u32[]{:S(2)}) collective-permute-start(bf16[384,768]{1,0:T(8,128)(2,1)} %newton.1.refs_0_), channel_id=1, source_target_pairs={{0,2},{1,3},{2,0},{3,1},{4,6},{5,7},{6,4},{7,5},{8,10},{9,11},{10,... | collective-permute-start | bytes 1769480 | tf_op jit(solution)/shard_map/ppermute | solution.py:103
  478.6 8.7 %collective-permute-start.46 = (bf16[384,768]{1,0:T(8,128)(2,1)}, bf16[384,768]{1,0:T(8,128)(2,1)S(1)}, u32[]{:S(2)}, u32[]{:S(2)}) collective-permute-start(bf16[384,768]{1,0:T(8,128)(2,1)} %newton.1.refs_0_), channel_id=1, source_target_pairs={{0,1},{1,0},{2,3},{3,2},{4,5},{5,4},{6,7},{7,6},{8,9},{9,8},{10,11... | collective-permute-start | bytes 1769480 | tf_op jit(solution)/shard_map/ppermute | solution.py:103
  (121 other events, 1128.5 us)
Sparse Core Ops, SparseCore 0:
  11.5 98.2 all-gather.4
  159.9 62.1 all-gather.6

commit v5 on v4

--- a/solution.py
+++ b/solution.py
@@ -806,13 +806,13 @@
             log_ref[0, pl.ds(head, 1), pl.ds(at, STRIP)] = peak + jnp.log(total)
             return carry
 
-        lax.fori_loop(0, SPAN // STRIP, body, 0)
+        lax.fori_loop(0, SPAN // STRIP, body, 0, unroll=SPAN // STRIP)
         mixed_turned[head_rows, :] = jnp.dot(
             values_head, prob_all[...], preferred_element_type=jnp.float32
         )
         return carry
 
-    lax.fori_loop(0, 2, one_head, 0)
+    lax.fori_loop(0, 2, one_head, 0, unroll=2)
     mixed_ref[...] = mixed_turned[...].T[0:SEQ_LEN, :].astype(jnp.bfloat16)
 
 
@@ -884,7 +884,7 @@
             score_all[:, pl.ds(at, STRIP)] = (prob_rows * (prob_grad - delta)).astype(jnp.bfloat16)
             return carry
 
-        lax.fori_loop(0, SPAN // STRIP, body, 0)
+        lax.fori_loop(0, SPAN // STRIP, body, 0, unroll=SPAN // STRIP)
         value_part = jnp.dot(prob_all[...], grad_all[...], preferred_element_type=jnp.float32)
         key_part = jnp.dot(score_all[...], q_all[...], preferred_element_type=jnp.float32)
         value_sum[...] = jnp.where(lane // HEAD_DIM == head, value_part, value_sum[...])
@@ -895,7 +895,7 @@
         )
         return carry
 
-    lax.fori_loop(0, 2, one_head, 0)
+    lax.fori_loop(0, 2, one_head, 0, unroll=2)
     cosine = cos_ref[...]
     sine_table = -sin_ref[...]
     hot = hot_ref[...]

time: 505 us -> 477 us (0.945)
  Pallas kernels: 208 us -> 171 us
  waiting for transfers between devices: 88.1 us -> 99.6 us
    pallas_call x3, Pallas kernels: 43.4 us -> 24.1 us  [attend_call(): pl.pallas_call(attend_kernel, grid=(count,), in_specs=[pl.BlockSpec(hot.s...]
    pallas_call x6, Pallas kernels: 54.2 us -> 36.8 us  [attend_back_call(): pl.pallas_call(attend_back_kernel, grid=(count,), in_specs=[pl.BlockSpec(...]
    all_gather x1, waiting for transfers between devices: 0.02 us -> 10.2 us  [on_device(): weights_low = lax.all_gather(packed_low[:int(starts[3])], BOTH, axis=0)]
  transfers between devices with their start and end apart: 51 -> 51, of which waited for: 21 -> 24; matrix products, arithmetic and copies ran while one was open for 16% -> 17% of each run, Pallas kernels for 28% -> 22%
where the time goes in v5:
time: 477 us; the launch traced here: 472 us
  Pallas kernels  171 us (36%)
  waiting for transfers between devices  99.6 us (21%)
  starting transfers between devices  59.6 us (12%)
  local copies, waits for them, and re-layouts  59 us (12%)
  matrix products  32.6 us (7%)
  other arithmetic  31.6 us (7%)
  between operations  18.4 us (4%)
    ppermute x49, waiting for transfers between devices, swap(): lax.ppermute(value, BOTH, [(spot, spot ^ mask) for spot in range(total)])  89.3 us
    ppermute x49, starting transfers between devices, swap(): lax.ppermute(value, BOTH, [(spot, spot ^ mask) for spot in range(total)])  59.5 us
    pallas_call x1, Pallas kernels, newton_rows(): pl.pallas_call(newton_kernel, out_shape=jax.ShapeDtypeStruct((count, D),...  40 us
    pallas_call x6, Pallas kernels, attend_back_call(): pl.pallas_call(attend_back_kernel, grid=(count,), in_specs=[pl.BlockSpec(...  36.8 us
    unnamed x239, local copies, waits for them, and re-layouts  24.5 us
    pallas_call x3, Pallas kernels, attend_call(): pl.pallas_call(attend_kernel, grid=(count,), in_specs=[pl.BlockSpec(hot.s...  24.1 us
    pallas_call x1, Pallas kernels, feed_call(): pl.pallas_call(partial(feed_kernel, starts), grid_spec=pltpu.PrefetchScal...  22.4 us
    dot_general x6, matrix products, trans_times(): lax.dot_general(left_side, right_side, (((0,), (0,)), ((), ())), preferre...  22.1 us
  transfers between devices with their start and end apart: 51, of which 24 were waited for; matrix products, arithmetic and copies ran while one was open for 17% of the time, Pallas kernels for 22%

profile of v5, /device:TPU:0, one launch (start us, length us, event | category | flops | bytes accessed | tf_op | source)
XLA Modules:
  0.0 472.3 jit_solution(1864775505254388434)
XLA Ops:
  11.2 4.1 collective-permute-start
  23.3 3.8 collective-permute-done.2
  31.0 3.1 collective-permute-start.3
  46.4 4.9 %collective-permute-done.5 = f32[4,70,72]{2,1,0:T(8,128)S(1)} collective-permute-done((f32[4,70,72]{2,1,0:T(8,128)S(1)}, f32[4,70,72]{2,1,0:T(8,128)S(1)}, u32[]{:S(2)}, u32[]{:S(2)}) %collective-permute-start.5) | collective-permute-done | bytes 80672 | tf_op jit(solution)/shard_map/ppermute | solution.py:103
  54.3 6.8 %collective-permute-done.6 = f32[8,70,72]{2,1,0:T(8,128)S(1)} collective-permute-done((f32[8,70,72]{2,1,0:T(8,128)S(1)}, f32[8,70,72]{2,1,0:T(8,128)S(1)}, u32[]{:S(2)}, u32[]{:S(2)}) %collective-permute-start.6) | collective-permute-done | bytes 161312 | tf_op jit(solution)/shard_map/ppermute | solution.py:103
  65.0 4.6 heads_table.1.tq_ref.tk_ref.tv_ref
  70.9 8.1 %attend.5 = (bf16[912,256]{1,0:T(8,128)(2,1)S(1)}, bf16[912,256]{1,0:T(8,128)(2,1)S(1)}, bf16[912,256]{1,0:T(8,128)(2,1)S(1)}, bf16[912,256]{1,0:T(8,128)(2,1)S(1)}, f32[2,2,1024]{2,1,0:T(2,128)S(1)}) custom-call(bf16[912,256]{1,0:T(8,128)(2,1)S(1)} %compare_convert_fusion.hot_ref.refs_0_, bf16[256,2304]{1,0:T(8,128)(2,1)S(1)} %copy-done.2, ...), custom_call_target="tpu_custom_call" | custom-call | flops 2097152 | bytes 65536 | tf_op jit(solution)/shard_map/attend/pallas_call | solution.py:824
  79.0 7.9 %attend.4 = (bf16[912,256]{1,0:T(8,128)(2,1)S(1)}, bf16[912,256]{1,0:T(8,128)(2,1)S(1)}, bf16[912,256]{1,0:T(8,128)(2,1)S(1)}, bf16[912,256]{1,0:T(8,128)(2,1)S(1)}, f32[2,2,1024]{2,1,0:T(2,128)S(1)}) custom-call(bf16[912,256]{1,0:T(8,128)(2,1)S(1)} %compare_convert_fusion.hot_ref.refs_0_, bf16[256,2304]{1,0:T(8,128)(2,1)S(1)} %copy-done.2, ...), custom_call_target="tpu_custom_call" | custom-call | flops 2097152 | bytes 65536 | tf_op jit(solution)/shard_map/attend/pallas_call | solution.py:824
  88.5 8.1 %attend.3 = (bf16[912,256]{1,0:T(8,128)(2,1)S(1)}, bf16[912,256]{1,0:T(8,128)(2,1)S(1)}, bf16[912,256]{1,0:T(8,128)(2,1)S(1)}, bf16[912,256]{1,0:T(8,128)(2,1)S(1)}, f32[2,2,1024]{2,1,0:T(2,128)S(1)}) custom-call(bf16[912,256]{1,0:T(8,128)(2,1)S(1)} %compare_convert_fusion.hot_ref.refs_0_, bf16[256,2304]{1,0:T(8,128)(2,1)S(1)} %copy-done.2, ...), custom_call_target="tpu_custom_call" | custom-call | flops 2097152 | bytes 65536 | tf_op jit(solution)/shard_map/attend/pallas_call | solution.py:824
  99.6 10.2 %all-gather.5.cloned.1.call-done = bf16[7168,768]{1,0:T(8,128)(2,1)} async-done(((bf16[224,768]{1,0:T(8,128)(2,1)}), bf16[7168,768]{1,0:T(8,128)(2,1)}) %all-gather.5.cloned.1.call-update) | async-done | bytes 11010064 | tf_op jit(solution)/shard_map/all_gather | solution.py:1157
  114.5 22.4 %feed.1 = (bf16[912,3072]{1,0:T(8,128)(2,1)}, bf16[912,3072]{1,0:T(8,128)(2,1)}, f32[912,768]{1,0:T(8,128)S(1)}) custom-call(s32[32]{0:T(128)S(1)} %broadcast_xor_fusion.place_ref, bf16[912,768]{1,0:T(8,128)(2,1)S(1)} %add_convert_fusion.1.rows_ref, f32[1,3072]{1,0:T(1,128)S(1)} %broadcast_in_dim_reshape.2.bias_ref, bf16[32,224,768]{2,1,0:T(8,128)(2,1)} %bitcast.225), custom_call_target="tpu_custom_call" | custom-call | flops 2151677952 | bytes 65536 | tf_op jit(solution)/shard_map/feed/pallas_call | solution.py:1019
  141.1 3.1 convert_reduce_fusion
  144.3 4.4 convolution_convert_fusion.1
  151.8 17.9 %feed_back.1 = (bf16[912,3072]{1,0:T(8,128)(2,1)}, f32[912,768]{1,0:T(8,128)S(1)}, f32[1,3072]{1,0:T(1,128)S(1)}) custom-call(s32[32]{0:T(128)S(1)} %broadcast_xor_fusion.place_ref, bf16[912,768]{1,0:T(8,128)(2,1)S(1)} %copy-done.5, bf16[912,3072]{1,0:T(8,128)(2,1)} %get-tuple-element.192.slope_ref, bf16[32,224,768]{2,1,0:T(8,128)(2,1)} %bitcast.226), custom_call_target="tpu_custom_call" | custom-call | flops 2151677952 | bytes 65536 | tf_op jit(solution)/shard_map/feed_back/pallas_call | solution.py:1075
  171.6 4.7 fusion.6
  176.3 2.5 convert_add_fusion.1
  181.3 4.0 convolution_convert_fusion
  191.4 2.7 collective-permute-done.11
  197.7 5.2 %convert_add_fusion = f32[1536,768]{1,0:T(8,128)S(1)} fusion(bf16[1536,768]{1,0:T(8,128)(2,1)} %collective-permute-done.10, bf16[912,768]{1,0:T(8,128)(2,1)S(1)} %add_convert_fusion.1.rows_ref, bf16[912,3072]{1,0:T(8,128)(2,1)} %get-tuple-element.201), kind=kOutput, calls=%fused_computation.6 | convolution fusion | flops 2154037248 | bytes 11280384 | tf_op jit(solution)/shard_map/dot_general | solution.py:49
  214.8 6.1 %attend_back.6 = (bf16[3,912,128]{2,1,0:T(8,128)(2,1)S(1)}, f32[3,128,128]{2,1,0:T(8,128)S(1)}) custom-call(bf16[128,912]{1,0:T(8,128)(2,1)S(1)} %compare_convert_fusion.1.hot_ref, bf16[912,256]{1,0:T(8,128)(2,1)S(1)} %copy-done.20, bf16[912,256]{1,0:T(8,128)(2,1)S(1)} %copy-done.22, bf16[912,256]{1,0:T(8,128)(2,1)S(1)} %copy-done.24, ...), custom_call_target="tpu_custom_call" | custom-call | flops 1048576 | bytes 65536 | tf_op jit(solution)/shard_map/attend_back/pallas_call | solution.py:916
  220.9 6.3 %attend_back.7 = (bf16[3,912,128]{2,1,0:T(8,128)(2,1)S(1)}, f32[3,128,128]{2,1,0:T(8,128)S(1)}) custom-call(bf16[128,912]{1,0:T(8,128)(2,1)S(1)} %compare_convert_fusion.1.hot_ref, bf16[912,256]{1,0:T(8,128)(2,1)S(1)} %copy-done.20, bf16[912,256]{1,0:T(8,128)(2,1)S(1)} %copy-done.22, bf16[912,256]{1,0:T(8,128)(2,1)S(1)} %copy-done.24, ...), custom_call_target="tpu_custom_call" | custom-call | flops 1048576 | bytes 65536 | tf_op jit(solution)/shard_map/attend_back/pallas_call | solution.py:916
  227.2 2.5 fusion.8
  241.1 6.1 %attend_back.8 = (bf16[3,912,128]{2,1,0:T(8,128)(2,1)S(1)}, f32[3,128,128]{2,1,0:T(8,128)S(1)}) custom-call(bf16[128,912]{1,0:T(8,128)(2,1)S(1)} %compare_convert_fusion.1.hot_ref, bf16[912,256]{1,0:T(8,128)(2,1)S(1)} %copy-done.14, bf16[912,256]{1,0:T(8,128)(2,1)S(1)} %copy-done.16, bf16[912,256]{1,0:T(8,128)(2,1)S(1)} %copy-done.18, ...), custom_call_target="tpu_custom_call" | custom-call | flops 1048576 | bytes 65536 | tf_op jit(solution)/shard_map/attend_back/pallas_call | solution.py:916
  252.9 6.1 %attend_back.9 = (bf16[3,912,128]{2,1,0:T(8,128)(2,1)S(1)}, f32[3,128,128]{2,1,0:T(8,128)S(1)}) custom-call(bf16[128,912]{1,0:T(8,128)(2,1)S(1)} %compare_convert_fusion.1.hot_ref, bf16[912,256]{1,0:T(8,128)(2,1)S(1)} %copy-done.14, bf16[912,256]{1,0:T(8,128)(2,1)S(1)} %copy-done.16, bf16[912,256]{1,0:T(8,128)(2,1)S(1)} %copy-done.18, ...), custom_call_target="tpu_custom_call" | custom-call | flops 1048576 | bytes 65536 | tf_op jit(solution)/shard_map/attend_back/pallas_call | solution.py:916
  262.1 6.1 %attend_back.10 = (bf16[3,912,128]{2,1,0:T(8,128)(2,1)S(1)}, f32[3,128,128]{2,1,0:T(8,128)S(1)}) custom-call(bf16[128,912]{1,0:T(8,128)(2,1)S(1)} %compare_convert_fusion.1.hot_ref, bf16[912,256]{1,0:T(8,128)(2,1)S(1)} %get-tuple-element.224.q_ref, bf16[912,256]{1,0:T(8,128)(2,1)S(1)} %copy-done.10, bf16[912,256]{1,0:T(8,128)(2,1)S(1)} %copy-done.12, ...), custom_call_target="tpu_custom_call" | custom-call | flops 1048576 | bytes 65536 | tf_op jit(solution)/shard_map/attend_back/pallas_call | solution.py:916
  270.3 6.2 %attend_back.11 = (bf16[3,912,128]{2,1,0:T(8,128)(2,1)S(1)}, f32[3,128,128]{2,1,0:T(8,128)S(1)}) custom-call(bf16[128,912]{1,0:T(8,128)(2,1)S(1)} %compare_convert_fusion.1.hot_ref, bf16[912,256]{1,0:T(8,128)(2,1)S(1)} %get-tuple-element.224.q_ref, bf16[912,256]{1,0:T(8,128)(2,1)S(1)} %copy-done.10, bf16[912,256]{1,0:T(8,128)(2,1)S(1)} %copy-done.12, ...), custom_call_target="tpu_custom_call" | custom-call | flops 1048576 | bytes 65536 | tf_op jit(solution)/shard_map/attend_back/pallas_call | solution.py:916
  287.2 2.4 fusion.61.head_ref
  294.0 11.6 %entry.1 = (f32[912,768]{1,0:T(8,128)}, f32[2,768]{1,0:T(2,128)S(1)}, f32[128,768]{1,0:T(8,128)S(1)}) custom-call(bf16[912,256]{1,0:T(8,128)(2,1)S(1)} %compare_convert_fusion.hot_ref.refs_0_, bf16[128,768]{1,0:T(8,128)(2,1)S(1)} %pad.12.refs_1_, f32[1,768]{1,0:T(1,128)S(1)} %slice.298.refs_2_, f32[912,768]{1,0:T(8,128)} %copy-done.64, ...), custom_call_target="tpu_custom_call" | custom-call | flops 1048576 | bytes 65536 | tf_op jit(solution)/shard_map/entry/pallas_call | solution.py:547
  306.9 3.0 small_grads.1
  312.3 3.0 collective-permute-done.24.core_ref
  318.0 5.5 %dense_step.1 = (f32[384,768]{1,0:T(8,128)}, f32[384,768]{1,0:T(8,128)}, f32[96,768]{1,0:T(8,128)}, f32[384,768]{1,0:T(8,128)}, f32[384,768]{1,0:T(8,128)}, /*in...) custom-call(s32[1]{0:T(128)} %bitcast.7.spot_ref, ...), custom_call_target="tpu_custom_call" | custom-call | flops 1048576 | bytes 65536 | tf_op jit(solution)/shard_map/dense_step/pallas_call | solution.py:681
  323.5 7.6 %collective-permute-done.27 = f32[2,2,86,384]{3,1,2,0:T(2,128)S(1)} collective-permute-done((f32[2,2,86,384]{3,1,2,0:T(2,128)S(1)}, f32[2,2,86,384]{3,1,2,0:T(2,128)S(1)}, u32[]{:S(2)}, u32[]{:S(2)}) %collective-permute-start.27) | collective-permute-done | bytes 528416 | tf_op jit(solution)/shard_map/ppermute | solution.py:103
  334.1 13.8 %collective-permute-done.30 = f32[2,86,384]{2,1,0:T(8,128)S(1)} collective-permute-done((f32[2,86,384]{2,1,0:T(8,128)S(1)}, f32[2,86,384]{2,1,0:T(8,128)S(1)}, u32[]{:S(2)}, u32[]{:S(2)}) %collective-permute-start.30) | collective-permute-done | bytes 264224 | tf_op jit(solution)/shard_map/ppermute | solution.py:103
  350.1 2.2 collective-permute-start.33
  352.3 5.3 %collective-permute-done.33 = f32[86,384]{1,0:T(8,128)S(1)} collective-permute-done((f32[86,384]{1,0:T(8,128)S(1)}, f32[86,384]{1,0:T(8,128)S(1)}, u32[]{:S(2)}, u32[]{:S(2)}) %collective-permute-start.33) | collective-permute-done | bytes 132128 | tf_op jit(solution)/shard_map/ppermute | solution.py:103
  361.1 3.3 collective-permute-done.34
  364.4 2.1 collective-permute-done.35
  367.5 2.3 collective-permute-start.39
  369.8 2.9 collective-permute-start.38
  372.8 3.6 collective-permute-done.37
  377.7 2.2 collective-permute-start.42
  380.6 11.0 %collective-permute-done.40 = f32[192,256]{1,0:T(8,128)S(1)} collective-permute-done((f32[192,256]{1,0:T(8,128)S(1)}, f32[192,256]{1,0:T(8,128)S(1)}, u32[]{:S(2)}, u32[]{:S(2)}) %collective-permute-start.40) | collective-permute-done | bytes 196640 | tf_op jit(solution)/shard_map/ppermute | solution.py:103
  396.5 2.3 collective-permute-start.45
  399.0 7.5 %collective-permute-done.45 = f32[70,838]{1,0:T(8,128)S(1)} collective-permute-done((f32[70,838]{1,0:T(8,128)S(1)}, f32[70,838]{1,0:T(8,128)S(1)}, u32[]{:S(2)}, u32[]{:S(2)}) %collective-permute-start.45) | collective-permute-done | bytes 234672 | tf_op jit(solution)/shard_map/ppermute | solution.py:103
  407.0 40.0 %newton.1.refs_0_ = bf16[384,768]{1,0:T(8,128)(2,1)} custom-call(f32[768,256]{1,0:T(8,128)S(1)} %maximum_select_fusion.low_ref, f32[768,256]{1,0:T(8,128)S(1)} %maximum_select_fusion.1.high_ref, f32[384,768]{1,0:T(8,128)S(1)} %pad_select_fusion.rows_ref, f32[70,768]{1,0:T(8,128)S(1)} %fusion.14.added_ref, bf16[70,768]{1,0:T(8,128)(2,1)S(1)} %copy-done.28), custom_call_target="tpu_custom_call" | custom-call | flops 27179089920 | bytes 4194304 | tf_op jit(solution)/shard_map/newton/pallas_call | solution.py:439
  447.1 3.9 collective-permute-start.47
  454.6 4.5 collective-permute-done.47.refs_2_
  461.4 3.6 update.1
  (521 shorter events, 142.3 us)
Async XLA Ops:
  7.2 102.6 %all-gather.5.cloned.1.call-start = ((), (), s32[]{:S(2)}) async-start(), calls=%async_computation | async-start | bytes 11354112 | tf_op jit(solution)/shard_map/all_gather | solution.py:1157
  11.1 199.9 %all-gather.7.cloned.1.call-start = ((), (), s32[]{:S(2)}) async-start(), calls=%async_computation.1 | async-start | bytes 3649536 | tf_op jit(solution)/shard_map/all_gather | solution.py:1229
  11.2 6.1 %collective-permute-start = (bf16[1,85,96]{2,1,0:T(8,128)(2,1)S(1)}, bf16[1,85,96]{2,1,0:T(8,128)(2,1)S(1)}, u32[]{:S(2)}, u32[]{:S(2)}) collective-permute-start(bf16[1,85,96]{2,1,0:T(8,128)(2,1)S(1)} %pad_maximum_fusion.17), channel_id=1, source_target_pairs={{0,16},{1,17},{2,18},{3,19},{4,20},{5,21},{6,22},{7,23},{8,24},{9,... | collective-permute-start | bytes 48968 | tf_op jit(solution)/shard_map/ppermute | solution.py:103
  17.3 4.1 collective-permute-start.1
  21.5 5.6 %collective-permute-start.2 = (bf16[4,85,96]{2,1,0:T(8,128)(2,1)S(1)}, bf16[4,85,96]{2,1,0:T(8,128)(2,1)S(1)}, u32[]{:S(2)}, u32[]{:S(2)}) collective-permute-start(bf16[4,85,96]{2,1,0:T(8,128)(2,1)S(1)} %pad_maximum_fusion.14), channel_id=1, source_target_pairs={{0,4},{1,5},{2,6},{3,7},{4,0},{5,1},{6,2},{7,3},{8,12},{9,13},{10,... | collective-permute-start | bytes 195848 | tf_op jit(solution)/shard_map/ppermute | solution.py:103
  31.0 6.0 %collective-permute-start.3 = (f32[1,70,72]{2,1,0:T(8,128)S(1)}, f32[1,70,72]{2,1,0:T(8,128)S(1)}, u32[]{:S(2)}, u32[]{:S(2)}) collective-permute-start(f32[1,70,72]{2,1,0:T(8,128)S(1)} %get-tuple-element.408), channel_id=1, source_target_pairs={{0,16},{1,17},{2,18},{3,19},{4,20},{5,21},{6,22},{7,23},{8,24},{9,... | collective-permute-start | bytes 60488 | tf_op jit(solution)/shard_map/ppermute | solution.py:103
  37.0 7.6 %collective-permute-start.4 = (f32[2,70,72]{2,1,0:T(8,128)S(1)}, f32[2,70,72]{2,1,0:T(8,128)S(1)}, u32[]{:S(2)}, u32[]{:S(2)}) collective-permute-start(f32[2,70,72]{2,1,0:T(8,128)S(1)} %pad_maximum_fusion.15), channel_id=1, source_target_pairs={{0,8},{1,9},{2,10},{3,11},{4,12},{5,13},{6,14},{7,15},{8,0},{9,1},... | collective-permute-start | bytes 120968 | tf_op jit(solution)/shard_map/ppermute | solution.py:103
  44.6 6.8 %collective-permute-start.5 = (f32[4,70,72]{2,1,0:T(8,128)S(1)}, f32[4,70,72]{2,1,0:T(8,128)S(1)}, u32[]{:S(2)}, u32[]{:S(2)}) collective-permute-start(f32[4,70,72]{2,1,0:T(8,128)S(1)} %pad_maximum_fusion.13), channel_id=1, source_target_pairs={{0,4},{1,5},{2,6},{3,7},{4,0},{5,1},{6,2},{7,3},{8,12},{9,13},{10,... | collective-permute-start | bytes 241928 | tf_op jit(solution)/shard_map/ppermute | solution.py:103
  51.4 9.7 %collective-permute-start.6 = (f32[8,70,72]{2,1,0:T(8,128)S(1)}, f32[8,70,72]{2,1,0:T(8,128)S(1)}, u32[]{:S(2)}, u32[]{:S(2)}) collective-permute-start(f32[8,70,72]{2,1,0:T(8,128)S(1)} %pad_maximum_fusion.10), channel_id=1, source_target_pairs={{0,2},{1,3},{2,0},{3,1},{4,6},{5,7},{6,4},{7,5},{8,10},{9,11},{10,... | collective-permute-start | bytes 483848 | tf_op jit(solution)/shard_map/ppermute | solution.py:103
  148.6 27.6 %collective-permute-start.8 = (bf16[1536,768]{1,0:T(8,128)(2,1)}, bf16[1536,768]{1,0:T(8,128)(2,1)}, u32[]{:S(2)}, u32[]{:S(2)}) collective-permute-start(bf16[1536,768]{1,0:T(8,128)(2,1)} %convolution_convert_fusion.1), channel_id=1, source_target_pairs={{0,1},{1,0},{2,3},{3,2},{4,5},{5,4},{6,7},{7,6},{8,9},{9,8},{10,11... | collective-permute-start | bytes 7077896 | tf_op jit(solution)/shard_map/ppermute | solution.py:103
  185.3 12.3 %collective-permute-start.10 = (bf16[1536,768]{1,0:T(8,128)(2,1)}, bf16[1536,768]{1,0:T(8,128)(2,1)}, u32[]{:S(2)}, u32[]{:S(2)}) collective-permute-start(bf16[1536,768]{1,0:T(8,128)(2,1)} %convolution_convert_fusion), channel_id=1, source_target_pairs={{0,1},{1,0},{2,3},{3,2},{4,5},{5,4},{6,7},{7,6},{8,9},{9,8},{10,11... | collective-permute-start | bytes 7077896 | tf_op jit(solution)/shard_map/ppermute | solution.py:103
  195.9 31.3 %collective-permute-start.9 = (bf16[768,384]{1,0:T(8,128)(2,1)}, bf16[768,384]{1,0:T(8,128)(2,1)}, u32[]{:S(2)}, u32[]{:S(2)}) collective-permute-start(bf16[768,384]{1,0:T(8,128)(2,1)} %bitcast.17), channel_id=1, source_target_pairs={{0,4},{1,5},{2,6},{3,7},{4,0},{5,1},{6,2},{7,3},{8,12},{9,13},{10,... | collective-permute-start | bytes 1769480 | tf_op jit(solution)/shard_map/ppermute | solution.py:103
  197.6 29.5 %collective-permute-start.15 = (bf16[768,384]{1,0:T(8,128)(2,1)}, bf16[768,384]{1,0:T(8,128)(2,1)}, u32[]{:S(2)}, u32[]{:S(2)}) collective-permute-start(bf16[768,384]{1,0:T(8,128)(2,1)} %bitcast.19), channel_id=1, source_target_pairs={{0,2},{1,3},{2,0},{3,1},{4,6},{5,7},{6,4},{7,5},{8,10},{9,11},{10,... | collective-permute-start | bytes 1769480 | tf_op jit(solution)/shard_map/ppermute | solution.py:103
  206.2 26.8 %collective-permute-start.14 = (bf16[960,384]{1,0:T(8,128)(2,1)}, bf16[960,384]{1,0:T(8,128)(2,1)}, u32[]{:S(2)}, u32[]{:S(2)}) collective-permute-start(bf16[960,384]{1,0:T(8,128)(2,1)} %pad_maximum_fusion.1), channel_id=1, source_target_pairs={{0,2},{1,3},{2,0},{3,1},{4,6},{5,7},{6,4},{7,5},{8,10},{9,11},{10,... | collective-permute-start | bytes 2211848 | tf_op jit(solution)/shard_map/ppermute | solution.py:103
  209.2 25.9 %collective-permute-start.13 = (bf16[960,384]{1,0:T(8,128)(2,1)}, bf16[960,384]{1,0:T(8,128)(2,1)}, u32[]{:S(2)}, u32[]{:S(2)}) collective-permute-start(bf16[960,384]{1,0:T(8,128)(2,1)} %pad_maximum_fusion), channel_id=1, source_target_pairs={{0,4},{1,5},{2,6},{3,7},{4,0},{5,1},{6,2},{7,3},{8,12},{9,13},{10,... | collective-permute-start | bytes 2211848 | tf_op jit(solution)/shard_map/ppermute | solution.py:103
  231.3 15.9 %collective-permute-start.16 = (bf16[384,384]{1,0:T(8,128)(2,1)}, bf16[384,384]{1,0:T(8,128)(2,1)}, u32[]{:S(2)}, u32[]{:S(2)}) collective-permute-start(bf16[384,384]{1,0:T(8,128)(2,1)} %bitcast.46), channel_id=1, source_target_pairs={{0,4},{1,5},{2,6},{3,7},{4,0},{5,1},{6,2},{7,3},{8,12},{9,13},{10,... | collective-permute-start | bytes 884744 | tf_op jit(solution)/shard_map/ppermute | solution.py:103
  232.9 15.6 %collective-permute-start.12 = (bf16[384,384]{1,0:T(8,128)(2,1)}, bf16[384,384]{1,0:T(8,128)(2,1)}, u32[]{:S(2)}, u32[]{:S(2)}) collective-permute-start(bf16[384,384]{1,0:T(8,128)(2,1)} %bitcast.31), channel_id=1, source_target_pairs={{0,2},{1,3},{2,0},{3,1},{4,6},{5,7},{6,4},{7,5},{8,10},{9,11},{10,... | collective-permute-start | bytes 884744 | tf_op jit(solution)/shard_map/ppermute | solution.py:103
  238.4 13.4 %collective-permute-start.19 = (bf16[480,384]{1,0:T(8,128)(2,1)S(1)}, bf16[480,384]{1,0:T(8,128)(2,1)S(1)}, u32[]{:S(2)}, u32[]{:S(2)}) collective-permute-start(bf16[480,384]{1,0:T(8,128)(2,1)S(1)} %pad_maximum_fusion.8), channel_id=1, source_target_pairs={{0,4},{1,5},{2,6},{3,7},{4,0},{5,1},{6,2},{7,3},{8,12},{9,13},{10,... | collective-permute-start | bytes 1105928 | tf_op jit(solution)/shard_map/ppermute | solution.py:103
  240.5 11.4 %collective-permute-start.18 = (bf16[480,384]{1,0:T(8,128)(2,1)S(1)}, bf16[480,384]{1,0:T(8,128)(2,1)S(1)}, u32[]{:S(2)}, u32[]{:S(2)}) collective-permute-start(bf16[480,384]{1,0:T(8,128)(2,1)S(1)} %pad_maximum_fusion.7), channel_id=1, source_target_pairs={{0,2},{1,3},{2,0},{3,1},{4,6},{5,7},{6,4},{7,5},{8,10},{9,11},{10,... | collective-permute-start | bytes 1105928 | tf_op jit(solution)/shard_map/ppermute | solution.py:103
  250.0 10.0 %collective-permute-start.17 = (bf16[192,768]{1,0:T(8,128)(2,1)S(1)}, bf16[192,768]{1,0:T(8,128)(2,1)S(1)}, u32[]{:S(2)}, u32[]{:S(2)}) collective-permute-start(bf16[192,768]{1,0:T(8,128)(2,1)S(1)} %bitcast.273), channel_id=1, source_target_pairs={{0,8},{1,9},{2,10},{3,11},{4,12},{5,13},{6,14},{7,15},{8,0},{9,1},... | collective-permute-start | bytes 884744 | tf_op jit(solution)/shard_map/ppermute | solution.py:103
  252.3 16.9 %collective-permute-start.21 = (bf16[240,768]{1,0:T(8,128)(2,1)S(1)}, bf16[240,768]{1,0:T(8,128)(2,1)S(1)}, u32[]{:S(2)}, u32[]{:S(2)}) collective-permute-start(bf16[240,768]{1,0:T(8,128)(2,1)S(1)} %pad_maximum_fusion.9), channel_id=1, source_target_pairs={{0,8},{1,9},{2,10},{3,11},{4,12},{5,13},{6,14},{7,15},{8,0},{9,1},... | collective-permute-start | bytes 1105928 | tf_op jit(solution)/shard_map/ppermute | solution.py:103
  260.1 16.6 %collective-permute-start.20 = (bf16[96,768]{1,0:T(8,128)(2,1)S(1)}, bf16[96,768]{1,0:T(8,128)(2,1)S(1)}, u32[]{:S(2)}, u32[]{:S(2)}) collective-permute-start(bf16[96,768]{1,0:T(8,128)(2,1)S(1)} %fusion.38), channel_id=1, source_target_pairs={{0,16},{1,17},{2,18},{3,19},{4,20},{5,21},{6,22},{7,23},{8,24},{9,... | collective-permute-start | bytes 442376 | tf_op jit(solution)/shard_map/ppermute | solution.py:103
  269.4 9.0 %collective-permute-start.22 = (bf16[120,768]{1,0:T(8,128)(2,1)S(1)}, bf16[120,768]{1,0:T(8,128)(2,1)S(1)}, u32[]{:S(2)}, u32[]{:S(2)}) collective-permute-start(bf16[120,768]{1,0:T(8,128)(2,1)S(1)} %pad_maximum_fusion.11), channel_id=1, source_target_pairs={{0,16},{1,17},{2,18},{3,19},{4,20},{5,21},{6,22},{7,23},{8,24},{9,... | collective-permute-start | bytes 552968 | tf_op jit(solution)/shard_map/ppermute | solution.py:103
  278.6 31.4 %collective-permute-start.23 = (f32[216,768]{1,0:T(8,128)S(1)}, f32[216,768]{1,0:T(8,128)S(1)}, u32[]{:S(2)}, u32[]{:S(2)}) collective-permute-start(f32[216,768]{1,0:T(8,128)S(1)} %pad_maximum_fusion.2.own_ref), channel_id=1, source_target_pairs={{0,2},{1,3},{2,0},{3,1},{4,6},{5,7},{6,4},{7,5},{8,10},{9,11},{10,... | collective-permute-start | bytes 1990664 | tf_op jit(solution)/shard_map/ppermute | solution.py:103
  311.7 4.6 collective-permute-start.26
  311.8 3.6 collective-permute-start.24
  312.3 4.1 collective-permute-start.25
  317.0 14.1 %collective-permute-start.27 = (f32[2,2,86,384]{3,1,2,0:T(2,128)S(1)}, f32[2,2,86,384]{3,1,2,0:T(2,128)S(1)}, u32[]{:S(2)}, u32[]{:S(2)}) collective-permute-start(f32[2,2,86,384]{3,1,2,0:T(2,128)S(1)} %bitcast.265), channel_id=1, source_target_pairs={{0,4},{1,5},{2,6},{3,7},{4,0},{5,1},{6,2},{7,3},{8,12},{9,13},{10,... | collective-permute-start | bytes 1585160 | tf_op jit(solution)/shard_map/ppermute | solution.py:103
  331.3 16.7 %collective-permute-start.28 = (f32[384,256]{1,0:T(8,128)S(1)}, f32[384,256]{1,0:T(8,128)S(1)}, u32[]{:S(2)}, u32[]{:S(2)}) collective-permute-start(f32[384,256]{1,0:T(8,128)S(1)} %dynamic-slice_bitcast_fusion.1), channel_id=1, source_target_pairs={{0,4},{1,5},{2,6},{3,7},{4,0},{5,1},{6,2},{7,3},{8,12},{9,13},{10,... | collective-permute-start | bytes 1179656 | tf_op jit(solution)/shard_map/ppermute | solution.py:103
  332.1 15.8 %collective-permute-start.29 = (f32[384,256]{1,0:T(8,128)S(1)}, f32[384,256]{1,0:T(8,128)S(1)}, u32[]{:S(2)}, u32[]{:S(2)}) collective-permute-start(f32[384,256]{1,0:T(8,128)S(1)} %dynamic-slice_bitcast_fusion), channel_id=1, source_target_pairs={{0,8},{1,9},{2,10},{3,11},{4,12},{5,13},{6,14},{7,15},{8,0},{9,1},... | collective-permute-start | bytes 1179656 | tf_op jit(solution)/shard_map/ppermute | solution.py:103
  332.4 15.6 %collective-permute-start.30 = (f32[2,86,384]{2,1,0:T(8,128)S(1)}, f32[2,86,384]{2,1,0:T(8,128)S(1)}, u32[]{:S(2)}, u32[]{:S(2)}) collective-permute-start(f32[2,86,384]{2,1,0:T(8,128)S(1)} %dynamic-slice_bitcast_fusion.2), channel_id=1, source_target_pairs={{0,8},{1,9},{2,10},{3,11},{4,12},{5,13},{6,14},{7,15},{8,0},{9,1},... | collective-permute-start | bytes 792584 | tf_op jit(solution)/shard_map/ppermute | solution.py:103
  348.2 9.4 %collective-permute-start.31 = (f32[192,256]{1,0:T(8,128)S(1)}, f32[192,256]{1,0:T(8,128)S(1)}, u32[]{:S(2)}, u32[]{:S(2)}) collective-permute-start(f32[192,256]{1,0:T(8,128)S(1)} %dynamic-slice_bitcast_fusion.4), channel_id=1, source_target_pairs={{0,8},{1,9},{2,10},{3,11},{4,12},{5,13},{6,14},{7,15},{8,0},{9,1},... | collective-permute-start | bytes 589832 | tf_op jit(solution)/shard_map/ppermute | solution.py:103
  348.6 9.0 %collective-permute-start.32 = (f32[192,256]{1,0:T(8,128)S(1)}, f32[192,256]{1,0:T(8,128)S(1)}, u32[]{:S(2)}, u32[]{:S(2)}) collective-permute-start(f32[192,256]{1,0:T(8,128)S(1)} %dynamic-slice_bitcast_fusion.3), channel_id=1, source_target_pairs={{0,4},{1,5},{2,6},{3,7},{4,0},{5,1},{6,2},{7,3},{8,12},{9,13},{10,... | collective-permute-start | bytes 589832 | tf_op jit(solution)/shard_map/ppermute | solution.py:103
  350.1 7.5 %collective-permute-start.33 = (f32[86,384]{1,0:T(8,128)S(1)}, f32[86,384]{1,0:T(8,128)S(1)}, u32[]{:S(2)}, u32[]{:S(2)}) collective-permute-start(f32[86,384]{1,0:T(8,128)S(1)} %dynamic-slice_bitcast_fusion.5), channel_id=1, source_target_pairs={{0,16},{1,17},{2,18},{3,19},{4,20},{5,21},{6,22},{7,23},{8,24},{9,... | collective-permute-start | bytes 396296 | tf_op jit(solution)/shard_map/ppermute | solution.py:103
  357.7 8.8 %collective-permute-start.36 = (f32[86,384]{1,0:T(8,128)S(1)}, f32[86,384]{1,0:T(8,128)S(1)}, u32[]{:S(2)}, u32[]{:S(2)}) collective-permute-start(f32[86,384]{1,0:T(8,128)S(1)} %bitcast_add_fusion.7), channel_id=1, source_target_pairs={{0,2},{1,3},{2,0},{3,1},{4,6},{5,7},{6,4},{7,5},{8,10},{9,11},{10,... | collective-permute-start | bytes 396296 | tf_op jit(solution)/shard_map/ppermute | solution.py:103
  358.2 6.2 %collective-permute-start.34 = (f32[96,256]{1,0:T(8,128)S(1)}, f32[96,256]{1,0:T(8,128)S(1)}, u32[]{:S(2)}, u32[]{:S(2)}) collective-permute-start(f32[96,256]{1,0:T(8,128)S(1)} %dynamic-slice_bitcast_fusion.7), channel_id=1, source_target_pairs={{0,16},{1,17},{2,18},{3,19},{4,20},{5,21},{6,22},{7,23},{8,24},{9,... | collective-permute-start | bytes 294920 | tf_op jit(solution)/shard_map/ppermute | solution.py:103
  359.1 7.4 %collective-permute-start.35 = (f32[96,256]{1,0:T(8,128)S(1)}, f32[96,256]{1,0:T(8,128)S(1)}, u32[]{:S(2)}, u32[]{:S(2)}) collective-permute-start(f32[96,256]{1,0:T(8,128)S(1)} %dynamic-slice_bitcast_fusion.6), channel_id=1, source_target_pairs={{0,16},{1,17},{2,18},{3,19},{4,20},{5,21},{6,22},{7,23},{8,24},{9,... | collective-permute-start | bytes 294920 | tf_op jit(solution)/shard_map/ppermute | solution.py:103
  367.5 10.0 %collective-permute-start.39 = (f32[70,838]{1,0:T(8,128)S(1)}, f32[70,838]{1,0:T(8,128)S(1)}, u32[]{:S(2)}, u32[]{:S(2)}) collective-permute-start(f32[70,838]{1,0:T(8,128)S(1)} %fusion.15), channel_id=1, source_target_pairs={{0,4},{1,5},{2,6},{3,7},{4,0},{5,1},{6,2},{7,3},{8,12},{9,13},{10,... | collective-permute-start | bytes 703928 | tf_op jit(solution)/shard_map/ppermute | solution.py:103
  369.8 6.5 %collective-permute-start.37 = (f32[96,256]{1,0:T(8,128)S(1)}, f32[96,256]{1,0:T(8,128)S(1)}, u32[]{:S(2)}, u32[]{:S(2)}) collective-permute-start(f32[96,256]{1,0:T(8,128)S(1)} %bitcast_add_fusion.9), channel_id=1, source_target_pairs={{0,16},{1,17},{2,18},{3,19},{4,20},{5,21},{6,22},{7,23},{8,24},{9,... | collective-permute-start | bytes 294920 | tf_op jit(solution)/shard_map/ppermute | solution.py:103
  369.8 7.8 %collective-permute-start.38 = (f32[96,256]{1,0:T(8,128)S(1)}, f32[96,256]{1,0:T(8,128)S(1)}, u32[]{:S(2)}, u32[]{:S(2)}) collective-permute-start(f32[96,256]{1,0:T(8,128)S(1)} %bitcast_add_fusion.8), channel_id=1, source_target_pairs={{0,16},{1,17},{2,18},{3,19},{4,20},{5,21},{6,22},{7,23},{8,24},{9,... | collective-permute-start | bytes 294920 | tf_op jit(solution)/shard_map/ppermute | solution.py:103
  377.7 14.0 %collective-permute-start.42 = (f32[70,838]{1,0:T(8,128)S(1)}, f32[70,838]{1,0:T(8,128)S(1)}, u32[]{:S(2)}, u32[]{:S(2)}) collective-permute-start(f32[70,838]{1,0:T(8,128)S(1)} %add.478), channel_id=1, source_target_pairs={{0,8},{1,9},{2,10},{3,11},{4,12},{5,13},{6,14},{7,15},{8,0},{9,1},... | collective-permute-start | bytes 703928 | tf_op jit(solution)/shard_map/ppermute | solution.py:103
  379.9 11.7 %collective-permute-start.40 = (f32[192,256]{1,0:T(8,128)S(1)}, f32[192,256]{1,0:T(8,128)S(1)}, u32[]{:S(2)}, u32[]{:S(2)}) collective-permute-start(f32[192,256]{1,0:T(8,128)S(1)} %maximum_select_fusion.4), channel_id=1, source_target_pairs={{0,8},{1,9},{2,10},{3,11},{4,12},{5,13},{6,14},{7,15},{8,0},{9,1},... | collective-permute-start | bytes 589832 | tf_op jit(solution)/shard_map/ppermute | solution.py:103
  380.0 11.7 %collective-permute-start.41 = (f32[192,256]{1,0:T(8,128)S(1)}, f32[192,256]{1,0:T(8,128)S(1)}, u32[]{:S(2)}, u32[]{:S(2)}) collective-permute-start(f32[192,256]{1,0:T(8,128)S(1)} %maximum_select_fusion.5), channel_id=1, source_target_pairs={{0,4},{1,5},{2,6},{3,7},{4,0},{5,1},{6,2},{7,3},{8,12},{9,13},{10,... | collective-permute-start | bytes 589832 | tf_op jit(solution)/shard_map/ppermute | solution.py:103
  391.8 14.7 %collective-permute-start.43 = (f32[384,256]{1,0:T(8,128)S(1)}, f32[384,256]{1,0:T(8,128)S(1)}, u32[]{:S(2)}, u32[]{:S(2)}) collective-permute-start(f32[384,256]{1,0:T(8,128)S(1)} %maximum_select_fusion.2), channel_id=1, source_target_pairs={{0,4},{1,5},{2,6},{3,7},{4,0},{5,1},{6,2},{7,3},{8,12},{9,13},{10,... | collective-permute-start | bytes 1179656 | tf_op jit(solution)/shard_map/ppermute | solution.py:103
  392.2 14.4 %collective-permute-start.44 = (f32[384,256]{1,0:T(8,128)S(1)}, f32[384,256]{1,0:T(8,128)S(1)}, u32[]{:S(2)}, u32[]{:S(2)}) collective-permute-start(f32[384,256]{1,0:T(8,128)S(1)} %maximum_select_fusion.3), channel_id=1, source_target_pairs={{0,8},{1,9},{2,10},{3,11},{4,12},{5,13},{6,14},{7,15},{8,0},{9,1},... | collective-permute-start | bytes 1179656 | tf_op jit(solution)/shard_map/ppermute | solution.py:103
  396.5 10.0 %collective-permute-start.45 = (f32[70,838]{1,0:T(8,128)S(1)}, f32[70,838]{1,0:T(8,128)S(1)}, u32[]{:S(2)}, u32[]{:S(2)}) collective-permute-start(f32[70,838]{1,0:T(8,128)S(1)} %add.479), channel_id=1, source_target_pairs={{0,16},{1,17},{2,18},{3,19},{4,20},{5,21},{6,22},{7,23},{8,24},{9,... | collective-permute-start | bytes 703928 | tf_op jit(solution)/shard_map/ppermute | solution.py:103
  447.1 12.0 %collective-permute-start.47 = (bf16[384,768]{1,0:T(8,128)(2,1)}, bf16[384,768]{1,0:T(8,128)(2,1)}, u32[]{:S(2)}, u32[]{:S(2)}) collective-permute-start(bf16[384,768]{1,0:T(8,128)(2,1)} %newton.1.refs_0_), channel_id=1, source_target_pairs={{0,2},{1,3},{2,0},{3,1},{4,6},{5,7},{6,4},{7,5},{8,10},{9,11},{10,... | collective-permute-start | bytes 1769480 | tf_op jit(solution)/shard_map/ppermute | solution.py:103
  451.7 8.7 %collective-permute-start.46 = (bf16[384,768]{1,0:T(8,128)(2,1)}, bf16[384,768]{1,0:T(8,128)(2,1)S(1)}, u32[]{:S(2)}, u32[]{:S(2)}) collective-permute-start(bf16[384,768]{1,0:T(8,128)(2,1)} %newton.1.refs_0_), channel_id=1, source_target_pairs={{0,1},{1,0},{2,3},{3,2},{4,5},{5,4},{6,7},{7,6},{8,9},{9,8},{10,11... | collective-permute-start | bytes 1769480 | tf_op jit(solution)/shard_map/ppermute | solution.py:103
  (121 other events, 1097.9 us)
Sparse Core Ops, SparseCore 0:
  11.5 98.2 all-gather.4
  150.6 60.3 all-gather.6

commit v6 on v5

--- a/solution.py
+++ b/solution.py
@@ -86,6 +86,7 @@
 SPAN = 1024
 STRIP = 256
 PARTS = 4
+FEED_STRIP = 304
 BLOCK = 96
 PART_BLOCKS = D // BLOCK
 LANES = 128
@@ -455,34 +456,35 @@
 
 
 def pack_kernel(spot_ref, *refs):
-    out_ref = refs[-1]
+    *refs, last_ref, out_ref, last_out_ref = refs
     at = 0
-    for ref in refs[:-1]:
+    for number, ref in enumerate(refs):
         count = ref.shape[0]
         out_ref[at : at + count, :] = ref[...].astype(jnp.bfloat16)
-        at += count
-        room = -count % 16
-        if room:
-            out_ref[at : at + room, :] = jnp.zeros((room, D), jnp.bfloat16)
-            at += room
+        at += count + (-count % 16 if number + 1 < len(refs) else 0)
+    last_out_ref[...] = last_ref[...].astype(jnp.bfloat16)
 
 
 def pack_rows(weights, spot):
     units = [weight.shape[0] // lax.axis_size("narrow") for weight in weights]
-    total = sum(unit + -unit % 16 for unit in units)
-    if any(unit % 8 for unit in units):
-        return jnp.concatenate(
-            [padded_rows(quarter_rows(weight).astype(jnp.bfloat16)) for weight in weights], axis=0
-        )
+    if any(unit % 8 for unit in units) or any(unit % 16 for unit in units[:-2]):
+        rows = [quarter_rows(weight).astype(jnp.bfloat16) for weight in weights]
+        return jnp.concatenate([padded_rows(row) for row in rows[:-2]] + rows[-2:-1], axis=0), rows[-1]
     return pl.pallas_call(
         pack_kernel,
         grid_spec=pltpu.PrefetchScalarGridSpec(
             num_scalar_prefetch=1,
             grid=(1,),
             in_specs=[pl.BlockSpec((unit, D), lambda step, spot: (spot[0], 0)) for unit in units],
-            out_specs=pl.BlockSpec((total, D), lambda step, spot: (0, 0)),
+            out_specs=[
+                pl.BlockSpec((sum(units[:-1]), D), lambda step, spot: (0, 0)),
+                pl.BlockSpec((units[-1], D), lambda step, spot: (0, 0)),
+            ],
         ),
-        out_shape=jax.ShapeDtypeStruct((total, D), jnp.bfloat16),
+        out_shape=[
+            jax.ShapeDtypeStruct((sum(units[:-1]), D), jnp.bfloat16),
+            jax.ShapeDtypeStruct((units[-1], D), jnp.bfloat16),
+        ],
         name="pack",
     )(spot[None].astype(jnp.int32), *weights)
 
@@ -998,20 +1000,17 @@
         start_parts(place_ref, source_ref, starts, held, sems)
 
     expand = wait_part(source_ref, 0, held, sems, step)
-    for at in range(0, SEQ_LEN, 304):
-        spot = slice(at, at + 304)
+    reduce = wait_part(source_ref, 1, held, sems, step)
+    for at in range(0, SEQ_LEN, FEED_STRIP):
+        spot = slice(at, at + FEED_STRIP)
         values = row_dot(rows_ref[spot, :], expand) + bias_ref[...]
         below, bell = normal_parts(values)
-        hidden_ref[spot, :] = (values * below).astype(jnp.bfloat16)
+        hidden = (values * below).astype(jnp.bfloat16)
+        hidden_ref[spot, :] = hidden
         slope_ref[spot, :] = (below + values * bell).astype(jnp.bfloat16)
-    reduce = wait_part(source_ref, 1, held, sems, step)
-    part = jnp.dot(hidden_ref[...], reduce, preferred_element_type=jnp.float32)
-    @pl.when(step == 0)
-    def _():
-        out_ref[...] = part
-    @pl.when(step > 0)
-    def _():
-        out_ref[...] += part
+        part = jnp.dot(hidden, reduce, preferred_element_type=jnp.float32)
+        out_ref[spot, :] = jnp.where(step == 0, 0.0, out_ref[spot, :]) + part
+
 
 def feed_call(place, rows, bias, source, starts):
     whole = lambda step, place: (0, 0)
@@ -1051,23 +1050,18 @@
         start_parts(place_ref, source_ref, starts, held, sems)
 
     reduce = wait_part(source_ref, 1, held, sems, step)
+    expand = wait_part(source_ref, 0, held, sems, step)
     total = jnp.zeros((1, D), jnp.float32)
-    for at in range(0, SEQ_LEN, 304):
-        spot = slice(at, at + 304)
+    for at in range(0, SEQ_LEN, SEQ_LEN):
+        spot = slice(at, at + SEQ_LEN)
         grad = row_dot(grad_ref[spot, :], reduce) * slope_ref[spot, :].astype(jnp.float32)
         low = grad.astype(jnp.bfloat16)
         pre_ref[spot, :] = low
         total = total + jnp.sum(low.astype(jnp.float32), axis=0, keepdims=True)
+        part = jnp.dot(low, expand, preferred_element_type=jnp.float32)
+        out_ref[spot, :] = jnp.where(step == 0, 0.0, out_ref[spot, :]) + part
     bias_ref[...] = total
-    low = pre_ref[...]
-    expand = wait_part(source_ref, 0, held, sems, step)
-    part = jnp.dot(low, expand, preferred_element_type=jnp.float32)
-    @pl.when(step == 0)
-    def _():
-        out_ref[...] = part
-    @pl.when(step > 0)
-    def _():
-        out_ref[...] += part
+
 
 def feed_back_call(place, grad, slope, source, starts):
     whole = lambda step, place: (0, 0)
@@ -1153,9 +1147,8 @@
     packed = (expand_weight, reduce_weight, mixing_weight, attend_weight)
     units = [weight.shape[0] // narrow_size for weight in packed]
     starts = np.cumsum([0] + [unit + -unit % 16 for unit in units])
-    packed_low = pack_rows(packed, lax.axis_index("narrow"))
-    weights_low = lax.all_gather(packed_low[: int(starts[3])], BOTH, axis=0)
-    attend_own = packed_low[int(starts[3]) : int(starts[3]) + units[3]]
+    packed_low, attend_own = pack_rows(packed, lax.axis_index("narrow"))
+    weights_low = lax.all_gather(packed_low, BOTH, axis=0)
 
     def weight_rows(number, unit):
         start = int(starts[number])

time: 477 us -> 474 us (level)
  waiting for transfers between devices: 99.6 us -> 106 us
    all_gather x1, waiting for transfers between devices: 0.04 us -> 6.06 us  [on_device(): attend_low = lax.all_gather(gate(attend_own, mixed_low), BOTH, axis=0)]
    unnamed x239 -> x241, local copies, waits for them, and re-layouts: 24.5 us -> 24.4 us
  transfers between devices with their start and end apart: 51 -> 51, of which waited for: 24 -> 25; matrix products, arithmetic and copies ran while one was open for 17% -> 16% of each run, Pallas kernels for 22% -> 21%
where the time goes in v6:
time: 474 us; the launch traced here: 469 us
  Pallas kernels  167 us (35%)
  waiting for transfers between devices  106 us (22%)
  starting transfers between devices  59.1 us (12%)
  local copies, waits for them, and re-layouts  55.6 us (12%)
  other arithmetic  31.8 us (7%)
  matrix products  31.3 us (7%)
  between operations  18.4 us (4%)
    ppermute x49, waiting for transfers between devices, swap(): lax.ppermute(value, BOTH, [(spot, spot ^ mask) for spot in range(total)])  91 us
    ppermute x49, starting transfers between devices, swap(): lax.ppermute(value, BOTH, [(spot, spot ^ mask) for spot in range(total)])  59 us
    pallas_call x1, Pallas kernels, newton_rows(): pl.pallas_call(newton_kernel, out_shape=jax.ShapeDtypeStruct((count, D),...  40 us
    pallas_call x6, Pallas kernels, attend_back_call(): pl.pallas_call(attend_back_kernel, grid=(count,), in_specs=[pl.BlockSpec(...  36.8 us
    unnamed x241, local copies, waits for them, and re-layouts  24.4 us
    pallas_call x3, Pallas kernels, attend_call(): pl.pallas_call(attend_kernel, grid=(count,), in_specs=[pl.BlockSpec(hot.s...  24.1 us
    dot_general x6, matrix products, trans_times(): lax.dot_general(left_side, right_side, (((0,), (0,)), ((), ())), preferre...  21.7 us
    pallas_call x1, Pallas kernels, feed_call(): pl.pallas_call(partial(feed_kernel, starts), grid_spec=pltpu.PrefetchScal...  20.7 us
  transfers between devices with their start and end apart: 51, of which 25 were waited for; matrix products, arithmetic and copies ran while one was open for 16% of the time, Pallas kernels for 21%

profile of v6, /device:TPU:0, one launch (start us, length us, event | category | flops | bytes accessed | tf_op | source)
XLA Modules:
  0.0 469.3 jit_solution(4296952012253787757)
XLA Ops:
  9.4 4.1 collective-permute-start
  21.5 2.8 collective-permute-done.2
  27.3 2.7 collective-permute-start.3
  42.5 5.0 %collective-permute-done.5 = f32[4,70,72]{2,1,0:T(8,128)S(1)} collective-permute-done((f32[4,70,72]{2,1,0:T(8,128)S(1)}, f32[4,70,72]{2,1,0:T(8,128)S(1)}, u32[]{:S(2)}, u32[]{:S(2)}) %collective-permute-start.5) | collective-permute-done | bytes 80672 | tf_op jit(solution)/shard_map/ppermute | solution.py:104
  51.0 7.4 %collective-permute-done.6 = f32[8,70,72]{2,1,0:T(8,128)S(1)} collective-permute-done((f32[8,70,72]{2,1,0:T(8,128)S(1)}, f32[8,70,72]{2,1,0:T(8,128)S(1)}, u32[]{:S(2)}, u32[]{:S(2)}) %collective-permute-start.6) | collective-permute-done | bytes 161312 | tf_op jit(solution)/shard_map/ppermute | solution.py:104
  62.3 4.6 heads_table.1.tq_ref.tk_ref.tv_ref
  68.2 8.1 %attend.5 = (bf16[912,256]{1,0:T(8,128)(2,1)S(1)}, bf16[912,256]{1,0:T(8,128)(2,1)S(1)}, bf16[912,256]{1,0:T(8,128)(2,1)S(1)}, bf16[912,256]{1,0:T(8,128)(2,1)S(1)}, f32[2,2,1024]{2,1,0:T(2,128)S(1)}) custom-call(bf16[912,256]{1,0:T(8,128)(2,1)S(1)} %compare_convert_fusion.hot_ref.refs_0_, bf16[256,2304]{1,0:T(8,128)(2,1)S(1)} %copy-done.2, ...), custom_call_target="tpu_custom_call" | custom-call | flops 2097152 | bytes 65536 | tf_op jit(solution)/shard_map/attend/pallas_call | solution.py:826
  76.3 7.9 %attend.4 = (bf16[912,256]{1,0:T(8,128)(2,1)S(1)}, bf16[912,256]{1,0:T(8,128)(2,1)S(1)}, bf16[912,256]{1,0:T(8,128)(2,1)S(1)}, bf16[912,256]{1,0:T(8,128)(2,1)S(1)}, f32[2,2,1024]{2,1,0:T(2,128)S(1)}) custom-call(bf16[912,256]{1,0:T(8,128)(2,1)S(1)} %compare_convert_fusion.hot_ref.refs_0_, bf16[256,2304]{1,0:T(8,128)(2,1)S(1)} %copy-done.2, ...), custom_call_target="tpu_custom_call" | custom-call | flops 2097152 | bytes 65536 | tf_op jit(solution)/shard_map/attend/pallas_call | solution.py:826
  85.8 8.1 %attend.3 = (bf16[912,256]{1,0:T(8,128)(2,1)S(1)}, bf16[912,256]{1,0:T(8,128)(2,1)S(1)}, bf16[912,256]{1,0:T(8,128)(2,1)S(1)}, bf16[912,256]{1,0:T(8,128)(2,1)S(1)}, f32[2,2,1024]{2,1,0:T(2,128)S(1)}) custom-call(bf16[912,256]{1,0:T(8,128)(2,1)S(1)} %compare_convert_fusion.hot_ref.refs_0_, bf16[256,2304]{1,0:T(8,128)(2,1)S(1)} %copy-done.2, ...), custom_call_target="tpu_custom_call" | custom-call | flops 2097152 | bytes 65536 | tf_op jit(solution)/shard_map/attend/pallas_call | solution.py:826
  96.9 9.2 %all-gather.5.cloned.1.call-done = bf16[6912,768]{1,0:T(8,128)(2,1)} async-done(((bf16[216,768]{1,0:T(8,128)(2,1)}), bf16[6912,768]{1,0:T(8,128)(2,1)}) %all-gather.5.cloned.1.call-update) | async-done | bytes 10616848 | tf_op jit(solution)/shard_map/all_gather | solution.py:1151
  110.8 20.7 %feed.1 = (bf16[912,3072]{1,0:T(8,128)(2,1)}, bf16[912,3072]{1,0:T(8,128)(2,1)}, f32[912,768]{1,0:T(8,128)S(1)}) custom-call(s32[32]{0:T(128)S(1)} %broadcast_xor_fusion.place_ref, bf16[912,768]{1,0:T(8,128)(2,1)S(1)} %add_convert_fusion.1.rows_ref, f32[1,3072]{1,0:T(1,128)S(1)} %broadcast_in_dim_reshape.2.bias_ref, bf16[32,216,768]{2,1,0:T(8,128)(2,1)} %bitcast.226), custom_call_target="tpu_custom_call" | custom-call | flops 2151677952 | bytes 65536 | tf_op jit(solution)/shard_map/feed/pallas_call | solution.py:1018
  135.7 3.1 convert_reduce_fusion
  138.9 4.0 convolution_convert_fusion.1
  144.5 14.8 %feed_back.1 = (bf16[912,3072]{1,0:T(8,128)(2,1)}, f32[912,768]{1,0:T(8,128)S(1)}, f32[1,3072]{1,0:T(1,128)S(1)}) custom-call(s32[32]{0:T(128)S(1)} %broadcast_xor_fusion.place_ref, bf16[912,768]{1,0:T(8,128)(2,1)S(1)} %copy-done.5, bf16[912,3072]{1,0:T(8,128)(2,1)} %get-tuple-element.196.slope_ref, bf16[32,216,768]{2,1,0:T(8,128)(2,1)} %bitcast.227), custom_call_target="tpu_custom_call" | custom-call | flops 2151677952 | bytes 65536 | tf_op jit(solution)/shard_map/feed_back/pallas_call | solution.py:1069
  161.2 4.7 fusion.6
  165.9 2.6 convert_add_fusion.1
  171.1 4.0 convolution_convert_fusion
  187.0 5.2 %convert_add_fusion = f32[1536,768]{1,0:T(8,128)S(1)} fusion(bf16[1536,768]{1,0:T(8,128)(2,1)} %collective-permute-done.10, bf16[912,768]{1,0:T(8,128)(2,1)S(1)} %add_convert_fusion.1.rows_ref, bf16[912,3072]{1,0:T(8,128)(2,1)} %get-tuple-element.205), kind=kOutput, calls=%fused_computation.6 | convolution fusion | flops 2154037248 | bytes 11280384 | tf_op jit(solution)/shard_map/dot_general | solution.py:49
  200.1 6.1 %all-gather.7.cloned.1.call-done = bf16[2304,768]{1,0:T(8,128)(2,1)} async-done(((bf16[72,768]{1,0:T(8,128)(2,1)}), bf16[2304,768]{1,0:T(8,128)(2,1)}) %all-gather.7.cloned.1.call-update) | async-done | bytes 3538960 | tf_op jit(solution)/shard_map/all_gather | solution.py:1222
  210.0 6.1 %attend_back.6 = (bf16[3,912,128]{2,1,0:T(8,128)(2,1)S(1)}, f32[3,128,128]{2,1,0:T(8,128)S(1)}) custom-call(bf16[128,912]{1,0:T(8,128)(2,1)S(1)} %compare_convert_fusion.1.hot_ref, bf16[912,256]{1,0:T(8,128)(2,1)S(1)} %copy-done.20, bf16[912,256]{1,0:T(8,128)(2,1)S(1)} %copy-done.22, bf16[912,256]{1,0:T(8,128)(2,1)S(1)} %copy-done.24, ...), custom_call_target="tpu_custom_call" | custom-call | flops 1048576 | bytes 65536 | tf_op jit(solution)/shard_map/attend_back/pallas_call | solution.py:918
  216.1 6.3 %attend_back.7 = (bf16[3,912,128]{2,1,0:T(8,128)(2,1)S(1)}, f32[3,128,128]{2,1,0:T(8,128)S(1)}) custom-call(bf16[128,912]{1,0:T(8,128)(2,1)S(1)} %compare_convert_fusion.1.hot_ref, bf16[912,256]{1,0:T(8,128)(2,1)S(1)} %copy-done.20, bf16[912,256]{1,0:T(8,128)(2,1)S(1)} %copy-done.22, bf16[912,256]{1,0:T(8,128)(2,1)S(1)} %copy-done.24, ...), custom_call_target="tpu_custom_call" | custom-call | flops 1048576 | bytes 65536 | tf_op jit(solution)/shard_map/attend_back/pallas_call | solution.py:918
  222.4 2.5 fusion.8
  236.4 6.1 %attend_back.8 = (bf16[3,912,128]{2,1,0:T(8,128)(2,1)S(1)}, f32[3,128,128]{2,1,0:T(8,128)S(1)}) custom-call(bf16[128,912]{1,0:T(8,128)(2,1)S(1)} %compare_convert_fusion.1.hot_ref, bf16[912,256]{1,0:T(8,128)(2,1)S(1)} %copy-done.14, bf16[912,256]{1,0:T(8,128)(2,1)S(1)} %copy-done.16, bf16[912,256]{1,0:T(8,128)(2,1)S(1)} %copy-done.18, ...), custom_call_target="tpu_custom_call" | custom-call | flops 1048576 | bytes 65536 | tf_op jit(solution)/shard_map/attend_back/pallas_call | solution.py:918
  245.2 3.0 collective-permute-start.17
  249.3 6.1 %attend_back.9 = (bf16[3,912,128]{2,1,0:T(8,128)(2,1)S(1)}, f32[3,128,128]{2,1,0:T(8,128)S(1)}) custom-call(bf16[128,912]{1,0:T(8,128)(2,1)S(1)} %compare_convert_fusion.1.hot_ref, bf16[912,256]{1,0:T(8,128)(2,1)S(1)} %copy-done.14, bf16[912,256]{1,0:T(8,128)(2,1)S(1)} %copy-done.16, bf16[912,256]{1,0:T(8,128)(2,1)S(1)} %copy-done.18, ...), custom_call_target="tpu_custom_call" | custom-call | flops 1048576 | bytes 65536 | tf_op jit(solution)/shard_map/attend_back/pallas_call | solution.py:918
  256.2 2.3 collective-permute-start.20
  258.5 6.1 %attend_back.10 = (bf16[3,912,128]{2,1,0:T(8,128)(2,1)S(1)}, f32[3,128,128]{2,1,0:T(8,128)S(1)}) custom-call(bf16[128,912]{1,0:T(8,128)(2,1)S(1)} %compare_convert_fusion.1.hot_ref, bf16[912,256]{1,0:T(8,128)(2,1)S(1)} %get-tuple-element.228.q_ref, bf16[912,256]{1,0:T(8,128)(2,1)S(1)} %copy-done.10, bf16[912,256]{1,0:T(8,128)(2,1)S(1)} %copy-done.12, ...), custom_call_target="tpu_custom_call" | custom-call | flops 1048576 | bytes 65536 | tf_op jit(solution)/shard_map/attend_back/pallas_call | solution.py:918
  266.4 6.2 %attend_back.11 = (bf16[3,912,128]{2,1,0:T(8,128)(2,1)S(1)}, f32[3,128,128]{2,1,0:T(8,128)S(1)}) custom-call(bf16[128,912]{1,0:T(8,128)(2,1)S(1)} %compare_convert_fusion.1.hot_ref, bf16[912,256]{1,0:T(8,128)(2,1)S(1)} %get-tuple-element.228.q_ref, bf16[912,256]{1,0:T(8,128)(2,1)S(1)} %copy-done.10, bf16[912,256]{1,0:T(8,128)(2,1)S(1)} %copy-done.12, ...), custom_call_target="tpu_custom_call" | custom-call | flops 1048576 | bytes 65536 | tf_op jit(solution)/shard_map/attend_back/pallas_call | solution.py:918
  283.5 2.4 fusion.60.head_ref
  290.3 11.6 %entry.1 = (f32[912,768]{1,0:T(8,128)}, f32[2,768]{1,0:T(2,128)S(1)}, f32[128,768]{1,0:T(8,128)S(1)}) custom-call(bf16[912,256]{1,0:T(8,128)(2,1)S(1)} %compare_convert_fusion.hot_ref.refs_0_, bf16[128,768]{1,0:T(8,128)(2,1)S(1)} %pad.12.refs_1_, f32[1,768]{1,0:T(1,128)S(1)} %slice.290.refs_2_, f32[912,768]{1,0:T(8,128)} %copy-done.64, ...), custom_call_target="tpu_custom_call" | custom-call | flops 1048576 | bytes 65536 | tf_op jit(solution)/shard_map/entry/pallas_call | solution.py:549
  303.2 3.0 small_grads.1
  308.6 3.0 collective-permute-done.24.core_ref
  314.3 5.5 %dense_step.1 = (f32[384,768]{1,0:T(8,128)}, f32[384,768]{1,0:T(8,128)}, f32[96,768]{1,0:T(8,128)}, f32[384,768]{1,0:T(8,128)}, f32[384,768]{1,0:T(8,128)}, /*in...) custom-call(s32[1]{0:T(128)} %bitcast.7.spot_ref, ...), custom_call_target="tpu_custom_call" | custom-call | flops 1048576 | bytes 65536 | tf_op jit(solution)/shard_map/dense_step/pallas_call | solution.py:683
  319.8 7.6 %collective-permute-done.27 = f32[2,2,86,384]{3,1,2,0:T(2,128)S(1)} collective-permute-done((f32[2,2,86,384]{3,1,2,0:T(2,128)S(1)}, f32[2,2,86,384]{3,1,2,0:T(2,128)S(1)}, u32[]{:S(2)}, u32[]{:S(2)}) %collective-permute-start.27) | collective-permute-done | bytes 528416 | tf_op jit(solution)/shard_map/ppermute | solution.py:104
  330.5 13.8 %collective-permute-done.30 = f32[2,86,384]{2,1,0:T(8,128)S(1)} collective-permute-done((f32[2,86,384]{2,1,0:T(8,128)S(1)}, f32[2,86,384]{2,1,0:T(8,128)S(1)}, u32[]{:S(2)}, u32[]{:S(2)}) %collective-permute-start.30) | collective-permute-done | bytes 264224 | tf_op jit(solution)/shard_map/ppermute | solution.py:104
  346.4 2.2 collective-permute-start.33
  348.6 5.2 %collective-permute-done.33 = f32[86,384]{1,0:T(8,128)S(1)} collective-permute-done((f32[86,384]{1,0:T(8,128)S(1)}, f32[86,384]{1,0:T(8,128)S(1)}, u32[]{:S(2)}, u32[]{:S(2)}) %collective-permute-start.33) | collective-permute-done | bytes 132128 | tf_op jit(solution)/shard_map/ppermute | solution.py:104
  357.5 3.4 collective-permute-done.34
  364.0 2.6 collective-permute-start.39
  366.6 2.9 collective-permute-start.38
  369.5 2.8 collective-permute-done.37
  374.3 3.3 collective-permute-start.42
  377.8 12.9 %collective-permute-done.40 = f32[192,256]{1,0:T(8,128)S(1)} collective-permute-done((f32[192,256]{1,0:T(8,128)S(1)}, f32[192,256]{1,0:T(8,128)S(1)}, u32[]{:S(2)}, u32[]{:S(2)}) %collective-permute-start.40) | collective-permute-done | bytes 196640 | tf_op jit(solution)/shard_map/ppermute | solution.py:104
  394.5 3.8 collective-permute-start.45
  398.4 6.9 %collective-permute-done.45 = f32[70,838]{1,0:T(8,128)S(1)} collective-permute-done((f32[70,838]{1,0:T(8,128)S(1)}, f32[70,838]{1,0:T(8,128)S(1)}, u32[]{:S(2)}, u32[]{:S(2)}) %collective-permute-start.45) | collective-permute-done | bytes 234672 | tf_op jit(solution)/shard_map/ppermute | solution.py:104
  405.9 40.0 %newton.1.refs_0_ = bf16[384,768]{1,0:T(8,128)(2,1)} custom-call(f32[768,256]{1,0:T(8,128)S(1)} %maximum_select_fusion.low_ref, f32[768,256]{1,0:T(8,128)S(1)} %maximum_select_fusion.1.high_ref, f32[384,768]{1,0:T(8,128)S(1)} %pad_select_fusion.rows_ref, f32[70,768]{1,0:T(8,128)S(1)} %fusion.14.added_ref, bf16[70,768]{1,0:T(8,128)(2,1)S(1)} %copy-done.28), custom_call_target="tpu_custom_call" | custom-call | flops 27179089920 | bytes 4194304 | tf_op jit(solution)/shard_map/newton/pallas_call | solution.py:440
  450.8 5.3 %collective-permute-done.47.refs_2_ = bf16[384,768]{1,0:T(8,128)(2,1)} collective-permute-done((bf16[384,768]{1,0:T(8,128)(2,1)}, bf16[384,768]{1,0:T(8,128)(2,1)}, u32[]{:S(2)}, u32[]{:S(2)}) %collective-permute-start.47) | collective-permute-done | bytes 589856 | tf_op jit(solution)/shard_map/ppermute | solution.py:104
  458.3 3.6 update.1
  (521 shorter events, 139.3 us)
Async XLA Ops:
  7.3 98.8 %all-gather.5.cloned.1.call-start = ((), (), s32[]{:S(2)}) async-start(), calls=%async_computation | async-start | bytes 10948608 | tf_op jit(solution)/shard_map/all_gather | solution.py:1151
  9.3 196.9 %all-gather.7.cloned.1.call-start = ((), (), s32[]{:S(2)}) async-start(), calls=%async_computation.1 | async-start | bytes 3649536 | tf_op jit(solution)/shard_map/all_gather | solution.py:1222
  9.4 6.1 %collective-permute-start = (bf16[1,85,96]{2,1,0:T(8,128)(2,1)S(1)}, bf16[1,85,96]{2,1,0:T(8,128)(2,1)S(1)}, u32[]{:S(2)}, u32[]{:S(2)}) collective-permute-start(bf16[1,85,96]{2,1,0:T(8,128)(2,1)S(1)} %pad_maximum_fusion.17), channel_id=1, source_target_pairs={{0,16},{1,17},{2,18},{3,19},{4,20},{5,21},{6,22},{7,23},{8,24},{9,... | collective-permute-start | bytes 48968 | tf_op jit(solution)/shard_map/ppermute | solution.py:104
  15.6 4.1 collective-permute-start.1
  19.7 4.6 collective-permute-start.2
  27.3 6.3 %collective-permute-start.3 = (f32[1,70,72]{2,1,0:T(8,128)S(1)}, f32[1,70,72]{2,1,0:T(8,128)S(1)}, u32[]{:S(2)}, u32[]{:S(2)}) collective-permute-start(f32[1,70,72]{2,1,0:T(8,128)S(1)} %get-tuple-element.412), channel_id=1, source_target_pairs={{0,16},{1,17},{2,18},{3,19},{4,20},{5,21},{6,22},{7,23},{8,24},{9,... | collective-permute-start | bytes 60488 | tf_op jit(solution)/shard_map/ppermute | solution.py:104
  33.6 6.6 %collective-permute-start.4 = (f32[2,70,72]{2,1,0:T(8,128)S(1)}, f32[2,70,72]{2,1,0:T(8,128)S(1)}, u32[]{:S(2)}, u32[]{:S(2)}) collective-permute-start(f32[2,70,72]{2,1,0:T(8,128)S(1)} %pad_maximum_fusion.15), channel_id=1, source_target_pairs={{0,8},{1,9},{2,10},{3,11},{4,12},{5,13},{6,14},{7,15},{8,0},{9,1},... | collective-permute-start | bytes 120968 | tf_op jit(solution)/shard_map/ppermute | solution.py:104
  40.2 7.3 %collective-permute-start.5 = (f32[4,70,72]{2,1,0:T(8,128)S(1)}, f32[4,70,72]{2,1,0:T(8,128)S(1)}, u32[]{:S(2)}, u32[]{:S(2)}) collective-permute-start(f32[4,70,72]{2,1,0:T(8,128)S(1)} %pad_maximum_fusion.13), channel_id=1, source_target_pairs={{0,4},{1,5},{2,6},{3,7},{4,0},{5,1},{6,2},{7,3},{8,12},{9,13},{10,... | collective-permute-start | bytes 241928 | tf_op jit(solution)/shard_map/ppermute | solution.py:104
  47.6 10.9 %collective-permute-start.6 = (f32[8,70,72]{2,1,0:T(8,128)S(1)}, f32[8,70,72]{2,1,0:T(8,128)S(1)}, u32[]{:S(2)}, u32[]{:S(2)}) collective-permute-start(f32[8,70,72]{2,1,0:T(8,128)S(1)} %pad_maximum_fusion.10), channel_id=1, source_target_pairs={{0,2},{1,3},{2,0},{3,1},{4,6},{5,7},{6,4},{7,5},{8,10},{9,11},{10,... | collective-permute-start | bytes 483848 | tf_op jit(solution)/shard_map/ppermute | solution.py:104
  142.9 23.0 %collective-permute-start.8 = (bf16[1536,768]{1,0:T(8,128)(2,1)}, bf16[1536,768]{1,0:T(8,128)(2,1)}, u32[]{:S(2)}, u32[]{:S(2)}) collective-permute-start(bf16[1536,768]{1,0:T(8,128)(2,1)} %convolution_convert_fusion.1), channel_id=1, source_target_pairs={{0,1},{1,0},{2,3},{3,2},{4,5},{5,4},{6,7},{7,6},{8,9},{9,8},{10,11... | collective-permute-start | bytes 7077896 | tf_op jit(solution)/shard_map/ppermute | solution.py:104
  175.1 11.9 %collective-permute-start.10 = (bf16[1536,768]{1,0:T(8,128)(2,1)}, bf16[1536,768]{1,0:T(8,128)(2,1)}, u32[]{:S(2)}, u32[]{:S(2)}) collective-permute-start(bf16[1536,768]{1,0:T(8,128)(2,1)} %convolution_convert_fusion), channel_id=1, source_target_pairs={{0,1},{1,0},{2,3},{3,2},{4,5},{5,4},{6,7},{7,6},{8,9},{9,8},{10,11... | collective-permute-start | bytes 7077896 | tf_op jit(solution)/shard_map/ppermute | solution.py:104
  185.1 37.3 %collective-permute-start.9 = (bf16[768,384]{1,0:T(8,128)(2,1)}, bf16[768,384]{1,0:T(8,128)(2,1)}, u32[]{:S(2)}, u32[]{:S(2)}) collective-permute-start(bf16[768,384]{1,0:T(8,128)(2,1)} %bitcast.17), channel_id=1, source_target_pairs={{0,4},{1,5},{2,6},{3,7},{4,0},{5,1},{6,2},{7,3},{8,12},{9,13},{10,... | collective-permute-start | bytes 1769480 | tf_op jit(solution)/shard_map/ppermute | solution.py:104
  186.5 35.8 %collective-permute-start.15 = (bf16[768,384]{1,0:T(8,128)(2,1)}, bf16[768,384]{1,0:T(8,128)(2,1)}, u32[]{:S(2)}, u32[]{:S(2)}) collective-permute-start(bf16[768,384]{1,0:T(8,128)(2,1)} %bitcast.19), channel_id=1, source_target_pairs={{0,2},{1,3},{2,0},{3,1},{4,6},{5,7},{6,4},{7,5},{8,10},{9,11},{10,... | collective-permute-start | bytes 1769480 | tf_op jit(solution)/shard_map/ppermute | solution.py:104
  195.5 33.0 %collective-permute-start.14 = (bf16[960,384]{1,0:T(8,128)(2,1)}, bf16[960,384]{1,0:T(8,128)(2,1)}, u32[]{:S(2)}, u32[]{:S(2)}) collective-permute-start(bf16[960,384]{1,0:T(8,128)(2,1)} %pad_maximum_fusion.1), channel_id=1, source_target_pairs={{0,2},{1,3},{2,0},{3,1},{4,6},{5,7},{6,4},{7,5},{8,10},{9,11},{10,... | collective-permute-start | bytes 2211848 | tf_op jit(solution)/shard_map/ppermute | solution.py:104
  198.1 32.5 %collective-permute-start.13 = (bf16[960,384]{1,0:T(8,128)(2,1)}, bf16[960,384]{1,0:T(8,128)(2,1)}, u32[]{:S(2)}, u32[]{:S(2)}) collective-permute-start(bf16[960,384]{1,0:T(8,128)(2,1)} %pad_maximum_fusion), channel_id=1, source_target_pairs={{0,4},{1,5},{2,6},{3,7},{4,0},{5,1},{6,2},{7,3},{8,12},{9,13},{10,... | collective-permute-start | bytes 2211848 | tf_op jit(solution)/shard_map/ppermute | solution.py:104
  226.5 16.0 %collective-permute-start.16 = (bf16[384,384]{1,0:T(8,128)(2,1)}, bf16[384,384]{1,0:T(8,128)(2,1)}, u32[]{:S(2)}, u32[]{:S(2)}) collective-permute-start(bf16[384,384]{1,0:T(8,128)(2,1)} %bitcast.46), channel_id=1, source_target_pairs={{0,4},{1,5},{2,6},{3,7},{4,0},{5,1},{6,2},{7,3},{8,12},{9,13},{10,... | collective-permute-start | bytes 884744 | tf_op jit(solution)/shard_map/ppermute | solution.py:104
  228.2 15.6 %collective-permute-start.12 = (bf16[384,384]{1,0:T(8,128)(2,1)}, bf16[384,384]{1,0:T(8,128)(2,1)}, u32[]{:S(2)}, u32[]{:S(2)}) collective-permute-start(bf16[384,384]{1,0:T(8,128)(2,1)} %bitcast.31), channel_id=1, source_target_pairs={{0,2},{1,3},{2,0},{3,1},{4,6},{5,7},{6,4},{7,5},{8,10},{9,11},{10,... | collective-permute-start | bytes 884744 | tf_op jit(solution)/shard_map/ppermute | solution.py:104
  233.9 14.3 %collective-permute-start.19 = (bf16[480,384]{1,0:T(8,128)(2,1)S(1)}, bf16[480,384]{1,0:T(8,128)(2,1)S(1)}, u32[]{:S(2)}, u32[]{:S(2)}) collective-permute-start(bf16[480,384]{1,0:T(8,128)(2,1)S(1)} %pad_maximum_fusion.8), channel_id=1, source_target_pairs={{0,4},{1,5},{2,6},{3,7},{4,0},{5,1},{6,2},{7,3},{8,12},{9,13},{10,... | collective-permute-start | bytes 1105928 | tf_op jit(solution)/shard_map/ppermute | solution.py:104
  235.6 12.7 %collective-permute-start.18 = (bf16[480,384]{1,0:T(8,128)(2,1)S(1)}, bf16[480,384]{1,0:T(8,128)(2,1)S(1)}, u32[]{:S(2)}, u32[]{:S(2)}) collective-permute-start(bf16[480,384]{1,0:T(8,128)(2,1)S(1)} %pad_maximum_fusion.7), channel_id=1, source_target_pairs={{0,2},{1,3},{2,0},{3,1},{4,6},{5,7},{6,4},{7,5},{8,10},{9,11},{10,... | collective-permute-start | bytes 1105928 | tf_op jit(solution)/shard_map/ppermute | solution.py:104
  245.2 10.9 %collective-permute-start.17 = (bf16[192,768]{1,0:T(8,128)(2,1)S(1)}, bf16[192,768]{1,0:T(8,128)(2,1)S(1)}, u32[]{:S(2)}, u32[]{:S(2)}) collective-permute-start(bf16[192,768]{1,0:T(8,128)(2,1)S(1)} %bitcast.274), channel_id=1, source_target_pairs={{0,8},{1,9},{2,10},{3,11},{4,12},{5,13},{6,14},{7,15},{8,0},{9,1},... | collective-permute-start | bytes 884744 | tf_op jit(solution)/shard_map/ppermute | solution.py:104
  248.7 16.9 %collective-permute-start.21 = (bf16[240,768]{1,0:T(8,128)(2,1)S(1)}, bf16[240,768]{1,0:T(8,128)(2,1)S(1)}, u32[]{:S(2)}, u32[]{:S(2)}) collective-permute-start(bf16[240,768]{1,0:T(8,128)(2,1)S(1)} %pad_maximum_fusion.9), channel_id=1, source_target_pairs={{0,8},{1,9},{2,10},{3,11},{4,12},{5,13},{6,14},{7,15},{8,0},{9,1},... | collective-permute-start | bytes 1105928 | tf_op jit(solution)/shard_map/ppermute | solution.py:104
  256.2 16.6 %collective-permute-start.20 = (bf16[96,768]{1,0:T(8,128)(2,1)S(1)}, bf16[96,768]{1,0:T(8,128)(2,1)S(1)}, u32[]{:S(2)}, u32[]{:S(2)}) collective-permute-start(bf16[96,768]{1,0:T(8,128)(2,1)S(1)} %fusion.38), channel_id=1, source_target_pairs={{0,16},{1,17},{2,18},{3,19},{4,20},{5,21},{6,22},{7,23},{8,24},{9,... | collective-permute-start | bytes 442376 | tf_op jit(solution)/shard_map/ppermute | solution.py:104
  265.8 9.0 %collective-permute-start.22 = (bf16[120,768]{1,0:T(8,128)(2,1)S(1)}, bf16[120,768]{1,0:T(8,128)(2,1)S(1)}, u32[]{:S(2)}, u32[]{:S(2)}) collective-permute-start(bf16[120,768]{1,0:T(8,128)(2,1)S(1)} %pad_maximum_fusion.11), channel_id=1, source_target_pairs={{0,16},{1,17},{2,18},{3,19},{4,20},{5,21},{6,22},{7,23},{8,24},{9,... | collective-permute-start | bytes 552968 | tf_op jit(solution)/shard_map/ppermute | solution.py:104
  275.0 31.3 %collective-permute-start.23 = (f32[216,768]{1,0:T(8,128)S(1)}, f32[216,768]{1,0:T(8,128)S(1)}, u32[]{:S(2)}, u32[]{:S(2)}) collective-permute-start(f32[216,768]{1,0:T(8,128)S(1)} %pad_maximum_fusion.2.own_ref), channel_id=1, source_target_pairs={{0,2},{1,3},{2,0},{3,1},{4,6},{5,7},{6,4},{7,5},{8,10},{9,11},{10,... | collective-permute-start | bytes 1990664 | tf_op jit(solution)/shard_map/ppermute | solution.py:104
  308.0 4.6 collective-permute-start.26
  308.0 3.6 collective-permute-start.24
  308.5 4.1 collective-permute-start.25
  313.3 14.1 %collective-permute-start.27 = (f32[2,2,86,384]{3,1,2,0:T(2,128)S(1)}, f32[2,2,86,384]{3,1,2,0:T(2,128)S(1)}, u32[]{:S(2)}, u32[]{:S(2)}) collective-permute-start(f32[2,2,86,384]{3,1,2,0:T(2,128)S(1)} %bitcast.266), channel_id=1, source_target_pairs={{0,4},{1,5},{2,6},{3,7},{4,0},{5,1},{6,2},{7,3},{8,12},{9,13},{10,... | collective-permute-start | bytes 1585160 | tf_op jit(solution)/shard_map/ppermute | solution.py:104
  327.6 16.8 %collective-permute-start.28 = (f32[384,256]{1,0:T(8,128)S(1)}, f32[384,256]{1,0:T(8,128)S(1)}, u32[]{:S(2)}, u32[]{:S(2)}) collective-permute-start(f32[384,256]{1,0:T(8,128)S(1)} %dynamic-slice_bitcast_fusion.1), channel_id=1, source_target_pairs={{0,4},{1,5},{2,6},{3,7},{4,0},{5,1},{6,2},{7,3},{8,12},{9,13},{10,... | collective-permute-start | bytes 1179656 | tf_op jit(solution)/shard_map/ppermute | solution.py:104
  328.5 15.8 %collective-permute-start.29 = (f32[384,256]{1,0:T(8,128)S(1)}, f32[384,256]{1,0:T(8,128)S(1)}, u32[]{:S(2)}, u32[]{:S(2)}) collective-permute-start(f32[384,256]{1,0:T(8,128)S(1)} %dynamic-slice_bitcast_fusion), channel_id=1, source_target_pairs={{0,8},{1,9},{2,10},{3,11},{4,12},{5,13},{6,14},{7,15},{8,0},{9,1},... | collective-permute-start | bytes 1179656 | tf_op jit(solution)/shard_map/ppermute | solution.py:104
  328.7 15.6 %collective-permute-start.30 = (f32[2,86,384]{2,1,0:T(8,128)S(1)}, f32[2,86,384]{2,1,0:T(8,128)S(1)}, u32[]{:S(2)}, u32[]{:S(2)}) collective-permute-start(f32[2,86,384]{2,1,0:T(8,128)S(1)} %dynamic-slice_bitcast_fusion.2), channel_id=1, source_target_pairs={{0,8},{1,9},{2,10},{3,11},{4,12},{5,13},{6,14},{7,15},{8,0},{9,1},... | collective-permute-start | bytes 792584 | tf_op jit(solution)/shard_map/ppermute | solution.py:104
  344.6 9.2 %collective-permute-start.31 = (f32[192,256]{1,0:T(8,128)S(1)}, f32[192,256]{1,0:T(8,128)S(1)}, u32[]{:S(2)}, u32[]{:S(2)}) collective-permute-start(f32[192,256]{1,0:T(8,128)S(1)} %dynamic-slice_bitcast_fusion.4), channel_id=1, source_target_pairs={{0,8},{1,9},{2,10},{3,11},{4,12},{5,13},{6,14},{7,15},{8,0},{9,1},... | collective-permute-start | bytes 589832 | tf_op jit(solution)/shard_map/ppermute | solution.py:104
  345.0 8.8 %collective-permute-start.32 = (f32[192,256]{1,0:T(8,128)S(1)}, f32[192,256]{1,0:T(8,128)S(1)}, u32[]{:S(2)}, u32[]{:S(2)}) collective-permute-start(f32[192,256]{1,0:T(8,128)S(1)} %dynamic-slice_bitcast_fusion.3), channel_id=1, source_target_pairs={{0,4},{1,5},{2,6},{3,7},{4,0},{5,1},{6,2},{7,3},{8,12},{9,13},{10,... | collective-permute-start | bytes 589832 | tf_op jit(solution)/shard_map/ppermute | solution.py:104
  346.4 7.4 %collective-permute-start.33 = (f32[86,384]{1,0:T(8,128)S(1)}, f32[86,384]{1,0:T(8,128)S(1)}, u32[]{:S(2)}, u32[]{:S(2)}) collective-permute-start(f32[86,384]{1,0:T(8,128)S(1)} %dynamic-slice_bitcast_fusion.5), channel_id=1, source_target_pairs={{0,16},{1,17},{2,18},{3,19},{4,20},{5,21},{6,22},{7,23},{8,24},{9,... | collective-permute-start | bytes 396296 | tf_op jit(solution)/shard_map/ppermute | solution.py:104
  353.9 9.0 %collective-permute-start.36 = (f32[86,384]{1,0:T(8,128)S(1)}, f32[86,384]{1,0:T(8,128)S(1)}, u32[]{:S(2)}, u32[]{:S(2)}) collective-permute-start(f32[86,384]{1,0:T(8,128)S(1)} %bitcast_add_fusion.7), channel_id=1, source_target_pairs={{0,2},{1,3},{2,0},{3,1},{4,6},{5,7},{6,4},{7,5},{8,10},{9,11},{10,... | collective-permute-start | bytes 396296 | tf_op jit(solution)/shard_map/ppermute | solution.py:104
  354.6 6.3 %collective-permute-start.34 = (f32[96,256]{1,0:T(8,128)S(1)}, f32[96,256]{1,0:T(8,128)S(1)}, u32[]{:S(2)}, u32[]{:S(2)}) collective-permute-start(f32[96,256]{1,0:T(8,128)S(1)} %dynamic-slice_bitcast_fusion.7), channel_id=1, source_target_pairs={{0,16},{1,17},{2,18},{3,19},{4,20},{5,21},{6,22},{7,23},{8,24},{9,... | collective-permute-start | bytes 294920 | tf_op jit(solution)/shard_map/ppermute | solution.py:104
  355.5 7.5 %collective-permute-start.35 = (f32[96,256]{1,0:T(8,128)S(1)}, f32[96,256]{1,0:T(8,128)S(1)}, u32[]{:S(2)}, u32[]{:S(2)}) collective-permute-start(f32[96,256]{1,0:T(8,128)S(1)} %dynamic-slice_bitcast_fusion.6), channel_id=1, source_target_pairs={{0,16},{1,17},{2,18},{3,19},{4,20},{5,21},{6,22},{7,23},{8,24},{9,... | collective-permute-start | bytes 294920 | tf_op jit(solution)/shard_map/ppermute | solution.py:104
  364.0 10.2 %collective-permute-start.39 = (f32[70,838]{1,0:T(8,128)S(1)}, f32[70,838]{1,0:T(8,128)S(1)}, u32[]{:S(2)}, u32[]{:S(2)}) collective-permute-start(f32[70,838]{1,0:T(8,128)S(1)} %fusion.15), channel_id=1, source_target_pairs={{0,4},{1,5},{2,6},{3,7},{4,0},{5,1},{6,2},{7,3},{8,12},{9,13},{10,... | collective-permute-start | bytes 703928 | tf_op jit(solution)/shard_map/ppermute | solution.py:104
  366.6 5.7 %collective-permute-start.37 = (f32[96,256]{1,0:T(8,128)S(1)}, f32[96,256]{1,0:T(8,128)S(1)}, u32[]{:S(2)}, u32[]{:S(2)}) collective-permute-start(f32[96,256]{1,0:T(8,128)S(1)} %bitcast_add_fusion.9), channel_id=1, source_target_pairs={{0,16},{1,17},{2,18},{3,19},{4,20},{5,21},{6,22},{7,23},{8,24},{9,... | collective-permute-start | bytes 294920 | tf_op jit(solution)/shard_map/ppermute | solution.py:104
  366.6 7.6 %collective-permute-start.38 = (f32[96,256]{1,0:T(8,128)S(1)}, f32[96,256]{1,0:T(8,128)S(1)}, u32[]{:S(2)}, u32[]{:S(2)}) collective-permute-start(f32[96,256]{1,0:T(8,128)S(1)} %bitcast_add_fusion.8), channel_id=1, source_target_pairs={{0,16},{1,17},{2,18},{3,19},{4,20},{5,21},{6,22},{7,23},{8,24},{9,... | collective-permute-start | bytes 294920 | tf_op jit(solution)/shard_map/ppermute | solution.py:104
  374.3 16.4 %collective-permute-start.42 = (f32[70,838]{1,0:T(8,128)S(1)}, f32[70,838]{1,0:T(8,128)S(1)}, u32[]{:S(2)}, u32[]{:S(2)}) collective-permute-start(f32[70,838]{1,0:T(8,128)S(1)} %add.478), channel_id=1, source_target_pairs={{0,8},{1,9},{2,10},{3,11},{4,12},{5,13},{6,14},{7,15},{8,0},{9,1},... | collective-permute-start | bytes 703928 | tf_op jit(solution)/shard_map/ppermute | solution.py:104
  377.7 13.0 %collective-permute-start.40 = (f32[192,256]{1,0:T(8,128)S(1)}, f32[192,256]{1,0:T(8,128)S(1)}, u32[]{:S(2)}, u32[]{:S(2)}) collective-permute-start(f32[192,256]{1,0:T(8,128)S(1)} %maximum_select_fusion.4), channel_id=1, source_target_pairs={{0,8},{1,9},{2,10},{3,11},{4,12},{5,13},{6,14},{7,15},{8,0},{9,1},... | collective-permute-start | bytes 589832 | tf_op jit(solution)/shard_map/ppermute | solution.py:104
  377.7 13.0 %collective-permute-start.41 = (f32[192,256]{1,0:T(8,128)S(1)}, f32[192,256]{1,0:T(8,128)S(1)}, u32[]{:S(2)}, u32[]{:S(2)}) collective-permute-start(f32[192,256]{1,0:T(8,128)S(1)} %maximum_select_fusion.5), channel_id=1, source_target_pairs={{0,4},{1,5},{2,6},{3,7},{4,0},{5,1},{6,2},{7,3},{8,12},{9,13},{10,... | collective-permute-start | bytes 589832 | tf_op jit(solution)/shard_map/ppermute | solution.py:104
  390.8 14.5 %collective-permute-start.43 = (f32[384,256]{1,0:T(8,128)S(1)}, f32[384,256]{1,0:T(8,128)S(1)}, u32[]{:S(2)}, u32[]{:S(2)}) collective-permute-start(f32[384,256]{1,0:T(8,128)S(1)} %maximum_select_fusion.2), channel_id=1, source_target_pairs={{0,4},{1,5},{2,6},{3,7},{4,0},{5,1},{6,2},{7,3},{8,12},{9,13},{10,... | collective-permute-start | bytes 1179656 | tf_op jit(solution)/shard_map/ppermute | solution.py:104
  390.9 14.5 %collective-permute-start.44 = (f32[384,256]{1,0:T(8,128)S(1)}, f32[384,256]{1,0:T(8,128)S(1)}, u32[]{:S(2)}, u32[]{:S(2)}) collective-permute-start(f32[384,256]{1,0:T(8,128)S(1)} %maximum_select_fusion.3), channel_id=1, source_target_pairs={{0,8},{1,9},{2,10},{3,11},{4,12},{5,13},{6,14},{7,15},{8,0},{9,1},... | collective-permute-start | bytes 1179656 | tf_op jit(solution)/shard_map/ppermute | solution.py:104
  394.5 10.9 %collective-permute-start.45 = (f32[70,838]{1,0:T(8,128)S(1)}, f32[70,838]{1,0:T(8,128)S(1)}, u32[]{:S(2)}, u32[]{:S(2)}) collective-permute-start(f32[70,838]{1,0:T(8,128)S(1)} %add.479), channel_id=1, source_target_pairs={{0,16},{1,17},{2,18},{3,19},{4,20},{5,21},{6,22},{7,23},{8,24},{9,... | collective-permute-start | bytes 703928 | tf_op jit(solution)/shard_map/ppermute | solution.py:104
  445.9 10.2 %collective-permute-start.47 = (bf16[384,768]{1,0:T(8,128)(2,1)}, bf16[384,768]{1,0:T(8,128)(2,1)}, u32[]{:S(2)}, u32[]{:S(2)}) collective-permute-start(bf16[384,768]{1,0:T(8,128)(2,1)} %newton.1.refs_0_), channel_id=1, source_target_pairs={{0,2},{1,3},{2,0},{3,1},{4,6},{5,7},{6,4},{7,5},{8,10},{9,11},{10,... | collective-permute-start | bytes 1769480 | tf_op jit(solution)/shard_map/ppermute | solution.py:104
  447.9 9.5 %collective-permute-start.46 = (bf16[384,768]{1,0:T(8,128)(2,1)}, bf16[384,768]{1,0:T(8,128)(2,1)S(1)}, u32[]{:S(2)}, u32[]{:S(2)}) collective-permute-start(bf16[384,768]{1,0:T(8,128)(2,1)} %newton.1.refs_0_), channel_id=1, source_target_pairs={{0,1},{1,0},{2,3},{3,2},{4,5},{5,4},{6,7},{7,6},{8,9},{9,8},{10,11... | collective-permute-start | bytes 1769480 | tf_op jit(solution)/shard_map/ppermute | solution.py:104
  (122 other events, 1101.1 us)
Sparse Core Ops, SparseCore 0:
  11.6 94.4 all-gather.4
  143.3 62.8 all-gather.6

commit v7 on v6

--- a/solution.py
+++ b/solution.py
@@ -586,6 +586,9 @@
     for kind in range(3):
         held[VOCAB + 6 + kind : VOCAB + 7 + kind, :] = bias[:, kind * D : (kind + 1) * D]
     for ref, at in zip(row_refs, spot_rows):
+        if len(ref.shape) == 1:
+            held[at : at + 1, :] = ref[...][None, :]
+            continue
         for row in range(ref.shape[0]):
             for part in range(ref.shape[1] // D):
                 held[at : at + 1, :] = ref[row : row + 1, part * D : (part + 1) * D]
@@ -1346,12 +1349,12 @@
             hist_part,
             (
                 (one_sums, 0),
-                (gain_two_grad[None, :], 2),
-                (bias_two_grad[None, :], 3),
-                (gain_last_grad[None, :], 4),
-                (bias_last_grad[None, :], 5),
-                (mixing_bias_grad[None, :], 9),
-                (reduce_bias_grad[None, :], 10),
+                (gain_two_grad, 2),
+                (bias_two_grad, 3),
+                (gain_last_grad, 4),
+                (bias_last_grad, 5),
+                (mixing_bias_grad, 9),
+                (reduce_bias_grad, 10),
                 (expand_ordered.reshape(1, FF), 11),
             ),
             wide_size,

time: 474 us -> 471 us (level)
    unnamed x241 -> x229, local copies, waits for them, and re-layouts: 24.4 us -> 24.4 us
  transfers between devices with their start and end apart: 51 -> 51, of which waited for: 25 -> 25; matrix products, arithmetic and copies ran while one was open for 16% -> 16% of each run, Pallas kernels for 21% -> 22%
where the time goes in v7:
time: 471 us; the launch traced here: 465 us
  Pallas kernels  167 us (35%)
  waiting for transfers between devices  106 us (23%)
  starting transfers between devices  59.2 us (13%)
  local copies, waits for them, and re-layouts  52.1 us (11%)
  other arithmetic  31.9 us (7%)
  matrix products  31.3 us (7%)
  between operations  18.4 us (4%)
    ppermute x49, waiting for transfers between devices, swap(): lax.ppermute(value, BOTH, [(spot, spot ^ mask) for spot in range(total)])  90.7 us
    ppermute x49, starting transfers between devices, swap(): lax.ppermute(value, BOTH, [(spot, spot ^ mask) for spot in range(total)])  59.1 us
    pallas_call x1, Pallas kernels, newton_rows(): pl.pallas_call(newton_kernel, out_shape=jax.ShapeDtypeStruct((count, D),...  40 us
    pallas_call x6, Pallas kernels, attend_back_call(): pl.pallas_call(attend_back_kernel, grid=(count,), in_specs=[pl.BlockSpec(...  36.8 us
    unnamed x229, local copies, waits for them, and re-layouts  24.4 us
    pallas_call x3, Pallas kernels, attend_call(): pl.pallas_call(attend_kernel, grid=(count,), in_specs=[pl.BlockSpec(hot.s...  24.1 us
    dot_general x6, matrix products, trans_times(): lax.dot_general(left_side, right_side, (((0,), (0,)), ((), ())), preferre...  21.7 us
    pallas_call x1, Pallas kernels, feed_call(): pl.pallas_call(partial(feed_kernel, starts), grid_spec=pltpu.PrefetchScal...  20.7 us
  transfers between devices with their start and end apart: 51, of which 25 were waited for; matrix products, arithmetic and copies ran while one was open for 16% of the time, Pallas kernels for 22%

profile of v7, /device:TPU:0, one launch (start us, length us, event | category | flops | bytes accessed | tf_op | source)
XLA Modules:
  0.0 465.4 jit_solution(7878462473862393574)
XLA Ops:
  9.4 4.1 collective-permute-start
  21.5 2.8 collective-permute-done.2
  27.3 2.7 collective-permute-start.3
  42.5 5.0 %collective-permute-done.5 = f32[4,70,72]{2,1,0:T(8,128)S(1)} collective-permute-done((f32[4,70,72]{2,1,0:T(8,128)S(1)}, f32[4,70,72]{2,1,0:T(8,128)S(1)}, u32[]{:S(2)}, u32[]{:S(2)}) %collective-permute-start.5) | collective-permute-done | bytes 80672 | tf_op jit(solution)/shard_map/ppermute | solution.py:104
  51.0 7.4 %collective-permute-done.6 = f32[8,70,72]{2,1,0:T(8,128)S(1)} collective-permute-done((f32[8,70,72]{2,1,0:T(8,128)S(1)}, f32[8,70,72]{2,1,0:T(8,128)S(1)}, u32[]{:S(2)}, u32[]{:S(2)}) %collective-permute-start.6) | collective-permute-done | bytes 161312 | tf_op jit(solution)/shard_map/ppermute | solution.py:104
  62.3 4.6 heads_table.1.tq_ref.tk_ref.tv_ref
  68.2 8.1 %attend.5 = (bf16[912,256]{1,0:T(8,128)(2,1)S(1)}, bf16[912,256]{1,0:T(8,128)(2,1)S(1)}, bf16[912,256]{1,0:T(8,128)(2,1)S(1)}, bf16[912,256]{1,0:T(8,128)(2,1)S(1)}, f32[2,2,1024]{2,1,0:T(2,128)S(1)}) custom-call(bf16[912,256]{1,0:T(8,128)(2,1)S(1)} %compare_convert_fusion.hot_ref.refs_0_, bf16[256,2304]{1,0:T(8,128)(2,1)S(1)} %copy-done.2, ...), custom_call_target="tpu_custom_call" | custom-call | flops 2097152 | bytes 65536 | tf_op jit(solution)/shard_map/attend/pallas_call | solution.py:829
  76.3 7.9 %attend.4 = (bf16[912,256]{1,0:T(8,128)(2,1)S(1)}, bf16[912,256]{1,0:T(8,128)(2,1)S(1)}, bf16[912,256]{1,0:T(8,128)(2,1)S(1)}, bf16[912,256]{1,0:T(8,128)(2,1)S(1)}, f32[2,2,1024]{2,1,0:T(2,128)S(1)}) custom-call(bf16[912,256]{1,0:T(8,128)(2,1)S(1)} %compare_convert_fusion.hot_ref.refs_0_, bf16[256,2304]{1,0:T(8,128)(2,1)S(1)} %copy-done.2, ...), custom_call_target="tpu_custom_call" | custom-call | flops 2097152 | bytes 65536 | tf_op jit(solution)/shard_map/attend/pallas_call | solution.py:829
  85.8 8.1 %attend.3 = (bf16[912,256]{1,0:T(8,128)(2,1)S(1)}, bf16[912,256]{1,0:T(8,128)(2,1)S(1)}, bf16[912,256]{1,0:T(8,128)(2,1)S(1)}, bf16[912,256]{1,0:T(8,128)(2,1)S(1)}, f32[2,2,1024]{2,1,0:T(2,128)S(1)}) custom-call(bf16[912,256]{1,0:T(8,128)(2,1)S(1)} %compare_convert_fusion.hot_ref.refs_0_, bf16[256,2304]{1,0:T(8,128)(2,1)S(1)} %copy-done.2, ...), custom_call_target="tpu_custom_call" | custom-call | flops 2097152 | bytes 65536 | tf_op jit(solution)/shard_map/attend/pallas_call | solution.py:829
  96.9 9.2 %all-gather.5.cloned.1.call-done = bf16[6912,768]{1,0:T(8,128)(2,1)} async-done(((bf16[216,768]{1,0:T(8,128)(2,1)}), bf16[6912,768]{1,0:T(8,128)(2,1)}) %all-gather.5.cloned.1.call-update) | async-done | bytes 10616848 | tf_op jit(solution)/shard_map/all_gather | solution.py:1154
  110.8 20.7 %feed.1 = (bf16[912,3072]{1,0:T(8,128)(2,1)}, bf16[912,3072]{1,0:T(8,128)(2,1)}, f32[912,768]{1,0:T(8,128)S(1)}) custom-call(s32[32]{0:T(128)S(1)} %broadcast_xor_fusion.place_ref, bf16[912,768]{1,0:T(8,128)(2,1)S(1)} %add_convert_fusion.1.rows_ref, f32[1,3072]{1,0:T(1,128)S(1)} %broadcast_in_dim_reshape.2.bias_ref, bf16[32,216,768]{2,1,0:T(8,128)(2,1)} %bitcast.226), custom_call_target="tpu_custom_call" | custom-call | flops 2151677952 | bytes 65536 | tf_op jit(solution)/shard_map/feed/pallas_call | solution.py:1021
  135.7 3.1 convert_reduce_fusion
  138.9 4.0 convolution_convert_fusion.1
  144.5 14.9 %feed_back.1 = (bf16[912,3072]{1,0:T(8,128)(2,1)}, f32[912,768]{1,0:T(8,128)S(1)}, f32[1,3072]{1,0:T(1,128)S(1)}) custom-call(s32[32]{0:T(128)S(1)} %broadcast_xor_fusion.place_ref, bf16[912,768]{1,0:T(8,128)(2,1)S(1)} %copy-done.5, bf16[912,3072]{1,0:T(8,128)(2,1)} %get-tuple-element.196.slope_ref, bf16[32,216,768]{2,1,0:T(8,128)(2,1)} %bitcast.227), custom_call_target="tpu_custom_call" | custom-call | flops 2151677952 | bytes 65536 | tf_op jit(solution)/shard_map/feed_back/pallas_call | solution.py:1072
  161.3 4.7 %fusion.6 = f32[1536,768]{1,0:T(8,128)S(1)} fusion(bf16[912,768]{1,0:T(8,128)(2,1)S(1)} %copy-done.5, bf16[912,3072]{1,0:T(8,128)(2,1)} %get-tuple-element.193), kind=kOutput, calls=%fused_computation.24 | convolution fusion | flops 2151677952 | bytes 8921088 | tf_op jit(solution)/shard_map/dot_general | solution.py:49
  166.0 2.6 convert_add_fusion.1
  171.2 4.0 convolution_convert_fusion
  187.0 5.2 %convert_add_fusion = f32[1536,768]{1,0:T(8,128)S(1)} fusion(bf16[1536,768]{1,0:T(8,128)(2,1)} %collective-permute-done.10, bf16[912,768]{1,0:T(8,128)(2,1)S(1)} %add_convert_fusion.1.rows_ref, bf16[912,3072]{1,0:T(8,128)(2,1)} %get-tuple-element.205), kind=kOutput, calls=%fused_computation.6 | convolution fusion | flops 2154037248 | bytes 11280384 | tf_op jit(solution)/shard_map/dot_general | solution.py:49
  200.3 5.9 %all-gather.7.cloned.1.call-done = bf16[2304,768]{1,0:T(8,128)(2,1)} async-done(((bf16[72,768]{1,0:T(8,128)(2,1)}), bf16[2304,768]{1,0:T(8,128)(2,1)}) %all-gather.7.cloned.1.call-update) | async-done | bytes 3538960 | tf_op jit(solution)/shard_map/all_gather | solution.py:1225
  210.0 6.1 %attend_back.6 = (bf16[3,912,128]{2,1,0:T(8,128)(2,1)S(1)}, f32[3,128,128]{2,1,0:T(8,128)S(1)}) custom-call(bf16[128,912]{1,0:T(8,128)(2,1)S(1)} %compare_convert_fusion.1.hot_ref, bf16[912,256]{1,0:T(8,128)(2,1)S(1)} %copy-done.20, bf16[912,256]{1,0:T(8,128)(2,1)S(1)} %copy-done.22, bf16[912,256]{1,0:T(8,128)(2,1)S(1)} %copy-done.24, ...), custom_call_target="tpu_custom_call" | custom-call | flops 1048576 | bytes 65536 | tf_op jit(solution)/shard_map/attend_back/pallas_call | solution.py:921
  216.1 6.3 %attend_back.7 = (bf16[3,912,128]{2,1,0:T(8,128)(2,1)S(1)}, f32[3,128,128]{2,1,0:T(8,128)S(1)}) custom-call(bf16[128,912]{1,0:T(8,128)(2,1)S(1)} %compare_convert_fusion.1.hot_ref, bf16[912,256]{1,0:T(8,128)(2,1)S(1)} %copy-done.20, bf16[912,256]{1,0:T(8,128)(2,1)S(1)} %copy-done.22, bf16[912,256]{1,0:T(8,128)(2,1)S(1)} %copy-done.24, ...), custom_call_target="tpu_custom_call" | custom-call | flops 1048576 | bytes 65536 | tf_op jit(solution)/shard_map/attend_back/pallas_call | solution.py:921
  222.4 2.5 fusion.8
  236.3 6.1 %attend_back.8 = (bf16[3,912,128]{2,1,0:T(8,128)(2,1)S(1)}, f32[3,128,128]{2,1,0:T(8,128)S(1)}) custom-call(bf16[128,912]{1,0:T(8,128)(2,1)S(1)} %compare_convert_fusion.1.hot_ref, bf16[912,256]{1,0:T(8,128)(2,1)S(1)} %copy-done.14, bf16[912,256]{1,0:T(8,128)(2,1)S(1)} %copy-done.16, bf16[912,256]{1,0:T(8,128)(2,1)S(1)} %copy-done.18, ...), custom_call_target="tpu_custom_call" | custom-call | flops 1048576 | bytes 65536 | tf_op jit(solution)/shard_map/attend_back/pallas_call | solution.py:921
  245.2 3.0 collective-permute-start.17
  249.3 6.1 %attend_back.9 = (bf16[3,912,128]{2,1,0:T(8,128)(2,1)S(1)}, f32[3,128,128]{2,1,0:T(8,128)S(1)}) custom-call(bf16[128,912]{1,0:T(8,128)(2,1)S(1)} %compare_convert_fusion.1.hot_ref, bf16[912,256]{1,0:T(8,128)(2,1)S(1)} %copy-done.14, bf16[912,256]{1,0:T(8,128)(2,1)S(1)} %copy-done.16, bf16[912,256]{1,0:T(8,128)(2,1)S(1)} %copy-done.18, ...), custom_call_target="tpu_custom_call" | custom-call | flops 1048576 | bytes 65536 | tf_op jit(solution)/shard_map/attend_back/pallas_call | solution.py:921
  256.2 2.3 collective-permute-start.20
  258.5 6.1 %attend_back.10 = (bf16[3,912,128]{2,1,0:T(8,128)(2,1)S(1)}, f32[3,128,128]{2,1,0:T(8,128)S(1)}) custom-call(bf16[128,912]{1,0:T(8,128)(2,1)S(1)} %compare_convert_fusion.1.hot_ref, bf16[912,256]{1,0:T(8,128)(2,1)S(1)} %get-tuple-element.228.q_ref, bf16[912,256]{1,0:T(8,128)(2,1)S(1)} %copy-done.10, bf16[912,256]{1,0:T(8,128)(2,1)S(1)} %copy-done.12, ...), custom_call_target="tpu_custom_call" | custom-call | flops 1048576 | bytes 65536 | tf_op jit(solution)/shard_map/attend_back/pallas_call | solution.py:921
  266.4 6.2 %attend_back.11 = (bf16[3,912,128]{2,1,0:T(8,128)(2,1)S(1)}, f32[3,128,128]{2,1,0:T(8,128)S(1)}) custom-call(bf16[128,912]{1,0:T(8,128)(2,1)S(1)} %compare_convert_fusion.1.hot_ref, bf16[912,256]{1,0:T(8,128)(2,1)S(1)} %get-tuple-element.228.q_ref, bf16[912,256]{1,0:T(8,128)(2,1)S(1)} %copy-done.10, bf16[912,256]{1,0:T(8,128)(2,1)S(1)} %copy-done.12, ...), custom_call_target="tpu_custom_call" | custom-call | flops 1048576 | bytes 65536 | tf_op jit(solution)/shard_map/attend_back/pallas_call | solution.py:921
  280.0 2.4 fusion.60.head_ref
  286.8 11.6 %entry.1 = (f32[912,768]{1,0:T(8,128)}, f32[2,768]{1,0:T(2,128)S(1)}, f32[128,768]{1,0:T(8,128)S(1)}) custom-call(bf16[912,256]{1,0:T(8,128)(2,1)S(1)} %compare_convert_fusion.hot_ref.refs_0_, bf16[128,768]{1,0:T(8,128)(2,1)S(1)} %pad.12.refs_1_, f32[1,768]{1,0:T(1,128)S(1)} %slice.290.refs_2_, f32[912,768]{1,0:T(8,128)} %copy-done.64, ...), custom_call_target="tpu_custom_call" | custom-call | flops 1048576 | bytes 65536 | tf_op jit(solution)/shard_map/entry/pallas_call | solution.py:549
  299.7 3.0 small_grads.1
  305.1 3.0 collective-permute-done.24.core_ref
  310.8 5.5 %dense_step.1 = (f32[384,768]{1,0:T(8,128)}, f32[384,768]{1,0:T(8,128)}, f32[96,768]{1,0:T(8,128)}, f32[384,768]{1,0:T(8,128)}, f32[384,768]{1,0:T(8,128)}, /*in...) custom-call(s32[1]{0:T(128)} %bitcast.7.spot_ref, ...), custom_call_target="tpu_custom_call" | custom-call | flops 1048576 | bytes 65536 | tf_op jit(solution)/shard_map/dense_step/pallas_call | solution.py:686
  316.3 7.6 %collective-permute-done.27 = f32[2,2,86,384]{3,1,2,0:T(2,128)S(1)} collective-permute-done((f32[2,2,86,384]{3,1,2,0:T(2,128)S(1)}, f32[2,2,86,384]{3,1,2,0:T(2,128)S(1)}, u32[]{:S(2)}, u32[]{:S(2)}) %collective-permute-start.27) | collective-permute-done | bytes 528416 | tf_op jit(solution)/shard_map/ppermute | solution.py:104
  327.0 13.8 %collective-permute-done.30 = f32[2,86,384]{2,1,0:T(8,128)S(1)} collective-permute-done((f32[2,86,384]{2,1,0:T(8,128)S(1)}, f32[2,86,384]{2,1,0:T(8,128)S(1)}, u32[]{:S(2)}, u32[]{:S(2)}) %collective-permute-start.30) | collective-permute-done | bytes 264224 | tf_op jit(solution)/shard_map/ppermute | solution.py:104
  342.9 2.2 collective-permute-start.33
  345.1 5.2 %collective-permute-done.33 = f32[86,384]{1,0:T(8,128)S(1)} collective-permute-done((f32[86,384]{1,0:T(8,128)S(1)}, f32[86,384]{1,0:T(8,128)S(1)}, u32[]{:S(2)}, u32[]{:S(2)}) %collective-permute-start.33) | collective-permute-done | bytes 132128 | tf_op jit(solution)/shard_map/ppermute | solution.py:104
  354.0 3.3 collective-permute-done.34
  360.4 2.5 collective-permute-start.39
  362.9 2.9 collective-permute-start.38
  365.8 2.7 collective-permute-done.37
  370.6 3.4 collective-permute-start.42
  374.2 12.9 %collective-permute-done.40 = f32[192,256]{1,0:T(8,128)S(1)} collective-permute-done((f32[192,256]{1,0:T(8,128)S(1)}, f32[192,256]{1,0:T(8,128)S(1)}, u32[]{:S(2)}, u32[]{:S(2)}) %collective-permute-start.40) | collective-permute-done | bytes 196640 | tf_op jit(solution)/shard_map/ppermute | solution.py:104
  390.8 3.7 collective-permute-start.45
  394.6 6.9 %collective-permute-done.45 = f32[70,838]{1,0:T(8,128)S(1)} collective-permute-done((f32[70,838]{1,0:T(8,128)S(1)}, f32[70,838]{1,0:T(8,128)S(1)}, u32[]{:S(2)}, u32[]{:S(2)}) %collective-permute-start.45) | collective-permute-done | bytes 234672 | tf_op jit(solution)/shard_map/ppermute | solution.py:104
  402.1 40.0 %newton.1.refs_0_ = bf16[384,768]{1,0:T(8,128)(2,1)} custom-call(f32[768,256]{1,0:T(8,128)S(1)} %maximum_select_fusion.low_ref, f32[768,256]{1,0:T(8,128)S(1)} %maximum_select_fusion.1.high_ref, f32[384,768]{1,0:T(8,128)S(1)} %pad_select_fusion.rows_ref, f32[70,768]{1,0:T(8,128)S(1)} %fusion.14.added_ref, bf16[70,768]{1,0:T(8,128)(2,1)S(1)} %copy-done.28), custom_call_target="tpu_custom_call" | custom-call | flops 27179089920 | bytes 4194304 | tf_op jit(solution)/shard_map/newton/pallas_call | solution.py:440
  447.3 5.0 %collective-permute-done.47.refs_2_ = bf16[384,768]{1,0:T(8,128)(2,1)} collective-permute-done((bf16[384,768]{1,0:T(8,128)(2,1)}, bf16[384,768]{1,0:T(8,128)(2,1)}, u32[]{:S(2)}, u32[]{:S(2)}) %collective-permute-start.47) | collective-permute-done | bytes 589856 | tf_op jit(solution)/shard_map/ppermute | solution.py:104
  454.5 3.6 update.1
  (503 shorter events, 136.3 us)
Async XLA Ops:
  7.3 98.8 %all-gather.5.cloned.1.call-start = ((), (), s32[]{:S(2)}) async-start(), calls=%async_computation | async-start | bytes 10948608 | tf_op jit(solution)/shard_map/all_gather | solution.py:1154
  9.3 196.9 %all-gather.7.cloned.1.call-start = ((), (), s32[]{:S(2)}) async-start(), calls=%async_computation.1 | async-start | bytes 3649536 | tf_op jit(solution)/shard_map/all_gather | solution.py:1225
  9.4 6.1 %collective-permute-start = (bf16[1,85,96]{2,1,0:T(8,128)(2,1)S(1)}, bf16[1,85,96]{2,1,0:T(8,128)(2,1)S(1)}, u32[]{:S(2)}, u32[]{:S(2)}) collective-permute-start(bf16[1,85,96]{2,1,0:T(8,128)(2,1)S(1)} %pad_maximum_fusion.17), channel_id=1, source_target_pairs={{0,16},{1,17},{2,18},{3,19},{4,20},{5,21},{6,22},{7,23},{8,24},{9,... | collective-permute-start | bytes 48968 | tf_op jit(solution)/shard_map/ppermute | solution.py:104
  15.6 4.1 collective-permute-start.1
  19.7 4.6 collective-permute-start.2
  27.3 6.3 %collective-permute-start.3 = (f32[1,70,72]{2,1,0:T(8,128)S(1)}, f32[1,70,72]{2,1,0:T(8,128)S(1)}, u32[]{:S(2)}, u32[]{:S(2)}) collective-permute-start(f32[1,70,72]{2,1,0:T(8,128)S(1)} %get-tuple-element.412), channel_id=1, source_target_pairs={{0,16},{1,17},{2,18},{3,19},{4,20},{5,21},{6,22},{7,23},{8,24},{9,... | collective-permute-start | bytes 60488 | tf_op jit(solution)/shard_map/ppermute | solution.py:104
  33.6 6.6 %collective-permute-start.4 = (f32[2,70,72]{2,1,0:T(8,128)S(1)}, f32[2,70,72]{2,1,0:T(8,128)S(1)}, u32[]{:S(2)}, u32[]{:S(2)}) collective-permute-start(f32[2,70,72]{2,1,0:T(8,128)S(1)} %pad_maximum_fusion.15), channel_id=1, source_target_pairs={{0,8},{1,9},{2,10},{3,11},{4,12},{5,13},{6,14},{7,15},{8,0},{9,1},... | collective-permute-start | bytes 120968 | tf_op jit(solution)/shard_map/ppermute | solution.py:104
  40.2 7.3 %collective-permute-start.5 = (f32[4,70,72]{2,1,0:T(8,128)S(1)}, f32[4,70,72]{2,1,0:T(8,128)S(1)}, u32[]{:S(2)}, u32[]{:S(2)}) collective-permute-start(f32[4,70,72]{2,1,0:T(8,128)S(1)} %pad_maximum_fusion.13), channel_id=1, source_target_pairs={{0,4},{1,5},{2,6},{3,7},{4,0},{5,1},{6,2},{7,3},{8,12},{9,13},{10,... | collective-permute-start | bytes 241928 | tf_op jit(solution)/shard_map/ppermute | solution.py:104
  47.6 10.9 %collective-permute-start.6 = (f32[8,70,72]{2,1,0:T(8,128)S(1)}, f32[8,70,72]{2,1,0:T(8,128)S(1)}, u32[]{:S(2)}, u32[]{:S(2)}) collective-permute-start(f32[8,70,72]{2,1,0:T(8,128)S(1)} %pad_maximum_fusion.10), channel_id=1, source_target_pairs={{0,2},{1,3},{2,0},{3,1},{4,6},{5,7},{6,4},{7,5},{8,10},{9,11},{10,... | collective-permute-start | bytes 483848 | tf_op jit(solution)/shard_map/ppermute | solution.py:104
  142.9 23.1 %collective-permute-start.8 = (bf16[1536,768]{1,0:T(8,128)(2,1)}, bf16[1536,768]{1,0:T(8,128)(2,1)}, u32[]{:S(2)}, u32[]{:S(2)}) collective-permute-start(bf16[1536,768]{1,0:T(8,128)(2,1)} %convolution_convert_fusion.1), channel_id=1, source_target_pairs={{0,1},{1,0},{2,3},{3,2},{4,5},{5,4},{6,7},{7,6},{8,9},{9,8},{10,11... | collective-permute-start | bytes 7077896 | tf_op jit(solution)/shard_map/ppermute | solution.py:104
  175.1 11.9 %collective-permute-start.10 = (bf16[1536,768]{1,0:T(8,128)(2,1)}, bf16[1536,768]{1,0:T(8,128)(2,1)}, u32[]{:S(2)}, u32[]{:S(2)}) collective-permute-start(bf16[1536,768]{1,0:T(8,128)(2,1)} %convolution_convert_fusion), channel_id=1, source_target_pairs={{0,1},{1,0},{2,3},{3,2},{4,5},{5,4},{6,7},{7,6},{8,9},{9,8},{10,11... | collective-permute-start | bytes 7077896 | tf_op jit(solution)/shard_map/ppermute | solution.py:104
  185.2 37.2 %collective-permute-start.9 = (bf16[768,384]{1,0:T(8,128)(2,1)}, bf16[768,384]{1,0:T(8,128)(2,1)}, u32[]{:S(2)}, u32[]{:S(2)}) collective-permute-start(bf16[768,384]{1,0:T(8,128)(2,1)} %bitcast.17), channel_id=1, source_target_pairs={{0,4},{1,5},{2,6},{3,7},{4,0},{5,1},{6,2},{7,3},{8,12},{9,13},{10,... | collective-permute-start | bytes 1769480 | tf_op jit(solution)/shard_map/ppermute | solution.py:104
  186.6 35.8 %collective-permute-start.15 = (bf16[768,384]{1,0:T(8,128)(2,1)}, bf16[768,384]{1,0:T(8,128)(2,1)}, u32[]{:S(2)}, u32[]{:S(2)}) collective-permute-start(bf16[768,384]{1,0:T(8,128)(2,1)} %bitcast.19), channel_id=1, source_target_pairs={{0,2},{1,3},{2,0},{3,1},{4,6},{5,7},{6,4},{7,5},{8,10},{9,11},{10,... | collective-permute-start | bytes 1769480 | tf_op jit(solution)/shard_map/ppermute | solution.py:104
  195.6 32.9 %collective-permute-start.14 = (bf16[960,384]{1,0:T(8,128)(2,1)}, bf16[960,384]{1,0:T(8,128)(2,1)}, u32[]{:S(2)}, u32[]{:S(2)}) collective-permute-start(bf16[960,384]{1,0:T(8,128)(2,1)} %pad_maximum_fusion.1), channel_id=1, source_target_pairs={{0,2},{1,3},{2,0},{3,1},{4,6},{5,7},{6,4},{7,5},{8,10},{9,11},{10,... | collective-permute-start | bytes 2211848 | tf_op jit(solution)/shard_map/ppermute | solution.py:104
  198.1 32.4 %collective-permute-start.13 = (bf16[960,384]{1,0:T(8,128)(2,1)}, bf16[960,384]{1,0:T(8,128)(2,1)}, u32[]{:S(2)}, u32[]{:S(2)}) collective-permute-start(bf16[960,384]{1,0:T(8,128)(2,1)} %pad_maximum_fusion), channel_id=1, source_target_pairs={{0,4},{1,5},{2,6},{3,7},{4,0},{5,1},{6,2},{7,3},{8,12},{9,13},{10,... | collective-permute-start | bytes 2211848 | tf_op jit(solution)/shard_map/ppermute | solution.py:104
  226.5 15.9 %collective-permute-start.16 = (bf16[384,384]{1,0:T(8,128)(2,1)}, bf16[384,384]{1,0:T(8,128)(2,1)}, u32[]{:S(2)}, u32[]{:S(2)}) collective-permute-start(bf16[384,384]{1,0:T(8,128)(2,1)} %bitcast.46), channel_id=1, source_target_pairs={{0,4},{1,5},{2,6},{3,7},{4,0},{5,1},{6,2},{7,3},{8,12},{9,13},{10,... | collective-permute-start | bytes 884744 | tf_op jit(solution)/shard_map/ppermute | solution.py:104
  228.1 15.6 %collective-permute-start.12 = (bf16[384,384]{1,0:T(8,128)(2,1)}, bf16[384,384]{1,0:T(8,128)(2,1)}, u32[]{:S(2)}, u32[]{:S(2)}) collective-permute-start(bf16[384,384]{1,0:T(8,128)(2,1)} %bitcast.31), channel_id=1, source_target_pairs={{0,2},{1,3},{2,0},{3,1},{4,6},{5,7},{6,4},{7,5},{8,10},{9,11},{10,... | collective-permute-start | bytes 884744 | tf_op jit(solution)/shard_map/ppermute | solution.py:104
  234.0 14.3 %collective-permute-start.19 = (bf16[480,384]{1,0:T(8,128)(2,1)S(1)}, bf16[480,384]{1,0:T(8,128)(2,1)S(1)}, u32[]{:S(2)}, u32[]{:S(2)}) collective-permute-start(bf16[480,384]{1,0:T(8,128)(2,1)S(1)} %pad_maximum_fusion.8), channel_id=1, source_target_pairs={{0,4},{1,5},{2,6},{3,7},{4,0},{5,1},{6,2},{7,3},{8,12},{9,13},{10,... | collective-permute-start | bytes 1105928 | tf_op jit(solution)/shard_map/ppermute | solution.py:104
  235.6 12.7 %collective-permute-start.18 = (bf16[480,384]{1,0:T(8,128)(2,1)S(1)}, bf16[480,384]{1,0:T(8,128)(2,1)S(1)}, u32[]{:S(2)}, u32[]{:S(2)}) collective-permute-start(bf16[480,384]{1,0:T(8,128)(2,1)S(1)} %pad_maximum_fusion.7), channel_id=1, source_target_pairs={{0,2},{1,3},{2,0},{3,1},{4,6},{5,7},{6,4},{7,5},{8,10},{9,11},{10,... | collective-permute-start | bytes 1105928 | tf_op jit(solution)/shard_map/ppermute | solution.py:104
  245.2 10.9 %collective-permute-start.17 = (bf16[192,768]{1,0:T(8,128)(2,1)S(1)}, bf16[192,768]{1,0:T(8,128)(2,1)S(1)}, u32[]{:S(2)}, u32[]{:S(2)}) collective-permute-start(bf16[192,768]{1,0:T(8,128)(2,1)S(1)} %bitcast.274), channel_id=1, source_target_pairs={{0,8},{1,9},{2,10},{3,11},{4,12},{5,13},{6,14},{7,15},{8,0},{9,1},... | collective-permute-start | bytes 884744 | tf_op jit(solution)/shard_map/ppermute | solution.py:104
  248.7 16.9 %collective-permute-start.21 = (bf16[240,768]{1,0:T(8,128)(2,1)S(1)}, bf16[240,768]{1,0:T(8,128)(2,1)S(1)}, u32[]{:S(2)}, u32[]{:S(2)}) collective-permute-start(bf16[240,768]{1,0:T(8,128)(2,1)S(1)} %pad_maximum_fusion.9), channel_id=1, source_target_pairs={{0,8},{1,9},{2,10},{3,11},{4,12},{5,13},{6,14},{7,15},{8,0},{9,1},... | collective-permute-start | bytes 1105928 | tf_op jit(solution)/shard_map/ppermute | solution.py:104
  256.2 16.6 %collective-permute-start.20 = (bf16[96,768]{1,0:T(8,128)(2,1)S(1)}, bf16[96,768]{1,0:T(8,128)(2,1)S(1)}, u32[]{:S(2)}, u32[]{:S(2)}) collective-permute-start(bf16[96,768]{1,0:T(8,128)(2,1)S(1)} %fusion.38), channel_id=1, source_target_pairs={{0,16},{1,17},{2,18},{3,19},{4,20},{5,21},{6,22},{7,23},{8,24},{9,... | collective-permute-start | bytes 442376 | tf_op jit(solution)/shard_map/ppermute | solution.py:104
  265.8 9.0 %collective-permute-start.22 = (bf16[120,768]{1,0:T(8,128)(2,1)S(1)}, bf16[120,768]{1,0:T(8,128)(2,1)S(1)}, u32[]{:S(2)}, u32[]{:S(2)}) collective-permute-start(bf16[120,768]{1,0:T(8,128)(2,1)S(1)} %pad_maximum_fusion.11), channel_id=1, source_target_pairs={{0,16},{1,17},{2,18},{3,19},{4,20},{5,21},{6,22},{7,23},{8,24},{9,... | collective-permute-start | bytes 552968 | tf_op jit(solution)/shard_map/ppermute | solution.py:104
  275.0 27.7 %collective-permute-start.23 = (f32[216,768]{1,0:T(8,128)S(1)}, f32[216,768]{1,0:T(8,128)S(1)}, u32[]{:S(2)}, u32[]{:S(2)}) collective-permute-start(f32[216,768]{1,0:T(8,128)S(1)} %pad_maximum_fusion.2.own_ref), channel_id=1, source_target_pairs={{0,2},{1,3},{2,0},{3,1},{4,6},{5,7},{6,4},{7,5},{8,10},{9,11},{10,... | collective-permute-start | bytes 1990664 | tf_op jit(solution)/shard_map/ppermute | solution.py:104
  304.4 4.6 collective-permute-start.26
  304.5 3.6 collective-permute-start.24
  305.0 4.1 collective-permute-start.25
  309.7 14.1 %collective-permute-start.27 = (f32[2,2,86,384]{3,1,2,0:T(2,128)S(1)}, f32[2,2,86,384]{3,1,2,0:T(2,128)S(1)}, u32[]{:S(2)}, u32[]{:S(2)}) collective-permute-start(f32[2,2,86,384]{3,1,2,0:T(2,128)S(1)} %bitcast.266), channel_id=1, source_target_pairs={{0,4},{1,5},{2,6},{3,7},{4,0},{5,1},{6,2},{7,3},{8,12},{9,13},{10,... | collective-permute-start | bytes 1585160 | tf_op jit(solution)/shard_map/ppermute | solution.py:104
  324.1 16.8 %collective-permute-start.28 = (f32[384,256]{1,0:T(8,128)S(1)}, f32[384,256]{1,0:T(8,128)S(1)}, u32[]{:S(2)}, u32[]{:S(2)}) collective-permute-start(f32[384,256]{1,0:T(8,128)S(1)} %dynamic-slice_bitcast_fusion.1), channel_id=1, source_target_pairs={{0,4},{1,5},{2,6},{3,7},{4,0},{5,1},{6,2},{7,3},{8,12},{9,13},{10,... | collective-permute-start | bytes 1179656 | tf_op jit(solution)/shard_map/ppermute | solution.py:104
  325.0 15.8 %collective-permute-start.29 = (f32[384,256]{1,0:T(8,128)S(1)}, f32[384,256]{1,0:T(8,128)S(1)}, u32[]{:S(2)}, u32[]{:S(2)}) collective-permute-start(f32[384,256]{1,0:T(8,128)S(1)} %dynamic-slice_bitcast_fusion), channel_id=1, source_target_pairs={{0,8},{1,9},{2,10},{3,11},{4,12},{5,13},{6,14},{7,15},{8,0},{9,1},... | collective-permute-start | bytes 1179656 | tf_op jit(solution)/shard_map/ppermute | solution.py:104
  325.2 15.6 %collective-permute-start.30 = (f32[2,86,384]{2,1,0:T(8,128)S(1)}, f32[2,86,384]{2,1,0:T(8,128)S(1)}, u32[]{:S(2)}, u32[]{:S(2)}) collective-permute-start(f32[2,86,384]{2,1,0:T(8,128)S(1)} %dynamic-slice_bitcast_fusion.2), channel_id=1, source_target_pairs={{0,8},{1,9},{2,10},{3,11},{4,12},{5,13},{6,14},{7,15},{8,0},{9,1},... | collective-permute-start | bytes 792584 | tf_op jit(solution)/shard_map/ppermute | solution.py:104
  341.1 9.2 %collective-permute-start.31 = (f32[192,256]{1,0:T(8,128)S(1)}, f32[192,256]{1,0:T(8,128)S(1)}, u32[]{:S(2)}, u32[]{:S(2)}) collective-permute-start(f32[192,256]{1,0:T(8,128)S(1)} %dynamic-slice_bitcast_fusion.4), channel_id=1, source_target_pairs={{0,8},{1,9},{2,10},{3,11},{4,12},{5,13},{6,14},{7,15},{8,0},{9,1},... | collective-permute-start | bytes 589832 | tf_op jit(solution)/shard_map/ppermute | solution.py:104
  341.4 8.8 %collective-permute-start.32 = (f32[192,256]{1,0:T(8,128)S(1)}, f32[192,256]{1,0:T(8,128)S(1)}, u32[]{:S(2)}, u32[]{:S(2)}) collective-permute-start(f32[192,256]{1,0:T(8,128)S(1)} %dynamic-slice_bitcast_fusion.3), channel_id=1, source_target_pairs={{0,4},{1,5},{2,6},{3,7},{4,0},{5,1},{6,2},{7,3},{8,12},{9,13},{10,... | collective-permute-start | bytes 589832 | tf_op jit(solution)/shard_map/ppermute | solution.py:104
  342.9 7.4 %collective-permute-start.33 = (f32[86,384]{1,0:T(8,128)S(1)}, f32[86,384]{1,0:T(8,128)S(1)}, u32[]{:S(2)}, u32[]{:S(2)}) collective-permute-start(f32[86,384]{1,0:T(8,128)S(1)} %dynamic-slice_bitcast_fusion.5), channel_id=1, source_target_pairs={{0,16},{1,17},{2,18},{3,19},{4,20},{5,21},{6,22},{7,23},{8,24},{9,... | collective-permute-start | bytes 396296 | tf_op jit(solution)/shard_map/ppermute | solution.py:104
  350.4 8.9 %collective-permute-start.36 = (f32[86,384]{1,0:T(8,128)S(1)}, f32[86,384]{1,0:T(8,128)S(1)}, u32[]{:S(2)}, u32[]{:S(2)}) collective-permute-start(f32[86,384]{1,0:T(8,128)S(1)} %bitcast_add_fusion.7), channel_id=1, source_target_pairs={{0,2},{1,3},{2,0},{3,1},{4,6},{5,7},{6,4},{7,5},{8,10},{9,11},{10,... | collective-permute-start | bytes 396296 | tf_op jit(solution)/shard_map/ppermute | solution.py:104
  351.1 6.2 %collective-permute-start.34 = (f32[96,256]{1,0:T(8,128)S(1)}, f32[96,256]{1,0:T(8,128)S(1)}, u32[]{:S(2)}, u32[]{:S(2)}) collective-permute-start(f32[96,256]{1,0:T(8,128)S(1)} %dynamic-slice_bitcast_fusion.7), channel_id=1, source_target_pairs={{0,16},{1,17},{2,18},{3,19},{4,20},{5,21},{6,22},{7,23},{8,24},{9,... | collective-permute-start | bytes 294920 | tf_op jit(solution)/shard_map/ppermute | solution.py:104
  352.0 7.4 %collective-permute-start.35 = (f32[96,256]{1,0:T(8,128)S(1)}, f32[96,256]{1,0:T(8,128)S(1)}, u32[]{:S(2)}, u32[]{:S(2)}) collective-permute-start(f32[96,256]{1,0:T(8,128)S(1)} %dynamic-slice_bitcast_fusion.6), channel_id=1, source_target_pairs={{0,16},{1,17},{2,18},{3,19},{4,20},{5,21},{6,22},{7,23},{8,24},{9,... | collective-permute-start | bytes 294920 | tf_op jit(solution)/shard_map/ppermute | solution.py:104
  360.4 10.1 %collective-permute-start.39 = (f32[70,838]{1,0:T(8,128)S(1)}, f32[70,838]{1,0:T(8,128)S(1)}, u32[]{:S(2)}, u32[]{:S(2)}) collective-permute-start(f32[70,838]{1,0:T(8,128)S(1)} %fusion.15), channel_id=1, source_target_pairs={{0,4},{1,5},{2,6},{3,7},{4,0},{5,1},{6,2},{7,3},{8,12},{9,13},{10,... | collective-permute-start | bytes 703928 | tf_op jit(solution)/shard_map/ppermute | solution.py:104
  362.9 5.7 %collective-permute-start.37 = (f32[96,256]{1,0:T(8,128)S(1)}, f32[96,256]{1,0:T(8,128)S(1)}, u32[]{:S(2)}, u32[]{:S(2)}) collective-permute-start(f32[96,256]{1,0:T(8,128)S(1)} %bitcast_add_fusion.9), channel_id=1, source_target_pairs={{0,16},{1,17},{2,18},{3,19},{4,20},{5,21},{6,22},{7,23},{8,24},{9,... | collective-permute-start | bytes 294920 | tf_op jit(solution)/shard_map/ppermute | solution.py:104
  362.9 7.6 %collective-permute-start.38 = (f32[96,256]{1,0:T(8,128)S(1)}, f32[96,256]{1,0:T(8,128)S(1)}, u32[]{:S(2)}, u32[]{:S(2)}) collective-permute-start(f32[96,256]{1,0:T(8,128)S(1)} %bitcast_add_fusion.8), channel_id=1, source_target_pairs={{0,16},{1,17},{2,18},{3,19},{4,20},{5,21},{6,22},{7,23},{8,24},{9,... | collective-permute-start | bytes 294920 | tf_op jit(solution)/shard_map/ppermute | solution.py:104
  370.6 16.4 %collective-permute-start.42 = (f32[70,838]{1,0:T(8,128)S(1)}, f32[70,838]{1,0:T(8,128)S(1)}, u32[]{:S(2)}, u32[]{:S(2)}) collective-permute-start(f32[70,838]{1,0:T(8,128)S(1)} %add.478), channel_id=1, source_target_pairs={{0,8},{1,9},{2,10},{3,11},{4,12},{5,13},{6,14},{7,15},{8,0},{9,1},... | collective-permute-start | bytes 703928 | tf_op jit(solution)/shard_map/ppermute | solution.py:104
  374.0 13.0 %collective-permute-start.40 = (f32[192,256]{1,0:T(8,128)S(1)}, f32[192,256]{1,0:T(8,128)S(1)}, u32[]{:S(2)}, u32[]{:S(2)}) collective-permute-start(f32[192,256]{1,0:T(8,128)S(1)} %maximum_select_fusion.4), channel_id=1, source_target_pairs={{0,8},{1,9},{2,10},{3,11},{4,12},{5,13},{6,14},{7,15},{8,0},{9,1},... | collective-permute-start | bytes 589832 | tf_op jit(solution)/shard_map/ppermute | solution.py:104
  374.1 12.9 %collective-permute-start.41 = (f32[192,256]{1,0:T(8,128)S(1)}, f32[192,256]{1,0:T(8,128)S(1)}, u32[]{:S(2)}, u32[]{:S(2)}) collective-permute-start(f32[192,256]{1,0:T(8,128)S(1)} %maximum_select_fusion.5), channel_id=1, source_target_pairs={{0,4},{1,5},{2,6},{3,7},{4,0},{5,1},{6,2},{7,3},{8,12},{9,13},{10,... | collective-permute-start | bytes 589832 | tf_op jit(solution)/shard_map/ppermute | solution.py:104
  387.2 14.4 %collective-permute-start.43 = (f32[384,256]{1,0:T(8,128)S(1)}, f32[384,256]{1,0:T(8,128)S(1)}, u32[]{:S(2)}, u32[]{:S(2)}) collective-permute-start(f32[384,256]{1,0:T(8,128)S(1)} %maximum_select_fusion.2), channel_id=1, source_target_pairs={{0,4},{1,5},{2,6},{3,7},{4,0},{5,1},{6,2},{7,3},{8,12},{9,13},{10,... | collective-permute-start | bytes 1179656 | tf_op jit(solution)/shard_map/ppermute | solution.py:104
  387.3 14.3 %collective-permute-start.44 = (f32[384,256]{1,0:T(8,128)S(1)}, f32[384,256]{1,0:T(8,128)S(1)}, u32[]{:S(2)}, u32[]{:S(2)}) collective-permute-start(f32[384,256]{1,0:T(8,128)S(1)} %maximum_select_fusion.3), channel_id=1, source_target_pairs={{0,8},{1,9},{2,10},{3,11},{4,12},{5,13},{6,14},{7,15},{8,0},{9,1},... | collective-permute-start | bytes 1179656 | tf_op jit(solution)/shard_map/ppermute | solution.py:104
  390.8 10.7 %collective-permute-start.45 = (f32[70,838]{1,0:T(8,128)S(1)}, f32[70,838]{1,0:T(8,128)S(1)}, u32[]{:S(2)}, u32[]{:S(2)}) collective-permute-start(f32[70,838]{1,0:T(8,128)S(1)} %add.479), channel_id=1, source_target_pairs={{0,16},{1,17},{2,18},{3,19},{4,20},{5,21},{6,22},{7,23},{8,24},{9,... | collective-permute-start | bytes 703928 | tf_op jit(solution)/shard_map/ppermute | solution.py:104
  442.1 10.2 %collective-permute-start.47 = (bf16[384,768]{1,0:T(8,128)(2,1)}, bf16[384,768]{1,0:T(8,128)(2,1)}, u32[]{:S(2)}, u32[]{:S(2)}) collective-permute-start(bf16[384,768]{1,0:T(8,128)(2,1)} %newton.1.refs_0_), channel_id=1, source_target_pairs={{0,2},{1,3},{2,0},{3,1},{4,6},{5,7},{6,4},{7,5},{8,10},{9,11},{10,... | collective-permute-start | bytes 1769480 | tf_op jit(solution)/shard_map/ppermute | solution.py:104
  444.4 9.2 %collective-permute-start.46 = (bf16[384,768]{1,0:T(8,128)(2,1)}, bf16[384,768]{1,0:T(8,128)(2,1)S(1)}, u32[]{:S(2)}, u32[]{:S(2)}) collective-permute-start(bf16[384,768]{1,0:T(8,128)(2,1)} %newton.1.refs_0_), channel_id=1, source_target_pairs={{0,1},{1,0},{2,3},{3,2},{4,5},{5,4},{6,7},{7,6},{8,9},{9,8},{10,11... | collective-permute-start | bytes 1769480 | tf_op jit(solution)/shard_map/ppermute | solution.py:104
  (116 other events, 1034.9 us)
Sparse Core Ops, SparseCore 0:
  11.6 94.4 all-gather.4
  143.3 62.8 all-gather.6
